TPU v7x, 32 devices: a whole 2x2x4 slice. The times are simulated.
32 devices in a mesh: groups: 2 (over y), wloop: 4 (over z), items: 4 (over x, core).
Axes of the slice: x: 2, y: 2, z: 4, core: 2. Of those that a mesh axis runs over, the one named last changes fastest.
Arguments:
- features: bfloat16 [2048, 16384], P(('groups', 'items'), 'wloop'), parts along dimension 0, may hold values from -6 to 6
- cotangent: bfloat16 [2048, 16384], P(('groups', 'items'), 'wloop'), parts along dimension 0, may hold values from -6 to 6
- block_weights: bfloat16 [256, 256, 256], P('wloop'), may hold values from -0.1875 to 0.1875
- block_rows: int32 [256], P('wloop'), may hold values from 0 to 63, as said below
- block_cols: int32 [256], P('wloop'), may hold values from 0 to 63, as said below
- lowrank_in: bfloat16 [128, 16384], P(None, 'wloop'), may hold values from -0.046875 to 0.046875
- lowrank_out: bfloat16 [128, 16384], P(None, 'wloop'), may hold values from -0.5 to 0.5
Outputs:
- mixed: bfloat16 [2048, 16384], P(('groups', 'items'), 'wloop'), parts along dimension 0
- block_grads: float32 [512, 256, 256], P(('groups', 'items'), 'wloop'), parts along dimension 0
- grad_in: float32 [256, 16384], P(('groups', 'items'), 'wloop'), parts along dimension 0
- grad_out: float32 [256, 16384], P(('groups', 'items'), 'wloop'), parts along dimension 0
There are 2 independent parts, one for each index of `groups`. A program takes and returns all parts, laid end to end along the dimension named above; an argument that names none is the same for every part. Nothing has to cross between parts.
Inputs may be any that keep to these rules, and one draw needn't show every extreme that they name: `block_rows`: the stored blocks form a strided block pattern: every input block column c appears in exactly 4 stored blocks, whose output blocks are c, c xor 1, c xor (16) and c xor (32); the stored blocks on one index of wloop are exactly those of its 16 input block columns, in an order drawn afresh. `block_cols`: the input block column of each stored block, as described for block_rows; the stored blocks on one index of wloop have input columns within that index's range of 16 columns.
All inputs are finite; a program needn't handle non-finite values.
Results may differ from a plain program's by a relative error of at most 0.0039.
Values may be sent and summed in bfloat16 or wider, within the bound.
No kernel may reach another device: no remote copies, remote signals or barrier semaphores. Data moves between devices by JAX's collectives and lax.ppermute only.
A program may use at most 128 MiB of HBM per device.

v0:
```python
import functools

import jax
import jax.numpy as jnp
from jax import lax
from jax.experimental import pallas as pl
from jax.experimental.pallas import tpu as pltpu
from jax.sharding import PartitionSpec as P


WIDTH = 16384
BLOCK = 256
CHUNKS = 4


F32 = jnp.float32
BF16 = jnp.bfloat16


def swapped(block, axis, apart):
    count = lax.axis_size(axis)
    return lax.ppermute(block, axis, [(one, one ^ (1 << apart)) for one in range(count)])


def pick(values, index, dim):
    return lax.dynamic_index_in_dim(values, index, dim, keepdims=False)


def grad_body(pairs, part, bit_ref, g_ref, *refs):
    f_refs, (send_ref, keep_ref, acc_ref) = refs[:-3], refs[-3:]
    bit = bit_ref[0]
    blocks = g_ref.shape[1] // BLOCK
    halves = send_ref.shape[0]
    for at in range(blocks):
        for slot, (f_at, flip) in enumerate(pairs):
            g_at = at ^ flip
            acc_ref[...] = lax.dot_general(
                g_ref[:, g_at * BLOCK : (g_at + 1) * BLOCK],
                f_refs[f_at][:, at * BLOCK : (at + 1) * BLOCK],
                (((0,), (0,)), ((), ())),
                preferred_element_type=F32,
            )
            for half in range(halves):
                first = pl.multiple_of((2 * half + bit) * part, part)
                other = pl.multiple_of((2 * half + 1 - bit) * part, part)
                keep_ref[half, slot, at] = acc_ref[pl.ds(first, part), :]
                send_ref[half, slot, at] = acc_ref[pl.ds(other, part), :].astype(BF16)


def pair_grads(bit, cotangent, features, pairs, first, count, parts):
    rows_here = cotangent.shape[0]
    part = BLOCK // parts
    step = min(2, count)
    shape = (parts // 2, 2, count, part, BLOCK)
    block = (parts // 2, 2, step, part, BLOCK)
    out_spec = pl.BlockSpec(block, lambda at, bit_ref: (0, 0, at, 0, 0))
    skip = first // step
    return pl.pallas_call(
        functools.partial(grad_body, pairs, part),
        grid_spec=pltpu.PrefetchScalarGridSpec(
            num_scalar_prefetch=1,
            grid=(count // step,),
            in_specs=[pl.BlockSpec((rows_here, step * BLOCK), lambda at, bit_ref: (0, at + skip))]
            + [pl.BlockSpec((rows_here, step * BLOCK), lambda at, bit_ref: (0, at))] * len(features),
            out_specs=(out_spec, out_spec),
            scratch_shapes=[pltpu.VMEM((BLOCK, BLOCK), F32)],
        ),
        out_shape=(jax.ShapeDtypeStruct(shape, BF16), jax.ShapeDtypeStruct(shape, F32)),
        cost_estimate=pl.CostEstimate(
            flops=4 * count * rows_here * BLOCK * BLOCK,
            bytes_accessed=count * BLOCK * (2 * rows_here * 3 + 6 * BLOCK),
            transcendentals=0,
        ),
        name="pair_grads",
    )(bit, cotangent, *features)


def low_body(part, bit_ref, b_ref, f_ref, c_ref, g_ref, send_ref, keep_ref, acc_ref):
    bit = bit_ref[0]
    for slot, (small, wide) in enumerate(((b_ref, f_ref), (c_ref, g_ref))):
        acc_ref[...] = lax.dot_general(
            small[...], wide[...], (((0,), (0,)), ((), ())), preferred_element_type=F32
        )
        for half in range(send_ref.shape[0]):
            first = pl.multiple_of((2 * half + bit) * part, part)
            other = pl.multiple_of((2 * half + 1 - bit) * part, part)
            keep_ref[half, slot] = acc_ref[pl.ds(first, part), :]
            send_ref[half, slot] = acc_ref[pl.ds(other, part), :].astype(BF16)


def low_kernel(bit, backs, features, codes, cotangent, parts):
    rows_here, width = features.shape
    rank = codes.shape[1]
    part = rank // parts
    step = min(1024, width)
    out_spec = pl.BlockSpec((parts // 2, 2, part, step), lambda at, bit_ref: (0, 0, 0, at))
    shape = (parts // 2, 2, part, width)
    wide = pl.BlockSpec((rows_here, step), lambda at, bit_ref: (0, at))
    small = pl.BlockSpec((rows_here, rank), lambda at, bit_ref: (0, 0))
    return pl.pallas_call(
        functools.partial(low_body, part),
        grid_spec=pltpu.PrefetchScalarGridSpec(
            num_scalar_prefetch=1,
            grid=(width // step,),
            in_specs=[small, wide, small, wide],
            out_specs=(out_spec, out_spec),
            scratch_shapes=[pltpu.VMEM((rank, step), F32)],
        ),
        out_shape=(jax.ShapeDtypeStruct(shape, BF16), jax.ShapeDtypeStruct(shape, F32)),
        cost_estimate=pl.CostEstimate(
            flops=4 * rank * rows_here * width,
            bytes_accessed=width * (4 * rows_here + 6 * rank),
            transcendentals=0,
        ),
        name="low_grads",
    )(bit, backs, features, codes, cotangent)


def items_sum(send, keep, index):
    bits = lax.axis_size("items").bit_length() - 1
    came = swapped(send, "items", 0)
    for level in range(1, bits):
        mine = (index >> level) & 1
        shape = (keep.shape[0] // 2, 2, *keep.shape[1:])
        keep, came = keep.reshape(shape), came.reshape(shape)
        leave = pick(keep, 1 - mine, 1) + pick(came, 1 - mine, 1).astype(F32)
        keep = pick(keep, mine, 1) + pick(came, mine, 1).astype(F32)
        came = swapped(leave.astype(BF16), "items", level)
    return (keep + came.astype(F32))[0]


def share_body(share, units, unit, pos_ref, item_ref, w_ref, out_ref, sems):
    pieces = BLOCK // unit
    copies = []
    for way in range(2):
        for one in range(units):
            number = item_ref[0] * units + one
            block = pos_ref[(2 + way) * share + lax.div(number, pieces)]
            first = pl.multiple_of(lax.rem(number, pieces) * unit, unit)
            copies.append(
                pltpu.make_async_copy(
                    w_ref.at[block, pl.ds(first, unit), :],
                    out_ref.at[way, one],
                    sems.at[way * units + one],
                )
            )
    for copy in copies:
        copy.start()
    for copy in copies:
        copy.wait()


def weight_share(block_weights, pos, item, share, unit, units):
    return pl.pallas_call(
        functools.partial(share_body, share, units, unit),
        in_specs=[
            pl.BlockSpec(memory_space=pltpu.SMEM),
            pl.BlockSpec(memory_space=pltpu.SMEM),
            pl.BlockSpec(memory_space=pl.ANY),
        ],
        out_specs=pl.BlockSpec(memory_space=pltpu.VMEM),
        out_shape=jax.ShapeDtypeStruct((2, units, unit, BLOCK), BF16),
        scratch_shapes=[pltpu.SemaphoreType.DMA((2 * units,))],
        cost_estimate=pl.CostEstimate(
            flops=0, bytes_accessed=8 * units * unit * BLOCK, transcendentals=0
        ),
        name="weight_share",
    )(pos, item, block_weights)


def mixed_body(share, chunks, units, unit, bits, pos_ref, item_ref, f_ref, w_ref, codes_ref, low_ref, *refs):
    far_refs, refs = refs[: 2 * chunks], refs[2 * chunks :]
    far_w, out_ref = refs[:2], refs[2]
    f_buf, low_buf, far_bufs, w_buf, out_buf, in_sems, w_sems, out_sems = (
        refs[3],
        refs[4],
        refs[5],
        refs[6],
        refs[7],
        refs[8],
        refs[9],
        refs[10],
    )
    dims = (((1,), (1,)), ((), ()))
    pieces = BLOCK // unit
    per = share // chunks
    wide = per * BLOCK
    item = item_ref[0]

    def slot_of(number):
        apart = lax.div(number, units) ^ item
        slot = jnp.int32(0)
        for level in range(bits):
            slot = slot * 2 + ((apart >> level) & 1)
        return slot * units + lax.rem(number, units)

    loads, weights = [], []
    for chunk in range(chunks):
        cols = pl.ds(chunk * wide, wide)
        loads.append(
            [
                pltpu.make_async_copy(f_ref.at[:, cols], f_buf.at[:, cols], in_sems.at[chunk, 0]),
                pltpu.make_async_copy(low_ref.at[:, cols], low_buf.at[:, cols], in_sems.at[chunk, 1]),
            ]
            + [
                pltpu.make_async_copy(
                    far_refs[way * chunks + chunk], far_bufs.at[way, chunk], in_sems.at[chunk, 2 + way]
                )
                for way in range(2)
            ]
        )
        chunk_weights = []
        for at in range(chunk * per, (chunk + 1) * per):
            chunk_weights.append(
                pltpu.make_async_copy(w_ref.at[pos_ref[at]], w_buf.at[0, at], w_sems.at[0, at, 0])
            )
            chunk_weights.append(
                pltpu.make_async_copy(
                    w_ref.at[pos_ref[share + (at ^ 1)]], w_buf.at[1, at], w_sems.at[1, at, 0]
                )
            )
            for way in range(2):
                for piece in range(pieces):
                    chunk_weights.append(
                        pltpu.make_async_copy(
                            far_w[way].at[slot_of(jnp.int32(at * pieces + piece))],
                            w_buf.at[2 + way, at, pl.ds(piece * unit, unit), :],
                            w_sems.at[2 + way, at, piece],
                        )
                    )
        weights.append(chunk_weights)
    for chunk in range(chunks):
        for copy in loads[chunk] + weights[chunk]:
            copy.start()
    stores = []
    for chunk in range(chunks):
        for copy in loads[chunk] + weights[chunk]:
            copy.wait()
        for at in range(chunk * per, (chunk + 1) * per):
            own = slice(at * BLOCK, (at + 1) * BLOCK)
            flip = slice((at ^ 1) * BLOCK, ((at ^ 1) + 1) * BLOCK)
            local = slice((at - chunk * per) * BLOCK, (at - chunk * per + 1) * BLOCK)
            total = lax.dot_general(f_buf[:, own], w_buf[0, at], dims, preferred_element_type=F32)
            total += lax.dot_general(f_buf[:, flip], w_buf[1, at], dims, preferred_element_type=F32)
            for way in range(2):
                total += lax.dot_general(
                    far_bufs[way, chunk, :, local],
                    w_buf[2 + way, at],
                    dims,
                    preferred_element_type=F32,
                )
            total += jnp.dot(codes_ref[...], low_buf[:, own], preferred_element_type=F32)
            out_buf[:, own] = total.astype(BF16)
        cols = pl.ds(chunk * wide, wide)
        store = pltpu.make_async_copy(out_buf.at[:, cols], out_ref.at[:, cols], out_sems.at[chunk])
        store.start()
        stores.append(store)
    for store in stores:
        store.wait()


def mixed_kernel(features, block_weights, codes, lowrank_out, far, far_weights, pos, item, units, bits):
    rows_here, width = features.shape
    share = width // BLOCK
    chunks = len(far[0])
    unit = far_weights[0].shape[1]
    hbm = pl.BlockSpec(memory_space=pl.ANY)
    smem = pl.BlockSpec(memory_space=pltpu.SMEM)
    return pl.pallas_call(
        functools.partial(mixed_body, share, chunks, units, unit, bits),
        in_specs=[smem, smem, hbm, hbm, pl.BlockSpec(memory_space=pltpu.VMEM), hbm]
        + [hbm] * (2 * chunks + 2),
        out_specs=hbm,
        out_shape=jax.ShapeDtypeStruct((rows_here, width), BF16),
        scratch_shapes=[
            pltpu.VMEM((rows_here, width), BF16),
            pltpu.VMEM(lowrank_out.shape, BF16),
            pltpu.VMEM((2, chunks, rows_here, width // chunks), BF16),
            pltpu.VMEM((4, share, BLOCK, BLOCK), BF16),
            pltpu.VMEM((rows_here, width), BF16),
            pltpu.SemaphoreType.DMA((chunks, 4)),
            pltpu.SemaphoreType.DMA((4, share, BLOCK // unit)),
            pltpu.SemaphoreType.DMA((chunks,)),
        ],
        cost_estimate=pl.CostEstimate(
            flops=9 * share * rows_here * BLOCK * BLOCK,
            bytes_accessed=share * BLOCK * 2 * (4 * rows_here + 4 * BLOCK),
            transcendentals=0,
        ),
        name="mixed",
    )(pos, item, features, block_weights, codes, lowrank_out, *far[0], *far[1], *far_weights)


def place_body(share, chunks, pos_ref, own_ref, *refs):
    far_refs, out_ref = refs[:-1], refs[-1]
    per = share // chunks
    for way in range(4):
        for at in range(share):
            if way < 2:
                block = own_ref[way, at]
            else:
                block = far_refs[(way - 2) * chunks + at // per][at % per].astype(F32)
            out_ref[:, pos_ref[way * share + at], :] = block


def place_kernel(own, far, pos):
    _, share, part, _ = own.shape
    chunks = len(far[0])
    per = share // chunks
    rows = 16
    far_spec = pl.BlockSpec((per, rows, BLOCK), lambda at, pos_ref: (0, at, 0))
    return pl.pallas_call(
        functools.partial(place_body, share, chunks),
        grid_spec=pltpu.PrefetchScalarGridSpec(
            num_scalar_prefetch=1,
            grid=(part // rows,),
            in_specs=[pl.BlockSpec((2, share, rows, BLOCK), lambda at, pos_ref: (0, 0, at, 0))]
            + [far_spec] * (2 * chunks),
            out_specs=pl.BlockSpec((rows, 4 * share, BLOCK), lambda at, pos_ref: (at, 0, 0)),
        ),
        out_shape=jax.ShapeDtypeStruct((part, 4 * share, BLOCK), F32),
        cost_estimate=pl.CostEstimate(
            flops=0, bytes_accessed=32 * share * part * BLOCK, transcendentals=0
        ),
        name="place",
    )(pos, own, *far[0], *far[1])


def layer(features, cotangent, block_weights, block_rows, block_cols, lowrank_in, lowrank_out):
    _, width = features.shape
    share = width // BLOCK
    count = WIDTH // BLOCK
    stored = block_weights.shape[0]
    chunks = min(CHUNKS, share)
    per = share // chunks
    items = lax.axis_size("items")
    item = lax.axis_index("items").astype(jnp.int32)
    item_arg = item.reshape(1)
    bits = items.bit_length() - 1
    place = lax.axis_index("wloop")
    way_bits = lax.axis_size("wloop").bit_length() - 1
    far_bits = (way_bits - 2, way_bits - 1)

    def hop(value, bit):
        return swapped(value, "wloop", bit)

    stride_of = jnp.bitwise_xor(block_rows, block_cols)
    stride_id = (stride_of == 1) * 1 + (stride_of == count // 4) * 2 + (stride_of == count // 2) * 3
    key = stride_id * share + block_cols % share
    pos = jnp.sum(
        jnp.where(
            key[None, :] == jnp.arange(4 * share, dtype=jnp.int32)[:, None],
            jnp.arange(stored, dtype=jnp.int32)[None, :],
            0,
        ),
        axis=1,
    ).astype(jnp.int32)

    far = [[], []]
    for one in range(chunks):
        piece = lax.optimization_barrier(features[:, one * per * BLOCK : (one + 1) * per * BLOCK])
        for way in range(2):
            far[way].append(hop(piece, far_bits[way]))

    unit = min(BLOCK, share * BLOCK // items)
    units = share * BLOCK // items // unit
    shares = weight_share(block_weights, pos, item_arg, share, unit, units)
    far_weights = []
    for way in range(2):
        held = hop(shares[way], far_bits[way])
        for level in range(bits - 1, -1, -1):
            held = jnp.concatenate([held, swapped(held, "items", level)], axis=0)
        far_weights.append(held)

    dims = (((1,), (1,)), ((), ()))
    codes = jnp.stack(
        [
            lax.dot_general(features, lowrank_in, dims, preferred_element_type=F32),
            lax.dot_general(cotangent, lowrank_out, dims, preferred_element_type=F32),
        ]
    )
    for level in range(way_bits - 1):
        mine = (place >> level) & 1
        split = codes.reshape(2, 2, codes.shape[1] // 2, codes.shape[2])
        codes = pick(split, mine, 1) + hop(pick(split, 1 - mine, 1), level)
    codes = codes + hop(codes, way_bits - 1)
    codes = codes.astype(BF16)
    for level in range(way_bits - 2, -1, -1):
        mine = (place >> level) & 1
        other = hop(codes, level)
        codes = jnp.where(
            mine == 0,
            jnp.concatenate([codes, other], axis=1),
            jnp.concatenate([other, codes], axis=1),
        )
    codes, backs = codes[0], codes[1]

    bit = item_arg & 1
    own = pair_grads(bit, cotangent, [features], ((0, 0), (0, 1)), 0, share, items)
    own = items_sum(*own, item)
    returned = [[], []]
    for one in range(chunks):
        pairs = pair_grads(
            bit,
            cotangent,
            [far[0][one], far[1][one]],
            ((0, 0), (1, 0)),
            one * per,
            per,
            items,
        )
        done = items_sum(*pairs, item).astype(BF16)
        for way in range(2):
            returned[way].append(hop(done[way], far_bits[way]))

    low = items_sum(*low_kernel(bit, backs, features, codes, cotangent, items), item)

    mixed = mixed_kernel(
        features,
        block_weights,
        codes,
        lowrank_out,
        far,
        far_weights,
        pos,
        item_arg,
        units,
        bits,
    )
    block_grads = place_kernel(own, returned, pos)
    return (mixed, block_grads, low[0], low[1])


def solution(mesh):
    return jax.shard_map(
        layer,
        mesh=mesh,
        in_specs=(
            P(("groups", "items"), "wloop"),
            P(("groups", "items"), "wloop"),
            P("wloop", None, None),
            P("wloop"),
            P("wloop"),
            P(None, "wloop"),
            P(None, "wloop"),
        ),
        out_specs=(
            P(("groups", "items"), "wloop"),
            P(("groups", "items"), "wloop", None),
            P(("groups", "items"), "wloop"),
            P(("groups", "items"), "wloop"),
        ),
        check_vma=False,
    )
```

profile of v0, /device:TPU:0, one launch (start us, length us, event | category | flops | bytes accessed | tf_op | source)
XLA Modules:
  0.0 277.3 jit_solution(1744578009467193303)
XLA Ops:
  0.7 1.2 copy-done
  1.9 2.4 fusion.11
  4.3 0.7 fusion.12
  5.0 3.1 %collective-permute-start = (f32[2,128,128]{2,1,0:T(8,128)S(1)}, f32[2,128,128]{2,1,0:T(8,128)S(1)}, u32[]{:S(2)}, u32[]{:S(2)}) collective-permute-start(f32[2,128,128]{2,1,0:T(8,128)S(1)} %fusion.1), channel_id=1, source_target_pairs={{0,4},{4,0},{8,12},{12,8},{1,5},{5,1},{9,13},{13,9},{2,6},{6,2},{1... | collective-permute-start | bytes 393224 | tf_op jit(solution)/shard_map/ppermute | solution.py:22
  8.2 0.7 select_reduce_fusion.pos_ref
  8.9 3.0 %weight_share.1 = bf16[2,4,256,256]{3,2,1,0:T(8,128)(2,1)} custom-call(s32[64]{0:T(128)} %select_reduce_fusion.pos_ref, s32[1]{0:T(128)} %bitcast.item_ref, bf16[64,256,256]{2,1,0:T(8,128)(2,1)} %w_ref.3), custom_call_target="tpu_custom_call" | custom-call | bytes 2097152 | tf_op jit(solution)/shard_map/weight_share/pallas_call | solution.py:154
  11.9 2.4 slice_bitcast_fusion.2
  14.3 2.6 collective-permute-start.14
  17.3 1.2 fusion.10
  18.5 2.6 collective-permute-start.9
  21.4 2.6 collective-permute-start.7
  24.0 55.3 %collective-permute-done.1 = f32[2,128,128]{2,1,0:T(8,128)S(1)} collective-permute-done((f32[2,128,128]{2,1,0:T(8,128)S(1)}, f32[2,128,128]{2,1,0:T(8,128)S(1)}, u32[]{:S(2)}, u32[]{:S(2)}) %collective-permute-start.1) | collective-permute-done | bytes 131104 | tf_op jit(solution)/shard_map/ppermute | solution.py:22
  79.3 0.9 collective-permute-start.2
  80.2 34.1 %collective-permute-done.2 = bf16[2,128,128]{2,1,0:T(8,128)(2,1)S(1)} collective-permute-done((bf16[2,128,128]{2,1,0:T(8,128)(2,1)S(1)}, bf16[2,128,128]{2,1,0:T(8,128)(2,1)S(1)}, u32[]{:S(2)}, u32[]{:S(2)}) %collective-permute-start.2) | collective-permute-done | bytes 65568 | tf_op jit(solution)/shard_map/ppermute | solution.py:22
  114.3 2.0 collective-permute-start.4
  116.4 1.9 collective-permute-start.11
  118.3 1.3 collective-permute-start.10
  119.6 20.7 %collective-permute-done.3.refs_0_ = bf16[256,1024]{1,0:T(8,128)(2,1)S(1)} collective-permute-done((bf16[256,1024]{1,0:T(8,128)(2,1)S(1)}, bf16[256,1024]{1,0:T(8,128)(2,1)S(1)}, u32[]{:S(2)}, u32[]{:S(2)}) %collective-permute-start.3) | collective-permute-done | bytes 524320 | tf_op jit(solution)/shard_map/ppermute | solution.py:22
  140.3 0.8 copy-done.10
  141.1 2.8 %pair_grads.6 = (bf16[2,2,4,64,256]{4,3,2,1,0:T(8,128)(2,1)}, f32[2,2,4,64,256]{4,3,2,1,0:T(8,128)}) custom-call(s32[1]{0:T(128)S(6)} %and.24.bit_ref, bf16[256,4096]{1,0:T(8,128)(2,1)} %g_ref.11, bf16[256,1024]{1,0:T(8,128)(2,1)} %copy-done.10, bf16[256,1024]{1,0:T(8,128)(2,1)} %copy-done.9), custom_call_target="tpu_custom_call" | custom-call | flops 268435456 | bytes 3145728 | tf_op jit(solution)/shard_map/pair_grads/pallas_call | solution.py:58
  143.9 7.6 %collective-permute-done.4.refs_1_.refs_0_ = bf16[256,1024]{1,0:T(8,128)(2,1)S(1)} collective-permute-done((bf16[256,1024]{1,0:T(8,128)(2,1)}, bf16[256,1024]{1,0:T(8,128)(2,1)S(1)}, u32[]{:S(2)}, u32[]{:S(2)}) %collective-permute-start.4) | collective-permute-done | bytes 524320 | tf_op jit(solution)/shard_map/ppermute | solution.py:22
  151.5 8.4 %pair_grads.5 = (bf16[2,2,16,64,256]{4,3,2,1,0:T(8,128)(2,1)}, f32[2,2,16,64,256]{4,3,2,1,0:T(8,128)}) custom-call(s32[1]{0:T(128)S(6)} %and.24.bit_ref, bf16[256,4096]{1,0:T(8,128)(2,1)} %g_ref.11, bf16[256,4096]{1,0:T(8,128)(2,1)} %f_ref.3), custom_call_target="tpu_custom_call" | custom-call | flops 1073741824 | bytes 12582912 | tf_op jit(solution)/shard_map/pair_grads/pallas_call | solution.py:58
  159.9 2.8 %pair_grads.7 = (bf16[2,2,4,64,256]{4,3,2,1,0:T(8,128)(2,1)}, f32[2,2,4,64,256]{4,3,2,1,0:T(8,128)}) custom-call(s32[1]{0:T(128)S(6)} %and.24.bit_ref, bf16[256,4096]{1,0:T(8,128)(2,1)} %g_ref.11, bf16[256,1024]{1,0:T(8,128)(2,1)} %copy-done.11, bf16[256,1024]{1,0:T(8,128)(2,1)} %copy-done.8), custom_call_target="tpu_custom_call" | custom-call | flops 268435456 | bytes 3145728 | tf_op jit(solution)/shard_map/pair_grads/pallas_call | solution.py:58
  163.6 2.8 %pair_grads.8 = (bf16[2,2,4,64,256]{4,3,2,1,0:T(8,128)(2,1)}, f32[2,2,4,64,256]{4,3,2,1,0:T(8,128)}) custom-call(s32[1]{0:T(128)S(6)} %and.24.bit_ref, bf16[256,4096]{1,0:T(8,128)(2,1)} %g_ref.11, bf16[256,1024]{1,0:T(8,128)(2,1)} %copy-done.12, bf16[256,1024]{1,0:T(8,128)(2,1)} %copy-done.7), custom_call_target="tpu_custom_call" | custom-call | flops 268435456 | bytes 3145728 | tf_op jit(solution)/shard_map/pair_grads/pallas_call | solution.py:58
  166.4 7.7 %collective-permute-done.11 = bf16[4,256,256]{2,1,0:T(8,128)(2,1)} collective-permute-done((bf16[4,256,256]{2,1,0:T(8,128)(2,1)}, bf16[4,256,256]{2,1,0:T(8,128)(2,1)}, u32[]{:S(2)}, u32[]{:S(2)}) %collective-permute-start.11) | collective-permute-done | bytes 524320 | tf_op jit(solution)/shard_map/ppermute | solution.py:22
  174.1 1.5 collective-permute-start.15
  175.7 0.6 slice_bitcast_fusion.12
  176.3 8.1 %collective-permute-done.6.refs_3_.refs_0_ = bf16[256,1024]{1,0:T(8,128)(2,1)} collective-permute-done((bf16[256,1024]{1,0:T(8,128)(2,1)}, bf16[256,1024]{1,0:T(8,128)(2,1)}, u32[]{:S(2)}, u32[]{:S(2)}) %collective-permute-start.6) | collective-permute-done | bytes 524320 | tf_op jit(solution)/shard_map/ppermute | solution.py:22
  184.4 1.5 collective-permute-start.12
  185.9 5.0 %low_grads.1 = (bf16[2,2,32,4096]{3,2,1,0:T(8,128)(2,1)}, f32[2,2,32,4096]{3,2,1,0:T(8,128)}) custom-call(s32[1]{0:T(128)S(6)} %and.24.bit_ref, bf16[256,128]{1,0:T(8,128)(2,1)} %get-tuple-element.44.b_ref, bf16[256,4096]{1,0:T(8,128)(2,1)} %f_ref.3, bf16[256,128]{1,0:T(8,128)(2,1)} %get-tuple-element.45.codes_ref.c_ref, bf16[256,4096]{1,0:T(8,128)(2,1)} %g_ref.11), custom_call_target="tpu_custom_call" | custom-call | flops 536870912 | bytes 7340032 | tf_op jit(solution)/shard_map/low_grads/pallas_call | solution.py:100
  191.0 2.9 %pair_grads.9 = (bf16[2,2,4,64,256]{4,3,2,1,0:T(8,128)(2,1)}, f32[2,2,4,64,256]{4,3,2,1,0:T(8,128)}) custom-call(s32[1]{0:T(128)S(6)} %and.24.bit_ref, bf16[256,4096]{1,0:T(8,128)(2,1)} %g_ref.11, bf16[256,1024]{1,0:T(8,128)(2,1)} %collective-permute-done.6.refs_3_.refs_0_, bf16[256,1024]{1,0:T(8,128)(2,1)} %collective-permute-done.10.refs_7_.refs_1_), custom_call_target="tpu_custom_call" | custom-call | flops 268435456 | bytes 3145728 | tf_op jit(solution)/shard_map/pair_grads/pallas_call | solution.py:58
  194.1 0.6 copy-done.22
  194.7 0.8 copy-done.24
  195.5 1.2 add_convert_fusion.7
  196.7 0.6 collective-permute-start.35
  197.2 1.1 pad_maximum_fusion.3
  198.9 1.1 add_convert_fusion.5
  200.2 1.4 pad_maximum_fusion.2
  201.6 1.6 collective-permute-start.23
  203.3 4.3 %collective-permute-done.20 = bf16[1,2,4,64,256]{4,3,2,1,0:T(8,128)(2,1)S(1)} collective-permute-done((bf16[1,2,4,64,256]{4,3,2,1,0:T(8,128)(2,1)S(1)}, bf16[1,2,4,64,256]{4,3,2,1,0:T(8,128)(2,1)S(1)}, u32[]{:S(2)}, u32[]{:S(2)}) %collective-permute-start.20) | collective-permute-done | bytes 262176 | tf_op jit(solution)/shard_map/ppermute | solution.py:22
  207.8 4.6 %collective-permute-done.23 = bf16[1,2,4,64,256]{4,3,2,1,0:T(8,128)(2,1)S(1)} collective-permute-done((bf16[1,2,4,64,256]{4,3,2,1,0:T(8,128)(2,1)S(1)}, bf16[1,2,4,64,256]{4,3,2,1,0:T(8,128)(2,1)S(1)}, u32[]{:S(2)}, u32[]{:S(2)}) %collective-permute-start.23) | collective-permute-done | bytes 262176 | tf_op jit(solution)/shard_map/ppermute | solution.py:22
  213.0 0.7 slice_bitcast_fusion.7
  213.8 6.1 %collective-permute-done.26 = bf16[1,2,4,64,256]{4,3,2,1,0:T(8,128)(2,1)S(1)} collective-permute-done((bf16[1,2,4,64,256]{4,3,2,1,0:T(8,128)(2,1)S(1)}, bf16[1,2,4,64,256]{4,3,2,1,0:T(8,128)(2,1)S(1)}, u32[]{:S(2)}, u32[]{:S(2)}) %collective-permute-start.26) | collective-permute-done | bytes 262176 | tf_op jit(solution)/shard_map/ppermute | solution.py:22
  220.4 1.1 add_convert_fusion.4
  221.6 1.6 collective-permute-start.36
  223.2 0.7 slice_bitcast_fusion.5
  223.8 5.2 %collective-permute-done.29 = bf16[1,2,4,64,256]{4,3,2,1,0:T(8,128)(2,1)S(1)} collective-permute-done((bf16[1,2,4,64,256]{4,3,2,1,0:T(8,128)(2,1)S(1)}, bf16[1,2,4,64,256]{4,3,2,1,0:T(8,128)(2,1)S(1)}, u32[]{:S(2)}, u32[]{:S(2)}) %collective-permute-start.29) | collective-permute-done | bytes 262176 | tf_op jit(solution)/shard_map/ppermute | solution.py:22
  229.1 1.4 collective-permute-start.31
  230.6 0.8 slice_bitcast_fusion.4
  231.3 6.4 %collective-permute-done.36 = bf16[1,2,32,4096]{3,2,1,0:T(8,128)(2,1)S(1)} collective-permute-done((bf16[1,2,32,4096]{3,2,1,0:T(8,128)(2,1)S(1)}, bf16[1,2,32,4096]{3,2,1,0:T(8,128)(2,1)S(1)}, u32[]{:S(2)}, u32[]{:S(2)}) %collective-permute-start.36) | collective-permute-done | bytes 524320 | tf_op jit(solution)/shard_map/ppermute | solution.py:22
  238.2 1.4 add_convert_fusion
  240.1 1.0 slice_bitcast_fusion
  241.1 2.9 %collective-permute-start.32 = (bf16[4,64,256]{2,1,0:T(8,128)(2,1)S(1)}, bf16[4,64,256]{2,1,0:T(8,128)(2,1)S(1)}, u32[]{:S(2)}, u32[]{:S(2)}) collective-permute-start(bf16[4,64,256]{2,1,0:T(8,128)(2,1)S(1)} %get-tuple-element.40), channel_id=1, source_target_pairs={{0,8},{4,12},{8,0},{12,4},{1,9},{5,13},{9,1},{13,5},{2,10},{6,14},... | collective-permute-start | bytes 393224 | tf_op jit(solution)/shard_map/ppermute | solution.py:22
  244.1 2.6 pad_maximum_fusion.1.refs_9_
  246.9 2.6 pad_maximum_fusion.refs_8_
  249.5 9.5 %mixed.1 = bf16[256,4096]{1,0:T(8,128)(2,1)} custom-call(s32[64]{0:T(128)} %select_reduce_fusion.pos_ref, s32[1]{0:T(128)} %bitcast.item_ref, bf16[256,4096]{1,0:T(8,128)(2,1)} %f_ref.3, bf16[64,256,256]{2,1,0:T(8,128)(2,1)} %w_ref.3, bf16[256,128]{1,0:T(8,128)(2,1)} %get-tuple-element.45.codes_ref.c_ref, bf16[128,4096]{1,0:T(8,128)(2,1)} %low_ref.1, ...), custom_call_target="tpu_custom_call" | custom-call | flops 2415919104 | bytes 16777216 | tf_op jit(solution)/shard_map/mixed/pallas_call | solution.py:269
  259.1 1.5 collective-permute-start.33
  261.0 0.7 copy-done.26
  261.6 2.8 %collective-permute-start.34 = (bf16[4,64,256]{2,1,0:T(8,128)(2,1)}, bf16[4,64,256]{2,1,0:T(8,128)(2,1)S(1)}, u32[]{:S(2)}, u32[]{:S(2)}) collective-permute-start(bf16[4,64,256]{2,1,0:T(8,128)(2,1)} %get-tuple-element.36), channel_id=1, source_target_pairs={{0,8},{4,12},{8,0},{12,4},{1,9},{5,13},{9,1},{13,5},{2,10},{6,14},... | collective-permute-start | bytes 393224 | tf_op jit(solution)/shard_map/ppermute | solution.py:22
  264.8 3.8 %add_bitcast_fusion.own_ref = f32[2,16,64,256]{3,2,1,0:T(8,128)} fusion(bf16[1,2,16,64,256]{4,3,2,1,0:T(8,128)(2,1)} %collective-permute-done.18, f32[2,2,16,64,256]{4,3,2,1,0:T(8,128)} %get-tuple-element.16, s32[]{:T(128)S(6)} %select_n.66, bf16[2,2,16,64,256]{4,3,2,1,0:T(8,128)(2,1)S(1)} %collective-permute-done.17), kind=kLoop, calls=%fused_computation.2 | loop fusion | flops 2097152 | bytes 6291460 | tf_op jit(solution)/shard_map/squeeze | solution.py:129
  268.6 0.6 copy-done.27
  269.2 1.4 collective-permute-done.34.refs_7_
  270.7 0.6 copy-done.29
  271.3 5.8 %place.1 = f32[64,64,256]{2,1,0:T(8,128)} custom-call(s32[64]{0:T(128)} %select_reduce_fusion.pos_ref, f32[2,16,64,256]{3,2,1,0:T(8,128)} %add_bitcast_fusion.own_ref, bf16[4,64,256]{2,1,0:T(8,128)(2,1)} %collective-permute-done.21.refs_0_, bf16[4,64,256]{2,1,0:T(8,128)(2,1)} %collective-permute-done.24.refs_1_, bf16[4,64,256]{2,1,0:T(8,128)(2,1)} %copy-done.28, ...), custom_call_target="tpu_custom_call" | custom-call | bytes 8388608 | tf_op jit(solution)/shard_map/place/pallas_call | solution.py:312
  (117 shorter events, 6.2 us)
Async XLA Ops:
  0.6 1.2 copy-start
  0.6 3.6 %copy-start.2 = (bf16[256,4096]{1,0:T(8,128)(2,1)S(1)}, bf16[256,4096]{1,0:T(8,128)(2,1)}, u32[]{:S(2)}) copy-start(bf16[256,4096]{1,0:T(8,128)(2,1)} %g_ref.11) | copy-start | bytes 6291460
  1.9 2.4 copy-start.4
  4.3 3.9 %copy-start.31 = (s32[64]{0:T(128)S(1)}, s32[64]{0:T(128)}, u32[]{:S(2)}) copy-start(s32[64]{0:T(128)} %param.11) | copy-start | bytes 772
  4.3 3.9 %copy-start.32 = (s32[64]{0:T(128)S(1)}, s32[64]{0:T(128)}, u32[]{:S(2)}) copy-start(s32[64]{0:T(128)} %param.10) | copy-start | bytes 772
  5.0 11.8 %collective-permute-start = (f32[2,128,128]{2,1,0:T(8,128)S(1)}, f32[2,128,128]{2,1,0:T(8,128)S(1)}, u32[]{:S(2)}, u32[]{:S(2)}) collective-permute-start(f32[2,128,128]{2,1,0:T(8,128)S(1)} %fusion.1), channel_id=1, source_target_pairs={{0,4},{4,0},{8,12},{12,8},{1,5},{5,1},{9,13},{13,9},{2,6},{6,2},{1... | collective-permute-start | bytes 393224 | tf_op jit(solution)/shard_map/ppermute | solution.py:22
  11.9 5.4 %copy-start.3 = (bf16[256,4096]{1,0:T(8,128)(2,1)S(1)}, bf16[256,4096]{1,0:T(8,128)(2,1)}, u32[]{:S(2)}) copy-start(bf16[256,4096]{1,0:T(8,128)(2,1)} %f_ref.3) | copy-start | bytes 6291460
  14.3 100.0 %collective-permute-start.14 = (bf16[4,256,256]{2,1,0:T(8,128)(2,1)}, bf16[4,256,256]{2,1,0:T(8,128)(2,1)}, u32[]{:S(2)}, u32[]{:S(2)}) collective-permute-start(bf16[4,256,256]{2,1,0:T(8,128)(2,1)} %get-tuple-element.34), channel_id=1, source_target_pairs={{0,8},{4,12},{8,0},{12,4},{1,9},{5,13},{9,1},{13,5},{2,10},{6,14},... | collective-permute-start | bytes 1572872 | tf_op jit(solution)/shard_map/ppermute | solution.py:22
  16.9 62.4 %collective-permute-start.1 = (f32[2,128,128]{2,1,0:T(8,128)S(1)}, f32[2,128,128]{2,1,0:T(8,128)S(1)}, u32[]{:S(2)}, u32[]{:S(2)}) collective-permute-start(f32[2,128,128]{2,1,0:T(8,128)S(1)} %fusion.4), channel_id=1, source_target_pairs={{0,8},{4,12},{8,0},{12,4},{1,9},{5,13},{9,1},{13,5},{2,10},{6,14},... | collective-permute-start | bytes 393224 | tf_op jit(solution)/shard_map/ppermute | solution.py:22
  18.5 97.8 %collective-permute-start.9 = (bf16[256,1024]{1,0:T(8,128)(2,1)}, bf16[256,1024]{1,0:T(8,128)(2,1)S(1)}, u32[]{:S(2)}, u32[]{:S(2)}) collective-permute-start(bf16[256,1024]{1,0:T(8,128)(2,1)} %get-tuple-element.29), channel_id=1, source_target_pairs={{0,8},{4,12},{8,0},{12,4},{1,9},{5,13},{9,1},{13,5},{2,10},{6,14},... | collective-permute-start | bytes 1572872 | tf_op jit(solution)/shard_map/ppermute | solution.py:22
  21.1 95.3 %collective-permute-start.8 = (bf16[256,1024]{1,0:T(8,128)(2,1)}, bf16[256,1024]{1,0:T(8,128)(2,1)S(1)}, u32[]{:S(2)}, u32[]{:S(2)}) collective-permute-start(bf16[256,1024]{1,0:T(8,128)(2,1)} %get-tuple-element.30), channel_id=1, source_target_pairs={{0,8},{4,12},{8,0},{12,4},{1,9},{5,13},{9,1},{13,5},{2,10},{6,14},... | collective-permute-start | bytes 1572872 | tf_op jit(solution)/shard_map/ppermute | solution.py:22
  21.4 96.9 %collective-permute-start.7 = (bf16[256,1024]{1,0:T(8,128)(2,1)S(1)}, bf16[256,1024]{1,0:T(8,128)(2,1)S(1)}, u32[]{:S(2)}, u32[]{:S(2)}) collective-permute-start(bf16[256,1024]{1,0:T(8,128)(2,1)S(1)} %get-tuple-element.31), channel_id=1, source_target_pairs={{0,8},{4,12},{8,0},{12,4},{1,9},{5,13},{9,1},{13,5},{2,10},{6,14},... | collective-permute-start | bytes 1572872 | tf_op jit(solution)/shard_map/ppermute | solution.py:22
  79.3 35.0 %collective-permute-start.2 = (bf16[2,128,128]{2,1,0:T(8,128)(2,1)S(1)}, bf16[2,128,128]{2,1,0:T(8,128)(2,1)S(1)}, u32[]{:S(2)}, u32[]{:S(2)}) collective-permute-start(bf16[2,128,128]{2,1,0:T(8,128)(2,1)S(1)} %add_convert_fusion.10), channel_id=1, source_target_pairs={{0,4},{4,0},{8,12},{12,8},{1,5},{5,1},{9,13},{13,9},{2,6},{6,2},{1... | collective-permute-start | bytes 196616 | tf_op jit(solution)/shard_map/ppermute | solution.py:22
  114.3 26.0 %collective-permute-start.3 = (bf16[256,1024]{1,0:T(8,128)(2,1)S(1)}, bf16[256,1024]{1,0:T(8,128)(2,1)S(1)}, u32[]{:S(2)}, u32[]{:S(2)}) collective-permute-start(bf16[256,1024]{1,0:T(8,128)(2,1)S(1)} %get-tuple-element.31), channel_id=1, source_target_pairs={{0,4},{4,0},{8,12},{12,8},{1,5},{5,1},{9,13},{13,9},{2,6},{6,2},{1... | collective-permute-start | bytes 1572872 | tf_op jit(solution)/shard_map/ppermute | solution.py:22
  114.3 37.3 %collective-permute-start.4 = (bf16[256,1024]{1,0:T(8,128)(2,1)}, bf16[256,1024]{1,0:T(8,128)(2,1)S(1)}, u32[]{:S(2)}, u32[]{:S(2)}) collective-permute-start(bf16[256,1024]{1,0:T(8,128)(2,1)} %get-tuple-element.30), channel_id=1, source_target_pairs={{0,4},{4,0},{8,12},{12,8},{1,5},{5,1},{9,13},{13,9},{2,6},{6,2},{1... | collective-permute-start | bytes 1572872 | tf_op jit(solution)/shard_map/ppermute | solution.py:22
  116.3 43.6 %copy-start.7 = (bf16[256,1024]{1,0:T(8,128)(2,1)}, bf16[256,1024]{1,0:T(8,128)(2,1)S(1)}, u32[]{:S(2)}) copy-start(bf16[256,1024]{1,0:T(8,128)(2,1)S(1)} %collective-permute-done.9.refs_6_.refs_1_) | copy-start | bytes 1572868
  116.3 46.5 %collective-permute-start.5 = (bf16[256,1024]{1,0:T(8,128)(2,1)}, bf16[256,1024]{1,0:T(8,128)(2,1)S(1)}, u32[]{:S(2)}, u32[]{:S(2)}) collective-permute-start(bf16[256,1024]{1,0:T(8,128)(2,1)} %get-tuple-element.29), channel_id=1, source_target_pairs={{0,4},{4,0},{8,12},{12,8},{1,5},{5,1},{9,13},{13,9},{2,6},{6,2},{1... | collective-permute-start | bytes 1572872 | tf_op jit(solution)/shard_map/ppermute | solution.py:22
  116.4 43.5 %copy-start.8 = (bf16[256,1024]{1,0:T(8,128)(2,1)}, bf16[256,1024]{1,0:T(8,128)(2,1)S(1)}, u32[]{:S(2)}) copy-start(bf16[256,1024]{1,0:T(8,128)(2,1)S(1)} %collective-permute-done.8.refs_5_.refs_1_) | copy-start | bytes 1572868
  116.4 57.7 %collective-permute-start.11 = (bf16[4,256,256]{2,1,0:T(8,128)(2,1)}, bf16[4,256,256]{2,1,0:T(8,128)(2,1)}, u32[]{:S(2)}, u32[]{:S(2)}) collective-permute-start(bf16[4,256,256]{2,1,0:T(8,128)(2,1)} %get-tuple-element.35), channel_id=1, source_target_pairs={{0,4},{4,0},{8,12},{12,8},{1,5},{5,1},{9,13},{13,9},{2,6},{6,2},{1... | collective-permute-start | bytes 1572872 | tf_op jit(solution)/shard_map/ppermute | solution.py:22
  118.3 22.0 %copy-start.9 = (bf16[256,1024]{1,0:T(8,128)(2,1)}, bf16[256,1024]{1,0:T(8,128)(2,1)S(1)}, u32[]{:S(2)}) copy-start(bf16[256,1024]{1,0:T(8,128)(2,1)S(1)} %collective-permute-done.7.refs_4_.refs_1_) | copy-start | bytes 1572868
  118.3 55.8 %collective-permute-start.10 = (bf16[256,1024]{1,0:T(8,128)(2,1)}, bf16[256,1024]{1,0:T(8,128)(2,1)}, u32[]{:S(2)}, u32[]{:S(2)}) collective-permute-start(bf16[256,1024]{1,0:T(8,128)(2,1)} %get-tuple-element.28), channel_id=1, source_target_pairs={{0,8},{4,12},{8,0},{12,4},{1,9},{5,13},{9,1},{13,5},{2,10},{6,14},... | collective-permute-start | bytes 1572872 | tf_op jit(solution)/shard_map/ppermute | solution.py:22
  140.3 44.1 %collective-permute-start.6 = (bf16[256,1024]{1,0:T(8,128)(2,1)}, bf16[256,1024]{1,0:T(8,128)(2,1)}, u32[]{:S(2)}, u32[]{:S(2)}) collective-permute-start(bf16[256,1024]{1,0:T(8,128)(2,1)} %get-tuple-element.28), channel_id=1, source_target_pairs={{0,4},{4,0},{8,12},{12,8},{1,5},{5,1},{9,13},{13,9},{2,6},{6,2},{1... | collective-permute-start | bytes 1572872 | tf_op jit(solution)/shard_map/ppermute | solution.py:22
  151.5 8.4 %copy-start.11 = (bf16[256,1024]{1,0:T(8,128)(2,1)}, bf16[256,1024]{1,0:T(8,128)(2,1)S(1)}, u32[]{:S(2)}) copy-start(bf16[256,1024]{1,0:T(8,128)(2,1)S(1)} %collective-permute-done.4.refs_1_.refs_0_) | copy-start | bytes 1572868
  151.5 42.3 %collective-permute-start.19 = (bf16[2,2,4,64,256]{4,3,2,1,0:T(8,128)(2,1)}, bf16[2,2,4,64,256]{4,3,2,1,0:T(8,128)(2,1)S(1)}, u32[]{:S(2)}, u32[]{:S(2)}) collective-permute-start(bf16[2,2,4,64,256]{4,3,2,1,0:T(8,128)(2,1)} %get-tuple-element.19), channel_id=1, source_target_pairs={{0,1},{1,0},{2,3},{3,2},{4,5},{5,4},{6,7},{7,6},{8,9},{9,8},{10,11... | collective-permute-start | bytes 1572872 | tf_op jit(solution)/shard_map/ppermute | solution.py:22
  162.8 0.8 copy-start.12
  162.8 31.3 %collective-permute-start.22 = (bf16[2,2,4,64,256]{4,3,2,1,0:T(8,128)(2,1)}, bf16[2,2,4,64,256]{4,3,2,1,0:T(8,128)(2,1)S(1)}, u32[]{:S(2)}, u32[]{:S(2)}) collective-permute-start(bf16[2,2,4,64,256]{4,3,2,1,0:T(8,128)(2,1)} %get-tuple-element.21), channel_id=1, source_target_pairs={{0,1},{1,0},{2,3},{3,2},{4,5},{5,4},{6,7},{7,6},{8,9},{9,8},{10,11... | collective-permute-start | bytes 1572872 | tf_op jit(solution)/shard_map/ppermute | solution.py:22
  174.1 24.3 %collective-permute-start.25 = (bf16[2,2,4,64,256]{4,3,2,1,0:T(8,128)(2,1)}, bf16[2,2,4,64,256]{4,3,2,1,0:T(8,128)(2,1)}, u32[]{:S(2)}, u32[]{:S(2)}) collective-permute-start(bf16[2,2,4,64,256]{4,3,2,1,0:T(8,128)(2,1)} %get-tuple-element.23), channel_id=1, source_target_pairs={{0,1},{1,0},{2,3},{3,2},{4,5},{5,4},{6,7},{7,6},{8,9},{9,8},{10,11... | collective-permute-start | bytes 1572872 | tf_op jit(solution)/shard_map/ppermute | solution.py:22
  174.1 22.5 %collective-permute-start.15 = (bf16[4,256,256]{2,1,0:T(8,128)(2,1)}, bf16[4,256,256]{2,1,0:T(8,128)(2,1)S(1)}, u32[]{:S(2)}, u32[]{:S(2)}) collective-permute-start(bf16[4,256,256]{2,1,0:T(8,128)(2,1)} %collective-permute-done.14), channel_id=1, source_target_pairs={{0,2},{1,3},{2,0},{3,1},{4,6},{5,7},{6,4},{7,5},{8,10},{9,11},{10,... | collective-permute-start | bytes 1572872 | tf_op jit(solution)/shard_map/ppermute | solution.py:22
  184.4 15.7 %collective-permute-start.12 = (bf16[4,256,256]{2,1,0:T(8,128)(2,1)}, bf16[4,256,256]{2,1,0:T(8,128)(2,1)S(1)}, u32[]{:S(2)}, u32[]{:S(2)}) collective-permute-start(bf16[4,256,256]{2,1,0:T(8,128)(2,1)} %collective-permute-done.11), channel_id=1, source_target_pairs={{0,2},{1,3},{2,0},{3,1},{4,6},{5,7},{6,4},{7,5},{8,10},{9,11},{10,... | collective-permute-start | bytes 1572872 | tf_op jit(solution)/shard_map/ppermute | solution.py:22
  191.0 3.0 %copy-start.18 = (f32[2,2,4,64,256]{4,3,2,1,0:T(8,128)S(1)}, f32[2,2,4,64,256]{4,3,2,1,0:T(8,128)}, u32[]{:S(2)}) copy-start(f32[2,2,4,64,256]{4,3,2,1,0:T(8,128)} %get-tuple-element.18) | copy-start | bytes 3145732
  193.9 2.8 %copy-start.30 = (bf16[2,2,32,4096]{3,2,1,0:T(8,128)(2,1)S(1)}, bf16[2,2,32,4096]{3,2,1,0:T(8,128)(2,1)}, u32[]{:S(2)}) copy-start(bf16[2,2,32,4096]{3,2,1,0:T(8,128)(2,1)} %get-tuple-element.27) | copy-start | bytes 3145732
  193.9 7.7 %collective-permute-start.28 = (bf16[2,2,4,64,256]{4,3,2,1,0:T(8,128)(2,1)}, bf16[2,2,4,64,256]{4,3,2,1,0:T(8,128)(2,1)S(1)}, u32[]{:S(2)}, u32[]{:S(2)}) collective-permute-start(bf16[2,2,4,64,256]{4,3,2,1,0:T(8,128)(2,1)} %get-tuple-element.25), channel_id=1, source_target_pairs={{0,1},{1,0},{2,3},{3,2},{4,5},{5,4},{6,7},{7,6},{8,9},{9,8},{10,11... | collective-permute-start | bytes 1572872 | tf_op jit(solution)/shard_map/ppermute | solution.py:22
  194.0 5.0 %copy-start.17 = (f32[2,2,4,64,256]{4,3,2,1,0:T(8,128)S(1)}, f32[2,2,4,64,256]{4,3,2,1,0:T(8,128)}, u32[]{:S(2)}) copy-start(f32[2,2,4,64,256]{4,3,2,1,0:T(8,128)} %get-tuple-element.22) | copy-start | bytes 3145732
  195.5 42.7 %collective-permute-start.17 = (bf16[2,2,16,64,256]{4,3,2,1,0:T(8,128)(2,1)}, bf16[2,2,16,64,256]{4,3,2,1,0:T(8,128)(2,1)S(1)}, u32[]{:S(2)}, u32[]{:S(2)}) collective-permute-start(bf16[2,2,16,64,256]{4,3,2,1,0:T(8,128)(2,1)} %get-tuple-element.17), channel_id=1, source_target_pairs={{0,1},{1,0},{2,3},{3,2},{4,5},{5,4},{6,7},{7,6},{8,9},{9,8},{10,11... | collective-permute-start | bytes 6291464 | tf_op jit(solution)/shard_map/ppermute | solution.py:22
  196.6 5.0 %copy-start.15 = (bf16[4,256,256]{2,1,0:T(8,128)(2,1)}, bf16[4,256,256]{2,1,0:T(8,128)(2,1)S(1)}, u32[]{:S(2)}) copy-start(bf16[4,256,256]{2,1,0:T(8,128)(2,1)S(1)} %collective-permute-done.15) | copy-start | bytes 1572868
  196.7 24.8 %collective-permute-start.35 = (bf16[2,2,32,4096]{3,2,1,0:T(8,128)(2,1)S(1)}, bf16[2,2,32,4096]{3,2,1,0:T(8,128)(2,1)S(1)}, u32[]{:S(2)}, u32[]{:S(2)}) collective-permute-start(bf16[2,2,32,4096]{3,2,1,0:T(8,128)(2,1)S(1)} %copy-done.30), channel_id=1, source_target_pairs={{0,1},{1,0},{2,3},{3,2},{4,5},{5,4},{6,7},{7,6},{8,9},{9,8},{10,11... | collective-permute-start | bytes 3145736 | tf_op jit(solution)/shard_map/ppermute | solution.py:22
  198.4 4.9 %copy-start.21 = (f32[2,2,4,64,256]{4,3,2,1,0:T(8,128)S(1)}, f32[2,2,4,64,256]{4,3,2,1,0:T(8,128)}, u32[]{:S(2)}) copy-start(f32[2,2,4,64,256]{4,3,2,1,0:T(8,128)} %get-tuple-element.24) | copy-start | bytes 3145732
  198.4 9.2 %collective-permute-start.20 = (bf16[1,2,4,64,256]{4,3,2,1,0:T(8,128)(2,1)S(1)}, bf16[1,2,4,64,256]{4,3,2,1,0:T(8,128)(2,1)S(1)}, u32[]{:S(2)}, u32[]{:S(2)}) collective-permute-start(bf16[1,2,4,64,256]{4,3,2,1,0:T(8,128)(2,1)S(1)} %add_convert_fusion.9), channel_id=1, source_target_pairs={{0,2},{1,3},{2,0},{3,1},{4,6},{5,7},{6,4},{7,5},{8,10},{9,11},{10,... | collective-permute-start | bytes 786440 | tf_op jit(solution)/shard_map/ppermute | solution.py:22
  198.9 8.7 %copy-start.19 = (f32[2,2,4,64,256]{4,3,2,1,0:T(8,128)S(1)}, f32[2,2,4,64,256]{4,3,2,1,0:T(8,128)}, u32[]{:S(2)}) copy-start(f32[2,2,4,64,256]{4,3,2,1,0:T(8,128)} %get-tuple-element.18) | copy-start | bytes 3145732
  198.9 8.7 %copy-start.23 = (bf16[2,2,4,64,256]{4,3,2,1,0:T(8,128)(2,1)S(1)}, bf16[2,2,4,64,256]{4,3,2,1,0:T(8,128)(2,1)}, u32[]{:S(2)}) copy-start(bf16[2,2,4,64,256]{4,3,2,1,0:T(8,128)(2,1)} %copy-done.22) | copy-start | bytes 1572868
  200.1 12.8 %copy-start.20 = (f32[2,2,4,64,256]{4,3,2,1,0:T(8,128)S(1)}, f32[2,2,4,64,256]{4,3,2,1,0:T(8,128)}, u32[]{:S(2)}) copy-start(f32[2,2,4,64,256]{4,3,2,1,0:T(8,128)} %get-tuple-element.20) | copy-start | bytes 3145732
  200.1 12.8 %copy-start.25 = (bf16[2,2,4,64,256]{4,3,2,1,0:T(8,128)(2,1)S(1)}, bf16[2,2,4,64,256]{4,3,2,1,0:T(8,128)(2,1)}, u32[]{:S(2)}) copy-start(bf16[2,2,4,64,256]{4,3,2,1,0:T(8,128)(2,1)} %copy-done.24) | copy-start | bytes 1572868
  200.1 7.6 %copy-start.13 = (bf16[4,256,256]{2,1,0:T(8,128)(2,1)}, bf16[4,256,256]{2,1,0:T(8,128)(2,1)S(1)}, u32[]{:S(2)}) copy-start(bf16[4,256,256]{2,1,0:T(8,128)(2,1)S(1)} %collective-permute-done.12) | copy-start | bytes 1572868
  200.1 41.0 %collective-permute-start.16 = (bf16[8,256,256]{2,1,0:T(8,128)(2,1)S(1)}, bf16[8,256,256]{2,1,0:T(8,128)(2,1)S(1)}, u32[]{:S(2)}, u32[]{:S(2)}) collective-permute-start(bf16[8,256,256]{2,1,0:T(8,128)(2,1)S(1)} %pad_maximum_fusion.3), channel_id=1, source_target_pairs={{0,1},{1,0},{2,3},{3,2},{4,5},{5,4},{6,7},{7,6},{8,9},{9,8},{10,11... | collective-permute-start | bytes 3145736 | tf_op jit(solution)/shard_map/ppermute | solution.py:22
  201.6 10.8 %collective-permute-start.23 = (bf16[1,2,4,64,256]{4,3,2,1,0:T(8,128)(2,1)S(1)}, bf16[1,2,4,64,256]{4,3,2,1,0:T(8,128)(2,1)S(1)}, u32[]{:S(2)}, u32[]{:S(2)}) collective-permute-start(bf16[1,2,4,64,256]{4,3,2,1,0:T(8,128)(2,1)S(1)} %add_convert_fusion.7), channel_id=1, source_target_pairs={{0,2},{1,3},{2,0},{3,1},{4,6},{5,7},{6,4},{7,5},{8,10},{9,11},{10,... | collective-permute-start | bytes 786440 | tf_op jit(solution)/shard_map/ppermute | solution.py:22
  207.6 39.0 %collective-permute-start.13 = (bf16[8,256,256]{2,1,0:T(8,128)(2,1)S(1)}, bf16[8,256,256]{2,1,0:T(8,128)(2,1)S(1)}, u32[]{:S(2)}, u32[]{:S(2)}) collective-permute-start(bf16[8,256,256]{2,1,0:T(8,128)(2,1)S(1)} %pad_maximum_fusion.2), channel_id=1, source_target_pairs={{0,1},{1,0},{2,3},{3,2},{4,5},{5,4},{6,7},{7,6},{8,9},{9,8},{10,11... | collective-permute-start | bytes 3145736 | tf_op jit(solution)/shard_map/ppermute | solution.py:22
  207.8 13.7 %copy-start.6 = (f32[2,2,32,4096]{3,2,1,0:T(8,128)S(1)}, f32[2,2,32,4096]{3,2,1,0:T(8,128)}, u32[]{:S(2)}) copy-start(f32[2,2,32,4096]{3,2,1,0:T(8,128)} %get-tuple-element.26) | copy-start | bytes 6291460
  212.4 7.5 %collective-permute-start.26 = (bf16[1,2,4,64,256]{4,3,2,1,0:T(8,128)(2,1)S(1)}, bf16[1,2,4,64,256]{4,3,2,1,0:T(8,128)(2,1)S(1)}, u32[]{:S(2)}, u32[]{:S(2)}) collective-permute-start(bf16[1,2,4,64,256]{4,3,2,1,0:T(8,128)(2,1)S(1)} %add_convert_fusion.5), channel_id=1, source_target_pairs={{0,2},{1,3},{2,0},{3,1},{4,6},{5,7},{6,4},{7,5},{8,10},{9,11},{10,... | collective-permute-start | bytes 786440 | tf_op jit(solution)/shard_map/ppermute | solution.py:22
  219.9 9.2 %collective-permute-start.29 = (bf16[1,2,4,64,256]{4,3,2,1,0:T(8,128)(2,1)S(1)}, bf16[1,2,4,64,256]{4,3,2,1,0:T(8,128)(2,1)S(1)}, u32[]{:S(2)}, u32[]{:S(2)}) collective-permute-start(bf16[1,2,4,64,256]{4,3,2,1,0:T(8,128)(2,1)S(1)} %add_convert_fusion.3), channel_id=1, source_target_pairs={{0,2},{1,3},{2,0},{3,1},{4,6},{5,7},{6,4},{7,5},{8,10},{9,11},{10,... | collective-permute-start | bytes 786440 | tf_op jit(solution)/shard_map/ppermute | solution.py:22
  221.6 16.2 %collective-permute-start.36 = (bf16[1,2,32,4096]{3,2,1,0:T(8,128)(2,1)S(1)}, bf16[1,2,32,4096]{3,2,1,0:T(8,128)(2,1)S(1)}, u32[]{:S(2)}, u32[]{:S(2)}) collective-permute-start(bf16[1,2,32,4096]{3,2,1,0:T(8,128)(2,1)S(1)} %add_convert_fusion.1), channel_id=1, source_target_pairs={{0,2},{1,3},{2,0},{3,1},{4,6},{5,7},{6,4},{7,5},{8,10},{9,11},{10,... | collective-permute-start | bytes 1572872 | tf_op jit(solution)/shard_map/ppermute | solution.py:22
  229.1 30.0 %collective-permute-start.31 = (bf16[4,64,256]{2,1,0:T(8,128)(2,1)}, bf16[4,64,256]{2,1,0:T(8,128)(2,1)}, u32[]{:S(2)}, u32[]{:S(2)}) collective-permute-start(bf16[4,64,256]{2,1,0:T(8,128)(2,1)} %get-tuple-element.42), channel_id=1, source_target_pairs={{0,8},{4,12},{8,0},{12,4},{1,9},{5,13},{9,1},{13,5},{2,10},{6,14},... | collective-permute-start | bytes 393224 | tf_op jit(solution)/shard_map/ppermute | solution.py:22
  230.5 7.7 %copy-start.5 = (f32[2,2,16,64,256]{4,3,2,1,0:T(8,128)S(1)}, f32[2,2,16,64,256]{4,3,2,1,0:T(8,128)}, u32[]{:S(2)}) copy-start(f32[2,2,16,64,256]{4,3,2,1,0:T(8,128)} %get-tuple-element.16) | copy-start | bytes 12582916
  237.7 22.9 %collective-permute-start.21 = (bf16[4,64,256]{2,1,0:T(8,128)(2,1)}, bf16[4,64,256]{2,1,0:T(8,128)(2,1)}, u32[]{:S(2)}, u32[]{:S(2)}) collective-permute-start(bf16[4,64,256]{2,1,0:T(8,128)(2,1)} %get-tuple-element.43), channel_id=1, source_target_pairs={{0,4},{4,0},{8,12},{12,8},{1,5},{5,1},{9,13},{13,9},{2,6},{6,2},{1... | collective-permute-start | bytes 393224 | tf_op jit(solution)/shard_map/ppermute | solution.py:22
  239.6 4.5 %copy-start.16 = (bf16[4,256,256]{2,1,0:T(8,128)(2,1)S(1)}, bf16[4,256,256]{2,1,0:T(8,128)(2,1)}, u32[]{:S(2)}) copy-start(bf16[4,256,256]{2,1,0:T(8,128)(2,1)} %copy-done.15) | copy-start | bytes 1572868
  239.6 24.8 %collective-permute-start.18 = (bf16[1,2,16,64,256]{4,3,2,1,0:T(8,128)(2,1)}, bf16[1,2,16,64,256]{4,3,2,1,0:T(8,128)(2,1)}, u32[]{:S(2)}, u32[]{:S(2)}) collective-permute-start(bf16[1,2,16,64,256]{4,3,2,1,0:T(8,128)(2,1)} %add_convert_fusion), channel_id=1, source_target_pairs={{0,2},{1,3},{2,0},{3,1},{4,6},{5,7},{6,4},{7,5},{8,10},{9,11},{10,... | collective-permute-start | bytes 3145736 | tf_op jit(solution)/shard_map/ppermute | solution.py:22
  241.1 5.8 %copy-start.14 = (bf16[4,256,256]{2,1,0:T(8,128)(2,1)S(1)}, bf16[4,256,256]{2,1,0:T(8,128)(2,1)}, u32[]{:S(2)}) copy-start(bf16[4,256,256]{2,1,0:T(8,128)(2,1)} %copy-done.13) | copy-start | bytes 1572868
  241.1 19.8 %collective-permute-start.32 = (bf16[4,64,256]{2,1,0:T(8,128)(2,1)S(1)}, bf16[4,64,256]{2,1,0:T(8,128)(2,1)S(1)}, u32[]{:S(2)}, u32[]{:S(2)}) collective-permute-start(bf16[4,64,256]{2,1,0:T(8,128)(2,1)S(1)} %get-tuple-element.40), channel_id=1, source_target_pairs={{0,8},{4,12},{8,0},{12,4},{1,9},{5,13},{9,1},{13,5},{2,10},{6,14},... | collective-permute-start | bytes 393224 | tf_op jit(solution)/shard_map/ppermute | solution.py:22
  246.6 22.0 %collective-permute-start.24 = (bf16[4,64,256]{2,1,0:T(8,128)(2,1)S(1)}, bf16[4,64,256]{2,1,0:T(8,128)(2,1)}, u32[]{:S(2)}, u32[]{:S(2)}) collective-permute-start(bf16[4,64,256]{2,1,0:T(8,128)(2,1)S(1)} %get-tuple-element.41), channel_id=1, source_target_pairs={{0,4},{4,0},{8,12},{12,8},{1,5},{5,1},{9,13},{13,9},{2,6},{6,2},{1... | collective-permute-start | bytes 393224 | tf_op jit(solution)/shard_map/ppermute | solution.py:22
  259.1 9.5 %collective-permute-start.33 = (bf16[4,64,256]{2,1,0:T(8,128)(2,1)}, bf16[4,64,256]{2,1,0:T(8,128)(2,1)S(1)}, u32[]{:S(2)}, u32[]{:S(2)}) collective-permute-start(bf16[4,64,256]{2,1,0:T(8,128)(2,1)} %get-tuple-element.38), channel_id=1, source_target_pairs={{0,8},{4,12},{8,0},{12,4},{1,9},{5,13},{9,1},{13,5},{2,10},{6,14},... | collective-permute-start | bytes 393224 | tf_op jit(solution)/shard_map/ppermute | solution.py:22
  260.6 8.0 %collective-permute-start.27 = (bf16[4,64,256]{2,1,0:T(8,128)(2,1)S(1)}, bf16[4,64,256]{2,1,0:T(8,128)(2,1)S(1)}, u32[]{:S(2)}, u32[]{:S(2)}) collective-permute-start(bf16[4,64,256]{2,1,0:T(8,128)(2,1)S(1)} %get-tuple-element.39), channel_id=1, source_target_pairs={{0,4},{4,0},{8,12},{12,8},{1,5},{5,1},{9,13},{13,9},{2,6},{6,2},{1... | collective-permute-start | bytes 393224 | tf_op jit(solution)/shard_map/ppermute | solution.py:22
  261.6 9.0 %collective-permute-start.34 = (bf16[4,64,256]{2,1,0:T(8,128)(2,1)}, bf16[4,64,256]{2,1,0:T(8,128)(2,1)S(1)}, u32[]{:S(2)}, u32[]{:S(2)}) collective-permute-start(bf16[4,64,256]{2,1,0:T(8,128)(2,1)} %get-tuple-element.36), channel_id=1, source_target_pairs={{0,8},{4,12},{8,0},{12,4},{1,9},{5,13},{9,1},{13,5},{2,10},{6,14},... | collective-permute-start | bytes 393224 | tf_op jit(solution)/shard_map/ppermute | solution.py:22
  264.5 6.2 %collective-permute-start.30 = (bf16[4,64,256]{2,1,0:T(8,128)(2,1)}, bf16[4,64,256]{2,1,0:T(8,128)(2,1)}, u32[]{:S(2)}, u32[]{:S(2)}) collective-permute-start(bf16[4,64,256]{2,1,0:T(8,128)(2,1)} %get-tuple-element.37), channel_id=1, source_target_pairs={{0,4},{4,0},{8,12},{12,8},{1,5},{5,1},{9,13},{13,9},{2,6},{6,2},{1... | collective-permute-start | bytes 393224 | tf_op jit(solution)/shard_map/ppermute | solution.py:22
  264.8 12.4 %copy-start.1 = (bf16[128,4096]{1,0:T(8,128)(2,1)S(1)}, bf16[128,4096]{1,0:T(8,128)(2,1)}, u32[]{:S(2)}) copy-start(bf16[128,4096]{1,0:T(8,128)(2,1)} %param.12) | copy-start | bytes 3145732
  269.2 1.4 copy-start.28
  (6 other events, 4.4 us)
where the time goes:
time: 278 us; the launch traced here: 277 us
  waiting for transfers between devices  162 us (58%)
  Pallas kernels  43.1 us (16%)
  starting transfers between devices  37.1 us (13%)
  other arithmetic  17.8 us (6%)
  local copies, waits for them, and re-layouts  13.3 us (5%)
  matrix products  3.08 us (1%)
    ppermute x37, waiting for transfers between devices, swapped(): lax.ppermute(block, axis, [(one, one ^ 1 << apart) for one in range(count)])  162 us
    ppermute x37, starting transfers between devices, swapped(): lax.ppermute(block, axis, [(one, one ^ 1 << apart) for one in range(count)])  37.1 us
    pallas_call x5, Pallas kernels, pair_grads(): pl.pallas_call(functools.partial(grad_body, pairs, part), grid_spec=pltpu...  19.7 us
    pallas_call x1, Pallas kernels, mixed_kernel(): pl.pallas_call(functools.partial(mixed_body, share, chunks, units, unit,...  9.52 us
    concatenate x4, other arithmetic, layer(): held = jnp.concatenate([held, swapped(held, 'items', level)], axis=0)  7.67 us
    unnamed x66, local copies, waits for them, and re-layouts  5.86 us
    pallas_call x1, Pallas kernels, place_kernel(): pl.pallas_call(functools.partial(place_body, share, chunks), grid_spec=pl...  5.84 us
  transfers between devices with their start and end apart: 37, of which 13 were waited for; matrix products, arithmetic and copies ran while one was open for 9% of the time, Pallas kernels for 13%

commit v1 on v0

--- a/solution.py
+++ b/solution.py
@@ -10,7 +10,7 @@
 
 WIDTH = 16384
 BLOCK = 256
-CHUNKS = 4
+CHUNK_SIZES = (4, 4, 4, 4)
 
 
 F32 = jnp.float32
@@ -20,6 +20,10 @@
 def swapped(block, axis, apart):
     count = lax.axis_size(axis)
     return lax.ppermute(block, axis, [(one, one ^ (1 << apart)) for one in range(count)])
+
+
+def after(value, *deps):
+    return lax.optimization_barrier((value, *deps))[0]
 
 
 def pick(values, index, dim):
@@ -126,7 +130,7 @@
         leave = pick(keep, 1 - mine, 1) + pick(came, 1 - mine, 1).astype(F32)
         keep = pick(keep, mine, 1) + pick(came, mine, 1).astype(F32)
         came = swapped(leave.astype(BF16), "items", level)
-    return (keep + came.astype(F32))[0]
+    return keep[0], came[0]
 
 
 def share_body(share, units, unit, pos_ref, item_ref, w_ref, out_ref, sems):
@@ -168,154 +172,152 @@
     )(pos, item, block_weights)
 
 
-def mixed_body(share, chunks, units, unit, bits, pos_ref, item_ref, f_ref, w_ref, codes_ref, low_ref, *refs):
-    far_refs, refs = refs[: 2 * chunks], refs[2 * chunks :]
-    far_w, out_ref = refs[:2], refs[2]
-    f_buf, low_buf, far_bufs, w_buf, out_buf, in_sems, w_sems, out_sems = (
-        refs[3],
-        refs[4],
-        refs[5],
-        refs[6],
-        refs[7],
-        refs[8],
-        refs[9],
-        refs[10],
-    )
+def mixed_body(share, sizes, first, last, units, unit, order, pos_ref, item_ref, f_ref, w_ref, codes_ref, low_ref, *refs):
+    steps = last - first
+    far_refs, refs = refs[: 2 * steps], refs[2 * steps :]
+    parts = len(order)
+    far_w, refs = refs[: 2 * parts], refs[2 * parts :]
+    out_ref, f_buf, low_buf, far_buf, w_buf, out_buf, in_sems, w_sems, far_w_sems, out_sems = refs[-10:]
     dims = (((1,), (1,)), ((), ()))
     pieces = BLOCK // unit
-    per = share // chunks
-    wide = per * BLOCK
     item = item_ref[0]
-
-    def slot_of(number):
-        apart = lax.div(number, units) ^ item
-        slot = jnp.int32(0)
-        for level in range(bits):
-            slot = slot * 2 + ((apart >> level) & 1)
-        return slot * units + lax.rem(number, units)
-
-    loads, weights = [], []
-    for chunk in range(chunks):
-        cols = pl.ds(chunk * wide, wide)
-        loads.append(
-            [
-                pltpu.make_async_copy(f_ref.at[:, cols], f_buf.at[:, cols], in_sems.at[chunk, 0]),
-                pltpu.make_async_copy(low_ref.at[:, cols], low_buf.at[:, cols], in_sems.at[chunk, 1]),
-            ]
-            + [
+    starts = [sum(sizes[:one]) for one in range(len(sizes))]
+
+    gathered = []
+    for way in range(2):
+        for slot, apart in enumerate(order):
+            owner = item ^ apart
+            source = far_w[way * parts + slot]
+            if pieces == 1:
+                into = w_buf.at[2 + way, pl.ds(owner * units, units)]
+            else:
+                rows = pl.ds(pl.multiple_of(lax.rem(owner, pieces) * unit, unit), unit)
+                source = source.at[0]
+                into = w_buf.at[2 + way, lax.div(owner, pieces), rows, :]
+            gathered.append(pltpu.make_async_copy(source, into, far_w_sems.at[way, slot]))
+    loads = []
+    for step in range(steps):
+        chunk = first + step
+        cols = pl.ds(starts[chunk] * BLOCK, sizes[chunk] * BLOCK)
+        copies = [
+            pltpu.make_async_copy(f_ref.at[:, cols], f_buf.at[:, cols], in_sems.at[step, 0]),
+            pltpu.make_async_copy(low_ref.at[:, cols], low_buf.at[:, cols], in_sems.at[step, 1]),
+        ]
+        for way in range(2):
+            copies.append(
                 pltpu.make_async_copy(
-                    far_refs[way * chunks + chunk], far_bufs.at[way, chunk], in_sems.at[chunk, 2 + way]
-                )
-                for way in range(2)
-            ]
-        )
-        chunk_weights = []
-        for at in range(chunk * per, (chunk + 1) * per):
-            chunk_weights.append(
-                pltpu.make_async_copy(w_ref.at[pos_ref[at]], w_buf.at[0, at], w_sems.at[0, at, 0])
-            )
-            chunk_weights.append(
-                pltpu.make_async_copy(
-                    w_ref.at[pos_ref[share + (at ^ 1)]], w_buf.at[1, at], w_sems.at[1, at, 0]
+                    far_refs[way * steps + step], far_buf.at[way, :, cols], in_sems.at[step, 2 + way]
                 )
             )
-            for way in range(2):
-                for piece in range(pieces):
-                    chunk_weights.append(
-                        pltpu.make_async_copy(
-                            far_w[way].at[slot_of(jnp.int32(at * pieces + piece))],
-                            w_buf.at[2 + way, at, pl.ds(piece * unit, unit), :],
-                            w_sems.at[2 + way, at, piece],
-                        )
-                    )
-        weights.append(chunk_weights)
-    for chunk in range(chunks):
-        for copy in loads[chunk] + weights[chunk]:
+        for at in range(starts[chunk], starts[chunk] + sizes[chunk]):
+            copies.append(
+                pltpu.make_async_copy(w_ref.at[pos_ref[at]], w_buf.at[0, at], w_sems.at[0, at])
+            )
+            copies.append(
+                pltpu.make_async_copy(
+                    w_ref.at[pos_ref[share + (at ^ 1)]], w_buf.at[1, at], w_sems.at[1, at]
+                )
+            )
+        loads.append(copies)
+    for copy in gathered:
+        copy.start()
+    for copies in loads:
+        for copy in copies:
             copy.start()
+    for copy in gathered:
+        copy.wait()
     stores = []
-    for chunk in range(chunks):
-        for copy in loads[chunk] + weights[chunk]:
+    for step in range(steps):
+        chunk = first + step
+        for copy in loads[step]:
             copy.wait()
-        for at in range(chunk * per, (chunk + 1) * per):
+        for at in range(starts[chunk], starts[chunk] + sizes[chunk]):
             own = slice(at * BLOCK, (at + 1) * BLOCK)
             flip = slice((at ^ 1) * BLOCK, ((at ^ 1) + 1) * BLOCK)
-            local = slice((at - chunk * per) * BLOCK, (at - chunk * per + 1) * BLOCK)
             total = lax.dot_general(f_buf[:, own], w_buf[0, at], dims, preferred_element_type=F32)
             total += lax.dot_general(f_buf[:, flip], w_buf[1, at], dims, preferred_element_type=F32)
             for way in range(2):
                 total += lax.dot_general(
-                    far_bufs[way, chunk, :, local],
-                    w_buf[2 + way, at],
-                    dims,
-                    preferred_element_type=F32,
+                    far_buf[way, :, own], w_buf[2 + way, at], dims, preferred_element_type=F32
                 )
             total += jnp.dot(codes_ref[...], low_buf[:, own], preferred_element_type=F32)
             out_buf[:, own] = total.astype(BF16)
-        cols = pl.ds(chunk * wide, wide)
-        store = pltpu.make_async_copy(out_buf.at[:, cols], out_ref.at[:, cols], out_sems.at[chunk])
+        cols = pl.ds(starts[chunk] * BLOCK, sizes[chunk] * BLOCK)
+        store = pltpu.make_async_copy(out_buf.at[:, cols], out_ref.at[:, cols], out_sems.at[step])
         store.start()
         stores.append(store)
     for store in stores:
         store.wait()
 
 
-def mixed_kernel(features, block_weights, codes, lowrank_out, far, far_weights, pos, item, units, bits):
+def mixed_kernel(
+    features, block_weights, codes, lowrank_out, far, far_weights, pos, item, sizes, first, last, units, order, held
+):
     rows_here, width = features.shape
     share = width // BLOCK
-    chunks = len(far[0])
-    unit = far_weights[0].shape[1]
+    unit = far_weights[0][0].shape[1]
     hbm = pl.BlockSpec(memory_space=pl.ANY)
     smem = pl.BlockSpec(memory_space=pltpu.SMEM)
+    far_inputs = [*far[0][first:last], *far[1][first:last], *far_weights[0], *far_weights[1]]
+    inputs = [pos, item, features, block_weights, codes, lowrank_out, *far_inputs]
+    if held is not None:
+        inputs.append(held)
+    columns = sum(sizes[first:last])
     return pl.pallas_call(
-        functools.partial(mixed_body, share, chunks, units, unit, bits),
+        functools.partial(mixed_body, share, sizes, first, last, units, unit, order),
         in_specs=[smem, smem, hbm, hbm, pl.BlockSpec(memory_space=pltpu.VMEM), hbm]
-        + [hbm] * (2 * chunks + 2),
+        + [hbm] * (len(inputs) - 6),
         out_specs=hbm,
         out_shape=jax.ShapeDtypeStruct((rows_here, width), BF16),
+        input_output_aliases={} if held is None else {len(inputs) - 1: 0},
         scratch_shapes=[
             pltpu.VMEM((rows_here, width), BF16),
             pltpu.VMEM(lowrank_out.shape, BF16),
-            pltpu.VMEM((2, chunks, rows_here, width // chunks), BF16),
+            pltpu.VMEM((2, rows_here, width), BF16),
             pltpu.VMEM((4, share, BLOCK, BLOCK), BF16),
             pltpu.VMEM((rows_here, width), BF16),
-            pltpu.SemaphoreType.DMA((chunks, 4)),
-            pltpu.SemaphoreType.DMA((4, share, BLOCK // unit)),
-            pltpu.SemaphoreType.DMA((chunks,)),
+            pltpu.SemaphoreType.DMA((last - first, 4)),
+            pltpu.SemaphoreType.DMA((2, share)),
+            pltpu.SemaphoreType.DMA((2, len(order))),
+            pltpu.SemaphoreType.DMA((last - first,)),
         ],
         cost_estimate=pl.CostEstimate(
-            flops=9 * share * rows_here * BLOCK * BLOCK,
-            bytes_accessed=share * BLOCK * 2 * (4 * rows_here + 4 * BLOCK),
+            flops=9 * columns * rows_here * BLOCK * BLOCK,
+            bytes_accessed=columns * BLOCK * 2 * (4 * rows_here + 4 * BLOCK),
             transcendentals=0,
         ),
         name="mixed",
-    )(pos, item, features, block_weights, codes, lowrank_out, *far[0], *far[1], *far_weights)
-
-
-def place_body(share, chunks, pos_ref, own_ref, *refs):
+    )(*inputs)
+
+
+def place_body(share, sizes, pos_ref, own_ref, *refs):
     far_refs, out_ref = refs[:-1], refs[-1]
-    per = share // chunks
+    chunks = len(sizes)
     for way in range(4):
-        for at in range(share):
-            if way < 2:
-                block = own_ref[way, at]
-            else:
-                block = far_refs[(way - 2) * chunks + at // per][at % per].astype(F32)
-            out_ref[:, pos_ref[way * share + at], :] = block
-
-
-def place_kernel(own, far, pos):
+        for chunk in range(chunks):
+            first = sum(sizes[:chunk])
+            for at in range(first, first + sizes[chunk]):
+                if way < 2:
+                    block = own_ref[way, at]
+                else:
+                    block = far_refs[(way - 2) * chunks + chunk][at - first].astype(F32)
+                out_ref[:, pos_ref[way * share + at], :] = block
+
+
+def place_kernel(own, far, pos, sizes):
     _, share, part, _ = own.shape
-    chunks = len(far[0])
-    per = share // chunks
     rows = 16
-    far_spec = pl.BlockSpec((per, rows, BLOCK), lambda at, pos_ref: (0, at, 0))
+    far_specs = [
+        pl.BlockSpec((size, rows, BLOCK), lambda at, pos_ref: (0, at, 0)) for size in sizes
+    ]
     return pl.pallas_call(
-        functools.partial(place_body, share, chunks),
+        functools.partial(place_body, share, sizes),
         grid_spec=pltpu.PrefetchScalarGridSpec(
             num_scalar_prefetch=1,
             grid=(part // rows,),
             in_specs=[pl.BlockSpec((2, share, rows, BLOCK), lambda at, pos_ref: (0, 0, at, 0))]
-            + [far_spec] * (2 * chunks),
+            + far_specs
+            + far_specs,
             out_specs=pl.BlockSpec((rows, 4 * share, BLOCK), lambda at, pos_ref: (at, 0, 0)),
         ),
         out_shape=jax.ShapeDtypeStruct((part, 4 * share, BLOCK), F32),
@@ -331,8 +333,8 @@
     share = width // BLOCK
     count = WIDTH // BLOCK
     stored = block_weights.shape[0]
-    chunks = min(CHUNKS, share)
-    per = share // chunks
+    sizes = chunk_sizes(share)
+    chunks = len(sizes)
     items = lax.axis_size("items")
     item = lax.axis_index("items").astype(jnp.int32)
     item_arg = item.reshape(1)
@@ -356,20 +358,25 @@
         axis=1,
     ).astype(jnp.int32)
 
-    far = [[], []]
+    far, source = [[], []], features
     for one in range(chunks):
-        piece = lax.optimization_barrier(features[:, one * per * BLOCK : (one + 1) * per * BLOCK])
+        first = sum(sizes[:one]) * BLOCK
+        piece = source[:, first : first + sizes[one] * BLOCK]
+        if one + 1 < chunks:
+            source = after(source, far[1][-1] if far[1] else piece)
         for way in range(2):
             far[way].append(hop(piece, far_bits[way]))
 
     unit = min(BLOCK, share * BLOCK // items)
     units = share * BLOCK // items // unit
     shares = weight_share(block_weights, pos, item_arg, share, unit, units)
-    far_weights = []
+    far_weights, order = [], []
     for way in range(2):
-        held = hop(shares[way], far_bits[way])
+        held, order = [hop(shares[way], far_bits[way])], [0]
         for level in range(bits - 1, -1, -1):
-            held = jnp.concatenate([held, swapped(held, "items", level)], axis=0)
+            for one in range(len(held)):
+                held.append(swapped(held[one], "items", level))
+                order.append(order[one] ^ (1 << level))
         far_weights.append(held)
 
     dims = (((1,), (1,)), ((), ()))
@@ -383,8 +390,8 @@
         mine = (place >> level) & 1
         split = codes.reshape(2, 2, codes.shape[1] // 2, codes.shape[2])
         codes = pick(split, mine, 1) + hop(pick(split, 1 - mine, 1), level)
-    codes = codes + hop(codes, way_bits - 1)
-    codes = codes.astype(BF16)
+    came = hop(codes, way_bits - 1)
+    codes = (codes + came).astype(BF16)
     for level in range(way_bits - 2, -1, -1):
         mine = (place >> level) & 1
         other = hop(codes, level)
@@ -398,6 +405,7 @@
     bit = item_arg & 1
     own = pair_grads(bit, cotangent, [features], ((0, 0), (0, 1)), 0, share, items)
     own = items_sum(*own, item)
+    own = own[0] + own[1].astype(F32)
     returned = [[], []]
     for one in range(chunks):
         pairs = pair_grads(
@@ -405,30 +413,43 @@
             cotangent,
             [far[0][one], far[1][one]],
             ((0, 0), (1, 0)),
-            one * per,
-            per,
+            sum(sizes[:one]),
+            sizes[one],
             items,
         )
-        done = items_sum(*pairs, item).astype(BF16)
+        keep, came = items_sum(*pairs, item)
         for way in range(2):
-            returned[way].append(hop(done[way], far_bits[way]))
-
-    low = items_sum(*low_kernel(bit, backs, features, codes, cotangent, items), item)
-
-    mixed = mixed_kernel(
-        features,
-        block_weights,
-        codes,
-        lowrank_out,
-        far,
-        far_weights,
-        pos,
-        item_arg,
-        units,
-        bits,
-    )
-    block_grads = place_kernel(own, returned, pos)
+            done = (keep[way] + came[way].astype(F32)).astype(BF16)
+            returned[way].append(hop(done, far_bits[way]))
+
+    low = low_kernel(bit, backs, features, codes, cotangent, items)
+    keep, came = items_sum(*low, item)
+    low = [keep[way] + came[way].astype(F32) for way in range(2)]
+
+    mixed = None
+    for first, last in ((0, chunks - 1), (chunks - 1, chunks)):
+        mixed = mixed_kernel(
+            features,
+            block_weights,
+            codes,
+            lowrank_out,
+            far,
+            far_weights,
+            pos,
+            item_arg,
+            sizes,
+            first,
+            last,
+            units,
+            order,
+            mixed,
+        )
+    block_grads = place_kernel(own, returned, pos, sizes)
     return (mixed, block_grads, low[0], low[1])
+
+
+def chunk_sizes(share):
+    return CHUNK_SIZES if sum(CHUNK_SIZES) == share else (1,) * share
 
 
 def solution(mesh):

time: 278 us -> 253 us (0.910)
  waiting for transfers between devices: 162 us -> 136 us
  Pallas kernels: 43.1 us -> 47.8 us
    ppermute x37 -> x39, waiting for transfers between devices: 162 us -> 136 us  [swapped(): lax.ppermute(block, axis, [(one, one ^ 1 << apart) for one in range(count)])]
    concatenate x4 -> x0, other arithmetic: 7.67 us -> none  [layer(): held = jnp.concatenate([held, swapped(held, 'items', level)], axis=0)]
    convert_element_type x6, other arithmetic: 3.99 us -> 10.2 us  [items_sum(): came = swapped(leave.astype(BF16), 'items', level)]
    pallas_call x2 -> x3, Pallas kernels: 15.4 us -> 19.8 us  [the longest x2 13.9 us: mixed_kernel(): pl.pallas_call(functools.partial(mixed_body, share, sizes, first, last, u...]
    squeeze x1 -> x0, other arithmetic: 3.83 us -> none  [items_sum(): return (keep + came.astype(F32))[0]]
    slice x1 -> x4, local copies, waits for them, and re-layouts: 1.18 us -> 4.62 us  [layer(): piece = source[:, first:first + sizes[one] * BLOCK]]
    squeeze x6 -> x1, local copies, waits for them, and re-layouts: 5.62 us -> 2.24 us  [layer(): held, order = ([hop(shares[way], far_bits[way])], [0])]
    unnamed x66 -> x56, local copies, waits for them, and re-layouts: 5.86 us -> 3.37 us
  transfers between devices with their start and end apart: 37 -> 39, of which waited for: 13 -> 14; matrix products, arithmetic and copies ran while one was open for 9% -> 10% of each run, Pallas kernels for 13% -> 17%
where the time goes in v1:
time: 253 us; the launch traced here: 252 us
  waiting for transfers between devices  136 us (54%)
  Pallas kernels  47.8 us (19%)
  starting transfers between devices  35.4 us (14%)
  other arithmetic  17.5 us (7%)
  local copies, waits for them, and re-layouts  10.9 us (4%)
  matrix products  3.08 us (1%)
    ppermute x39, waiting for transfers between devices, swapped(): lax.ppermute(block, axis, [(one, one ^ 1 << apart) for one in range(count)])  136 us
    ppermute x39, starting transfers between devices, swapped(): lax.ppermute(block, axis, [(one, one ^ 1 << apart) for one in range(count)])  35.4 us
    pallas_call x5, Pallas kernels, pair_grads(): pl.pallas_call(functools.partial(grad_body, pairs, part), grid_spec=pltpu...  19.8 us
    pallas_call x2, Pallas kernels, mixed_kernel(): pl.pallas_call(functools.partial(mixed_body, share, sizes, first, last, u...  13.9 us
    convert_element_type x6, other arithmetic, items_sum(): came = swapped(leave.astype(BF16), 'items', level)  10.2 us
    pallas_call x1, Pallas kernels, place_kernel(): pl.pallas_call(functools.partial(place_body, share, sizes), grid_spec=plt...  5.84 us
    pallas_call x1, Pallas kernels, low_kernel(): pl.pallas_call(functools.partial(low_body, part), grid_spec=pltpu.Prefetc...  5.21 us
  transfers between devices with their start and end apart: 39, of which 14 were waited for; matrix products, arithmetic and copies ran while one was open for 10% of the time, Pallas kernels for 17%

profile of v1, /device:TPU:0, one launch (start us, length us, event | category | flops | bytes accessed | tf_op | source)
XLA Modules:
  0.0 251.8 jit_solution(8344326966441104206)
XLA Ops:
  0.7 1.2 copy-done
  1.9 2.4 fusion.28
  4.3 0.7 fusion.29
  5.0 3.1 %collective-permute-start = (f32[2,128,128]{2,1,0:T(8,128)S(1)}, f32[2,128,128]{2,1,0:T(8,128)S(1)}, u32[]{:S(2)}, u32[]{:S(2)}) collective-permute-start(f32[2,128,128]{2,1,0:T(8,128)S(1)} %fusion.19), channel_id=1, source_target_pairs={{0,4},{4,0},{8,12},{12,8},{1,5},{5,1},{9,13},{13,9},{2,6},{6,2},{1... | collective-permute-start | bytes 393224 | tf_op jit(solution)/shard_map/ppermute | solution.py:22
  8.2 0.8 slice.106
  9.1 0.8 collective-permute-start.16
  9.8 2.6 %collective-permute-start.4 = (bf16[256,1024]{1,0:T(8,128)(2,1)}, bf16[256,1024]{1,0:T(8,128)(2,1)S(1)}, u32[]{:S(2)}, u32[]{:S(2)}) collective-permute-start(bf16[256,1024]{1,0:T(8,128)(2,1)} %slice.106), channel_id=1, source_target_pairs={{0,8},{4,12},{8,0},{12,4},{1,9},{5,13},{9,1},{13,5},{2,10},{6,14},... | collective-permute-start | bytes 1572872 | tf_op jit(solution)/shard_map/ppermute | solution.py:22
  12.4 1.3 collective-permute-start.15
  14.0 2.6 %collective-permute-start.1 = (f32[2,128,128]{2,1,0:T(8,128)S(1)}, f32[2,128,128]{2,1,0:T(8,128)S(1)}, u32[]{:S(2)}, u32[]{:S(2)}) collective-permute-start(f32[2,128,128]{2,1,0:T(8,128)S(1)} %fusion.22), channel_id=1, source_target_pairs={{0,8},{4,12},{8,0},{12,4},{1,9},{5,13},{9,1},{13,5},{2,10},{6,14},... | collective-permute-start | bytes 393224 | tf_op jit(solution)/shard_map/ppermute | solution.py:22
  16.7 0.7 select_reduce_fusion.pos_ref
  17.4 3.0 %weight_share.1 = bf16[2,4,256,256]{3,2,1,0:T(8,128)(2,1)} custom-call(s32[64]{0:T(128)} %select_reduce_fusion.pos_ref, s32[1]{0:T(128)} %bitcast.item_ref, bf16[64,256,256]{2,1,0:T(8,128)(2,1)} %w_ref.5), custom_call_target="tpu_custom_call" | custom-call | bytes 2097152 | tf_op jit(solution)/shard_map/weight_share/pallas_call | solution.py:158
  20.4 43.3 %collective-permute-done.1 = f32[2,128,128]{2,1,0:T(8,128)S(1)} collective-permute-done((f32[2,128,128]{2,1,0:T(8,128)S(1)}, f32[2,128,128]{2,1,0:T(8,128)S(1)}, u32[]{:S(2)}, u32[]{:S(2)}) %collective-permute-start.1) | collective-permute-done | bytes 131104 | tf_op jit(solution)/shard_map/ppermute | solution.py:22
  64.0 2.2 slice_bitcast_fusion
  66.2 1.8 collective-permute-done.2
  68.1 1.5 collective-permute-start.11
  69.6 2.0 collective-permute-start.7
  71.7 1.9 slice.110
  73.6 1.3 collective-permute-start.17
  74.9 3.0 %pair_grads.6 = (bf16[2,2,4,64,256]{4,3,2,1,0:T(8,128)(2,1)}, f32[2,2,4,64,256]{4,3,2,1,0:T(8,128)}) custom-call(s32[1]{0:T(128)S(6)} %and.24.bit_ref, bf16[256,4096]{1,0:T(8,128)(2,1)} %g_ref.11, bf16[256,1024]{1,0:T(8,128)(2,1)} %copy-done.10, bf16[256,1024]{1,0:T(8,128)(2,1)} %copy-done.11), custom_call_target="tpu_custom_call" | custom-call | flops 268435456 | bytes 3145728 | tf_op jit(solution)/shard_map/pair_grads/pallas_call | solution.py:62
  78.1 8.3 %pair_grads.5 = (bf16[2,2,16,64,256]{4,3,2,1,0:T(8,128)(2,1)}, f32[2,2,16,64,256]{4,3,2,1,0:T(8,128)}) custom-call(s32[1]{0:T(128)S(6)} %and.24.bit_ref, bf16[256,4096]{1,0:T(8,128)(2,1)} %g_ref.11, bf16[256,4096]{1,0:T(8,128)(2,1)} %f_ref.5), custom_call_target="tpu_custom_call" | custom-call | flops 1073741824 | bytes 12582912 | tf_op jit(solution)/shard_map/pair_grads/pallas_call | solution.py:62
  86.3 1.9 slice.107
  88.2 2.8 %pair_grads.7 = (bf16[2,2,4,64,256]{4,3,2,1,0:T(8,128)(2,1)}, f32[2,2,4,64,256]{4,3,2,1,0:T(8,128)}) custom-call(s32[1]{0:T(128)S(6)} %and.24.bit_ref, bf16[256,4096]{1,0:T(8,128)(2,1)} %g_ref.11, bf16[256,1024]{1,0:T(8,128)(2,1)} %copy-done.8, bf16[256,1024]{1,0:T(8,128)(2,1)} %copy-done.9), custom_call_target="tpu_custom_call" | custom-call | flops 268435456 | bytes 3145728 | tf_op jit(solution)/shard_map/pair_grads/pallas_call | solution.py:62
  91.0 4.5 %collective-permute-done.11.refs_10_.refs_6_ = bf16[4,256,256]{2,1,0:T(8,128)(2,1)} collective-permute-done((bf16[4,256,256]{2,1,0:T(8,128)(2,1)}, bf16[4,256,256]{2,1,0:T(8,128)(2,1)}, u32[]{:S(2)}, u32[]{:S(2)}) %collective-permute-start.11) | collective-permute-done | bytes 524320 | tf_op jit(solution)/shard_map/ppermute | solution.py:22
  96.0 21.9 %collective-permute-done.18.refs_5_.refs_1_ = bf16[256,1024]{1,0:T(8,128)(2,1)S(1)} collective-permute-done((bf16[256,1024]{1,0:T(8,128)(2,1)}, bf16[256,1024]{1,0:T(8,128)(2,1)S(1)}, u32[]{:S(2)}, u32[]{:S(2)}) %collective-permute-start.18) | collective-permute-done | bytes 524320 | tf_op jit(solution)/shard_map/ppermute | solution.py:22
  117.9 0.7 slice_bitcast_fusion.2
  118.6 5.2 %low_grads.1 = (bf16[2,2,32,4096]{3,2,1,0:T(8,128)(2,1)}, f32[2,2,32,4096]{3,2,1,0:T(8,128)}) custom-call(s32[1]{0:T(128)S(6)} %and.24.bit_ref, bf16[256,128]{1,0:T(8,128)(2,1)} %get-tuple-element.56.b_ref, bf16[256,4096]{1,0:T(8,128)(2,1)} %f_ref.5, bf16[256,128]{1,0:T(8,128)(2,1)} %get-tuple-element.57.codes_ref.c_ref, bf16[256,4096]{1,0:T(8,128)(2,1)} %g_ref.11), custom_call_target="tpu_custom_call" | custom-call | flops 536870912 | bytes 7340032 | tf_op jit(solution)/shard_map/low_grads/pallas_call | solution.py:104
  124.3 1.2 add_convert_fusion.5
  125.5 11.5 %collective-permute-done.6.refs_1_ = bf16[256,1024]{1,0:T(8,128)(2,1)S(1)} collective-permute-done((bf16[256,1024]{1,0:T(8,128)(2,1)}, bf16[256,1024]{1,0:T(8,128)(2,1)S(1)}, u32[]{:S(2)}, u32[]{:S(2)}) %collective-permute-start.6) | collective-permute-done | bytes 524320 | tf_op jit(solution)/shard_map/ppermute | solution.py:22
  137.0 1.6 collective-permute-start.22
  138.6 1.2 add_convert_fusion.4
  139.7 1.7 collective-permute-done.5.refs_0_
  141.4 1.5 collective-permute-start.25
  143.5 2.8 %collective-permute-done.22 = bf16[1,2,4,64,256]{4,3,2,1,0:T(8,128)(2,1)S(1)} collective-permute-done((bf16[1,2,4,64,256]{4,3,2,1,0:T(8,128)(2,1)S(1)}, bf16[1,2,4,64,256]{4,3,2,1,0:T(8,128)(2,1)S(1)}, u32[]{:S(2)}, u32[]{:S(2)}) %collective-permute-start.22) | collective-permute-done | bytes 262176 | tf_op jit(solution)/shard_map/ppermute | solution.py:22
  146.3 0.7 copy-done.18
  146.9 1.5 collective-permute-start.8
  148.4 2.8 %pair_grads.9 = (bf16[2,2,4,64,256]{4,3,2,1,0:T(8,128)(2,1)}, f32[2,2,4,64,256]{4,3,2,1,0:T(8,128)}) custom-call(s32[1]{0:T(128)S(6)} %and.24.bit_ref, bf16[256,4096]{1,0:T(8,128)(2,1)} %g_ref.11, bf16[256,1024]{1,0:T(8,128)(2,1)} %collective-permute-done.5.refs_0_, bf16[256,1024]{1,0:T(8,128)(2,1)} %copy-done.14), custom_call_target="tpu_custom_call" | custom-call | flops 268435456 | bytes 3145728 | tf_op jit(solution)/shard_map/pair_grads/pallas_call | solution.py:62
  151.2 0.7 collective-permute-done.25
  152.0 2.9 %pair_grads.8 = (bf16[2,2,4,64,256]{4,3,2,1,0:T(8,128)(2,1)}, f32[2,2,4,64,256]{4,3,2,1,0:T(8,128)}) custom-call(s32[1]{0:T(128)S(6)} %and.24.bit_ref, bf16[256,4096]{1,0:T(8,128)(2,1)} %g_ref.11, bf16[256,1024]{1,0:T(8,128)(2,1)} %copy-done.13, bf16[256,1024]{1,0:T(8,128)(2,1)} %copy-done.12), custom_call_target="tpu_custom_call" | custom-call | flops 268435456 | bytes 3145728 | tf_op jit(solution)/shard_map/pair_grads/pallas_call | solution.py:62
  154.8 0.8 fusion.14
  155.6 1.7 fusion.15
  157.3 5.9 %collective-permute-done.12.refs_11_.refs_7_ = bf16[4,256,256]{2,1,0:T(8,128)(2,1)} collective-permute-done((bf16[4,256,256]{2,1,0:T(8,128)(2,1)}, bf16[4,256,256]{2,1,0:T(8,128)(2,1)}, u32[]{:S(2)}, u32[]{:S(2)}) %collective-permute-start.12) | collective-permute-done | bytes 524320 | tf_op jit(solution)/shard_map/ppermute | solution.py:22
  163.2 10.7 %collective-permute-done.8.refs_7_.refs_3_ = bf16[4,256,256]{2,1,0:T(8,128)(2,1)} collective-permute-done((bf16[4,256,256]{2,1,0:T(8,128)(2,1)}, bf16[4,256,256]{2,1,0:T(8,128)(2,1)}, u32[]{:S(2)}, u32[]{:S(2)}) %collective-permute-start.8) | collective-permute-done | bytes 524320 | tf_op jit(solution)/shard_map/ppermute | solution.py:22
  174.5 2.3 add_convert_fusion.1
  176.9 2.0 add_convert_fusion.2
  178.8 3.2 %collective-permute-start.23 = (bf16[4,64,256]{2,1,0:T(8,128)(2,1)}, bf16[4,64,256]{2,1,0:T(8,128)(2,1)}, u32[]{:S(2)}, u32[]{:S(2)}) collective-permute-start(bf16[4,64,256]{2,1,0:T(8,128)(2,1)} %get-tuple-element.55), channel_id=1, source_target_pairs={{0,4},{4,0},{8,12},{12,8},{1,5},{5,1},{9,13},{13,9},{2,6},{6,2},{1... | collective-permute-start | bytes 393224 | tf_op jit(solution)/shard_map/ppermute | solution.py:22
  182.1 1.5 collective-permute-start.31
  183.6 8.0 %mixed.2.refs_10_ = bf16[256,4096]{1,0:T(8,128)(2,1)} custom-call(s32[64]{0:T(128)} %select_reduce_fusion.pos_ref, s32[1]{0:T(128)} %bitcast.item_ref, bf16[256,4096]{1,0:T(8,128)(2,1)} %f_ref.5, bf16[64,256,256]{2,1,0:T(8,128)(2,1)} %w_ref.5, bf16[256,128]{1,0:T(8,128)(2,1)} %get-tuple-element.57.codes_ref.c_ref, bf16[128,4096]{1,0:T(8,128)(2,1)} %low_ref.3, ...), custom_call_target="tpu_custom_call" | custom-call | flops 1811939328 | bytes 12582912 | tf_op jit(solution)/shard_map/mixed/pallas_call | solution.py:266
  191.6 5.9 %mixed.3 = bf16[256,4096]{1,0:T(8,128)(2,1)} custom-call(s32[64]{0:T(128)} %select_reduce_fusion.pos_ref, s32[1]{0:T(128)} %bitcast.item_ref, bf16[256,4096]{1,0:T(8,128)(2,1)} %f_ref.5, bf16[64,256,256]{2,1,0:T(8,128)(2,1)} %w_ref.5, bf16[256,128]{1,0:T(8,128)(2,1)} %get-tuple-element.57.codes_ref.c_ref, ...), custom_call_target="tpu_custom_call", output_to_operand_aliasing={{}: (16, {})} | custom-call | flops 603979776 | bytes 4194304 | tf_op jit(solution)/shard_map/mixed/pallas_call | solution.py:266
  198.2 1.5 add_convert_fusion.3
  199.6 1.6 collective-permute-start.28
  201.2 1.0 fusion.17
  202.4 2.1 add_convert_fusion
  204.5 12.4 %collective-permute-done.28 = bf16[1,2,4,64,256]{4,3,2,1,0:T(8,128)(2,1)S(1)} collective-permute-done((bf16[1,2,4,64,256]{4,3,2,1,0:T(8,128)(2,1)S(1)}, bf16[1,2,4,64,256]{4,3,2,1,0:T(8,128)(2,1)S(1)}, u32[]{:S(2)}, u32[]{:S(2)}) %collective-permute-start.28) | collective-permute-done | bytes 262176 | tf_op jit(solution)/shard_map/ppermute | solution.py:22
  218.0 1.1 fusion
  219.1 1.3 collective-permute-start.36
  220.4 0.7 collective-permute-start.32
  221.1 2.6 %collective-permute-start.35 = (bf16[4,64,256]{2,1,0:T(8,128)(2,1)S(1)}, bf16[4,64,256]{2,1,0:T(8,128)(2,1)S(1)}, u32[]{:S(2)}, u32[]{:S(2)}) collective-permute-start(bf16[4,64,256]{2,1,0:T(8,128)(2,1)S(1)} %get-tuple-element.50), channel_id=1, source_target_pairs={{0,8},{4,12},{8,0},{12,4},{1,9},{5,13},{9,1},{13,5},{2,10},{6,14},... | collective-permute-start | bytes 393224 | tf_op jit(solution)/shard_map/ppermute | solution.py:22
  223.6 17.1 %collective-permute-done.20 = bf16[1,2,16,64,256]{4,3,2,1,0:T(8,128)(2,1)S(1)} collective-permute-done((bf16[1,2,16,64,256]{4,3,2,1,0:T(8,128)(2,1)S(1)}, bf16[1,2,16,64,256]{4,3,2,1,0:T(8,128)(2,1)S(1)}, u32[]{:S(2)}, u32[]{:S(2)}) %collective-permute-start.20) | collective-permute-done | bytes 1048608 | tf_op jit(solution)/shard_map/ppermute | solution.py:22
  240.7 0.7 collective-permute-start.29
  241.4 1.8 add_bitcast_fusion.own_ref
  243.2 0.6 copy-done.22
  244.0 0.7 copy-done.25
  244.6 1.1 collective-permute-done.29.refs_2_
  245.8 5.8 %place.1 = f32[64,64,256]{2,1,0:T(8,128)} custom-call(s32[64]{0:T(128)} %select_reduce_fusion.pos_ref, f32[2,16,64,256]{3,2,1,0:T(8,128)} %add_bitcast_fusion.own_ref, bf16[4,64,256]{2,1,0:T(8,128)(2,1)} %collective-permute-done.23.refs_0_, bf16[4,64,256]{2,1,0:T(8,128)(2,1)} %copy-done.22, bf16[4,64,256]{2,1,0:T(8,128)(2,1)} %collective-permute-done.29.refs_2_, ...), custom_call_target="tpu_custom_call" | custom-call | bytes 8388608 | tf_op jit(solution)/shard_map/place/pallas_call | solution.py:313
  (106 shorter events, 5.0 us)
Async XLA Ops:
  0.6 1.2 copy-start
  0.6 3.6 %copy-start.2 = (bf16[256,4096]{1,0:T(8,128)(2,1)S(1)}, bf16[256,4096]{1,0:T(8,128)(2,1)}, u32[]{:S(2)}) copy-start(bf16[256,4096]{1,0:T(8,128)(2,1)} %g_ref.11) | copy-start | bytes 6291460
  1.9 2.4 copy-start.4
  4.3 3.9 %copy-start.3 = (bf16[256,4096]{1,0:T(8,128)(2,1)S(1)}, bf16[256,4096]{1,0:T(8,128)(2,1)}, u32[]{:S(2)}) copy-start(bf16[256,4096]{1,0:T(8,128)(2,1)} %f_ref.5) | copy-start | bytes 6291460
  5.0 11.7 %copy-start.26 = (s32[64]{0:T(128)S(1)}, s32[64]{0:T(128)}, u32[]{:S(2)}) copy-start(s32[64]{0:T(128)} %param.11) | copy-start | bytes 772
  5.0 11.7 %copy-start.27 = (s32[64]{0:T(128)S(1)}, s32[64]{0:T(128)}, u32[]{:S(2)}) copy-start(s32[64]{0:T(128)} %param.10) | copy-start | bytes 772
  5.0 9.0 %collective-permute-start = (f32[2,128,128]{2,1,0:T(8,128)S(1)}, f32[2,128,128]{2,1,0:T(8,128)S(1)}, u32[]{:S(2)}, u32[]{:S(2)}) collective-permute-start(f32[2,128,128]{2,1,0:T(8,128)S(1)} %fusion.19), channel_id=1, source_target_pairs={{0,4},{4,0},{8,12},{12,8},{1,5},{5,1},{9,13},{13,9},{2,6},{6,2},{1... | collective-permute-start | bytes 393224 | tf_op jit(solution)/shard_map/ppermute | solution.py:22
  9.1 64.5 %collective-permute-start.16 = (bf16[256,1024]{1,0:T(8,128)(2,1)}, bf16[256,1024]{1,0:T(8,128)(2,1)S(1)}, u32[]{:S(2)}, u32[]{:S(2)}) collective-permute-start(bf16[256,1024]{1,0:T(8,128)(2,1)} %slice.106), channel_id=1, source_target_pairs={{0,4},{4,0},{8,12},{12,8},{1,5},{5,1},{9,13},{13,9},{2,6},{6,2},{1... | collective-permute-start | bytes 1572872 | tf_op jit(solution)/shard_map/ppermute | solution.py:22
  9.8 68.2 %collective-permute-start.4 = (bf16[256,1024]{1,0:T(8,128)(2,1)}, bf16[256,1024]{1,0:T(8,128)(2,1)S(1)}, u32[]{:S(2)}, u32[]{:S(2)}) collective-permute-start(bf16[256,1024]{1,0:T(8,128)(2,1)} %slice.106), channel_id=1, source_target_pairs={{0,8},{4,12},{8,0},{12,4},{1,9},{5,13},{9,1},{13,5},{2,10},{6,14},... | collective-permute-start | bytes 1572872 | tf_op jit(solution)/shard_map/ppermute | solution.py:22
  12.4 61.2 %collective-permute-start.15 = (bf16[256,1024]{1,0:T(8,128)(2,1)S(1)}, bf16[256,1024]{1,0:T(8,128)(2,1)S(1)}, u32[]{:S(2)}, u32[]{:S(2)}) collective-permute-start(bf16[256,1024]{1,0:T(8,128)(2,1)S(1)} %slice.105), channel_id=1, source_target_pairs={{0,4},{4,0},{8,12},{12,8},{1,5},{5,1},{9,13},{13,9},{2,6},{6,2},{1... | collective-permute-start | bytes 1572872 | tf_op jit(solution)/shard_map/ppermute | solution.py:22
  13.7 56.0 %collective-permute-start.3 = (bf16[256,1024]{1,0:T(8,128)(2,1)S(1)}, bf16[256,1024]{1,0:T(8,128)(2,1)S(1)}, u32[]{:S(2)}, u32[]{:S(2)}) collective-permute-start(bf16[256,1024]{1,0:T(8,128)(2,1)S(1)} %slice.105), channel_id=1, source_target_pairs={{0,8},{4,12},{8,0},{12,4},{1,9},{5,13},{9,1},{13,5},{2,10},{6,14},... | collective-permute-start | bytes 1572872 | tf_op jit(solution)/shard_map/ppermute | solution.py:22
  14.0 49.7 %collective-permute-start.1 = (f32[2,128,128]{2,1,0:T(8,128)S(1)}, f32[2,128,128]{2,1,0:T(8,128)S(1)}, u32[]{:S(2)}, u32[]{:S(2)}) collective-permute-start(f32[2,128,128]{2,1,0:T(8,128)S(1)} %fusion.22), channel_id=1, source_target_pairs={{0,8},{4,12},{8,0},{12,4},{1,9},{5,13},{9,1},{13,5},{2,10},{6,14},... | collective-permute-start | bytes 393224 | tf_op jit(solution)/shard_map/ppermute | solution.py:22
  63.7 4.3 %collective-permute-start.2 = (bf16[2,128,128]{2,1,0:T(8,128)(2,1)S(1)}, bf16[2,128,128]{2,1,0:T(8,128)(2,1)S(1)}, u32[]{:S(2)}, u32[]{:S(2)}) collective-permute-start(bf16[2,128,128]{2,1,0:T(8,128)(2,1)S(1)} %add_convert_fusion.6), channel_id=1, source_target_pairs={{0,4},{4,0},{8,12},{12,8},{1,5},{5,1},{9,13},{13,9},{2,6},{6,2},{1... | collective-permute-start | bytes 196616 | tf_op jit(solution)/shard_map/ppermute | solution.py:22
  68.1 27.4 %collective-permute-start.11 = (bf16[4,256,256]{2,1,0:T(8,128)(2,1)}, bf16[4,256,256]{2,1,0:T(8,128)(2,1)}, u32[]{:S(2)}, u32[]{:S(2)}) collective-permute-start(bf16[4,256,256]{2,1,0:T(8,128)(2,1)} %get-tuple-element.46), channel_id=1, source_target_pairs={{0,8},{4,12},{8,0},{12,4},{1,9},{5,13},{9,1},{13,5},{2,10},{6,14},... | collective-permute-start | bytes 1572872 | tf_op jit(solution)/shard_map/ppermute | solution.py:22
  69.6 5.3 %copy-start.11 = (bf16[256,1024]{1,0:T(8,128)(2,1)}, bf16[256,1024]{1,0:T(8,128)(2,1)S(1)}, u32[]{:S(2)}) copy-start(bf16[256,1024]{1,0:T(8,128)(2,1)S(1)} %collective-permute-done.3.refs_3_.refs_1_) | copy-start | bytes 1572868
  69.6 26.3 %collective-permute-start.7 = (bf16[4,256,256]{2,1,0:T(8,128)(2,1)}, bf16[4,256,256]{2,1,0:T(8,128)(2,1)}, u32[]{:S(2)}, u32[]{:S(2)}) collective-permute-start(bf16[4,256,256]{2,1,0:T(8,128)(2,1)} %get-tuple-element.47), channel_id=1, source_target_pairs={{0,4},{4,0},{8,12},{12,8},{1,5},{5,1},{9,13},{13,9},{2,6},{6,2},{1... | collective-permute-start | bytes 1572872 | tf_op jit(solution)/shard_map/ppermute | solution.py:22
  73.5 12.8 %copy-start.8 = (bf16[256,1024]{1,0:T(8,128)(2,1)}, bf16[256,1024]{1,0:T(8,128)(2,1)S(1)}, u32[]{:S(2)}) copy-start(bf16[256,1024]{1,0:T(8,128)(2,1)S(1)} %collective-permute-done.16.refs_1_.refs_0_) | copy-start | bytes 1572868
  73.5 44.4 %collective-permute-start.18 = (bf16[256,1024]{1,0:T(8,128)(2,1)}, bf16[256,1024]{1,0:T(8,128)(2,1)S(1)}, u32[]{:S(2)}, u32[]{:S(2)}) collective-permute-start(bf16[256,1024]{1,0:T(8,128)(2,1)} %slice.110), channel_id=1, source_target_pairs={{0,8},{4,12},{8,0},{12,4},{1,9},{5,13},{9,1},{13,5},{2,10},{6,14},... | collective-permute-start | bytes 1572872 | tf_op jit(solution)/shard_map/ppermute | solution.py:22
  73.6 1.3 copy-start.10
  73.6 45.0 %collective-permute-start.17 = (bf16[256,1024]{1,0:T(8,128)(2,1)}, bf16[256,1024]{1,0:T(8,128)(2,1)S(1)}, u32[]{:S(2)}, u32[]{:S(2)}) collective-permute-start(bf16[256,1024]{1,0:T(8,128)(2,1)} %slice.110), channel_id=1, source_target_pairs={{0,4},{4,0},{8,12},{12,8},{1,5},{5,1},{9,13},{13,9},{2,6},{6,2},{1... | collective-permute-start | bytes 1572872 | tf_op jit(solution)/shard_map/ppermute | solution.py:22
  78.0 8.4 %copy-start.9 = (bf16[256,1024]{1,0:T(8,128)(2,1)}, bf16[256,1024]{1,0:T(8,128)(2,1)S(1)}, u32[]{:S(2)}) copy-start(bf16[256,1024]{1,0:T(8,128)(2,1)S(1)} %collective-permute-done.4.refs_4_.refs_1_) | copy-start | bytes 1572868
  78.0 45.9 %collective-permute-start.21 = (bf16[2,2,4,64,256]{4,3,2,1,0:T(8,128)(2,1)}, bf16[2,2,4,64,256]{4,3,2,1,0:T(8,128)(2,1)}, u32[]{:S(2)}, u32[]{:S(2)}) collective-permute-start(bf16[2,2,4,64,256]{4,3,2,1,0:T(8,128)(2,1)} %get-tuple-element.25), channel_id=1, source_target_pairs={{0,1},{1,0},{2,3},{3,2},{4,5},{5,4},{6,7},{7,6},{8,9},{9,8},{10,11... | collective-permute-start | bytes 1572872 | tf_op jit(solution)/shard_map/ppermute | solution.py:22
  95.5 41.5 %collective-permute-start.6 = (bf16[256,1024]{1,0:T(8,128)(2,1)}, bf16[256,1024]{1,0:T(8,128)(2,1)S(1)}, u32[]{:S(2)}, u32[]{:S(2)}) collective-permute-start(bf16[256,1024]{1,0:T(8,128)(2,1)} %slice.107), channel_id=1, source_target_pairs={{0,8},{4,12},{8,0},{12,4},{1,9},{5,13},{9,1},{13,5},{2,10},{6,14},... | collective-permute-start | bytes 1572872 | tf_op jit(solution)/shard_map/ppermute | solution.py:22
  96.0 41.0 %collective-permute-start.24 = (bf16[2,2,4,64,256]{4,3,2,1,0:T(8,128)(2,1)}, bf16[2,2,4,64,256]{4,3,2,1,0:T(8,128)(2,1)}, u32[]{:S(2)}, u32[]{:S(2)}) collective-permute-start(bf16[2,2,4,64,256]{4,3,2,1,0:T(8,128)(2,1)} %get-tuple-element.27), channel_id=1, source_target_pairs={{0,1},{1,0},{2,3},{3,2},{4,5},{5,4},{6,7},{7,6},{8,9},{9,8},{10,11... | collective-permute-start | bytes 1572872 | tf_op jit(solution)/shard_map/ppermute | solution.py:22
  117.9 5.9 %copy-start.12 = (bf16[256,1024]{1,0:T(8,128)(2,1)}, bf16[256,1024]{1,0:T(8,128)(2,1)S(1)}, u32[]{:S(2)}) copy-start(bf16[256,1024]{1,0:T(8,128)(2,1)S(1)} %collective-permute-done.18.refs_5_.refs_1_) | copy-start | bytes 1572868
  117.9 23.5 %collective-permute-start.5 = (bf16[256,1024]{1,0:T(8,128)(2,1)}, bf16[256,1024]{1,0:T(8,128)(2,1)}, u32[]{:S(2)}, u32[]{:S(2)}) collective-permute-start(bf16[256,1024]{1,0:T(8,128)(2,1)} %slice.107), channel_id=1, source_target_pairs={{0,4},{4,0},{8,12},{12,8},{1,5},{5,1},{9,13},{13,9},{2,6},{6,2},{1... | collective-permute-start | bytes 1572872 | tf_op jit(solution)/shard_map/ppermute | solution.py:22
  118.6 5.2 %copy-start.13 = (bf16[256,1024]{1,0:T(8,128)(2,1)}, bf16[256,1024]{1,0:T(8,128)(2,1)S(1)}, u32[]{:S(2)}) copy-start(bf16[256,1024]{1,0:T(8,128)(2,1)S(1)} %collective-permute-done.17.refs_2_.refs_0_) | copy-start | bytes 1572868
  118.6 24.3 %collective-permute-start.13 = (bf16[4,256,256]{2,1,0:T(8,128)(2,1)}, bf16[4,256,256]{2,1,0:T(8,128)(2,1)}, u32[]{:S(2)}, u32[]{:S(2)}) collective-permute-start(bf16[4,256,256]{2,1,0:T(8,128)(2,1)} %collective-permute-done.11.refs_10_.refs_6_), channel_id=1, source_target_pairs={{0,1},{1,0},{2,3},{3,2},{4,5},{5,4},{6,7},{7,6},{8,9},{9,8},{10,11... | collective-permute-start | bytes 1572872 | tf_op jit(solution)/shard_map/ppermute | solution.py:22
  118.6 5.7 %copy-start.15 = (f32[2,2,4,64,256]{4,3,2,1,0:T(8,128)S(1)}, f32[2,2,4,64,256]{4,3,2,1,0:T(8,128)}, u32[]{:S(2)}) copy-start(f32[2,2,4,64,256]{4,3,2,1,0:T(8,128)} %get-tuple-element.24) | copy-start | bytes 3145732
  123.9 14.7 %copy-start.16 = (f32[2,2,4,64,256]{4,3,2,1,0:T(8,128)S(1)}, f32[2,2,4,64,256]{4,3,2,1,0:T(8,128)}, u32[]{:S(2)}) copy-start(f32[2,2,4,64,256]{4,3,2,1,0:T(8,128)} %get-tuple-element.26) | copy-start | bytes 3145732
  123.9 50.0 %collective-permute-start.37 = (bf16[2,2,32,4096]{3,2,1,0:T(8,128)(2,1)}, bf16[2,2,32,4096]{3,2,1,0:T(8,128)(2,1)}, u32[]{:S(2)}, u32[]{:S(2)}) collective-permute-start(bf16[2,2,32,4096]{3,2,1,0:T(8,128)(2,1)} %get-tuple-element.33), channel_id=1, source_target_pairs={{0,1},{1,0},{2,3},{3,2},{4,5},{5,4},{6,7},{7,6},{8,9},{9,8},{10,11... | collective-permute-start | bytes 3145736 | tf_op jit(solution)/shard_map/ppermute | solution.py:22
  137.0 1.6 copy-start.14
  137.0 65.2 %collective-permute-start.19 = (bf16[2,2,16,64,256]{4,3,2,1,0:T(8,128)(2,1)}, bf16[2,2,16,64,256]{4,3,2,1,0:T(8,128)(2,1)S(1)}, u32[]{:S(2)}, u32[]{:S(2)}) collective-permute-start(bf16[2,2,16,64,256]{4,3,2,1,0:T(8,128)(2,1)} %get-tuple-element.23), channel_id=1, source_target_pairs={{0,1},{1,0},{2,3},{3,2},{4,5},{5,4},{6,7},{7,6},{8,9},{9,8},{10,11... | collective-permute-start | bytes 6291464 | tf_op jit(solution)/shard_map/ppermute | solution.py:22
  137.0 9.2 %collective-permute-start.22 = (bf16[1,2,4,64,256]{4,3,2,1,0:T(8,128)(2,1)S(1)}, bf16[1,2,4,64,256]{4,3,2,1,0:T(8,128)(2,1)S(1)}, u32[]{:S(2)}, u32[]{:S(2)}) collective-permute-start(bf16[1,2,4,64,256]{4,3,2,1,0:T(8,128)(2,1)S(1)} %get-tuple-element.44), channel_id=1, source_target_pairs={{0,2},{1,3},{2,0},{3,1},{4,6},{5,7},{6,4},{7,5},{8,10},{9,11},{10,... | collective-permute-start | bytes 786440 | tf_op jit(solution)/shard_map/ppermute | solution.py:22
  141.4 10.5 %collective-permute-start.25 = (bf16[1,2,4,64,256]{4,3,2,1,0:T(8,128)(2,1)S(1)}, bf16[1,2,4,64,256]{4,3,2,1,0:T(8,128)(2,1)}, u32[]{:S(2)}, u32[]{:S(2)}) collective-permute-start(bf16[1,2,4,64,256]{4,3,2,1,0:T(8,128)(2,1)S(1)} %get-tuple-element.42), channel_id=1, source_target_pairs={{0,2},{1,3},{2,0},{3,1},{4,6},{5,7},{6,4},{7,5},{8,10},{9,11},{10,... | collective-permute-start | bytes 786440 | tf_op jit(solution)/shard_map/ppermute | solution.py:22
  142.9 20.3 %collective-permute-start.12 = (bf16[4,256,256]{2,1,0:T(8,128)(2,1)}, bf16[4,256,256]{2,1,0:T(8,128)(2,1)}, u32[]{:S(2)}, u32[]{:S(2)}) collective-permute-start(bf16[4,256,256]{2,1,0:T(8,128)(2,1)} %collective-permute-done.11.refs_10_.refs_6_), channel_id=1, source_target_pairs={{0,2},{1,3},{2,0},{3,1},{4,6},{5,7},{6,4},{7,5},{8,10},{9,11},{10,... | collective-permute-start | bytes 1572872 | tf_op jit(solution)/shard_map/ppermute | solution.py:22
  146.2 0.7 copy-start.18
  146.9 27.0 %collective-permute-start.8 = (bf16[4,256,256]{2,1,0:T(8,128)(2,1)}, bf16[4,256,256]{2,1,0:T(8,128)(2,1)}, u32[]{:S(2)}, u32[]{:S(2)}) collective-permute-start(bf16[4,256,256]{2,1,0:T(8,128)(2,1)} %collective-permute-done.7.refs_6_.refs_2_), channel_id=1, source_target_pairs={{0,2},{1,3},{2,0},{3,1},{4,6},{5,7},{6,4},{7,5},{8,10},{9,11},{10,... | collective-permute-start | bytes 1572872 | tf_op jit(solution)/shard_map/ppermute | solution.py:22
  152.0 2.9 %copy-start.19 = (bf16[1,2,4,64,256]{4,3,2,1,0:T(8,128)(2,1)S(1)}, bf16[1,2,4,64,256]{4,3,2,1,0:T(8,128)(2,1)}, u32[]{:S(2)}) copy-start(bf16[1,2,4,64,256]{4,3,2,1,0:T(8,128)(2,1)} %copy-done.18) | copy-start | bytes 786436
  152.0 22.5 %collective-permute-start.30 = (bf16[2,2,4,64,256]{4,3,2,1,0:T(8,128)(2,1)}, bf16[2,2,4,64,256]{4,3,2,1,0:T(8,128)(2,1)}, u32[]{:S(2)}, u32[]{:S(2)}) collective-permute-start(bf16[2,2,4,64,256]{4,3,2,1,0:T(8,128)(2,1)} %get-tuple-element.31), channel_id=1, source_target_pairs={{0,1},{1,0},{2,3},{3,2},{4,5},{5,4},{6,7},{7,6},{8,9},{9,8},{10,11... | collective-permute-start | bytes 1572872 | tf_op jit(solution)/shard_map/ppermute | solution.py:22
  154.8 19.7 %copy-start.6 = (f32[2,2,32,4096]{3,2,1,0:T(8,128)S(1)}, f32[2,2,32,4096]{3,2,1,0:T(8,128)}, u32[]{:S(2)}) copy-start(f32[2,2,32,4096]{3,2,1,0:T(8,128)} %get-tuple-element.32) | copy-start | bytes 6291460
  163.2 15.6 %collective-permute-start.9 = (bf16[4,256,256]{2,1,0:T(8,128)(2,1)}, bf16[4,256,256]{2,1,0:T(8,128)(2,1)}, u32[]{:S(2)}, u32[]{:S(2)}) collective-permute-start(bf16[4,256,256]{2,1,0:T(8,128)(2,1)} %collective-permute-done.7.refs_6_.refs_2_), channel_id=1, source_target_pairs={{0,1},{1,0},{2,3},{3,2},{4,5},{5,4},{6,7},{7,6},{8,9},{9,8},{10,11... | collective-permute-start | bytes 1572872 | tf_op jit(solution)/shard_map/ppermute | solution.py:22
  173.9 23.6 %collective-permute-start.27 = (bf16[2,2,4,64,256]{4,3,2,1,0:T(8,128)(2,1)}, bf16[2,2,4,64,256]{4,3,2,1,0:T(8,128)(2,1)}, u32[]{:S(2)}, u32[]{:S(2)}) collective-permute-start(bf16[2,2,4,64,256]{4,3,2,1,0:T(8,128)(2,1)} %get-tuple-element.29), channel_id=1, source_target_pairs={{0,1},{1,0},{2,3},{3,2},{4,5},{5,4},{6,7},{7,6},{8,9},{9,8},{10,11... | collective-permute-start | bytes 1572872 | tf_op jit(solution)/shard_map/ppermute | solution.py:22
  173.9 4.9 %collective-permute-start.14 = (bf16[4,256,256]{2,1,0:T(8,128)(2,1)}, bf16[4,256,256]{2,1,0:T(8,128)(2,1)}, u32[]{:S(2)}, u32[]{:S(2)}) collective-permute-start(bf16[4,256,256]{2,1,0:T(8,128)(2,1)} %collective-permute-done.12.refs_11_.refs_7_), channel_id=1, source_target_pairs={{0,1},{1,0},{2,3},{3,2},{4,5},{5,4},{6,7},{7,6},{8,9},{9,8},{10,11... | collective-permute-start | bytes 1572872 | tf_op jit(solution)/shard_map/ppermute | solution.py:22
  174.4 7.6 %collective-permute-start.10 = (bf16[4,256,256]{2,1,0:T(8,128)(2,1)}, bf16[4,256,256]{2,1,0:T(8,128)(2,1)}, u32[]{:S(2)}, u32[]{:S(2)}) collective-permute-start(bf16[4,256,256]{2,1,0:T(8,128)(2,1)} %collective-permute-done.8.refs_7_.refs_3_), channel_id=1, source_target_pairs={{0,1},{1,0},{2,3},{3,2},{4,5},{5,4},{6,7},{7,6},{8,9},{9,8},{10,11... | collective-permute-start | bytes 1572872 | tf_op jit(solution)/shard_map/ppermute | solution.py:22
  174.5 2.3 copy-start.17
  178.8 40.2 %collective-permute-start.33 = (bf16[4,64,256]{2,1,0:T(8,128)(2,1)}, bf16[4,64,256]{2,1,0:T(8,128)(2,1)}, u32[]{:S(2)}, u32[]{:S(2)}) collective-permute-start(bf16[4,64,256]{2,1,0:T(8,128)(2,1)} %get-tuple-element.54), channel_id=1, source_target_pairs={{0,8},{4,12},{8,0},{12,4},{1,9},{5,13},{9,1},{13,5},{2,10},{6,14},... | collective-permute-start | bytes 393224 | tf_op jit(solution)/shard_map/ppermute | solution.py:22
  178.8 41.5 %collective-permute-start.23 = (bf16[4,64,256]{2,1,0:T(8,128)(2,1)}, bf16[4,64,256]{2,1,0:T(8,128)(2,1)}, u32[]{:S(2)}, u32[]{:S(2)}) collective-permute-start(bf16[4,64,256]{2,1,0:T(8,128)(2,1)} %get-tuple-element.55), channel_id=1, source_target_pairs={{0,4},{4,0},{8,12},{12,8},{1,5},{5,1},{9,13},{13,9},{2,6},{6,2},{1... | collective-permute-start | bytes 393224 | tf_op jit(solution)/shard_map/ppermute | solution.py:22
  182.1 17.6 %collective-permute-start.31 = (bf16[1,2,4,64,256]{4,3,2,1,0:T(8,128)(2,1)S(1)}, bf16[1,2,4,64,256]{4,3,2,1,0:T(8,128)(2,1)}, u32[]{:S(2)}, u32[]{:S(2)}) collective-permute-start(bf16[1,2,4,64,256]{4,3,2,1,0:T(8,128)(2,1)S(1)} %get-tuple-element.38), channel_id=1, source_target_pairs={{0,2},{1,3},{2,0},{3,1},{4,6},{5,7},{6,4},{7,5},{8,10},{9,11},{10,... | collective-permute-start | bytes 786440 | tf_op jit(solution)/shard_map/ppermute | solution.py:22
  197.5 3.7 %copy-start.7 = (f32[1,2,4,64,256]{4,3,2,1,0:T(8,128)S(1)}, f32[1,2,4,64,256]{4,3,2,1,0:T(8,128)}, u32[]{:S(2)}) copy-start(f32[1,2,4,64,256]{4,3,2,1,0:T(8,128)} %get-tuple-element.39) | copy-start | bytes 1572868
  197.5 4.7 %copy-start.20 = (bf16[4,64,256]{2,1,0:T(8,128)(2,1)S(1)}, bf16[4,64,256]{2,1,0:T(8,128)(2,1)}, u32[]{:S(2)}) copy-start(bf16[4,64,256]{2,1,0:T(8,128)(2,1)} %get-tuple-element.52) | copy-start | bytes 393220
  197.6 19.9 %collective-permute-start.38 = (bf16[1,2,32,4096]{3,2,1,0:T(8,128)(2,1)}, bf16[1,2,32,4096]{3,2,1,0:T(8,128)(2,1)S(1)}, u32[]{:S(2)}, u32[]{:S(2)}) collective-permute-start(bf16[1,2,32,4096]{3,2,1,0:T(8,128)(2,1)} %get-tuple-element.34), channel_id=1, source_target_pairs={{0,2},{1,3},{2,0},{3,1},{4,6},{5,7},{6,4},{7,5},{8,10},{9,11},{10,... | collective-permute-start | bytes 1572872 | tf_op jit(solution)/shard_map/ppermute | solution.py:22
  199.6 17.2 %collective-permute-start.28 = (bf16[1,2,4,64,256]{4,3,2,1,0:T(8,128)(2,1)S(1)}, bf16[1,2,4,64,256]{4,3,2,1,0:T(8,128)(2,1)S(1)}, u32[]{:S(2)}, u32[]{:S(2)}) collective-permute-start(bf16[1,2,4,64,256]{4,3,2,1,0:T(8,128)(2,1)S(1)} %get-tuple-element.40), channel_id=1, source_target_pairs={{0,2},{1,3},{2,0},{3,1},{4,6},{5,7},{6,4},{7,5},{8,10},{9,11},{10,... | collective-permute-start | bytes 786440 | tf_op jit(solution)/shard_map/ppermute | solution.py:22
  202.3 18.8 %collective-permute-start.34 = (bf16[4,64,256]{2,1,0:T(8,128)(2,1)S(1)}, bf16[4,64,256]{2,1,0:T(8,128)(2,1)S(1)}, u32[]{:S(2)}, u32[]{:S(2)}) collective-permute-start(bf16[4,64,256]{2,1,0:T(8,128)(2,1)S(1)} %copy-done.20), channel_id=1, source_target_pairs={{0,8},{4,12},{8,0},{12,4},{1,9},{5,13},{9,1},{13,5},{2,10},{6,14},... | collective-permute-start | bytes 393224 | tf_op jit(solution)/shard_map/ppermute | solution.py:22
  202.4 39.0 %copy-start.5 = (f32[2,2,16,64,256]{4,3,2,1,0:T(8,128)S(1)}, f32[2,2,16,64,256]{4,3,2,1,0:T(8,128)}, u32[]{:S(2)}) copy-start(f32[2,2,16,64,256]{4,3,2,1,0:T(8,128)} %get-tuple-element.22) | copy-start | bytes 12582916
  216.9 23.8 %collective-permute-start.20 = (bf16[1,2,16,64,256]{4,3,2,1,0:T(8,128)(2,1)S(1)}, bf16[1,2,16,64,256]{4,3,2,1,0:T(8,128)(2,1)S(1)}, u32[]{:S(2)}, u32[]{:S(2)}) collective-permute-start(bf16[1,2,16,64,256]{4,3,2,1,0:T(8,128)(2,1)S(1)} %add_convert_fusion), channel_id=1, source_target_pairs={{0,2},{1,3},{2,0},{3,1},{4,6},{5,7},{6,4},{7,5},{8,10},{9,11},{10,... | collective-permute-start | bytes 3145736 | tf_op jit(solution)/shard_map/ppermute | solution.py:22
  217.5 25.7 %collective-permute-start.26 = (bf16[4,64,256]{2,1,0:T(8,128)(2,1)S(1)}, bf16[4,64,256]{2,1,0:T(8,128)(2,1)S(1)}, u32[]{:S(2)}, u32[]{:S(2)}) collective-permute-start(bf16[4,64,256]{2,1,0:T(8,128)(2,1)S(1)} %get-tuple-element.53), channel_id=1, source_target_pairs={{0,4},{4,0},{8,12},{12,8},{1,5},{5,1},{9,13},{13,9},{2,6},{6,2},{1... | collective-permute-start | bytes 393224 | tf_op jit(solution)/shard_map/ppermute | solution.py:22
  219.1 24.2 %collective-permute-start.36 = (bf16[4,64,256]{2,1,0:T(8,128)(2,1)S(1)}, bf16[4,64,256]{2,1,0:T(8,128)(2,1)S(1)}, u32[]{:S(2)}, u32[]{:S(2)}) collective-permute-start(bf16[4,64,256]{2,1,0:T(8,128)(2,1)S(1)} %get-tuple-element.48), channel_id=1, source_target_pairs={{0,8},{4,12},{8,0},{12,4},{1,9},{5,13},{9,1},{13,5},{2,10},{6,14},... | collective-permute-start | bytes 393224 | tf_op jit(solution)/shard_map/ppermute | solution.py:22
  220.4 22.8 %collective-permute-start.32 = (bf16[4,64,256]{2,1,0:T(8,128)(2,1)S(1)}, bf16[4,64,256]{2,1,0:T(8,128)(2,1)S(1)}, u32[]{:S(2)}, u32[]{:S(2)}) collective-permute-start(bf16[4,64,256]{2,1,0:T(8,128)(2,1)S(1)} %get-tuple-element.49), channel_id=1, source_target_pairs={{0,4},{4,0},{8,12},{12,8},{1,5},{5,1},{9,13},{13,9},{2,6},{6,2},{1... | collective-permute-start | bytes 393224 | tf_op jit(solution)/shard_map/ppermute | solution.py:22
  221.1 22.1 %copy-start.21 = (bf16[4,64,256]{2,1,0:T(8,128)(2,1)}, bf16[4,64,256]{2,1,0:T(8,128)(2,1)S(1)}, u32[]{:S(2)}) copy-start(bf16[4,64,256]{2,1,0:T(8,128)(2,1)S(1)} %collective-permute-done.34.refs_5_) | copy-start | bytes 393220
  221.1 22.2 %collective-permute-start.35 = (bf16[4,64,256]{2,1,0:T(8,128)(2,1)S(1)}, bf16[4,64,256]{2,1,0:T(8,128)(2,1)S(1)}, u32[]{:S(2)}, u32[]{:S(2)}) collective-permute-start(bf16[4,64,256]{2,1,0:T(8,128)(2,1)S(1)} %get-tuple-element.50), channel_id=1, source_target_pairs={{0,8},{4,12},{8,0},{12,4},{1,9},{5,13},{9,1},{13,5},{2,10},{6,14},... | collective-permute-start | bytes 393224 | tf_op jit(solution)/shard_map/ppermute | solution.py:22
  240.7 5.1 %collective-permute-start.29 = (bf16[4,64,256]{2,1,0:T(8,128)(2,1)S(1)}, bf16[4,64,256]{2,1,0:T(8,128)(2,1)}, u32[]{:S(2)}, u32[]{:S(2)}) collective-permute-start(bf16[4,64,256]{2,1,0:T(8,128)(2,1)S(1)} %get-tuple-element.51), channel_id=1, source_target_pairs={{0,4},{4,0},{8,12},{12,8},{1,5},{5,1},{9,13},{13,9},{2,6},{6,2},{1... | collective-permute-start | bytes 393224 | tf_op jit(solution)/shard_map/ppermute | solution.py:22
  241.4 10.2 %copy-start.1 = (bf16[128,4096]{1,0:T(8,128)(2,1)S(1)}, bf16[128,4096]{1,0:T(8,128)(2,1)}, u32[]{:S(2)}) copy-start(bf16[128,4096]{1,0:T(8,128)(2,1)} %param.12) | copy-start | bytes 3145732
  243.2 0.7 copy-start.24
  (3 other events, 2.0 us)

commit v2 on v1

--- a/solution.py
+++ b/solution.py
@@ -10,7 +10,8 @@
 
 WIDTH = 16384
 BLOCK = 256
-CHUNK_SIZES = (4, 4, 4, 4)
+CHUNK_SIZES = (4, 6, 4, 2)
+EARLY_CHUNKS = 2
 
 
 F32 = jnp.float32
@@ -133,7 +134,8 @@
     return keep[0], came[0]
 
 
-def share_body(share, units, unit, pos_ref, item_ref, w_ref, out_ref, sems):
+def share_body(share, units, unit, pos_ref, item_ref, w_ref, *refs):
+    out_refs, sems = refs[:2], refs[2]
     pieces = BLOCK // unit
     copies = []
     for way in range(2):
@@ -144,7 +146,7 @@
             copies.append(
                 pltpu.make_async_copy(
                     w_ref.at[block, pl.ds(first, unit), :],
-                    out_ref.at[way, one],
+                    out_refs[way].at[one],
                     sems.at[way * units + one],
                 )
             )
@@ -162,8 +164,8 @@
             pl.BlockSpec(memory_space=pltpu.SMEM),
             pl.BlockSpec(memory_space=pl.ANY),
         ],
-        out_specs=pl.BlockSpec(memory_space=pltpu.VMEM),
-        out_shape=jax.ShapeDtypeStruct((2, units, unit, BLOCK), BF16),
+        out_specs=(pl.BlockSpec(memory_space=pltpu.VMEM),) * 2,
+        out_shape=(jax.ShapeDtypeStruct((units, unit, BLOCK), BF16),) * 2,
         scratch_shapes=[pltpu.SemaphoreType.DMA((2 * units,))],
         cost_estimate=pl.CostEstimate(
             flops=0, bytes_accessed=8 * units * unit * BLOCK, transcendentals=0
@@ -363,7 +365,7 @@
         first = sum(sizes[:one]) * BLOCK
         piece = source[:, first : first + sizes[one] * BLOCK]
         if one + 1 < chunks:
-            source = after(source, far[1][-1] if far[1] else piece)
+            source = after(source, piece)
         for way in range(2):
             far[way].append(hop(piece, far_bits[way]))
 
@@ -427,7 +429,8 @@
     low = [keep[way] + came[way].astype(F32) for way in range(2)]
 
     mixed = None
-    for first, last in ((0, chunks - 1), (chunks - 1, chunks)):
+    early = min(EARLY_CHUNKS, chunks - 1)
+    for first, last in ((0, early), (early, chunks)):
         mixed = mixed_kernel(
             features,
             block_weights,

time: 253 us -> 256 us (1.012)
  starting transfers between devices: 35.4 us -> 40.4 us
  local copies, waits for them, and re-layouts: 10.9 us -> 6.65 us
  other arithmetic: 17.5 us -> 20.1 us
    ppermute x39, starting transfers between devices: 35.4 us -> 40.4 us  [swapped(): lax.ppermute(block, axis, [(one, one ^ 1 << apart) for one in range(count)])]
  transfers between devices with their start and end apart: 39 -> 39, of which waited for: 14 -> 11; matrix products, arithmetic and copies ran while one was open for 10% -> 9% of each run, Pallas kernels for 17% -> 17%
where the time goes in v2:
time: 256 us
  waiting for transfers between devices  135 us (53%)
  Pallas kernels  48.9 us (19%)
  starting transfers between devices  40.4 us (16%)
  other arithmetic  20.1 us (8%)
  local copies, waits for them, and re-layouts  6.65 us (3%)
  matrix products  3.08 us (1%)
    ppermute x39, waiting for transfers between devices, swapped(): lax.ppermute(block, axis, [(one, one ^ 1 << apart) for one in range(count)])  135 us
    ppermute x39, starting transfers between devices, swapped(): lax.ppermute(block, axis, [(one, one ^ 1 << apart) for one in range(count)])  40.4 us
    pallas_call x5, Pallas kernels, pair_grads(): pl.pallas_call(functools.partial(grad_body, pairs, part), grid_spec=pltpu...  21 us
    pallas_call x2, Pallas kernels, mixed_kernel(): pl.pallas_call(functools.partial(mixed_body, share, sizes, first, last, u...  14.2 us
    convert_element_type x6, other arithmetic, items_sum(): came = swapped(leave.astype(BF16), 'items', level)  9.77 us
    pallas_call x1, Pallas kernels, place_kernel(): pl.pallas_call(functools.partial(place_body, share, sizes), grid_spec=plt...  5.83 us
  transfers between devices with their start and end apart: 39, of which 11 were waited for; matrix products, arithmetic and copies ran while one was open for 9% of the time, Pallas kernels for 17%

profile of v2, /device:TPU:0, one launch (start us, length us, event | category | flops | bytes accessed | tf_op | source)
XLA Modules:
  0.0 255.6 jit_solution(16224617783941949366)
XLA Ops:
  0.7 1.2 copy-done
  1.9 2.4 fusion.28
  4.3 0.7 fusion.29
  5.0 3.1 %collective-permute-start = (f32[2,128,128]{2,1,0:T(8,128)S(1)}, f32[2,128,128]{2,1,0:T(8,128)S(1)}, u32[]{:S(2)}, u32[]{:S(2)}) collective-permute-start(f32[2,128,128]{2,1,0:T(8,128)S(1)} %fusion.15), channel_id=1, source_target_pairs={{0,4},{4,0},{8,12},{12,8},{1,5},{5,1},{9,13},{13,9},{2,6},{6,2},{1... | collective-permute-start | bytes 393224 | tf_op jit(solution)/shard_map/ppermute | solution.py:23
  8.1 0.8 slice.99
  9.0 2.6 %collective-permute-start.17 = (bf16[256,1024]{1,0:T(8,128)(2,1)}, bf16[256,1024]{1,0:T(8,128)(2,1)S(1)}, u32[]{:S(2)}, u32[]{:S(2)}) collective-permute-start(bf16[256,1024]{1,0:T(8,128)(2,1)} %slice.99), channel_id=1, source_target_pairs={{0,8},{4,12},{8,0},{12,4},{1,9},{5,13},{9,1},{13,5},{2,10},{6,14},... | collective-permute-start | bytes 1572872 | tf_op jit(solution)/shard_map/ppermute | solution.py:23
  11.6 0.8 collective-permute-start.15
  12.4 0.9 slice.100
  13.3 0.8 slice.101
  14.5 1.2 collective-permute-start.4
  15.8 2.6 %collective-permute-start.1 = (f32[2,128,128]{2,1,0:T(8,128)S(1)}, f32[2,128,128]{2,1,0:T(8,128)S(1)}, u32[]{:S(2)}, u32[]{:S(2)}) collective-permute-start(f32[2,128,128]{2,1,0:T(8,128)S(1)} %fusion.18), channel_id=1, source_target_pairs={{0,8},{4,12},{8,0},{12,4},{1,9},{5,13},{9,1},{13,5},{2,10},{6,14},... | collective-permute-start | bytes 393224 | tf_op jit(solution)/shard_map/ppermute | solution.py:23
  18.5 33.2 %collective-permute-done.1 = f32[2,128,128]{2,1,0:T(8,128)S(1)} collective-permute-done((f32[2,128,128]{2,1,0:T(8,128)S(1)}, f32[2,128,128]{2,1,0:T(8,128)S(1)}, u32[]{:S(2)}, u32[]{:S(2)}) %collective-permute-start.1) | collective-permute-done | bytes 131104 | tf_op jit(solution)/shard_map/ppermute | solution.py:23
  51.7 3.6 %collective-permute-start.3 = (bf16[256,1024]{1,0:T(8,128)(2,1)}, bf16[256,1024]{1,0:T(8,128)(2,1)}, u32[]{:S(2)}, u32[]{:S(2)}) collective-permute-start(bf16[256,1024]{1,0:T(8,128)(2,1)} %slice.101), channel_id=1, source_target_pairs={{0,4},{4,0},{8,12},{12,8},{1,5},{5,1},{9,13},{13,9},{2,6},{6,2},{1... | collective-permute-start | bytes 1572872 | tf_op jit(solution)/shard_map/ppermute | solution.py:23
  55.4 0.6 select_reduce_fusion.pos_ref
  56.0 3.0 %weight_share.1 = (bf16[4,256,256]{2,1,0:T(8,128)(2,1)}, bf16[4,256,256]{2,1,0:T(8,128)(2,1)}) custom-call(s32[64]{0:T(128)} %select_reduce_fusion.pos_ref, s32[1]{0:T(128)} %bitcast.item_ref, bf16[64,256,256]{2,1,0:T(8,128)(2,1)} %w_ref.5), custom_call_target="tpu_custom_call" | custom-call | bytes 2097152 | tf_op jit(solution)/shard_map/weight_share/pallas_call | solution.py:160
  59.0 19.6 %collective-permute-done.2 = bf16[2,128,128]{2,1,0:T(8,128)(2,1)S(1)} collective-permute-done((bf16[2,128,128]{2,1,0:T(8,128)(2,1)S(1)}, bf16[2,128,128]{2,1,0:T(8,128)(2,1)S(1)}, u32[]{:S(2)}, u32[]{:S(2)}) %collective-permute-start.2) | collective-permute-done | bytes 65568 | tf_op jit(solution)/shard_map/ppermute | solution.py:23
  78.6 3.0 %collective-permute-start.18 = (bf16[256,1536]{1,0:T(8,128)(2,1)}, bf16[256,1536]{1,0:T(8,128)(2,1)S(1)}, u32[]{:S(2)}, u32[]{:S(2)}) collective-permute-start(bf16[256,1536]{1,0:T(8,128)(2,1)} %slice.100), channel_id=1, source_target_pairs={{0,8},{4,12},{8,0},{12,4},{1,9},{5,13},{9,1},{13,5},{2,10},{6,14},... | collective-permute-start | bytes 2359304 | tf_op jit(solution)/shard_map/ppermute | solution.py:23
  81.6 2.4 pair_grads.9
  84.0 0.8 copy-done.16
  85.0 0.6 copy-done.17
  85.6 1.1 collective-permute-start.16
  86.8 3.0 %pair_grads.8 = (bf16[2,2,4,64,256]{4,3,2,1,0:T(8,128)(2,1)}, f32[2,2,4,64,256]{4,3,2,1,0:T(8,128)}) custom-call(s32[1]{0:T(128)S(6)} %and.24.bit_ref, bf16[256,4096]{1,0:T(8,128)(2,1)} %g_ref.11, bf16[256,1024]{1,0:T(8,128)(2,1)} %collective-permute-done.3.refs_0_, bf16[256,1024]{1,0:T(8,128)(2,1)} %copy-done.17), custom_call_target="tpu_custom_call" | custom-call | flops 268435456 | bytes 3145728 | tf_op jit(solution)/shard_map/pair_grads/pallas_call | solution.py:63
  89.9 1.2 add_convert_fusion.5
  91.0 12.8 %collective-permute-done.7.refs_4_ = bf16[4,256,256]{2,1,0:T(8,128)(2,1)S(1)} collective-permute-done((bf16[4,256,256]{2,1,0:T(8,128)(2,1)}, bf16[4,256,256]{2,1,0:T(8,128)(2,1)S(1)}, u32[]{:S(2)}, u32[]{:S(2)}) %collective-permute-start.7) | collective-permute-done | bytes 524320 | tf_op jit(solution)/shard_map/ppermute | solution.py:23
  103.9 1.5 collective-permute-start.31
  105.4 0.7 slice_bitcast_fusion
  106.0 2.8 %pair_grads.6 = (bf16[2,2,4,64,256]{4,3,2,1,0:T(8,128)(2,1)}, f32[2,2,4,64,256]{4,3,2,1,0:T(8,128)}) custom-call(s32[1]{0:T(128)S(6)} %and.24.bit_ref, bf16[256,4096]{1,0:T(8,128)(2,1)} %g_ref.11, bf16[256,1024]{1,0:T(8,128)(2,1)} %copy-done.16, bf16[256,1024]{1,0:T(8,128)(2,1)} %copy-done.15), custom_call_target="tpu_custom_call" | custom-call | flops 268435456 | bytes 3145728 | tf_op jit(solution)/shard_map/pair_grads/pallas_call | solution.py:63
  108.9 28.7 %collective-permute-done.11.refs_8_ = bf16[4,256,256]{2,1,0:T(8,128)(2,1)S(1)} collective-permute-done((bf16[4,256,256]{2,1,0:T(8,128)(2,1)}, bf16[4,256,256]{2,1,0:T(8,128)(2,1)S(1)}, u32[]{:S(2)}, u32[]{:S(2)}) %collective-permute-start.11) | collective-permute-done | bytes 524320 | tf_op jit(solution)/shard_map/ppermute | solution.py:23
  138.1 5.0 %low_grads.1 = (bf16[2,2,32,4096]{3,2,1,0:T(8,128)(2,1)}, f32[2,2,32,4096]{3,2,1,0:T(8,128)}) custom-call(s32[1]{0:T(128)S(6)} %and.24.bit_ref, bf16[256,128]{1,0:T(8,128)(2,1)} %get-tuple-element.58.b_ref, bf16[256,4096]{1,0:T(8,128)(2,1)} %f_ref.5, bf16[256,128]{1,0:T(8,128)(2,1)} %get-tuple-element.59.codes_ref.c_ref, bf16[256,4096]{1,0:T(8,128)(2,1)} %g_ref.11), custom_call_target="tpu_custom_call" | custom-call | flops 536870912 | bytes 7340032 | tf_op jit(solution)/shard_map/low_grads/pallas_call | solution.py:105
  143.2 8.3 %pair_grads.5 = (bf16[2,2,16,64,256]{4,3,2,1,0:T(8,128)(2,1)}, f32[2,2,16,64,256]{4,3,2,1,0:T(8,128)}) custom-call(s32[1]{0:T(128)S(6)} %and.24.bit_ref, bf16[256,4096]{1,0:T(8,128)(2,1)} %g_ref.11, bf16[256,4096]{1,0:T(8,128)(2,1)} %f_ref.5), custom_call_target="tpu_custom_call" | custom-call | flops 1073741824 | bytes 12582912 | tf_op jit(solution)/shard_map/pair_grads/pallas_call | solution.py:63
  151.9 2.3 add_convert_fusion.3
  154.1 1.5 collective-permute-start.28
  155.6 0.6 collective-permute-start.8
  156.2 7.1 %collective-permute-done.28 = bf16[1,2,4,64,256]{4,3,2,1,0:T(8,128)(2,1)S(1)} collective-permute-done((bf16[1,2,4,64,256]{4,3,2,1,0:T(8,128)(2,1)S(1)}, bf16[1,2,4,64,256]{4,3,2,1,0:T(8,128)(2,1)S(1)}, u32[]{:S(2)}, u32[]{:S(2)}) %collective-permute-start.28) | collective-permute-done | bytes 262176 | tf_op jit(solution)/shard_map/ppermute | solution.py:23
  163.3 1.5 collective-permute-start.12
  164.8 1.6 fusion.22
  166.4 4.5 %pair_grads.7 = (bf16[2,2,6,64,256]{4,3,2,1,0:T(8,128)(2,1)}, f32[2,2,6,64,256]{4,3,2,1,0:T(8,128)}) custom-call(s32[1]{0:T(128)S(6)} %and.24.bit_ref, bf16[256,4096]{1,0:T(8,128)(2,1)} %g_ref.11, bf16[256,1536]{1,0:T(8,128)(2,1)} %copy-done.7, bf16[256,1536]{1,0:T(8,128)(2,1)} %copy-done.6), custom_call_target="tpu_custom_call" | custom-call | flops 402653184 | bytes 4718592 | tf_op jit(solution)/shard_map/pair_grads/pallas_call | solution.py:63
  170.9 1.6 add_convert_fusion.4
  172.5 1.8 fusion.13
  174.6 1.6 collective-permute-start.22
  176.1 9.8 %collective-permute-done.12.refs_9_ = bf16[4,256,256]{2,1,0:T(8,128)(2,1)} collective-permute-done((bf16[4,256,256]{2,1,0:T(8,128)(2,1)S(1)}, bf16[4,256,256]{2,1,0:T(8,128)(2,1)}, u32[]{:S(2)}, u32[]{:S(2)}) %collective-permute-start.12) | collective-permute-done | bytes 524320 | tf_op jit(solution)/shard_map/ppermute | solution.py:23
  186.4 2.2 add_convert_fusion.1
  188.6 2.0 collective-permute-done.22
  190.7 1.5 collective-permute-start.38
  192.2 0.8 fusion.12
  193.0 3.1 %collective-permute-start.32 = (bf16[2,64,256]{2,1,0:T(8,128)(2,1)}, bf16[2,64,256]{2,1,0:T(8,128)(2,1)}, u32[]{:S(2)}, u32[]{:S(2)}) collective-permute-start(bf16[2,64,256]{2,1,0:T(8,128)(2,1)} %get-tuple-element.57), channel_id=1, source_target_pairs={{0,4},{4,0},{8,12},{12,8},{1,5},{5,1},{9,13},{13,9},{2,6},{6,2},{1... | collective-permute-start | bytes 196616 | tf_op jit(solution)/shard_map/ppermute | solution.py:23
  196.1 7.6 %mixed.2.refs_12_ = bf16[256,4096]{1,0:T(8,128)(2,1)} custom-call(s32[64]{0:T(128)} %select_reduce_fusion.pos_ref, s32[1]{0:T(128)} %bitcast.item_ref, bf16[256,4096]{1,0:T(8,128)(2,1)} %f_ref.5, bf16[64,256,256]{2,1,0:T(8,128)(2,1)} %w_ref.5, bf16[256,128]{1,0:T(8,128)(2,1)} %get-tuple-element.59.codes_ref.c_ref, bf16[128,4096]{1,0:T(8,128)(2,1)} %low_ref.3, ...), custom_call_target="tpu_custom_call" | custom-call | flops 1509949440 | bytes 10485760 | tf_op jit(solution)/shard_map/mixed/pallas_call | solution.py:268
  203.8 6.5 %mixed.3 = bf16[256,4096]{1,0:T(8,128)(2,1)} custom-call(s32[64]{0:T(128)} %select_reduce_fusion.pos_ref, s32[1]{0:T(128)} %bitcast.item_ref, bf16[256,4096]{1,0:T(8,128)(2,1)} %f_ref.5, bf16[64,256,256]{2,1,0:T(8,128)(2,1)} %w_ref.5, bf16[256,128]{1,0:T(8,128)(2,1)} %get-tuple-element.59.codes_ref.c_ref, ...), custom_call_target="tpu_custom_call", output_to_operand_aliasing={{}: (18, {})} | custom-call | flops 905969664 | bytes 6291456 | tf_op jit(solution)/shard_map/mixed/pallas_call | solution.py:268
  210.3 0.6 collective-permute-start.35
  211.2 0.6 collective-permute-start.25
  211.8 2.2 add_convert_fusion
  214.1 1.6 collective-permute-start.20
  215.6 2.2 fusion
  217.9 5.4 %collective-permute-done.25 = bf16[1,2,6,64,256]{4,3,2,1,0:T(8,128)(2,1)S(1)} collective-permute-done((bf16[1,2,6,64,256]{4,3,2,1,0:T(8,128)(2,1)S(1)}, bf16[1,2,6,64,256]{4,3,2,1,0:T(8,128)(2,1)S(1)}, u32[]{:S(2)}, u32[]{:S(2)}) %collective-permute-start.25) | collective-permute-done | bytes 393248 | tf_op jit(solution)/shard_map/ppermute | solution.py:23
  223.2 1.2 collective-permute-start.29
  224.6 2.0 collective-permute-start.33
  226.6 1.2 collective-permute-start.23
  227.9 0.5 collective-permute-start.34
  228.4 14.9 %collective-permute-done.20 = bf16[1,2,16,64,256]{4,3,2,1,0:T(8,128)(2,1)S(1)} collective-permute-done((bf16[1,2,16,64,256]{4,3,2,1,0:T(8,128)(2,1)S(1)}, bf16[1,2,16,64,256]{4,3,2,1,0:T(8,128)(2,1)S(1)}, u32[]{:S(2)}, u32[]{:S(2)}) %collective-permute-start.20) | collective-permute-done | bytes 1048608 | tf_op jit(solution)/shard_map/ppermute | solution.py:23
  243.3 1.0 collective-permute-start.26
  244.2 3.2 %add_bitcast_fusion.own_ref = f32[2,16,64,256]{3,2,1,0:T(8,128)} fusion(bf16[1,2,16,64,256]{4,3,2,1,0:T(8,128)(2,1)S(1)} %collective-permute-done.20, f32[2,2,16,64,256]{4,3,2,1,0:T(8,128)S(1)} %copy-done.5, s32[]{:T(128)S(6)} %select_n.70, bf16[2,2,16,64,256]{4,3,2,1,0:T(8,128)(2,1)} %collective-permute-done.19), kind=kLoop, calls=%fused_computation | loop fusion | flops 2097152 | bytes 6291460 | tf_op jit(solution)/shard_map/add | solution.py:410
  247.5 1.5 collective-permute-done.26.refs_1_
  249.0 0.7 copy-done.24
  249.6 5.8 %place.1 = f32[64,64,256]{2,1,0:T(8,128)} custom-call(s32[64]{0:T(128)} %select_reduce_fusion.pos_ref, f32[2,16,64,256]{3,2,1,0:T(8,128)} %add_bitcast_fusion.own_ref, bf16[4,64,256]{2,1,0:T(8,128)(2,1)} %copy-done.30, bf16[6,64,256]{2,1,0:T(8,128)(2,1)} %copy-done.24, bf16[4,64,256]{2,1,0:T(8,128)(2,1)} %copy-done.28, ...), custom_call_target="tpu_custom_call" | custom-call | bytes 8388608 | tf_op jit(solution)/shard_map/place/pallas_call | solution.py:315
  (115 shorter events, 3.2 us)
Async XLA Ops:
  0.6 3.6 %copy-start.2 = (bf16[256,4096]{1,0:T(8,128)(2,1)S(1)}, bf16[256,4096]{1,0:T(8,128)(2,1)}, u32[]{:S(2)}) copy-start(bf16[256,4096]{1,0:T(8,128)(2,1)} %g_ref.11) | copy-start | bytes 6291460
  1.9 2.4 copy-start.4
  4.3 3.9 %copy-start.3 = (bf16[256,4096]{1,0:T(8,128)(2,1)S(1)}, bf16[256,4096]{1,0:T(8,128)(2,1)}, u32[]{:S(2)}) copy-start(bf16[256,4096]{1,0:T(8,128)(2,1)} %f_ref.5) | copy-start | bytes 6291460
  5.0 10.8 %collective-permute-start = (f32[2,128,128]{2,1,0:T(8,128)S(1)}, f32[2,128,128]{2,1,0:T(8,128)S(1)}, u32[]{:S(2)}, u32[]{:S(2)}) collective-permute-start(f32[2,128,128]{2,1,0:T(8,128)S(1)} %fusion.15), channel_id=1, source_target_pairs={{0,4},{4,0},{8,12},{12,8},{1,5},{5,1},{9,13},{13,9},{2,6},{6,2},{1... | collective-permute-start | bytes 393224 | tf_op jit(solution)/shard_map/ppermute | solution.py:23
  9.0 9.5 %copy-start.31 = (s32[64]{0:T(128)S(1)}, s32[64]{0:T(128)}, u32[]{:S(2)}) copy-start(s32[64]{0:T(128)} %param.11) | copy-start | bytes 772
  9.0 9.5 %copy-start.32 = (s32[64]{0:T(128)S(1)}, s32[64]{0:T(128)}, u32[]{:S(2)}) copy-start(s32[64]{0:T(128)} %param.10) | copy-start | bytes 772
  9.0 69.6 %collective-permute-start.17 = (bf16[256,1024]{1,0:T(8,128)(2,1)}, bf16[256,1024]{1,0:T(8,128)(2,1)S(1)}, u32[]{:S(2)}, u32[]{:S(2)}) collective-permute-start(bf16[256,1024]{1,0:T(8,128)(2,1)} %slice.99), channel_id=1, source_target_pairs={{0,8},{4,12},{8,0},{12,4},{1,9},{5,13},{9,1},{13,5},{2,10},{6,14},... | collective-permute-start | bytes 1572872 | tf_op jit(solution)/shard_map/ppermute | solution.py:23
  11.6 72.4 %collective-permute-start.15 = (bf16[256,1024]{1,0:T(8,128)(2,1)}, bf16[256,1024]{1,0:T(8,128)(2,1)S(1)}, u32[]{:S(2)}, u32[]{:S(2)}) collective-permute-start(bf16[256,1024]{1,0:T(8,128)(2,1)} %slice.99), channel_id=1, source_target_pairs={{0,4},{4,0},{8,12},{12,8},{1,5},{5,1},{9,13},{13,9},{2,6},{6,2},{1... | collective-permute-start | bytes 1572872 | tf_op jit(solution)/shard_map/ppermute | solution.py:23
  14.1 37.5 %collective-permute-start.6 = (bf16[256,512]{1,0:T(8,128)(2,1)S(1)}, bf16[256,512]{1,0:T(8,128)(2,1)S(1)}, u32[]{:S(2)}, u32[]{:S(2)}) collective-permute-start(bf16[256,512]{1,0:T(8,128)(2,1)S(1)} %slice.102), channel_id=1, source_target_pairs={{0,8},{4,12},{8,0},{12,4},{1,9},{5,13},{9,1},{13,5},{2,10},{6,14},... | collective-permute-start | bytes 786440 | tf_op jit(solution)/shard_map/ppermute | solution.py:23
  14.5 40.8 %collective-permute-start.4 = (bf16[256,512]{1,0:T(8,128)(2,1)S(1)}, bf16[256,512]{1,0:T(8,128)(2,1)S(1)}, u32[]{:S(2)}, u32[]{:S(2)}) collective-permute-start(bf16[256,512]{1,0:T(8,128)(2,1)S(1)} %slice.102), channel_id=1, source_target_pairs={{0,4},{4,0},{8,12},{12,8},{1,5},{5,1},{9,13},{13,9},{2,6},{6,2},{1... | collective-permute-start | bytes 786440 | tf_op jit(solution)/shard_map/ppermute | solution.py:23
  15.8 35.8 %collective-permute-start.1 = (f32[2,128,128]{2,1,0:T(8,128)S(1)}, f32[2,128,128]{2,1,0:T(8,128)S(1)}, u32[]{:S(2)}, u32[]{:S(2)}) collective-permute-start(f32[2,128,128]{2,1,0:T(8,128)S(1)} %fusion.18), channel_id=1, source_target_pairs={{0,8},{4,12},{8,0},{12,4},{1,9},{5,13},{9,1},{13,5},{2,10},{6,14},... | collective-permute-start | bytes 393224 | tf_op jit(solution)/shard_map/ppermute | solution.py:23
  51.7 32.4 %collective-permute-start.5 = (bf16[256,1024]{1,0:T(8,128)(2,1)}, bf16[256,1024]{1,0:T(8,128)(2,1)S(1)}, u32[]{:S(2)}, u32[]{:S(2)}) collective-permute-start(bf16[256,1024]{1,0:T(8,128)(2,1)} %slice.101), channel_id=1, source_target_pairs={{0,8},{4,12},{8,0},{12,4},{1,9},{5,13},{9,1},{13,5},{2,10},{6,14},... | collective-permute-start | bytes 1572872 | tf_op jit(solution)/shard_map/ppermute | solution.py:23
  51.7 7.4 %copy-start.19 = (bf16[256,512]{1,0:T(8,128)(2,1)}, bf16[256,512]{1,0:T(8,128)(2,1)S(1)}, u32[]{:S(2)}) copy-start(bf16[256,512]{1,0:T(8,128)(2,1)S(1)} %collective-permute-done.6.refs_3_.refs_1_) | copy-start | bytes 786436
  51.7 33.9 %collective-permute-start.3 = (bf16[256,1024]{1,0:T(8,128)(2,1)}, bf16[256,1024]{1,0:T(8,128)(2,1)}, u32[]{:S(2)}, u32[]{:S(2)}) collective-permute-start(bf16[256,1024]{1,0:T(8,128)(2,1)} %slice.101), channel_id=1, source_target_pairs={{0,4},{4,0},{8,12},{12,8},{1,5},{5,1},{9,13},{13,9},{2,6},{6,2},{1... | collective-permute-start | bytes 1572872 | tf_op jit(solution)/shard_map/ppermute | solution.py:23
  55.3 3.7 %copy-start.20 = (bf16[256,512]{1,0:T(8,128)(2,1)}, bf16[256,512]{1,0:T(8,128)(2,1)S(1)}, u32[]{:S(2)}) copy-start(bf16[256,512]{1,0:T(8,128)(2,1)S(1)} %collective-permute-done.4.refs_1_.refs_0_) | copy-start | bytes 786436
  55.3 23.3 %collective-permute-start.2 = (bf16[2,128,128]{2,1,0:T(8,128)(2,1)S(1)}, bf16[2,128,128]{2,1,0:T(8,128)(2,1)S(1)}, u32[]{:S(2)}, u32[]{:S(2)}) collective-permute-start(bf16[2,128,128]{2,1,0:T(8,128)(2,1)S(1)} %add_convert_fusion.6), channel_id=1, source_target_pairs={{0,4},{4,0},{8,12},{12,8},{1,5},{5,1},{9,13},{13,9},{2,6},{6,2},{1... | collective-permute-start | bytes 196616 | tf_op jit(solution)/shard_map/ppermute | solution.py:23
  78.6 25.3 %collective-permute-start.7 = (bf16[4,256,256]{2,1,0:T(8,128)(2,1)}, bf16[4,256,256]{2,1,0:T(8,128)(2,1)S(1)}, u32[]{:S(2)}, u32[]{:S(2)}) collective-permute-start(bf16[4,256,256]{2,1,0:T(8,128)(2,1)} %get-tuple-element.24), channel_id=1, source_target_pairs={{0,4},{4,0},{8,12},{12,8},{1,5},{5,1},{9,13},{13,9},{2,6},{6,2},{1... | collective-permute-start | bytes 1572872 | tf_op jit(solution)/shard_map/ppermute | solution.py:23
  78.6 11.2 %copy-start.15 = (bf16[256,1024]{1,0:T(8,128)(2,1)}, bf16[256,1024]{1,0:T(8,128)(2,1)S(1)}, u32[]{:S(2)}) copy-start(bf16[256,1024]{1,0:T(8,128)(2,1)S(1)} %collective-permute-done.17.refs_2_.refs_1_) | copy-start | bytes 1572868
  78.6 64.4 %collective-permute-start.18 = (bf16[256,1536]{1,0:T(8,128)(2,1)}, bf16[256,1536]{1,0:T(8,128)(2,1)S(1)}, u32[]{:S(2)}, u32[]{:S(2)}) collective-permute-start(bf16[256,1536]{1,0:T(8,128)(2,1)} %slice.100), channel_id=1, source_target_pairs={{0,8},{4,12},{8,0},{12,4},{1,9},{5,13},{9,1},{13,5},{2,10},{6,14},... | collective-permute-start | bytes 2359304 | tf_op jit(solution)/shard_map/ppermute | solution.py:23
  84.0 5.8 %collective-permute-start.30 = (bf16[2,2,2,64,256]{4,3,2,1,0:T(8,128)(2,1)}, bf16[2,2,2,64,256]{4,3,2,1,0:T(8,128)(2,1)}, u32[]{:S(2)}, u32[]{:S(2)}) collective-permute-start(bf16[2,2,2,64,256]{4,3,2,1,0:T(8,128)(2,1)} %get-tuple-element.35), channel_id=1, source_target_pairs={{0,1},{1,0},{2,3},{3,2},{4,5},{5,4},{6,7},{7,6},{8,9},{9,8},{10,11... | collective-permute-start | bytes 786440 | tf_op jit(solution)/shard_map/ppermute | solution.py:23
  84.8 52.7 %collective-permute-start.11 = (bf16[4,256,256]{2,1,0:T(8,128)(2,1)}, bf16[4,256,256]{2,1,0:T(8,128)(2,1)S(1)}, u32[]{:S(2)}, u32[]{:S(2)}) collective-permute-start(bf16[4,256,256]{2,1,0:T(8,128)(2,1)} %get-tuple-element.25), channel_id=1, source_target_pairs={{0,8},{4,12},{8,0},{12,4},{1,9},{5,13},{9,1},{13,5},{2,10},{6,14},... | collective-permute-start | bytes 1572872 | tf_op jit(solution)/shard_map/ppermute | solution.py:23
  85.6 68.6 %collective-permute-start.16 = (bf16[256,1536]{1,0:T(8,128)(2,1)}, bf16[256,1536]{1,0:T(8,128)(2,1)S(1)}, u32[]{:S(2)}, u32[]{:S(2)}) collective-permute-start(bf16[256,1536]{1,0:T(8,128)(2,1)} %slice.100), channel_id=1, source_target_pairs={{0,4},{4,0},{8,12},{12,8},{1,5},{5,1},{9,13},{13,9},{2,6},{6,2},{1... | collective-permute-start | bytes 2359304 | tf_op jit(solution)/shard_map/ppermute | solution.py:23
  89.8 61.7 %collective-permute-start.27 = (bf16[2,2,4,64,256]{4,3,2,1,0:T(8,128)(2,1)}, bf16[2,2,4,64,256]{4,3,2,1,0:T(8,128)(2,1)}, u32[]{:S(2)}, u32[]{:S(2)}) collective-permute-start(bf16[2,2,4,64,256]{4,3,2,1,0:T(8,128)(2,1)} %get-tuple-element.33), channel_id=1, source_target_pairs={{0,1},{1,0},{2,3},{3,2},{4,5},{5,4},{6,7},{7,6},{8,9},{9,8},{10,11... | collective-permute-start | bytes 1572872 | tf_op jit(solution)/shard_map/ppermute | solution.py:23
  103.9 51.8 %copy-start.8 = (bf16[4,256,256]{2,1,0:T(8,128)(2,1)}, bf16[4,256,256]{2,1,0:T(8,128)(2,1)S(1)}, u32[]{:S(2)}) copy-start(bf16[4,256,256]{2,1,0:T(8,128)(2,1)S(1)} %collective-permute-done.7.refs_4_) | copy-start | bytes 1572868
  103.9 33.7 %collective-permute-start.31 = (bf16[1,2,2,64,256]{4,3,2,1,0:T(8,128)(2,1)S(1)}, bf16[1,2,2,64,256]{4,3,2,1,0:T(8,128)(2,1)}, u32[]{:S(2)}, u32[]{:S(2)}) collective-permute-start(bf16[1,2,2,64,256]{4,3,2,1,0:T(8,128)(2,1)S(1)} %get-tuple-element.54), channel_id=1, source_target_pairs={{0,2},{1,3},{2,0},{3,1},{4,6},{5,7},{6,4},{7,5},{8,10},{9,11},{10,... | collective-permute-start | bytes 393224 | tf_op jit(solution)/shard_map/ppermute | solution.py:23
  137.5 25.8 %copy-start.9 = (bf16[4,256,256]{2,1,0:T(8,128)(2,1)}, bf16[4,256,256]{2,1,0:T(8,128)(2,1)S(1)}, u32[]{:S(2)}) copy-start(bf16[4,256,256]{2,1,0:T(8,128)(2,1)S(1)} %collective-permute-done.11.refs_8_) | copy-start | bytes 1572868
  137.5 18.7 %collective-permute-start.21 = (bf16[2,2,4,64,256]{4,3,2,1,0:T(8,128)(2,1)}, bf16[2,2,4,64,256]{4,3,2,1,0:T(8,128)(2,1)}, u32[]{:S(2)}, u32[]{:S(2)}) collective-permute-start(bf16[2,2,4,64,256]{4,3,2,1,0:T(8,128)(2,1)} %get-tuple-element.29), channel_id=1, source_target_pairs={{0,1},{1,0},{2,3},{3,2},{4,5},{5,4},{6,7},{7,6},{8,9},{9,8},{10,11... | collective-permute-start | bytes 1572872 | tf_op jit(solution)/shard_map/ppermute | solution.py:23
  137.5 18.1 %collective-permute-start.9 = (bf16[4,256,256]{2,1,0:T(8,128)(2,1)S(1)}, bf16[4,256,256]{2,1,0:T(8,128)(2,1)S(1)}, u32[]{:S(2)}, u32[]{:S(2)}) collective-permute-start(bf16[4,256,256]{2,1,0:T(8,128)(2,1)S(1)} %collective-permute-done.7.refs_4_), channel_id=1, source_target_pairs={{0,1},{1,0},{2,3},{3,2},{4,5},{5,4},{6,7},{7,6},{8,9},{9,8},{10,11... | collective-permute-start | bytes 1572872 | tf_op jit(solution)/shard_map/ppermute | solution.py:23
  143.0 8.5 %copy-start.6 = (bf16[256,1536]{1,0:T(8,128)(2,1)}, bf16[256,1536]{1,0:T(8,128)(2,1)S(1)}, u32[]{:S(2)}) copy-start(bf16[256,1536]{1,0:T(8,128)(2,1)S(1)} %collective-permute-done.18.refs_3_.refs_1_) | copy-start | bytes 2359300
  143.1 42.9 %collective-permute-start.37 = (bf16[2,2,32,4096]{3,2,1,0:T(8,128)(2,1)}, bf16[2,2,32,4096]{3,2,1,0:T(8,128)(2,1)}, u32[]{:S(2)}, u32[]{:S(2)}) collective-permute-start(bf16[2,2,32,4096]{3,2,1,0:T(8,128)(2,1)} %get-tuple-element.37), channel_id=1, source_target_pairs={{0,1},{1,0},{2,3},{3,2},{4,5},{5,4},{6,7},{7,6},{8,9},{9,8},{10,11... | collective-permute-start | bytes 3145736 | tf_op jit(solution)/shard_map/ppermute | solution.py:23
  151.5 59.7 %collective-permute-start.19 = (bf16[2,2,16,64,256]{4,3,2,1,0:T(8,128)(2,1)}, bf16[2,2,16,64,256]{4,3,2,1,0:T(8,128)(2,1)}, u32[]{:S(2)}, u32[]{:S(2)}) collective-permute-start(bf16[2,2,16,64,256]{4,3,2,1,0:T(8,128)(2,1)} %get-tuple-element.27), channel_id=1, source_target_pairs={{0,1},{1,0},{2,3},{3,2},{4,5},{5,4},{6,7},{7,6},{8,9},{9,8},{10,11... | collective-permute-start | bytes 6291464 | tf_op jit(solution)/shard_map/ppermute | solution.py:23
  154.1 12.3 %copy-start.7 = (bf16[256,1536]{1,0:T(8,128)(2,1)}, bf16[256,1536]{1,0:T(8,128)(2,1)S(1)}, u32[]{:S(2)}) copy-start(bf16[256,1536]{1,0:T(8,128)(2,1)S(1)} %collective-permute-done.16.refs_1_.refs_0_) | copy-start | bytes 2359300
  154.1 9.2 %collective-permute-start.28 = (bf16[1,2,4,64,256]{4,3,2,1,0:T(8,128)(2,1)S(1)}, bf16[1,2,4,64,256]{4,3,2,1,0:T(8,128)(2,1)S(1)}, u32[]{:S(2)}, u32[]{:S(2)}) collective-permute-start(bf16[1,2,4,64,256]{4,3,2,1,0:T(8,128)(2,1)S(1)} %get-tuple-element.44), channel_id=1, source_target_pairs={{0,2},{1,3},{2,0},{3,1},{4,6},{5,7},{6,4},{7,5},{8,10},{9,11},{10,... | collective-permute-start | bytes 786440 | tf_op jit(solution)/shard_map/ppermute | solution.py:23
  155.6 15.2 %copy-start.10 = (bf16[4,256,256]{2,1,0:T(8,128)(2,1)}, bf16[4,256,256]{2,1,0:T(8,128)(2,1)S(1)}, u32[]{:S(2)}) copy-start(bf16[4,256,256]{2,1,0:T(8,128)(2,1)S(1)} %collective-permute-done.9.refs_6_) | copy-start | bytes 1572868
  155.6 18.9 %collective-permute-start.8 = (bf16[4,256,256]{2,1,0:T(8,128)(2,1)S(1)}, bf16[4,256,256]{2,1,0:T(8,128)(2,1)S(1)}, u32[]{:S(2)}, u32[]{:S(2)}) collective-permute-start(bf16[4,256,256]{2,1,0:T(8,128)(2,1)S(1)} %collective-permute-done.7.refs_4_), channel_id=1, source_target_pairs={{0,2},{1,3},{2,0},{3,1},{4,6},{5,7},{6,4},{7,5},{8,10},{9,11},{10,... | collective-permute-start | bytes 1572872 | tf_op jit(solution)/shard_map/ppermute | solution.py:23
  156.2 18.3 %collective-permute-start.13 = (bf16[4,256,256]{2,1,0:T(8,128)(2,1)S(1)}, bf16[4,256,256]{2,1,0:T(8,128)(2,1)}, u32[]{:S(2)}, u32[]{:S(2)}) collective-permute-start(bf16[4,256,256]{2,1,0:T(8,128)(2,1)S(1)} %collective-permute-done.11.refs_8_), channel_id=1, source_target_pairs={{0,1},{1,0},{2,3},{3,2},{4,5},{5,4},{6,7},{7,6},{8,9},{9,8},{10,11... | collective-permute-start | bytes 1572872 | tf_op jit(solution)/shard_map/ppermute | solution.py:23
  163.3 22.6 %collective-permute-start.12 = (bf16[4,256,256]{2,1,0:T(8,128)(2,1)S(1)}, bf16[4,256,256]{2,1,0:T(8,128)(2,1)}, u32[]{:S(2)}, u32[]{:S(2)}) collective-permute-start(bf16[4,256,256]{2,1,0:T(8,128)(2,1)S(1)} %collective-permute-done.11.refs_8_), channel_id=1, source_target_pairs={{0,2},{1,3},{2,0},{3,1},{4,6},{5,7},{6,4},{7,5},{8,10},{9,11},{10,... | collective-permute-start | bytes 1572872 | tf_op jit(solution)/shard_map/ppermute | solution.py:23
  170.9 1.7 copy-start.22
  170.9 15.6 %copy-start.14 = (f32[2,2,32,4096]{3,2,1,0:T(8,128)S(1)}, f32[2,2,32,4096]{3,2,1,0:T(8,128)}, u32[]{:S(2)}) copy-start(f32[2,2,32,4096]{3,2,1,0:T(8,128)} %get-tuple-element.36) | copy-start | bytes 6291460
  174.6 14.1 %copy-start.11 = (bf16[4,256,256]{2,1,0:T(8,128)(2,1)}, bf16[4,256,256]{2,1,0:T(8,128)(2,1)S(1)}, u32[]{:S(2)}) copy-start(bf16[4,256,256]{2,1,0:T(8,128)(2,1)S(1)} %collective-permute-done.8.refs_5_) | copy-start | bytes 1572868
  174.6 35.7 %collective-permute-start.24 = (bf16[2,2,6,64,256]{4,3,2,1,0:T(8,128)(2,1)}, bf16[2,2,6,64,256]{4,3,2,1,0:T(8,128)(2,1)S(1)}, u32[]{:S(2)}, u32[]{:S(2)}) collective-permute-start(bf16[2,2,6,64,256]{4,3,2,1,0:T(8,128)(2,1)} %get-tuple-element.31), channel_id=1, source_target_pairs={{0,1},{1,0},{2,3},{3,2},{4,5},{5,4},{6,7},{7,6},{8,9},{9,8},{10,11... | collective-permute-start | bytes 2359304 | tf_op jit(solution)/shard_map/ppermute | solution.py:23
  174.6 16.1 %collective-permute-start.22 = (bf16[1,2,4,64,256]{4,3,2,1,0:T(8,128)(2,1)S(1)}, bf16[1,2,4,64,256]{4,3,2,1,0:T(8,128)(2,1)S(1)}, u32[]{:S(2)}, u32[]{:S(2)}) collective-permute-start(bf16[1,2,4,64,256]{4,3,2,1,0:T(8,128)(2,1)S(1)} %get-tuple-element.46), channel_id=1, source_target_pairs={{0,2},{1,3},{2,0},{3,1},{4,6},{5,7},{6,4},{7,5},{8,10},{9,11},{10,... | collective-permute-start | bytes 786440 | tf_op jit(solution)/shard_map/ppermute | solution.py:23
  185.9 7.0 %collective-permute-start.10 = (bf16[4,256,256]{2,1,0:T(8,128)(2,1)S(1)}, bf16[4,256,256]{2,1,0:T(8,128)(2,1)S(1)}, u32[]{:S(2)}, u32[]{:S(2)}) collective-permute-start(bf16[4,256,256]{2,1,0:T(8,128)(2,1)S(1)} %collective-permute-done.8.refs_5_), channel_id=1, source_target_pairs={{0,1},{1,0},{2,3},{3,2},{4,5},{5,4},{6,7},{7,6},{8,9},{9,8},{10,11... | collective-permute-start | bytes 1572872 | tf_op jit(solution)/shard_map/ppermute | solution.py:23
  185.9 7.0 %collective-permute-start.14 = (bf16[4,256,256]{2,1,0:T(8,128)(2,1)}, bf16[4,256,256]{2,1,0:T(8,128)(2,1)S(1)}, u32[]{:S(2)}, u32[]{:S(2)}) collective-permute-start(bf16[4,256,256]{2,1,0:T(8,128)(2,1)} %collective-permute-done.12.refs_9_), channel_id=1, source_target_pairs={{0,1},{1,0},{2,3},{3,2},{4,5},{5,4},{6,7},{7,6},{8,9},{9,8},{10,11... | collective-permute-start | bytes 1572872 | tf_op jit(solution)/shard_map/ppermute | solution.py:23
  190.7 23.4 %collective-permute-start.38 = (bf16[1,2,32,4096]{3,2,1,0:T(8,128)(2,1)}, bf16[1,2,32,4096]{3,2,1,0:T(8,128)(2,1)}, u32[]{:S(2)}, u32[]{:S(2)}) collective-permute-start(bf16[1,2,32,4096]{3,2,1,0:T(8,128)(2,1)} %get-tuple-element.38), channel_id=1, source_target_pairs={{0,2},{1,3},{2,0},{3,1},{4,6},{5,7},{6,4},{7,5},{8,10},{9,11},{10,... | collective-permute-start | bytes 1572872 | tf_op jit(solution)/shard_map/ppermute | solution.py:23
  192.9 3.2 %copy-start.12 = (bf16[4,256,256]{2,1,0:T(8,128)(2,1)}, bf16[4,256,256]{2,1,0:T(8,128)(2,1)S(1)}, u32[]{:S(2)}) copy-start(bf16[4,256,256]{2,1,0:T(8,128)(2,1)S(1)} %collective-permute-done.10.refs_7_) | copy-start | bytes 1572868
  192.9 31.7 %collective-permute-start.36 = (bf16[2,64,256]{2,1,0:T(8,128)(2,1)}, bf16[2,64,256]{2,1,0:T(8,128)(2,1)}, u32[]{:S(2)}, u32[]{:S(2)}) collective-permute-start(bf16[2,64,256]{2,1,0:T(8,128)(2,1)} %get-tuple-element.56), channel_id=1, source_target_pairs={{0,8},{4,12},{8,0},{12,4},{1,9},{5,13},{9,1},{13,5},{2,10},{6,14},... | collective-permute-start | bytes 196616 | tf_op jit(solution)/shard_map/ppermute | solution.py:23
  193.0 3.2 %copy-start.13 = (bf16[4,256,256]{2,1,0:T(8,128)(2,1)}, bf16[4,256,256]{2,1,0:T(8,128)(2,1)S(1)}, u32[]{:S(2)}) copy-start(bf16[4,256,256]{2,1,0:T(8,128)(2,1)S(1)} %collective-permute-done.14.refs_11_) | copy-start | bytes 1572868
  193.0 33.6 %collective-permute-start.32 = (bf16[2,64,256]{2,1,0:T(8,128)(2,1)}, bf16[2,64,256]{2,1,0:T(8,128)(2,1)}, u32[]{:S(2)}, u32[]{:S(2)}) collective-permute-start(bf16[2,64,256]{2,1,0:T(8,128)(2,1)} %get-tuple-element.57), channel_id=1, source_target_pairs={{0,4},{4,0},{8,12},{12,8},{1,5},{5,1},{9,13},{13,9},{2,6},{6,2},{1... | collective-permute-start | bytes 196616 | tf_op jit(solution)/shard_map/ppermute | solution.py:23
  203.8 7.2 %copy-start.18 = (f32[2,2,6,64,256]{4,3,2,1,0:T(8,128)S(1)}, f32[2,2,6,64,256]{4,3,2,1,0:T(8,128)}, u32[]{:S(2)}) copy-start(f32[2,2,6,64,256]{4,3,2,1,0:T(8,128)} %get-tuple-element.30) | copy-start | bytes 4718596
  210.3 17.5 %collective-permute-start.35 = (bf16[4,64,256]{2,1,0:T(8,128)(2,1)}, bf16[4,64,256]{2,1,0:T(8,128)(2,1)S(1)}, u32[]{:S(2)}, u32[]{:S(2)}) collective-permute-start(bf16[4,64,256]{2,1,0:T(8,128)(2,1)} %get-tuple-element.50), channel_id=1, source_target_pairs={{0,8},{4,12},{8,0},{12,4},{1,9},{5,13},{9,1},{13,5},{2,10},{6,14},... | collective-permute-start | bytes 393224 | tf_op jit(solution)/shard_map/ppermute | solution.py:23
  211.2 12.1 %collective-permute-start.25 = (bf16[1,2,6,64,256]{4,3,2,1,0:T(8,128)(2,1)S(1)}, bf16[1,2,6,64,256]{4,3,2,1,0:T(8,128)(2,1)S(1)}, u32[]{:S(2)}, u32[]{:S(2)}) collective-permute-start(bf16[1,2,6,64,256]{4,3,2,1,0:T(8,128)(2,1)S(1)} %get-tuple-element.40), channel_id=1, source_target_pairs={{0,2},{1,3},{2,0},{3,1},{4,6},{5,7},{6,4},{7,5},{8,10},{9,11},{10,... | collective-permute-start | bytes 1179656 | tf_op jit(solution)/shard_map/ppermute | solution.py:23
  211.8 12.8 %copy-start.26 = (bf16[4,64,256]{2,1,0:T(8,128)(2,1)S(1)}, bf16[4,64,256]{2,1,0:T(8,128)(2,1)}, u32[]{:S(2)}) copy-start(bf16[4,64,256]{2,1,0:T(8,128)(2,1)} %get-tuple-element.52) | copy-start | bytes 393220
  211.8 14.8 %copy-start.25 = (bf16[4,64,256]{2,1,0:T(8,128)(2,1)S(1)}, bf16[4,64,256]{2,1,0:T(8,128)(2,1)}, u32[]{:S(2)}) copy-start(bf16[4,64,256]{2,1,0:T(8,128)(2,1)} %get-tuple-element.53) | copy-start | bytes 393220
  214.1 29.2 %collective-permute-start.20 = (bf16[1,2,16,64,256]{4,3,2,1,0:T(8,128)(2,1)S(1)}, bf16[1,2,16,64,256]{4,3,2,1,0:T(8,128)(2,1)S(1)}, u32[]{:S(2)}, u32[]{:S(2)}) collective-permute-start(bf16[1,2,16,64,256]{4,3,2,1,0:T(8,128)(2,1)S(1)} %add_convert_fusion), channel_id=1, source_target_pairs={{0,2},{1,3},{2,0},{3,1},{4,6},{5,7},{6,4},{7,5},{8,10},{9,11},{10,... | collective-permute-start | bytes 3145736 | tf_op jit(solution)/shard_map/ppermute | solution.py:23
  215.6 28.6 %copy-start.5 = (f32[2,2,16,64,256]{4,3,2,1,0:T(8,128)S(1)}, f32[2,2,16,64,256]{4,3,2,1,0:T(8,128)}, u32[]{:S(2)}) copy-start(f32[2,2,16,64,256]{4,3,2,1,0:T(8,128)} %get-tuple-element.26) | copy-start | bytes 12582916
  223.2 24.2 %collective-permute-start.29 = (bf16[4,64,256]{2,1,0:T(8,128)(2,1)S(1)}, bf16[4,64,256]{2,1,0:T(8,128)(2,1)S(1)}, u32[]{:S(2)}, u32[]{:S(2)}) collective-permute-start(bf16[4,64,256]{2,1,0:T(8,128)(2,1)S(1)} %get-tuple-element.51), channel_id=1, source_target_pairs={{0,4},{4,0},{8,12},{12,8},{1,5},{5,1},{9,13},{13,9},{2,6},{6,2},{1... | collective-permute-start | bytes 393224 | tf_op jit(solution)/shard_map/ppermute | solution.py:23
  224.6 22.8 %collective-permute-start.33 = (bf16[4,64,256]{2,1,0:T(8,128)(2,1)S(1)}, bf16[4,64,256]{2,1,0:T(8,128)(2,1)S(1)}, u32[]{:S(2)}, u32[]{:S(2)}) collective-permute-start(bf16[4,64,256]{2,1,0:T(8,128)(2,1)S(1)} %copy-done.26), channel_id=1, source_target_pairs={{0,8},{4,12},{8,0},{12,4},{1,9},{5,13},{9,1},{13,5},{2,10},{6,14},... | collective-permute-start | bytes 393224 | tf_op jit(solution)/shard_map/ppermute | solution.py:23
  226.6 20.8 %collective-permute-start.23 = (bf16[4,64,256]{2,1,0:T(8,128)(2,1)S(1)}, bf16[4,64,256]{2,1,0:T(8,128)(2,1)S(1)}, u32[]{:S(2)}, u32[]{:S(2)}) collective-permute-start(bf16[4,64,256]{2,1,0:T(8,128)(2,1)S(1)} %copy-done.25), channel_id=1, source_target_pairs={{0,4},{4,0},{8,12},{12,8},{1,5},{5,1},{9,13},{13,9},{2,6},{6,2},{1... | collective-permute-start | bytes 393224 | tf_op jit(solution)/shard_map/ppermute | solution.py:23
  227.9 19.5 %copy-start.27 = (bf16[4,64,256]{2,1,0:T(8,128)(2,1)}, bf16[4,64,256]{2,1,0:T(8,128)(2,1)S(1)}, u32[]{:S(2)}) copy-start(bf16[4,64,256]{2,1,0:T(8,128)(2,1)S(1)} %collective-permute-done.35.refs_6_) | copy-start | bytes 393220
  227.9 19.6 %collective-permute-start.34 = (bf16[6,64,256]{2,1,0:T(8,128)(2,1)S(1)}, bf16[6,64,256]{2,1,0:T(8,128)(2,1)S(1)}, u32[]{:S(2)}, u32[]{:S(2)}) collective-permute-start(bf16[6,64,256]{2,1,0:T(8,128)(2,1)S(1)} %get-tuple-element.48), channel_id=1, source_target_pairs={{0,8},{4,12},{8,0},{12,4},{1,9},{5,13},{9,1},{13,5},{2,10},{6,14},... | collective-permute-start | bytes 589832 | tf_op jit(solution)/shard_map/ppermute | solution.py:23
  243.3 5.7 %collective-permute-start.26 = (bf16[6,64,256]{2,1,0:T(8,128)(2,1)S(1)}, bf16[6,64,256]{2,1,0:T(8,128)(2,1)S(1)}, u32[]{:S(2)}, u32[]{:S(2)}) collective-permute-start(bf16[6,64,256]{2,1,0:T(8,128)(2,1)S(1)} %get-tuple-element.49), channel_id=1, source_target_pairs={{0,4},{4,0},{8,12},{12,8},{1,5},{5,1},{9,13},{13,9},{2,6},{6,2},{1... | collective-permute-start | bytes 589832 | tf_op jit(solution)/shard_map/ppermute | solution.py:23
  244.2 11.2 %copy-start.1 = (bf16[128,4096]{1,0:T(8,128)(2,1)S(1)}, bf16[128,4096]{1,0:T(8,128)(2,1)}, u32[]{:S(2)}) copy-start(bf16[128,4096]{1,0:T(8,128)(2,1)} %param.12) | copy-start | bytes 3145732
  247.4 1.5 copy-start.28
  (8 other events, 9.6 us)

commit v3 on v2

--- a/solution.py
+++ b/solution.py
@@ -10,7 +10,7 @@
 
 WIDTH = 16384
 BLOCK = 256
-CHUNK_SIZES = (4, 6, 4, 2)
+CHUNK_SIZES = (4, 4, 6, 2)
 EARLY_CHUNKS = 2
 
 
@@ -31,45 +31,76 @@
     return lax.dynamic_index_in_dim(values, index, dim, keepdims=False)
 
 
-def grad_body(pairs, part, bit_ref, g_ref, *refs):
-    f_refs, (send_ref, keep_ref, acc_ref) = refs[:-3], refs[-3:]
+def grad_body(pairs, part, first, step, bit_ref, g_ref, *refs):
+    count = (len(refs) - 7) // 2
+    f_refs, (send_ref, keep_ref, g_buf), refs = refs[:count], refs[count : count + 3], refs[count + 3 :]
+    f_bufs, (send_buf, keep_buf, in_sems, out_sems) = refs[:count], refs[count:]
     bit = bit_ref[0]
-    blocks = g_ref.shape[1] // BLOCK
+    groups = g_buf.shape[1] // (step * BLOCK)
     halves = send_ref.shape[0]
-    for at in range(blocks):
-        for slot, (f_at, flip) in enumerate(pairs):
-            g_at = at ^ flip
-            acc_ref[...] = lax.dot_general(
-                g_ref[:, g_at * BLOCK : (g_at + 1) * BLOCK],
-                f_refs[f_at][:, at * BLOCK : (at + 1) * BLOCK],
-                (((0,), (0,)), ((), ())),
-                preferred_element_type=F32,
+    loads = []
+    for group in range(groups):
+        cols = pl.ds(group * step * BLOCK, step * BLOCK)
+        there = pl.ds((first + group * step) * BLOCK, step * BLOCK)
+        loads.append(
+            [pltpu.make_async_copy(g_ref.at[:, there], g_buf.at[:, cols], in_sems.at[group, 0])]
+            + [
+                pltpu.make_async_copy(
+                    f_refs[one].at[:, cols], f_bufs[one].at[:, cols], in_sems.at[group, 1 + one]
+                )
+                for one in range(count)
+            ]
+        )
+    for copies in loads:
+        for copy in copies:
+            copy.start()
+    stores = []
+    for group in range(groups):
+        for copy in loads[group]:
+            copy.wait()
+        for at in range(group * step, (group + 1) * step):
+            for slot, (f_at, flip) in enumerate(pairs):
+                g_at = at ^ flip
+                total = lax.dot_general(
+                    g_buf[:, g_at * BLOCK : (g_at + 1) * BLOCK],
+                    f_bufs[f_at][:, at * BLOCK : (at + 1) * BLOCK],
+                    (((0,), (0,)), ((), ())),
+                    preferred_element_type=F32,
+                )
+                for half in range(halves):
+                    low = total[2 * half * part : (2 * half + 1) * part]
+                    high = total[(2 * half + 1) * part : (2 * half + 2) * part]
+                    keep_buf[half, slot, at] = jnp.where(bit == 0, low, high)
+                    send_buf[half, slot, at] = jnp.where(bit == 0, high, low).astype(BF16)
+        span = pl.ds(group * step, step)
+        for which, (buf, ref) in enumerate(((send_buf, send_ref), (keep_buf, keep_ref))):
+            copy = pltpu.make_async_copy(
+                buf.at[:, :, span], ref.at[:, :, span], out_sems.at[group, which]
             )
-            for half in range(halves):
-                first = pl.multiple_of((2 * half + bit) * part, part)
-                other = pl.multiple_of((2 * half + 1 - bit) * part, part)
-                keep_ref[half, slot, at] = acc_ref[pl.ds(first, part), :]
-                send_ref[half, slot, at] = acc_ref[pl.ds(other, part), :].astype(BF16)
+            copy.start()
+            stores.append(copy)
+    for copy in stores:
+        copy.wait()
 
 
 def pair_grads(bit, cotangent, features, pairs, first, count, parts):
     rows_here = cotangent.shape[0]
     part = BLOCK // parts
-    step = min(2, count)
+    step = 2 if count % 2 == 0 else 1
     shape = (parts // 2, 2, count, part, BLOCK)
-    block = (parts // 2, 2, step, part, BLOCK)
-    out_spec = pl.BlockSpec(block, lambda at, bit_ref: (0, 0, at, 0, 0))
-    skip = first // step
+    wide = pltpu.VMEM((rows_here, count * BLOCK), BF16)
+    hbm = pl.BlockSpec(memory_space=pltpu.HBM)
     return pl.pallas_call(
-        functools.partial(grad_body, pairs, part),
-        grid_spec=pltpu.PrefetchScalarGridSpec(
-            num_scalar_prefetch=1,
-            grid=(count // step,),
-            in_specs=[pl.BlockSpec((rows_here, step * BLOCK), lambda at, bit_ref: (0, at + skip))]
-            + [pl.BlockSpec((rows_here, step * BLOCK), lambda at, bit_ref: (0, at))] * len(features),
-            out_specs=(out_spec, out_spec),
-            scratch_shapes=[pltpu.VMEM((BLOCK, BLOCK), F32)],
-        ),
+        functools.partial(grad_body, pairs, part, first, step),
+        in_specs=[pl.BlockSpec(memory_space=pltpu.SMEM)] + [hbm] * (1 + len(features)),
+        out_specs=(hbm, hbm),
+        scratch_shapes=[wide] * (1 + len(features))
+        + [
+            pltpu.VMEM(shape, BF16),
+            pltpu.VMEM(shape, F32),
+            pltpu.SemaphoreType.DMA((count // step, 1 + len(features))),
+            pltpu.SemaphoreType.DMA((count // step, 2)),
+        ],
         out_shape=(jax.ShapeDtypeStruct(shape, BF16), jax.ShapeDtypeStruct(shape, F32)),
         cost_estimate=pl.CostEstimate(
             flops=4 * count * rows_here * BLOCK * BLOCK,
@@ -185,18 +216,20 @@
     item = item_ref[0]
     starts = [sum(sizes[:one]) for one in range(len(sizes))]
 
+    first_col, last_col = starts[first], starts[last - 1] + sizes[last - 1]
     gathered = []
     for way in range(2):
         for slot, apart in enumerate(order):
-            owner = item ^ apart
-            source = far_w[way * parts + slot]
-            if pieces == 1:
-                into = w_buf.at[2 + way, pl.ds(owner * units, units)]
-            else:
-                rows = pl.ds(pl.multiple_of(lax.rem(owner, pieces) * unit, unit), unit)
-                source = source.at[0]
-                into = w_buf.at[2 + way, lax.div(owner, pieces), rows, :]
-            gathered.append(pltpu.make_async_copy(source, into, far_w_sems.at[way, slot]))
+            for one in range(units):
+                number = (item ^ apart) * units + one
+                block, piece = lax.div(number, pieces), lax.rem(number, pieces)
+                rows = pl.ds(pl.multiple_of(piece * unit, unit), unit)
+                copy = pltpu.make_async_copy(
+                    far_w[way * parts + slot].at[one],
+                    w_buf.at[2 + way, block, rows, :],
+                    far_w_sems.at[way, number],
+                )
+                gathered.append(((block >= first_col) & (block < last_col), copy))
     loads = []
     for step in range(steps):
         chunk = first + step
@@ -221,13 +254,24 @@
                 )
             )
         loads.append(copies)
-    for copy in gathered:
+    for copy in loads[0]:
         copy.start()
-    for copies in loads:
+    for wanted, copy in gathered:
+        pl.when(wanted)(copy.start)
+    for copies in loads[1:]:
         for copy in copies:
             copy.start()
-    for copy in gathered:
-        copy.wait()
+    for way in range(2):
+        for at in range(first_col, last_col):
+            for piece in range(pieces):
+                rows = pl.ds(piece * unit, unit)
+                loads[[starts[one] <= at < starts[one] + sizes[one] for one in range(first, last)].index(True)].append(
+                    pltpu.make_async_copy(
+                        far_w[way * parts].at[0],
+                        w_buf.at[2 + way, at, rows, :],
+                        far_w_sems.at[way, at * pieces + piece],
+                    )
+                )
     stores = []
     for step in range(steps):
         chunk = first + step
@@ -258,7 +302,7 @@
     rows_here, width = features.shape
     share = width // BLOCK
     unit = far_weights[0][0].shape[1]
-    hbm = pl.BlockSpec(memory_space=pl.ANY)
+    hbm = pl.BlockSpec(memory_space=pltpu.HBM)
     smem = pl.BlockSpec(memory_space=pltpu.SMEM)
     far_inputs = [*far[0][first:last], *far[1][first:last], *far_weights[0], *far_weights[1]]
     inputs = [pos, item, features, block_weights, codes, lowrank_out, *far_inputs]
@@ -280,7 +324,7 @@
             pltpu.VMEM((rows_here, width), BF16),
             pltpu.SemaphoreType.DMA((last - first, 4)),
             pltpu.SemaphoreType.DMA((2, share)),
-            pltpu.SemaphoreType.DMA((2, len(order))),
+            pltpu.SemaphoreType.DMA((2, len(order) * units)),
             pltpu.SemaphoreType.DMA((last - first,)),
         ],
         cost_estimate=pl.CostEstimate(
@@ -292,42 +336,57 @@
     )(*inputs)
 
 
-def place_body(share, sizes, pos_ref, own_ref, *refs):
-    far_refs, out_ref = refs[:-1], refs[-1]
-    chunks = len(sizes)
-    for way in range(4):
-        for chunk in range(chunks):
-            first = sum(sizes[:chunk])
-            for at in range(first, first + sizes[chunk]):
-                if way < 2:
-                    block = own_ref[way, at]
-                else:
-                    block = far_refs[(way - 2) * chunks + chunk][at - first].astype(F32)
-                out_ref[:, pos_ref[way * share + at], :] = block
-
-
-def place_kernel(own, far, pos, sizes):
-    _, share, part, _ = own.shape
-    rows = 16
-    far_specs = [
-        pl.BlockSpec((size, rows, BLOCK), lambda at, pos_ref: (0, at, 0)) for size in sizes
+def place_body(keys, pairs, pos_ref, *refs):
+    count = len(keys) * (2 if pairs else 1)
+    inputs, refs = refs[:count], refs[-(count + 4) :]
+    out_ref, bufs, (rows_ref, in_sems, out_sems) = refs[0], refs[1 : 1 + count], refs[1 + count :]
+    loads = [
+        pltpu.make_async_copy(inputs[one], bufs[one], in_sems.at[one]) for one in range(count)
     ]
+    for copy in loads:
+        copy.start()
+    copies = []
+    per = 2 if pairs else 1
+    for one, numbers in enumerate(keys):
+        for copy in loads[per * one : per * (one + 1)]:
+            copy.wait()
+        for at, key in enumerate(numbers):
+            block = bufs[per * one][at].astype(F32)
+            if pairs:
+                block += bufs[per * one + 1][at].astype(F32)
+            slot = len(copies)
+            rows_ref[slot, :, 0, :] = block
+            copy = pltpu.make_async_copy(
+                rows_ref.at[slot], out_ref.at[:, pl.ds(pos_ref[key], 1), :], out_sems.at[slot]
+            )
+            copy.start()
+            copies.append(copy)
+    for copy in copies:
+        copy.wait()
+
+
+def place_kernel(pieces, keys, pos, held, stored, pairs=False):
+    part = pieces[0].shape[1]
+    total = sum(len(numbers) for numbers in keys)
+    hbm = pl.BlockSpec(memory_space=pltpu.HBM)
+    inputs = [pos, *pieces] + ([] if held is None else [held])
     return pl.pallas_call(
-        functools.partial(place_body, share, sizes),
-        grid_spec=pltpu.PrefetchScalarGridSpec(
-            num_scalar_prefetch=1,
-            grid=(part // rows,),
-            in_specs=[pl.BlockSpec((2, share, rows, BLOCK), lambda at, pos_ref: (0, 0, at, 0))]
-            + far_specs
-            + far_specs,
-            out_specs=pl.BlockSpec((rows, 4 * share, BLOCK), lambda at, pos_ref: (at, 0, 0)),
-        ),
-        out_shape=jax.ShapeDtypeStruct((part, 4 * share, BLOCK), F32),
+        functools.partial(place_body, keys, pairs),
+        in_specs=[pl.BlockSpec(memory_space=pltpu.SMEM)] + [hbm] * (len(inputs) - 1),
+        out_specs=hbm,
+        out_shape=jax.ShapeDtypeStruct((part, stored, BLOCK), F32),
+        input_output_aliases={} if held is None else {len(inputs) - 1: 0},
+        scratch_shapes=[pltpu.VMEM(piece.shape, piece.dtype) for piece in pieces]
+        + [
+            pltpu.VMEM((total, part, 1, BLOCK), F32),
+            pltpu.SemaphoreType.DMA((len(pieces),)),
+            pltpu.SemaphoreType.DMA((total,)),
+        ],
         cost_estimate=pl.CostEstimate(
-            flops=0, bytes_accessed=32 * share * part * BLOCK, transcendentals=0
+            flops=0, bytes_accessed=8 * total * part * BLOCK, transcendentals=0
         ),
         name="place",
-    )(pos, own, *far[0], *far[1])
+    )(*inputs)
 
 
 def layer(features, cotangent, block_weights, block_rows, block_cols, lowrank_in, lowrank_out):
@@ -407,7 +466,14 @@
     bit = item_arg & 1
     own = pair_grads(bit, cotangent, [features], ((0, 0), (0, 1)), 0, share, items)
     own = items_sum(*own, item)
-    own = own[0] + own[1].astype(F32)
+    block_grads = place_kernel(
+        [part for way in range(2) for part in (own[0][way], own[1][way])],
+        [list(range(way * share, (way + 1) * share)) for way in range(2)],
+        pos,
+        None,
+        stored,
+        pairs=True,
+    )
     returned = [[], []]
     for one in range(chunks):
         pairs = pair_grads(
@@ -447,7 +513,14 @@
             order,
             mixed,
         )
-    block_grads = place_kernel(own, returned, pos, sizes)
+    for first, last in ((0, chunks - 1), (chunks - 1, chunks)):
+        pieces, keys = [], []
+        for way in range(2):
+            for one in range(first, last):
+                start = (2 + way) * share + sum(sizes[:one])
+                pieces.append(returned[way][one])
+                keys.append(list(range(start, start + sizes[one])))
+        block_grads = place_kernel(pieces, keys, pos, block_grads, stored)
     return (mixed, block_grads, low[0], low[1])
 
 

time: 256 us -> 254 us (level)
  waiting for transfers between devices: 135 us -> 131 us
  starting transfers between devices: 40.4 us -> 43.6 us
    ppermute x39, waiting for transfers between devices: 135 us -> 131 us  [swapped(): lax.ppermute(block, axis, [(one, one ^ 1 << apart) for one in range(count)])]
    ppermute x39, starting transfers between devices: 40.4 us -> 43.6 us  [swapped(): lax.ppermute(block, axis, [(one, one ^ 1 << apart) for one in range(count)])]
    add x1 -> x0, other arithmetic: 3.16 us -> none  [layer(): own = own[0] + own[1].astype(F32)]
    squeeze x0 -> x2, local copies, waits for them, and re-layouts: none -> 2.56 us  [the longest x1 1.54 us: layer(): own[0][way]]
    pallas_call x6 -> x8, Pallas kernels: 26.8 us -> 25.8 us  [the longest x5 16.4 us: pair_grads(): pl.pallas_call(functools.partial(grad_body, pairs, part, first, step), in...]
  transfers between devices with their start and end apart: 39 -> 39, of which waited for: 11 -> 13; matrix products, arithmetic and copies ran while one was open for 9% -> 9% of each run, Pallas kernels for 17% -> 18%
where the time goes in v3:
time: 254 us; the launch traced here: 253 us
  waiting for transfers between devices  131 us (52%)
  Pallas kernels  47.7 us (19%)
  starting transfers between devices  43.6 us (17%)
  other arithmetic  17.7 us (7%)
  local copies, waits for them, and re-layouts  9.17 us (4%)
  matrix products  3.08 us (1%)
    ppermute x39, waiting for transfers between devices, swapped(): lax.ppermute(block, axis, [(one, one ^ 1 << apart) for one in range(count)])  131 us
    ppermute x39, starting transfers between devices, swapped(): lax.ppermute(block, axis, [(one, one ^ 1 << apart) for one in range(count)])  43.6 us
    pallas_call x5, Pallas kernels, pair_grads(): pl.pallas_call(functools.partial(grad_body, pairs, part, first, step), in...  16.4 us
    pallas_call x2, Pallas kernels, mixed_kernel(): pl.pallas_call(functools.partial(mixed_body, share, sizes, first, last, u...  13.8 us
    convert_element_type x6, other arithmetic, items_sum(): came = swapped(leave.astype(BF16), 'items', level)  10.7 us
    pallas_call x3, Pallas kernels, place_kernel(): pl.pallas_call(functools.partial(place_body, keys, pairs), in_specs=[pl.B...  9.4 us
  transfers between devices with their start and end apart: 39, of which 13 were waited for; matrix products, arithmetic and copies ran while one was open for 9% of the time, Pallas kernels for 18%

profile of v3, /device:TPU:0, one launch (start us, length us, event | category | flops | bytes accessed | tf_op | source)
XLA Modules:
  0.0 253.2 jit_solution(13660213618040380599)
XLA Ops:
  0.7 1.2 copy-done
  1.9 2.4 fusion.28
  4.3 0.7 fusion.29
  5.0 3.1 %collective-permute-start = (f32[2,128,128]{2,1,0:T(8,128)S(1)}, f32[2,128,128]{2,1,0:T(8,128)S(1)}, u32[]{:S(2)}, u32[]{:S(2)}) collective-permute-start(f32[2,128,128]{2,1,0:T(8,128)S(1)} %fusion.15), channel_id=1, source_target_pairs={{0,4},{4,0},{8,12},{12,8},{1,5},{5,1},{9,13},{13,9},{2,6},{6,2},{1... | collective-permute-start | bytes 393224 | tf_op jit(solution)/shard_map/ppermute | solution.py:23
  8.2 3.5 %collective-permute-done = f32[2,128,128]{2,1,0:T(8,128)S(1)} collective-permute-done((f32[2,128,128]{2,1,0:T(8,128)S(1)}, f32[2,128,128]{2,1,0:T(8,128)S(1)}, u32[]{:S(2)}, u32[]{:S(2)}) %collective-permute-start) | collective-permute-done | bytes 131104 | tf_op jit(solution)/shard_map/ppermute | solution.py:23
  11.7 2.8 %collective-permute-start.1 = (f32[2,128,128]{2,1,0:T(8,128)S(1)}, f32[2,128,128]{2,1,0:T(8,128)}, u32[]{:S(2)}, u32[]{:S(2)}) collective-permute-start(f32[2,128,128]{2,1,0:T(8,128)S(1)} %fusion.18), channel_id=1, source_target_pairs={{0,8},{4,12},{8,0},{12,4},{1,9},{5,13},{9,1},{13,5},{2,10},{6,14},... | collective-permute-start | bytes 393224 | tf_op jit(solution)/shard_map/ppermute | solution.py:23
  15.1 3.1 %weight_share.1 = (bf16[4,256,256]{2,1,0:T(8,128)(2,1)}, bf16[4,256,256]{2,1,0:T(8,128)(2,1)}) custom-call(s32[64]{0:T(128)} %select_reduce_fusion.pos_ref, s32[1]{0:T(128)} %bitcast.item_ref, bf16[64,256,256]{2,1,0:T(8,128)(2,1)} %w_ref.5), custom_call_target="tpu_custom_call" | custom-call | bytes 2097152 | tf_op jit(solution)/shard_map/weight_share/pallas_call | solution.py:191
  18.2 1.6 collective-permute-start.7
  19.8 0.8 slice.115
  21.3 0.8 slice.116
  22.2 0.9 slice.117
  23.1 1.8 collective-permute-start.4
  24.9 2.6 %collective-permute-start.6 = (bf16[256,512]{1,0:T(8,128)(2,1)S(1)}, bf16[256,512]{1,0:T(8,128)(2,1)S(1)}, u32[]{:S(2)}, u32[]{:S(2)}) collective-permute-start(bf16[256,512]{1,0:T(8,128)(2,1)S(1)} %slice.118), channel_id=1, source_target_pairs={{0,8},{4,12},{8,0},{12,4},{1,9},{5,13},{9,1},{13,5},{2,10},{6,14},... | collective-permute-start | bytes 786440 | tf_op jit(solution)/shard_map/ppermute | solution.py:23
  27.5 0.9 add_convert_fusion.6
  28.4 36.6 %collective-permute-done.4.refs_1_.refs_0_ = bf16[256,512]{1,0:T(8,128)(2,1)S(1)} collective-permute-done((bf16[256,512]{1,0:T(8,128)(2,1)S(1)}, bf16[256,512]{1,0:T(8,128)(2,1)S(1)}, u32[]{:S(2)}, u32[]{:S(2)}) %collective-permute-start.4) | collective-permute-done | bytes 262176 | tf_op jit(solution)/shard_map/ppermute | solution.py:23
  65.1 2.0 collective-permute-start.16
  67.1 2.9 %collective-permute-done.2 = bf16[2,128,128]{2,1,0:T(8,128)(2,1)S(1)} collective-permute-done((bf16[2,128,128]{2,1,0:T(8,128)(2,1)S(1)}, bf16[2,128,128]{2,1,0:T(8,128)(2,1)S(1)}, u32[]{:S(2)}, u32[]{:S(2)}) %collective-permute-start.2) | collective-permute-done | bytes 65568 | tf_op jit(solution)/shard_map/ppermute | solution.py:23
  70.0 1.2 collective-permute-start.18
  71.2 2.4 pair_grads.5
  73.8 1.8 collective-permute-start.11
  75.5 0.9 collective-permute-start.3
  76.4 2.9 %pair_grads.6 = (bf16[2,2,4,64,256]{4,3,2,1,0:T(8,128)(2,1)}, f32[2,2,4,64,256]{4,3,2,1,0:T(8,128)}) custom-call(s32[1]{0:T(128)S(6)} %and.24.bit_ref, bf16[256,4096]{1,0:T(8,128)(2,1)} %g_ref.11, bf16[256,1024]{1,0:T(8,128)(2,1)} %copy-done.13, bf16[256,1024]{1,0:T(8,128)(2,1)} %collective-permute-done.17.refs_2_.refs_1_), custom_call_target="tpu_custom_call" | custom-call | flops 268435456 | bytes 3145728 | tf_op jit(solution)/shard_map/pair_grads/pallas_call | solution.py:93
  79.6 12.6 %collective-permute-done.16.refs_1_.refs_0_ = bf16[256,1024]{1,0:T(8,128)(2,1)} collective-permute-done((bf16[256,1024]{1,0:T(8,128)(2,1)}, bf16[256,1024]{1,0:T(8,128)(2,1)}, u32[]{:S(2)}, u32[]{:S(2)}) %collective-permute-start.16) | collective-permute-done | bytes 524320 | tf_op jit(solution)/shard_map/ppermute | solution.py:23
  92.2 16.4 %collective-permute-done.18.refs_3_.refs_1_ = bf16[256,1024]{1,0:T(8,128)(2,1)} collective-permute-done((bf16[256,1024]{1,0:T(8,128)(2,1)}, bf16[256,1024]{1,0:T(8,128)(2,1)}, u32[]{:S(2)}, u32[]{:S(2)}) %collective-permute-start.18) | collective-permute-done | bytes 524320 | tf_op jit(solution)/shard_map/ppermute | solution.py:23
  108.6 1.4 collective-permute-start.20
  110.0 2.8 %pair_grads.7 = (bf16[2,2,4,64,256]{4,3,2,1,0:T(8,128)(2,1)}, f32[2,2,4,64,256]{4,3,2,1,0:T(8,128)}) custom-call(s32[1]{0:T(128)S(6)} %and.24.bit_ref, bf16[256,4096]{1,0:T(8,128)(2,1)} %g_ref.11, bf16[256,1024]{1,0:T(8,128)(2,1)} %collective-permute-done.16.refs_1_.refs_0_, bf16[256,1024]{1,0:T(8,128)(2,1)} %collective-permute-done.18.refs_3_.refs_1_), custom_call_target="tpu_custom_call" | custom-call | flops 268435456 | bytes 3145728 | tf_op jit(solution)/shard_map/pair_grads/pallas_call | solution.py:93
  112.8 6.9 %collective-permute-done.11.refs_8_ = bf16[4,256,256]{2,1,0:T(8,128)(2,1)S(1)} collective-permute-done((bf16[4,256,256]{2,1,0:T(8,128)(2,1)}, bf16[4,256,256]{2,1,0:T(8,128)(2,1)S(1)}, u32[]{:S(2)}, u32[]{:S(2)}) %collective-permute-start.11) | collective-permute-done | bytes 524320 | tf_op jit(solution)/shard_map/ppermute | solution.py:23
  119.7 1.4 collective-permute-start.8
  121.8 5.0 %low_grads.1 = (bf16[2,2,32,4096]{3,2,1,0:T(8,128)(2,1)}, f32[2,2,32,4096]{3,2,1,0:T(8,128)}) custom-call(s32[1]{0:T(128)S(6)} %and.24.bit_ref, bf16[256,128]{1,0:T(8,128)(2,1)} %get-tuple-element.64.b_ref, bf16[256,4096]{1,0:T(8,128)(2,1)} %f_ref.5, bf16[256,128]{1,0:T(8,128)(2,1)} %get-tuple-element.65.codes_ref.c_ref, bf16[256,4096]{1,0:T(8,128)(2,1)} %g_ref.11), custom_call_target="tpu_custom_call" | custom-call | flops 536870912 | bytes 7340032 | tf_op jit(solution)/shard_map/low_grads/pallas_call | solution.py:136
  127.0 5.1 %pair_grads.9 = (bf16[2,2,16,64,256]{4,3,2,1,0:T(8,128)(2,1)}, f32[2,2,16,64,256]{4,3,2,1,0:T(8,128)}) custom-call(s32[1]{0:T(128)S(6)} %and.24.bit_ref, bf16[256,4096]{1,0:T(8,128)(2,1)} %g_ref.11, bf16[256,4096]{1,0:T(8,128)(2,1)} %f_ref.5), custom_call_target="tpu_custom_call" | custom-call | flops 1073741824 | bytes 12582912 | tf_op jit(solution)/shard_map/pair_grads/pallas_call | solution.py:93
  132.5 2.3 add_convert_fusion.4
  134.8 14.9 %collective-permute-done.5.refs_2_.refs_1_ = bf16[256,1536]{1,0:T(8,128)(2,1)S(1)} collective-permute-done((bf16[256,1536]{1,0:T(8,128)(2,1)}, bf16[256,1536]{1,0:T(8,128)(2,1)S(1)}, u32[]{:S(2)}, u32[]{:S(2)}) %collective-permute-start.5) | collective-permute-done | bytes 786464 | tf_op jit(solution)/shard_map/ppermute | solution.py:23
  149.7 1.6 collective-permute-start.12
  152.5 1.2 add_convert_fusion.3
  153.6 16.0 %collective-permute-done.24 = bf16[1,2,4,64,256]{4,3,2,1,0:T(8,128)(2,1)S(1)} collective-permute-done((bf16[1,2,4,64,256]{4,3,2,1,0:T(8,128)(2,1)S(1)}, bf16[1,2,4,64,256]{4,3,2,1,0:T(8,128)(2,1)S(1)}, u32[]{:S(2)}, u32[]{:S(2)}) %collective-permute-start.24) | collective-permute-done | bytes 262176 | tf_op jit(solution)/shard_map/ppermute | solution.py:23
  169.7 0.7 copy-done.21
  170.4 1.5 collective-permute-start.27
  171.9 3.2 %pair_grads.8 = (bf16[2,2,6,64,256]{4,3,2,1,0:T(8,128)(2,1)}, f32[2,2,6,64,256]{4,3,2,1,0:T(8,128)}) custom-call(s32[1]{0:T(128)S(6)} %and.24.bit_ref, bf16[256,4096]{1,0:T(8,128)(2,1)} %g_ref.11, bf16[256,1536]{1,0:T(8,128)(2,1)} %copy-done.5, bf16[256,1536]{1,0:T(8,128)(2,1)} %copy-done.6), custom_call_target="tpu_custom_call" | custom-call | flops 402653184 | bytes 4718592 | tf_op jit(solution)/shard_map/pair_grads/pallas_call | solution.py:93
  175.1 1.9 fusion.12
  177.6 0.7 collective-permute-done.27
  178.8 1.7 fusion.13
  180.5 2.3 add_convert_fusion.1
  182.8 2.4 collective-permute-start.21
  185.3 1.1 collective-permute-start.38
  186.4 6.7 %mixed.2.refs_12_ = bf16[256,4096]{1,0:T(8,128)(2,1)} custom-call(s32[64]{0:T(128)} %select_reduce_fusion.pos_ref, s32[1]{0:T(128)} %bitcast.item_ref, bf16[256,4096]{1,0:T(8,128)(2,1)} %f_ref.5, bf16[64,256,256]{2,1,0:T(8,128)(2,1)} %w_ref.5, bf16[256,128]{1,0:T(8,128)(2,1)} %get-tuple-element.65.codes_ref.c_ref, bf16[128,4096]{1,0:T(8,128)(2,1)} %low_ref.3, ...), custom_call_target="tpu_custom_call" | custom-call | flops 1207959552 | bytes 8388608 | tf_op jit(solution)/shard_map/mixed/pallas_call | solution.py:312
  193.2 7.1 %mixed.3 = bf16[256,4096]{1,0:T(8,128)(2,1)} custom-call(s32[64]{0:T(128)} %select_reduce_fusion.pos_ref, s32[1]{0:T(128)} %bitcast.item_ref, bf16[256,4096]{1,0:T(8,128)(2,1)} %f_ref.5, bf16[64,256,256]{2,1,0:T(8,128)(2,1)} %w_ref.5, bf16[256,128]{1,0:T(8,128)(2,1)} %get-tuple-element.65.codes_ref.c_ref, ...), custom_call_target="tpu_custom_call", output_to_operand_aliasing={{}: (18, {})} | custom-call | flops 1207959552 | bytes 8388608 | tf_op jit(solution)/shard_map/mixed/pallas_call | solution.py:312
  200.3 1.4 collective-permute-start.28
  201.7 1.3 add_convert_fusion.2
  203.1 1.6 collective-permute-start.30
  204.6 3.6 %add_convert_fusion = (bf16[1,2,16,64,256]{4,3,2,1,0:T(8,128)(2,1)S(1)}, f32[1,2,16,64,256]{4,3,2,1,0:T(8,128)S(1)}) fusion(f32[2,2,16,64,256]{4,3,2,1,0:T(8,128)} %get-tuple-element.34, s32[]{:T(128)S(6)} %select_n.71, bf16[2,2,16,64,256]{4,3,2,1,0:T(8,128)(2,1)} %collective-permute-done.35, s32[]{:T(128)S(6)} %select_n.70), kind=kLoop, calls=%fused_computation | loop fusion | flops 2621440 | bytes 9437192 | tf_op jit(solution)/shard_map/convert_element_type | solution.py:164
  208.8 1.1 fusion
  209.9 5.2 %collective-permute-done.30 = bf16[1,2,6,64,256]{4,3,2,1,0:T(8,128)(2,1)S(1)} collective-permute-done((bf16[1,2,6,64,256]{4,3,2,1,0:T(8,128)(2,1)S(1)}, bf16[1,2,6,64,256]{4,3,2,1,0:T(8,128)(2,1)S(1)}, u32[]{:S(2)}, u32[]{:S(2)}) %collective-permute-start.30) | collective-permute-done | bytes 393248 | tf_op jit(solution)/shard_map/ppermute | solution.py:23
  215.1 3.3 %collective-permute-start.32 = (bf16[4,64,256]{2,1,0:T(8,128)(2,1)S(1)}, bf16[4,64,256]{2,1,0:T(8,128)(2,1)S(1)}, u32[]{:S(2)}, u32[]{:S(2)}) collective-permute-start(bf16[4,64,256]{2,1,0:T(8,128)(2,1)S(1)} %get-tuple-element.58), channel_id=1, source_target_pairs={{0,8},{4,12},{8,0},{12,4},{1,9},{5,13},{9,1},{13,5},{2,10},{6,14},... | collective-permute-start | bytes 393224 | tf_op jit(solution)/shard_map/ppermute | solution.py:23
  218.5 1.5 slice_bitcast_fusion
  220.2 2.9 %collective-permute-start.33 = (bf16[4,64,256]{2,1,0:T(8,128)(2,1)S(1)}, bf16[4,64,256]{2,1,0:T(8,128)(2,1)S(1)}, u32[]{:S(2)}, u32[]{:S(2)}) collective-permute-start(bf16[4,64,256]{2,1,0:T(8,128)(2,1)S(1)} %copy-done.29), channel_id=1, source_target_pairs={{0,8},{4,12},{8,0},{12,4},{1,9},{5,13},{9,1},{13,5},{2,10},{6,14},... | collective-permute-start | bytes 393224 | tf_op jit(solution)/shard_map/ppermute | solution.py:23
  223.2 5.1 %collective-permute-done.32.refs_3_ = bf16[4,64,256]{2,1,0:T(8,128)(2,1)S(1)} collective-permute-done((bf16[4,64,256]{2,1,0:T(8,128)(2,1)S(1)}, bf16[4,64,256]{2,1,0:T(8,128)(2,1)S(1)}, u32[]{:S(2)}, u32[]{:S(2)}) %collective-permute-start.32) | collective-permute-done | bytes 131104 | tf_op jit(solution)/shard_map/ppermute | solution.py:23
  228.2 7.3 %collective-permute-done.36 = bf16[1,2,16,64,256]{4,3,2,1,0:T(8,128)(2,1)S(1)} collective-permute-done((bf16[1,2,16,64,256]{4,3,2,1,0:T(8,128)(2,1)S(1)}, bf16[1,2,16,64,256]{4,3,2,1,0:T(8,128)(2,1)S(1)}, u32[]{:S(2)}, u32[]{:S(2)}) %collective-permute-start.36) | collective-permute-done | bytes 1048608 | tf_op jit(solution)/shard_map/ppermute | solution.py:23
  235.5 3.3 %collective-permute-start.34 = (bf16[6,64,256]{2,1,0:T(8,128)(2,1)S(1)}, bf16[6,64,256]{2,1,0:T(8,128)(2,1)S(1)}, u32[]{:S(2)}, u32[]{:S(2)}) collective-permute-start(bf16[6,64,256]{2,1,0:T(8,128)(2,1)S(1)} %get-tuple-element.52), channel_id=1, source_target_pairs={{0,8},{4,12},{8,0},{12,4},{1,9},{5,13},{9,1},{13,5},{2,10},{6,14},... | collective-permute-start | bytes 589832 | tf_op jit(solution)/shard_map/ppermute | solution.py:23
  238.8 1.0 slice_bitcast_fusion.2
  239.8 3.9 %place.3.refs_6_ = f32[64,64,256]{2,1,0:T(8,128)} custom-call(s32[64]{0:T(128)} %select_reduce_fusion.pos_ref, f32[16,64,256]{2,1,0:T(8,128)} %get-tuple-element.45.refs_0_, bf16[16,64,256]{2,1,0:T(8,128)(2,1)} %get-tuple-element.55.refs_1_, f32[16,64,256]{2,1,0:T(8,128)} %get-tuple-element.44.refs_2_, bf16[16,64,256]{2,1,0:T(8,128)(2,1)} %get-tuple-element.54.refs_3_), custom_call_target="tpu_custom_call" | custom-call | bytes 4194304 | tf_op jit(solution)/shard_map/place/pallas_call | solution.py:373
  243.8 2.3 collective-permute-done.34.refs_5_
  246.1 0.7 copy-done.24
  246.8 3.1 %place.4.refs_2_ = f32[64,64,256]{2,1,0:T(8,128)} custom-call(s32[64]{0:T(128)} %select_reduce_fusion.pos_ref, bf16[4,64,256]{2,1,0:T(8,128)(2,1)} %copy-done.25, bf16[4,64,256]{2,1,0:T(8,128)(2,1)} %copy-done.26, bf16[6,64,256]{2,1,0:T(8,128)(2,1)} %copy-done.23, bf16[4,64,256]{2,1,0:T(8,128)(2,1)} %copy-done.27, ...), custom_call_target="tpu_custom_call", output_to_operand_aliasing={{}: (7, {})} | custom-call | bytes 3670016 | tf_op jit(solution)/shard_map/place/pallas_call | solution.py:373
  250.6 2.4 place.5
  (120 shorter events, 6.8 us)
Async XLA Ops:
  0.6 3.6 %copy-start.2 = (bf16[256,4096]{1,0:T(8,128)(2,1)S(1)}, bf16[256,4096]{1,0:T(8,128)(2,1)}, u32[]{:S(2)}) copy-start(bf16[256,4096]{1,0:T(8,128)(2,1)} %g_ref.11) | copy-start | bytes 6291460
  1.9 2.4 copy-start.4
  4.3 3.9 %copy-start.32 = (s32[64]{0:T(128)S(1)}, s32[64]{0:T(128)}, u32[]{:S(2)}) copy-start(s32[64]{0:T(128)} %param.11) | copy-start | bytes 772
  4.3 3.9 %copy-start.33 = (s32[64]{0:T(128)S(1)}, s32[64]{0:T(128)}, u32[]{:S(2)}) copy-start(s32[64]{0:T(128)} %param.10) | copy-start | bytes 772
  5.0 6.6 %collective-permute-start = (f32[2,128,128]{2,1,0:T(8,128)S(1)}, f32[2,128,128]{2,1,0:T(8,128)S(1)}, u32[]{:S(2)}, u32[]{:S(2)}) collective-permute-start(f32[2,128,128]{2,1,0:T(8,128)S(1)} %fusion.15), channel_id=1, source_target_pairs={{0,4},{4,0},{8,12},{12,8},{1,5},{5,1},{9,13},{13,9},{2,6},{6,2},{1... | collective-permute-start | bytes 393224 | tf_op jit(solution)/shard_map/ppermute | solution.py:23
  11.7 13.2 %collective-permute-start.1 = (f32[2,128,128]{2,1,0:T(8,128)S(1)}, f32[2,128,128]{2,1,0:T(8,128)}, u32[]{:S(2)}, u32[]{:S(2)}) collective-permute-start(f32[2,128,128]{2,1,0:T(8,128)S(1)} %fusion.18), channel_id=1, source_target_pairs={{0,8},{4,12},{8,0},{12,4},{1,9},{5,13},{9,1},{13,5},{2,10},{6,14},... | collective-permute-start | bytes 393224 | tf_op jit(solution)/shard_map/ppermute | solution.py:23
  15.1 4.8 %copy-start.3 = (bf16[256,4096]{1,0:T(8,128)(2,1)S(1)}, bf16[256,4096]{1,0:T(8,128)(2,1)}, u32[]{:S(2)}) copy-start(bf16[256,4096]{1,0:T(8,128)(2,1)} %f_ref.5) | copy-start | bytes 6291460
  18.2 55.5 %collective-permute-start.7 = (bf16[4,256,256]{2,1,0:T(8,128)(2,1)}, bf16[4,256,256]{2,1,0:T(8,128)(2,1)S(1)}, u32[]{:S(2)}, u32[]{:S(2)}) collective-permute-start(bf16[4,256,256]{2,1,0:T(8,128)(2,1)} %get-tuple-element.24), channel_id=1, source_target_pairs={{0,4},{4,0},{8,12},{12,8},{1,5},{5,1},{9,13},{13,9},{2,6},{6,2},{1... | collective-permute-start | bytes 1572872 | tf_op jit(solution)/shard_map/ppermute | solution.py:23
  20.7 53.1 %collective-permute-start.15 = (bf16[256,1024]{1,0:T(8,128)(2,1)}, bf16[256,1024]{1,0:T(8,128)(2,1)S(1)}, u32[]{:S(2)}, u32[]{:S(2)}) collective-permute-start(bf16[256,1024]{1,0:T(8,128)(2,1)} %slice.115), channel_id=1, source_target_pairs={{0,4},{4,0},{8,12},{12,8},{1,5},{5,1},{9,13},{13,9},{2,6},{6,2},{1... | collective-permute-start | bytes 1572872 | tf_op jit(solution)/shard_map/ppermute | solution.py:23
  21.1 54.4 %collective-permute-start.17 = (bf16[256,1024]{1,0:T(8,128)(2,1)}, bf16[256,1024]{1,0:T(8,128)(2,1)}, u32[]{:S(2)}, u32[]{:S(2)}) collective-permute-start(bf16[256,1024]{1,0:T(8,128)(2,1)} %slice.115), channel_id=1, source_target_pairs={{0,8},{4,12},{8,0},{12,4},{1,9},{5,13},{9,1},{13,5},{2,10},{6,14},... | collective-permute-start | bytes 1572872 | tf_op jit(solution)/shard_map/ppermute | solution.py:23
  23.1 41.9 %collective-permute-start.4 = (bf16[256,512]{1,0:T(8,128)(2,1)S(1)}, bf16[256,512]{1,0:T(8,128)(2,1)S(1)}, u32[]{:S(2)}, u32[]{:S(2)}) collective-permute-start(bf16[256,512]{1,0:T(8,128)(2,1)S(1)} %slice.118), channel_id=1, source_target_pairs={{0,4},{4,0},{8,12},{12,8},{1,5},{5,1},{9,13},{13,9},{2,6},{6,2},{1... | collective-permute-start | bytes 786440 | tf_op jit(solution)/shard_map/ppermute | solution.py:23
  24.9 40.1 %collective-permute-start.6 = (bf16[256,512]{1,0:T(8,128)(2,1)S(1)}, bf16[256,512]{1,0:T(8,128)(2,1)S(1)}, u32[]{:S(2)}, u32[]{:S(2)}) collective-permute-start(bf16[256,512]{1,0:T(8,128)(2,1)S(1)} %slice.118), channel_id=1, source_target_pairs={{0,8},{4,12},{8,0},{12,4},{1,9},{5,13},{9,1},{13,5},{2,10},{6,14},... | collective-permute-start | bytes 786440 | tf_op jit(solution)/shard_map/ppermute | solution.py:23
  28.4 47.1 %copy-start.19 = (bf16[2,128,128]{2,1,0:T(8,128)(2,1)}, bf16[2,128,128]{2,1,0:T(8,128)(2,1)S(1)}, u32[]{:S(2)}) copy-start(bf16[2,128,128]{2,1,0:T(8,128)(2,1)S(1)} %add_convert_fusion.6) | copy-start | bytes 196612
  65.0 6.2 %copy-start.15 = (bf16[256,512]{1,0:T(8,128)(2,1)}, bf16[256,512]{1,0:T(8,128)(2,1)S(1)}, u32[]{:S(2)}) copy-start(bf16[256,512]{1,0:T(8,128)(2,1)S(1)} %collective-permute-done.4.refs_1_.refs_0_) | copy-start | bytes 786436
  65.0 5.0 %collective-permute-start.2 = (bf16[2,128,128]{2,1,0:T(8,128)(2,1)S(1)}, bf16[2,128,128]{2,1,0:T(8,128)(2,1)S(1)}, u32[]{:S(2)}, u32[]{:S(2)}) collective-permute-start(bf16[2,128,128]{2,1,0:T(8,128)(2,1)S(1)} %add_convert_fusion.6), channel_id=1, source_target_pairs={{0,4},{4,0},{8,12},{12,8},{1,5},{5,1},{9,13},{13,9},{2,6},{6,2},{1... | collective-permute-start | bytes 196616 | tf_op jit(solution)/shard_map/ppermute | solution.py:23
  65.1 6.2 %copy-start.16 = (bf16[256,512]{1,0:T(8,128)(2,1)}, bf16[256,512]{1,0:T(8,128)(2,1)S(1)}, u32[]{:S(2)}) copy-start(bf16[256,512]{1,0:T(8,128)(2,1)S(1)} %collective-permute-done.6.refs_3_.refs_1_) | copy-start | bytes 786436
  65.1 27.1 %collective-permute-start.16 = (bf16[256,1024]{1,0:T(8,128)(2,1)}, bf16[256,1024]{1,0:T(8,128)(2,1)}, u32[]{:S(2)}, u32[]{:S(2)}) collective-permute-start(bf16[256,1024]{1,0:T(8,128)(2,1)} %slice.116), channel_id=1, source_target_pairs={{0,4},{4,0},{8,12},{12,8},{1,5},{5,1},{9,13},{13,9},{2,6},{6,2},{1... | collective-permute-start | bytes 1572872 | tf_op jit(solution)/shard_map/ppermute | solution.py:23
  70.0 38.6 %collective-permute-start.18 = (bf16[256,1024]{1,0:T(8,128)(2,1)}, bf16[256,1024]{1,0:T(8,128)(2,1)}, u32[]{:S(2)}, u32[]{:S(2)}) collective-permute-start(bf16[256,1024]{1,0:T(8,128)(2,1)} %slice.116), channel_id=1, source_target_pairs={{0,8},{4,12},{8,0},{12,4},{1,9},{5,13},{9,1},{13,5},{2,10},{6,14},... | collective-permute-start | bytes 1572872 | tf_op jit(solution)/shard_map/ppermute | solution.py:23
  73.6 5.9 %copy-start.18 = (f32[2,2,2,64,256]{4,3,2,1,0:T(8,128)S(1)}, f32[2,2,2,64,256]{4,3,2,1,0:T(8,128)}, u32[]{:S(2)}) copy-start(f32[2,2,2,64,256]{4,3,2,1,0:T(8,128)} %get-tuple-element.26) | copy-start | bytes 1572868
  73.7 76.0 %copy-start.7 = (bf16[4,256,256]{2,1,0:T(8,128)(2,1)}, bf16[4,256,256]{2,1,0:T(8,128)(2,1)S(1)}, u32[]{:S(2)}) copy-start(bf16[4,256,256]{2,1,0:T(8,128)(2,1)S(1)} %collective-permute-done.7.refs_4_) | copy-start | bytes 1572868
  73.7 5.6 %collective-permute-start.19 = (bf16[2,2,2,64,256]{4,3,2,1,0:T(8,128)(2,1)}, bf16[2,2,2,64,256]{4,3,2,1,0:T(8,128)(2,1)S(1)}, u32[]{:S(2)}, u32[]{:S(2)}) collective-permute-start(bf16[2,2,2,64,256]{4,3,2,1,0:T(8,128)(2,1)} %get-tuple-element.27), channel_id=1, source_target_pairs={{0,1},{1,0},{2,3},{3,2},{4,5},{5,4},{6,7},{7,6},{8,9},{9,8},{10,11... | collective-permute-start | bytes 786440 | tf_op jit(solution)/shard_map/ppermute | solution.py:23
  73.8 2.7 %copy-start.13 = (bf16[256,1024]{1,0:T(8,128)(2,1)}, bf16[256,1024]{1,0:T(8,128)(2,1)S(1)}, u32[]{:S(2)}) copy-start(bf16[256,1024]{1,0:T(8,128)(2,1)S(1)} %collective-permute-done.15.refs_0_) | copy-start | bytes 1572868
  73.8 45.9 %collective-permute-start.11 = (bf16[4,256,256]{2,1,0:T(8,128)(2,1)}, bf16[4,256,256]{2,1,0:T(8,128)(2,1)S(1)}, u32[]{:S(2)}, u32[]{:S(2)}) collective-permute-start(bf16[4,256,256]{2,1,0:T(8,128)(2,1)} %get-tuple-element.25), channel_id=1, source_target_pairs={{0,8},{4,12},{8,0},{12,4},{1,9},{5,13},{9,1},{13,5},{2,10},{6,14},... | collective-permute-start | bytes 1572872 | tf_op jit(solution)/shard_map/ppermute | solution.py:23
  75.5 51.3 %collective-permute-start.3 = (bf16[256,1536]{1,0:T(8,128)(2,1)}, bf16[256,1536]{1,0:T(8,128)(2,1)S(1)}, u32[]{:S(2)}, u32[]{:S(2)}) collective-permute-start(bf16[256,1536]{1,0:T(8,128)(2,1)} %slice.117), channel_id=1, source_target_pairs={{0,4},{4,0},{8,12},{12,8},{1,5},{5,1},{9,13},{13,9},{2,6},{6,2},{1... | collective-permute-start | bytes 2359304 | tf_op jit(solution)/shard_map/ppermute | solution.py:23
  76.4 33.5 %copy-start.20 = (bf16[2,128,128]{2,1,0:T(8,128)(2,1)S(1)}, bf16[2,128,128]{2,1,0:T(8,128)(2,1)}, u32[]{:S(2)}) copy-start(bf16[2,128,128]{2,1,0:T(8,128)(2,1)} %copy-done.19) | copy-start | bytes 196612
  79.3 52.9 %collective-permute-start.23 = (bf16[2,2,4,64,256]{4,3,2,1,0:T(8,128)(2,1)}, bf16[2,2,4,64,256]{4,3,2,1,0:T(8,128)(2,1)}, u32[]{:S(2)}, u32[]{:S(2)}) collective-permute-start(bf16[2,2,4,64,256]{4,3,2,1,0:T(8,128)(2,1)} %get-tuple-element.29), channel_id=1, source_target_pairs={{0,1},{1,0},{2,3},{3,2},{4,5},{5,4},{6,7},{7,6},{8,9},{9,8},{10,11... | collective-permute-start | bytes 1572872 | tf_op jit(solution)/shard_map/ppermute | solution.py:23
  92.2 57.5 %collective-permute-start.5 = (bf16[256,1536]{1,0:T(8,128)(2,1)}, bf16[256,1536]{1,0:T(8,128)(2,1)S(1)}, u32[]{:S(2)}, u32[]{:S(2)}) collective-permute-start(bf16[256,1536]{1,0:T(8,128)(2,1)} %slice.117), channel_id=1, source_target_pairs={{0,8},{4,12},{8,0},{12,4},{1,9},{5,13},{9,1},{13,5},{2,10},{6,14},... | collective-permute-start | bytes 2359304 | tf_op jit(solution)/shard_map/ppermute | solution.py:23
  108.6 11.1 %collective-permute-start.20 = (bf16[1,2,2,64,256]{4,3,2,1,0:T(8,128)(2,1)S(1)}, bf16[1,2,2,64,256]{4,3,2,1,0:T(8,128)(2,1)S(1)}, u32[]{:S(2)}, u32[]{:S(2)}) collective-permute-start(bf16[1,2,2,64,256]{4,3,2,1,0:T(8,128)(2,1)S(1)} %get-tuple-element.60), channel_id=1, source_target_pairs={{0,2},{1,3},{2,0},{3,1},{4,6},{5,7},{6,4},{7,5},{8,10},{9,11},{10,... | collective-permute-start | bytes 393224 | tf_op jit(solution)/shard_map/ppermute | solution.py:23
  119.7 57.3 %copy-start.8 = (bf16[4,256,256]{2,1,0:T(8,128)(2,1)}, bf16[4,256,256]{2,1,0:T(8,128)(2,1)S(1)}, u32[]{:S(2)}) copy-start(bf16[4,256,256]{2,1,0:T(8,128)(2,1)S(1)} %collective-permute-done.11.refs_8_) | copy-start | bytes 1572868
  119.7 31.6 %collective-permute-start.26 = (bf16[2,2,4,64,256]{4,3,2,1,0:T(8,128)(2,1)}, bf16[2,2,4,64,256]{4,3,2,1,0:T(8,128)(2,1)}, u32[]{:S(2)}, u32[]{:S(2)}) collective-permute-start(bf16[2,2,4,64,256]{4,3,2,1,0:T(8,128)(2,1)} %get-tuple-element.31), channel_id=1, source_target_pairs={{0,1},{1,0},{2,3},{3,2},{4,5},{5,4},{6,7},{7,6},{8,9},{9,8},{10,11... | collective-permute-start | bytes 1572872 | tf_op jit(solution)/shard_map/ppermute | solution.py:23
  119.7 30.0 %collective-permute-start.8 = (bf16[4,256,256]{2,1,0:T(8,128)(2,1)S(1)}, bf16[4,256,256]{2,1,0:T(8,128)(2,1)}, u32[]{:S(2)}, u32[]{:S(2)}) collective-permute-start(bf16[4,256,256]{2,1,0:T(8,128)(2,1)S(1)} %collective-permute-done.7.refs_4_), channel_id=1, source_target_pairs={{0,2},{1,3},{2,0},{3,1},{4,6},{5,7},{6,4},{7,5},{8,10},{9,11},{10,... | collective-permute-start | bytes 1572872 | tf_op jit(solution)/shard_map/ppermute | solution.py:23
  126.8 5.3 %copy-start.5 = (bf16[256,1536]{1,0:T(8,128)(2,1)}, bf16[256,1536]{1,0:T(8,128)(2,1)S(1)}, u32[]{:S(2)}) copy-start(bf16[256,1536]{1,0:T(8,128)(2,1)S(1)} %collective-permute-done.3.refs_0_) | copy-start | bytes 2359300
  126.8 51.5 %collective-permute-start.37 = (bf16[2,2,32,4096]{3,2,1,0:T(8,128)(2,1)}, bf16[2,2,32,4096]{3,2,1,0:T(8,128)(2,1)}, u32[]{:S(2)}, u32[]{:S(2)}) collective-permute-start(bf16[2,2,32,4096]{3,2,1,0:T(8,128)(2,1)} %get-tuple-element.37), channel_id=1, source_target_pairs={{0,1},{1,0},{2,3},{3,2},{4,5},{5,4},{6,7},{7,6},{8,9},{9,8},{10,11... | collective-permute-start | bytes 3145736 | tf_op jit(solution)/shard_map/ppermute | solution.py:23
  132.2 20.3 %copy-start.17 = (f32[2,2,4,64,256]{4,3,2,1,0:T(8,128)S(1)}, f32[2,2,4,64,256]{4,3,2,1,0:T(8,128)}, u32[]{:S(2)}) copy-start(f32[2,2,4,64,256]{4,3,2,1,0:T(8,128)} %get-tuple-element.30) | copy-start | bytes 3145732
  132.2 70.9 %collective-permute-start.35 = (bf16[2,2,16,64,256]{4,3,2,1,0:T(8,128)(2,1)}, bf16[2,2,16,64,256]{4,3,2,1,0:T(8,128)(2,1)}, u32[]{:S(2)}, u32[]{:S(2)}) collective-permute-start(bf16[2,2,16,64,256]{4,3,2,1,0:T(8,128)(2,1)} %get-tuple-element.35), channel_id=1, source_target_pairs={{0,1},{1,0},{2,3},{3,2},{4,5},{5,4},{6,7},{7,6},{8,9},{9,8},{10,11... | collective-permute-start | bytes 6291464 | tf_op jit(solution)/shard_map/ppermute | solution.py:23
  149.7 22.2 %copy-start.6 = (bf16[256,1536]{1,0:T(8,128)(2,1)}, bf16[256,1536]{1,0:T(8,128)(2,1)S(1)}, u32[]{:S(2)}) copy-start(bf16[256,1536]{1,0:T(8,128)(2,1)S(1)} %collective-permute-done.5.refs_2_.refs_1_) | copy-start | bytes 2359300
  149.7 27.3 %collective-permute-start.9 = (bf16[4,256,256]{2,1,0:T(8,128)(2,1)S(1)}, bf16[4,256,256]{2,1,0:T(8,128)(2,1)S(1)}, u32[]{:S(2)}, u32[]{:S(2)}) collective-permute-start(bf16[4,256,256]{2,1,0:T(8,128)(2,1)S(1)} %collective-permute-done.7.refs_4_), channel_id=1, source_target_pairs={{0,1},{1,0},{2,3},{3,2},{4,5},{5,4},{6,7},{7,6},{8,9},{9,8},{10,11... | collective-permute-start | bytes 1572872 | tf_op jit(solution)/shard_map/ppermute | solution.py:23
  149.7 27.4 %collective-permute-start.12 = (bf16[4,256,256]{2,1,0:T(8,128)(2,1)S(1)}, bf16[4,256,256]{2,1,0:T(8,128)(2,1)}, u32[]{:S(2)}, u32[]{:S(2)}) collective-permute-start(bf16[4,256,256]{2,1,0:T(8,128)(2,1)S(1)} %collective-permute-done.11.refs_8_), channel_id=1, source_target_pairs={{0,2},{1,3},{2,0},{3,1},{4,6},{5,7},{6,4},{7,5},{8,10},{9,11},{10,... | collective-permute-start | bytes 1572872 | tf_op jit(solution)/shard_map/ppermute | solution.py:23
  151.3 18.4 %collective-permute-start.24 = (bf16[1,2,4,64,256]{4,3,2,1,0:T(8,128)(2,1)S(1)}, bf16[1,2,4,64,256]{4,3,2,1,0:T(8,128)(2,1)S(1)}, u32[]{:S(2)}, u32[]{:S(2)}) collective-permute-start(bf16[1,2,4,64,256]{4,3,2,1,0:T(8,128)(2,1)S(1)} %get-tuple-element.50), channel_id=1, source_target_pairs={{0,2},{1,3},{2,0},{3,1},{4,6},{5,7},{6,4},{7,5},{8,10},{9,11},{10,... | collective-permute-start | bytes 786440 | tf_op jit(solution)/shard_map/ppermute | solution.py:23
  170.4 4.7 %copy-start.22 = (bf16[1,2,4,64,256]{4,3,2,1,0:T(8,128)(2,1)S(1)}, bf16[1,2,4,64,256]{4,3,2,1,0:T(8,128)(2,1)}, u32[]{:S(2)}) copy-start(bf16[1,2,4,64,256]{4,3,2,1,0:T(8,128)(2,1)} %copy-done.21) | copy-start | bytes 786436
  170.4 7.9 %collective-permute-start.27 = (bf16[1,2,4,64,256]{4,3,2,1,0:T(8,128)(2,1)S(1)}, bf16[1,2,4,64,256]{4,3,2,1,0:T(8,128)(2,1)}, u32[]{:S(2)}, u32[]{:S(2)}) collective-permute-start(bf16[1,2,4,64,256]{4,3,2,1,0:T(8,128)(2,1)S(1)} %get-tuple-element.48), channel_id=1, source_target_pairs={{0,2},{1,3},{2,0},{3,1},{4,6},{5,7},{6,4},{7,5},{8,10},{9,11},{10,... | collective-permute-start | bytes 786440 | tf_op jit(solution)/shard_map/ppermute | solution.py:23
  175.1 5.4 %copy-start.12 = (f32[2,2,32,4096]{3,2,1,0:T(8,128)S(1)}, f32[2,2,32,4096]{3,2,1,0:T(8,128)}, u32[]{:S(2)}) copy-start(f32[2,2,32,4096]{3,2,1,0:T(8,128)} %get-tuple-element.36) | copy-start | bytes 6291460
  177.0 5.8 %copy-start.9 = (bf16[4,256,256]{2,1,0:T(8,128)(2,1)}, bf16[4,256,256]{2,1,0:T(8,128)(2,1)S(1)}, u32[]{:S(2)}) copy-start(bf16[4,256,256]{2,1,0:T(8,128)(2,1)S(1)} %collective-permute-done.9.refs_6_) | copy-start | bytes 1572868
  177.0 5.8 %collective-permute-start.13 = (bf16[4,256,256]{2,1,0:T(8,128)(2,1)S(1)}, bf16[4,256,256]{2,1,0:T(8,128)(2,1)S(1)}, u32[]{:S(2)}, u32[]{:S(2)}) collective-permute-start(bf16[4,256,256]{2,1,0:T(8,128)(2,1)S(1)} %collective-permute-done.11.refs_8_), channel_id=1, source_target_pairs={{0,1},{1,0},{2,3},{3,2},{4,5},{5,4},{6,7},{7,6},{8,9},{9,8},{10,11... | collective-permute-start | bytes 1572872 | tf_op jit(solution)/shard_map/ppermute | solution.py:23
  177.1 23.2 %collective-permute-start.29 = (bf16[2,2,6,64,256]{4,3,2,1,0:T(8,128)(2,1)}, bf16[2,2,6,64,256]{4,3,2,1,0:T(8,128)(2,1)}, u32[]{:S(2)}, u32[]{:S(2)}) collective-permute-start(bf16[2,2,6,64,256]{4,3,2,1,0:T(8,128)(2,1)} %get-tuple-element.33), channel_id=1, source_target_pairs={{0,1},{1,0},{2,3},{3,2},{4,5},{5,4},{6,7},{7,6},{8,9},{9,8},{10,11... | collective-permute-start | bytes 2359304 | tf_op jit(solution)/shard_map/ppermute | solution.py:23
  178.3 7.0 %collective-permute-start.10 = (bf16[4,256,256]{2,1,0:T(8,128)(2,1)}, bf16[4,256,256]{2,1,0:T(8,128)(2,1)S(1)}, u32[]{:S(2)}, u32[]{:S(2)}) collective-permute-start(bf16[4,256,256]{2,1,0:T(8,128)(2,1)} %collective-permute-done.8.refs_5_), channel_id=1, source_target_pairs={{0,1},{1,0},{2,3},{3,2},{4,5},{5,4},{6,7},{7,6},{8,9},{9,8},{10,11... | collective-permute-start | bytes 1572872 | tf_op jit(solution)/shard_map/ppermute | solution.py:23
  178.3 7.0 %collective-permute-start.14 = (bf16[4,256,256]{2,1,0:T(8,128)(2,1)}, bf16[4,256,256]{2,1,0:T(8,128)(2,1)}, u32[]{:S(2)}, u32[]{:S(2)}) collective-permute-start(bf16[4,256,256]{2,1,0:T(8,128)(2,1)} %collective-permute-done.12.refs_9_), channel_id=1, source_target_pairs={{0,1},{1,0},{2,3},{3,2},{4,5},{5,4},{6,7},{7,6},{8,9},{9,8},{10,11... | collective-permute-start | bytes 1572872 | tf_op jit(solution)/shard_map/ppermute | solution.py:23
  182.8 3.6 %copy-start.10 = (bf16[4,256,256]{2,1,0:T(8,128)(2,1)}, bf16[4,256,256]{2,1,0:T(8,128)(2,1)S(1)}, u32[]{:S(2)}) copy-start(bf16[4,256,256]{2,1,0:T(8,128)(2,1)S(1)} %collective-permute-done.13.refs_10_) | copy-start | bytes 1572868
  182.8 67.2 %collective-permute-start.21 = (bf16[2,64,256]{2,1,0:T(8,128)(2,1)}, bf16[2,64,256]{2,1,0:T(8,128)(2,1)}, u32[]{:S(2)}, u32[]{:S(2)}) collective-permute-start(bf16[2,64,256]{2,1,0:T(8,128)(2,1)} %get-tuple-element.63), channel_id=1, source_target_pairs={{0,4},{4,0},{8,12},{12,8},{1,5},{5,1},{9,13},{13,9},{2,6},{6,2},{1... | collective-permute-start | bytes 196616 | tf_op jit(solution)/shard_map/ppermute | solution.py:23
  185.2 34.9 %collective-permute-start.25 = (bf16[4,64,256]{2,1,0:T(8,128)(2,1)}, bf16[4,64,256]{2,1,0:T(8,128)(2,1)S(1)}, u32[]{:S(2)}, u32[]{:S(2)}) collective-permute-start(bf16[4,64,256]{2,1,0:T(8,128)(2,1)} %get-tuple-element.59), channel_id=1, source_target_pairs={{0,4},{4,0},{8,12},{12,8},{1,5},{5,1},{9,13},{13,9},{2,6},{6,2},{1... | collective-permute-start | bytes 393224 | tf_op jit(solution)/shard_map/ppermute | solution.py:23
  185.3 22.9 %collective-permute-start.38 = (bf16[1,2,32,4096]{3,2,1,0:T(8,128)(2,1)}, bf16[1,2,32,4096]{3,2,1,0:T(8,128)(2,1)S(1)}, u32[]{:S(2)}, u32[]{:S(2)}) collective-permute-start(bf16[1,2,32,4096]{3,2,1,0:T(8,128)(2,1)} %get-tuple-element.40), channel_id=1, source_target_pairs={{0,2},{1,3},{2,0},{3,1},{4,6},{5,7},{6,4},{7,5},{8,10},{9,11},{10,... | collective-permute-start | bytes 1572872 | tf_op jit(solution)/shard_map/ppermute | solution.py:23
  193.2 8.6 %copy-start.14 = (f32[2,2,6,64,256]{4,3,2,1,0:T(8,128)S(1)}, f32[2,2,6,64,256]{4,3,2,1,0:T(8,128)}, u32[]{:S(2)}) copy-start(f32[2,2,6,64,256]{4,3,2,1,0:T(8,128)} %get-tuple-element.32) | copy-start | bytes 4718596
  200.3 19.9 %collective-permute-start.28 = (bf16[4,64,256]{2,1,0:T(8,128)(2,1)}, bf16[4,64,256]{2,1,0:T(8,128)(2,1)S(1)}, u32[]{:S(2)}, u32[]{:S(2)}) collective-permute-start(bf16[4,64,256]{2,1,0:T(8,128)(2,1)} %get-tuple-element.57), channel_id=1, source_target_pairs={{0,4},{4,0},{8,12},{12,8},{1,5},{5,1},{9,13},{13,9},{2,6},{6,2},{1... | collective-permute-start | bytes 393224 | tf_op jit(solution)/shard_map/ppermute | solution.py:23
  203.1 12.1 %collective-permute-start.30 = (bf16[1,2,6,64,256]{4,3,2,1,0:T(8,128)(2,1)S(1)}, bf16[1,2,6,64,256]{4,3,2,1,0:T(8,128)(2,1)S(1)}, u32[]{:S(2)}, u32[]{:S(2)}) collective-permute-start(bf16[1,2,6,64,256]{4,3,2,1,0:T(8,128)(2,1)S(1)} %get-tuple-element.42), channel_id=1, source_target_pairs={{0,2},{1,3},{2,0},{3,1},{4,6},{5,7},{6,4},{7,5},{8,10},{9,11},{10,... | collective-permute-start | bytes 1179656 | tf_op jit(solution)/shard_map/ppermute | solution.py:23
  208.2 27.3 %collective-permute-start.36 = (bf16[1,2,16,64,256]{4,3,2,1,0:T(8,128)(2,1)S(1)}, bf16[1,2,16,64,256]{4,3,2,1,0:T(8,128)(2,1)S(1)}, u32[]{:S(2)}, u32[]{:S(2)}) collective-permute-start(bf16[1,2,16,64,256]{4,3,2,1,0:T(8,128)(2,1)S(1)} %get-tuple-element.38), channel_id=1, source_target_pairs={{0,2},{1,3},{2,0},{3,1},{4,6},{5,7},{6,4},{7,5},{8,10},{9,11},{10,... | collective-permute-start | bytes 3145736 | tf_op jit(solution)/shard_map/ppermute | solution.py:23
  215.1 13.1 %collective-permute-start.32 = (bf16[4,64,256]{2,1,0:T(8,128)(2,1)S(1)}, bf16[4,64,256]{2,1,0:T(8,128)(2,1)S(1)}, u32[]{:S(2)}, u32[]{:S(2)}) collective-permute-start(bf16[4,64,256]{2,1,0:T(8,128)(2,1)S(1)} %get-tuple-element.58), channel_id=1, source_target_pairs={{0,8},{4,12},{8,0},{12,4},{1,9},{5,13},{9,1},{13,5},{2,10},{6,14},... | collective-permute-start | bytes 393224 | tf_op jit(solution)/shard_map/ppermute | solution.py:23
  220.1 23.6 %copy-start.25 = (bf16[4,64,256]{2,1,0:T(8,128)(2,1)}, bf16[4,64,256]{2,1,0:T(8,128)(2,1)S(1)}, u32[]{:S(2)}) copy-start(bf16[4,64,256]{2,1,0:T(8,128)(2,1)S(1)} %collective-permute-done.25.refs_0_) | copy-start | bytes 393220
  220.1 29.9 %collective-permute-start.22 = (bf16[2,64,256]{2,1,0:T(8,128)(2,1)S(1)}, bf16[2,64,256]{2,1,0:T(8,128)(2,1)S(1)}, u32[]{:S(2)}, u32[]{:S(2)}) collective-permute-start(bf16[2,64,256]{2,1,0:T(8,128)(2,1)S(1)} %copy-done.31), channel_id=1, source_target_pairs={{0,8},{4,12},{8,0},{12,4},{1,9},{5,13},{9,1},{13,5},{2,10},{6,14},... | collective-permute-start | bytes 196616 | tf_op jit(solution)/shard_map/ppermute | solution.py:23
  220.2 23.5 %copy-start.26 = (bf16[4,64,256]{2,1,0:T(8,128)(2,1)}, bf16[4,64,256]{2,1,0:T(8,128)(2,1)S(1)}, u32[]{:S(2)}) copy-start(bf16[4,64,256]{2,1,0:T(8,128)(2,1)S(1)} %collective-permute-done.28.refs_1_) | copy-start | bytes 393220
  220.2 23.5 %collective-permute-start.33 = (bf16[4,64,256]{2,1,0:T(8,128)(2,1)S(1)}, bf16[4,64,256]{2,1,0:T(8,128)(2,1)S(1)}, u32[]{:S(2)}, u32[]{:S(2)}) collective-permute-start(bf16[4,64,256]{2,1,0:T(8,128)(2,1)S(1)} %copy-done.29), channel_id=1, source_target_pairs={{0,8},{4,12},{8,0},{12,4},{1,9},{5,13},{9,1},{13,5},{2,10},{6,14},... | collective-permute-start | bytes 393224 | tf_op jit(solution)/shard_map/ppermute | solution.py:23
  228.2 15.5 %copy-start.27 = (bf16[4,64,256]{2,1,0:T(8,128)(2,1)}, bf16[4,64,256]{2,1,0:T(8,128)(2,1)S(1)}, u32[]{:S(2)}) copy-start(bf16[4,64,256]{2,1,0:T(8,128)(2,1)S(1)} %collective-permute-done.32.refs_3_) | copy-start | bytes 393220
  228.2 15.5 %collective-permute-start.31 = (bf16[6,64,256]{2,1,0:T(8,128)(2,1)S(1)}, bf16[6,64,256]{2,1,0:T(8,128)(2,1)S(1)}, u32[]{:S(2)}, u32[]{:S(2)}) collective-permute-start(bf16[6,64,256]{2,1,0:T(8,128)(2,1)S(1)} %get-tuple-element.53), channel_id=1, source_target_pairs={{0,4},{4,0},{8,12},{12,8},{1,5},{5,1},{9,13},{13,9},{2,6},{6,2},{1... | collective-permute-start | bytes 589832 | tf_op jit(solution)/shard_map/ppermute | solution.py:23
  235.5 10.6 %collective-permute-start.34 = (bf16[6,64,256]{2,1,0:T(8,128)(2,1)S(1)}, bf16[6,64,256]{2,1,0:T(8,128)(2,1)S(1)}, u32[]{:S(2)}, u32[]{:S(2)}) collective-permute-start(bf16[6,64,256]{2,1,0:T(8,128)(2,1)S(1)} %get-tuple-element.52), channel_id=1, source_target_pairs={{0,8},{4,12},{8,0},{12,4},{1,9},{5,13},{9,1},{13,5},{2,10},{6,14},... | collective-permute-start | bytes 589832 | tf_op jit(solution)/shard_map/ppermute | solution.py:23
  250.6 2.4 copy-start.1
  (9 other events, 12.4 us)

commit v4 on v3

--- a/solution.py
+++ b/solution.py
@@ -10,7 +10,8 @@
 
 WIDTH = 16384
 BLOCK = 256
-CHUNK_SIZES = (4, 4, 6, 2)
+VMEM_LIMIT = 67_043_328
+CHUNK_SIZES = (6, 6, 4)
 EARLY_CHUNKS = 2
 
 
@@ -102,6 +103,7 @@
             pltpu.SemaphoreType.DMA((count // step, 2)),
         ],
         out_shape=(jax.ShapeDtypeStruct(shape, BF16), jax.ShapeDtypeStruct(shape, F32)),
+        compiler_params=pltpu.CompilerParams(vmem_limit_bytes=VMEM_LIMIT),
         cost_estimate=pl.CostEstimate(
             flops=4 * count * rows_here * BLOCK * BLOCK,
             bytes_accessed=count * BLOCK * (2 * rows_here * 3 + 6 * BLOCK),
@@ -143,6 +145,7 @@
             scratch_shapes=[pltpu.VMEM((rank, step), F32)],
         ),
         out_shape=(jax.ShapeDtypeStruct(shape, BF16), jax.ShapeDtypeStruct(shape, F32)),
+        compiler_params=pltpu.CompilerParams(vmem_limit_bytes=VMEM_LIMIT),
         cost_estimate=pl.CostEstimate(
             flops=4 * rank * rows_here * width,
             bytes_accessed=width * (4 * rows_here + 6 * rank),
@@ -198,6 +201,7 @@
         out_specs=(pl.BlockSpec(memory_space=pltpu.VMEM),) * 2,
         out_shape=(jax.ShapeDtypeStruct((units, unit, BLOCK), BF16),) * 2,
         scratch_shapes=[pltpu.SemaphoreType.DMA((2 * units,))],
+        compiler_params=pltpu.CompilerParams(vmem_limit_bytes=VMEM_LIMIT),
         cost_estimate=pl.CostEstimate(
             flops=0, bytes_accessed=8 * units * unit * BLOCK, transcendentals=0
         ),
@@ -209,7 +213,7 @@
     steps = last - first
     far_refs, refs = refs[: 2 * steps], refs[2 * steps :]
     parts = len(order)
-    far_w, refs = refs[: 2 * parts], refs[2 * parts :]
+    far_w, refs = refs[:parts], refs[parts:]
     out_ref, f_buf, low_buf, far_buf, w_buf, out_buf, in_sems, w_sems, far_w_sems, out_sems = refs[-10:]
     dims = (((1,), (1,)), ((), ()))
     pieces = BLOCK // unit
@@ -225,7 +229,7 @@
                 block, piece = lax.div(number, pieces), lax.rem(number, pieces)
                 rows = pl.ds(pl.multiple_of(piece * unit, unit), unit)
                 copy = pltpu.make_async_copy(
-                    far_w[way * parts + slot].at[one],
+                    far_w[slot].at[way, one],
                     w_buf.at[2 + way, block, rows, :],
                     far_w_sems.at[way, number],
                 )
@@ -267,7 +271,7 @@
                 rows = pl.ds(piece * unit, unit)
                 loads[[starts[one] <= at < starts[one] + sizes[one] for one in range(first, last)].index(True)].append(
                     pltpu.make_async_copy(
-                        far_w[way * parts].at[0],
+                        far_w[0].at[way, 0],
                         w_buf.at[2 + way, at, rows, :],
                         far_w_sems.at[way, at * pieces + piece],
                     )
@@ -301,10 +305,10 @@
 ):
     rows_here, width = features.shape
     share = width // BLOCK
-    unit = far_weights[0][0].shape[1]
+    unit = far_weights[0].shape[2]
     hbm = pl.BlockSpec(memory_space=pltpu.HBM)
     smem = pl.BlockSpec(memory_space=pltpu.SMEM)
-    far_inputs = [*far[0][first:last], *far[1][first:last], *far_weights[0], *far_weights[1]]
+    far_inputs = [*far[0][first:last], *far[1][first:last], *far_weights]
     inputs = [pos, item, features, block_weights, codes, lowrank_out, *far_inputs]
     if held is not None:
         inputs.append(held)
@@ -327,6 +331,7 @@
             pltpu.SemaphoreType.DMA((2, len(order) * units)),
             pltpu.SemaphoreType.DMA((last - first,)),
         ],
+        compiler_params=pltpu.CompilerParams(vmem_limit_bytes=VMEM_LIMIT),
         cost_estimate=pl.CostEstimate(
             flops=9 * columns * rows_here * BLOCK * BLOCK,
             bytes_accessed=columns * BLOCK * 2 * (4 * rows_here + 4 * BLOCK),
@@ -382,6 +387,7 @@
             pltpu.SemaphoreType.DMA((len(pieces),)),
             pltpu.SemaphoreType.DMA((total,)),
         ],
+        compiler_params=pltpu.CompilerParams(vmem_limit_bytes=VMEM_LIMIT),
         cost_estimate=pl.CostEstimate(
             flops=0, bytes_accessed=8 * total * part * BLOCK, transcendentals=0
         ),
@@ -399,6 +405,10 @@
     items = lax.axis_size("items")
     item = lax.axis_index("items").astype(jnp.int32)
     item_arg = item.reshape(1)
+    groups = lax.axis_size("groups")
+    sharer = (lax.axis_index("groups").astype(jnp.int32) * items + item).reshape(1)
+    sharers = groups * items
+    part = BLOCK // items
     bits = items.bit_length() - 1
     place = lax.axis_index("wloop")
     way_bits = lax.axis_size("wloop").bit_length() - 1
@@ -428,17 +438,18 @@
         for way in range(2):
             far[way].append(hop(piece, far_bits[way]))
 
-    unit = min(BLOCK, share * BLOCK // items)
-    units = share * BLOCK // items // unit
-    shares = weight_share(block_weights, pos, item_arg, share, unit, units)
-    far_weights, order = [], []
-    for way in range(2):
-        held, order = [hop(shares[way], far_bits[way])], [0]
-        for level in range(bits - 1, -1, -1):
-            for one in range(len(held)):
-                held.append(swapped(held[one], "items", level))
-                order.append(order[one] ^ (1 << level))
-        far_weights.append(held)
+    unit = min(BLOCK, share * BLOCK // sharers)
+    units = share * BLOCK // sharers // unit
+    shares = weight_share(block_weights, pos, sharer, share, unit, units)
+    held = [hop(shares[way], far_bits[way]) for way in range(2)]
+    far_weights, order = [jnp.stack(held)], [0]
+    hops = [("items", level, 1 << level) for level in range(bits - 1, 0, -1)]
+    hops += [("groups", level, items << level) for level in range(groups.bit_length() - 1)]
+    hops += [("items", 0, 1)]
+    for axis, level, apart in hops:
+        for one in range(len(order)):
+            far_weights.append(swapped(far_weights[one], axis, level))
+            order.append(order[one] ^ apart)
 
     dims = (((1,), (1,)), ((), ()))
     codes = jnp.stack(
@@ -466,9 +477,10 @@
     bit = item_arg & 1
     own = pair_grads(bit, cotangent, [features], ((0, 0), (0, 1)), 0, share, items)
     own = items_sum(*own, item)
+    shape = (2 * share, part, BLOCK)
     block_grads = place_kernel(
-        [part for way in range(2) for part in (own[0][way], own[1][way])],
-        [list(range(way * share, (way + 1) * share)) for way in range(2)],
+        [own[0].reshape(shape), own[1].reshape(shape)],
+        [list(range(2 * share))],
         pos,
         None,
         stored,
@@ -505,7 +517,7 @@
             far,
             far_weights,
             pos,
-            item_arg,
+            sharer,
             sizes,
             first,
             last,

time: 254 us -> 252 us (level)
  other arithmetic: 17.7 us -> 27.4 us
  starting transfers between devices: 43.6 us -> 34.5 us
  local copies, waits for them, and re-layouts: 9.17 us -> 4.99 us
  waiting for transfers between devices: 131 us -> 135 us
    ppermute x39 -> x34, starting transfers between devices: 43.6 us -> 34.5 us  [swapped(): lax.ppermute(block, axis, [(one, one ^ 1 << apart) for one in range(count)])]
    ppermute x39 -> x34, waiting for transfers between devices: 131 us -> 135 us  [swapped(): lax.ppermute(block, axis, [(one, one ^ 1 << apart) for one in range(count)])]
    convert_element_type x6 -> x5, other arithmetic: 10.7 us -> 13.3 us  [items_sum(): came = swapped(leave.astype(BF16), 'items', level)]
    squeeze x2 -> x0, local copies, waits for them, and re-layouts: 2.56 us -> none  [the longest x1 1.54 us: layer(): own[0][way]]
    pallas_call x5 -> x4, Pallas kernels: 16.4 us -> 14.4 us  [pair_grads(): pl.pallas_call(functools.partial(grad_body, pairs, part, first, step), in...]
    convert_element_type x4 -> x3, other arithmetic: 4.36 us -> 6.16 us  [layer(): done = (keep[way] + came[way].astype(F32)).astype(BF16)]
  transfers between devices with their start and end apart: 39 -> 34, of which waited for: 13 -> 11; matrix products, arithmetic and copies ran while one was open for 9% -> 12% of each run, Pallas kernels for 18% -> 17%
where the time goes in v4:
time: 252 us; the launch traced here: 251 us
  waiting for transfers between devices  135 us (54%)
  Pallas kernels  45.5 us (18%)
  starting transfers between devices  34.5 us (14%)
  other arithmetic  27.4 us (11%)
  local copies, waits for them, and re-layouts  4.99 us (2%)
  matrix products  3.41 us (1%)
    ppermute x34, waiting for transfers between devices, swapped(): lax.ppermute(block, axis, [(one, one ^ 1 << apart) for one in range(count)])  135 us
    ppermute x34, starting transfers between devices, swapped(): lax.ppermute(block, axis, [(one, one ^ 1 << apart) for one in range(count)])  34.5 us
    pallas_call x4, Pallas kernels, pair_grads(): pl.pallas_call(functools.partial(grad_body, pairs, part, first, step), in...  14.4 us
    pallas_call x2, Pallas kernels, mixed_kernel(): pl.pallas_call(functools.partial(mixed_body, share, sizes, first, last, u...  13.8 us
    convert_element_type x5, other arithmetic, items_sum(): came = swapped(leave.astype(BF16), 'items', level)  13.3 us
    pallas_call x3, Pallas kernels, place_kernel(): pl.pallas_call(functools.partial(place_body, keys, pairs), in_specs=[pl.B...  9.77 us
    convert_element_type x3, other arithmetic, layer(): done = (keep[way] + came[way].astype(F32)).astype(BF16)  6.16 us
  transfers between devices with their start and end apart: 34, of which 11 were waited for; matrix products, arithmetic and copies ran while one was open for 12% of the time, Pallas kernels for 17%

profile of v4, /device:TPU:0, one launch (start us, length us, event | category | flops | bytes accessed | tf_op | source)
XLA Modules:
  0.0 251.4 jit_solution(815168396365578343)
XLA Ops:
  0.7 2.7 %fusion.24 = f32[256,128]{1,0:T(8,128)S(1)} fusion(bf16[256,4096]{1,0:T(8,128)(2,1)} %f_ref.5, bf16[128,4096]{1,0:T(8,128)(2,1)} %param.12), kind=kOutput, calls=%fused_computation.59 | convolution fusion | flops 268435456 | bytes 3276800 | tf_op jit(solution)/shard_map/dot_general | solution.py:457
  3.4 0.7 fusion.25
  4.2 0.7 fusion.15
  4.9 3.0 %collective-permute-start = (f32[2,128,128]{2,1,0:T(8,128)}, f32[2,128,128]{2,1,0:T(8,128)}, u32[]{:S(2)}, u32[]{:S(2)}) collective-permute-start(f32[2,128,128]{2,1,0:T(8,128)} %fusion.15), channel_id=1, source_target_pairs={{0,4},{4,0},{8,12},{12,8},{1,5},{5,1},{9,13},{13,9},{2,6},{6,2},{1... | collective-permute-start | bytes 393224 | tf_op jit(solution)/shard_map/ppermute | solution.py:24
  7.9 1.0 slice.80
  8.9 0.9 slice.81
  9.8 0.8 slice.82
  10.9 0.6 select_reduce_fusion.pos_ref
  11.5 2.6 %weight_share.1 = (bf16[2,256,256]{2,1,0:T(8,128)(2,1)}, bf16[2,256,256]{2,1,0:T(8,128)(2,1)}) custom-call(s32[64]{0:T(128)} %select_reduce_fusion.pos_ref, s32[1]{0:T(128)} %bitcast.item_ref, bf16[64,256,256]{2,1,0:T(8,128)(2,1)} %w_ref.5), custom_call_target="tpu_custom_call" | custom-call | bytes 1048576 | tf_op jit(solution)/shard_map/weight_share/pallas_call | solution.py:194
  14.1 2.9 %collective-permute-start.6 = (bf16[2,256,256]{2,1,0:T(8,128)(2,1)}, bf16[2,256,256]{2,1,0:T(8,128)(2,1)}, u32[]{:S(2)}, u32[]{:S(2)}) collective-permute-start(bf16[2,256,256]{2,1,0:T(8,128)(2,1)} %get-tuple-element.21), channel_id=1, source_target_pairs={{0,8},{4,12},{8,0},{12,4},{1,9},{5,13},{9,1},{13,5},{2,10},{6,14},... | collective-permute-start | bytes 786440 | tf_op jit(solution)/shard_map/ppermute | solution.py:24
  17.0 5.0 %pair_grads.7 = (bf16[2,2,16,64,256]{4,3,2,1,0:T(8,128)(2,1)}, f32[2,2,16,64,256]{4,3,2,1,0:T(8,128)}) custom-call(s32[1]{0:T(128)} %bitcast.10.bit_ref, bf16[256,4096]{1,0:T(8,128)(2,1)} %g_ref.9, bf16[256,4096]{1,0:T(8,128)(2,1)} %f_ref.5), custom_call_target="tpu_custom_call" | custom-call | flops 1073741824 | bytes 12582912 | tf_op jit(solution)/shard_map/pair_grads/pallas_call | solution.py:94
  22.2 1.0 fusion.18
  23.3 1.8 collective-permute-start.5
  25.1 12.3 %collective-permute-done.1 = f32[2,128,128]{2,1,0:T(8,128)S(1)} collective-permute-done((f32[2,128,128]{2,1,0:T(8,128)S(1)}, f32[2,128,128]{2,1,0:T(8,128)S(1)}, u32[]{:S(2)}, u32[]{:S(2)}) %collective-permute-start.1) | collective-permute-done | bytes 131104 | tf_op jit(solution)/shard_map/ppermute | solution.py:24
  37.4 1.2 collective-permute-start.16
  38.6 3.7 %collective-permute-start.4 = (bf16[256,1024]{1,0:T(8,128)(2,1)}, bf16[256,1024]{1,0:T(8,128)(2,1)}, u32[]{:S(2)}, u32[]{:S(2)}) collective-permute-start(bf16[256,1024]{1,0:T(8,128)(2,1)} %slice.82), channel_id=1, source_target_pairs={{0,8},{4,12},{8,0},{12,4},{1,9},{5,13},{9,1},{13,5},{2,10},{6,14},... | collective-permute-start | bytes 1572872 | tf_op jit(solution)/shard_map/ppermute | solution.py:24
  42.3 0.6 add_convert_fusion.5
  43.0 54.3 %collective-permute-done.4.refs_1_ = bf16[256,1024]{1,0:T(8,128)(2,1)} collective-permute-done((bf16[256,1024]{1,0:T(8,128)(2,1)}, bf16[256,1024]{1,0:T(8,128)(2,1)}, u32[]{:S(2)}, u32[]{:S(2)}) %collective-permute-start.4) | collective-permute-done | bytes 524320 | tf_op jit(solution)/shard_map/ppermute | solution.py:24
  97.3 2.8 %pair_grads.4 = (bf16[2,2,4,64,256]{4,3,2,1,0:T(8,128)(2,1)}, f32[2,2,4,64,256]{4,3,2,1,0:T(8,128)}) custom-call(s32[1]{0:T(128)} %bitcast.10.bit_ref, bf16[256,4096]{1,0:T(8,128)(2,1)} %g_ref.9, bf16[256,1024]{1,0:T(8,128)(2,1)} %collective-permute-done.3.refs_0_, bf16[256,1024]{1,0:T(8,128)(2,1)} %collective-permute-done.4.refs_1_), custom_call_target="tpu_custom_call" | custom-call | flops 268435456 | bytes 3145728 | tf_op jit(solution)/shard_map/pair_grads/pallas_call | solution.py:94
  100.1 2.1 collective-permute-start.2
  102.2 1.9 pad_maximum_fusion.refs_4_.refs_2_
  104.1 3.2 %pair_grads.5 = (bf16[2,2,6,64,256]{4,3,2,1,0:T(8,128)(2,1)}, f32[2,2,6,64,256]{4,3,2,1,0:T(8,128)}) custom-call(s32[1]{0:T(128)} %bitcast.10.bit_ref, bf16[256,4096]{1,0:T(8,128)(2,1)} %g_ref.9, bf16[256,1536]{1,0:T(8,128)(2,1)} %collective-permute-done.14.refs_0_, bf16[256,1536]{1,0:T(8,128)(2,1)} %collective-permute-done.16.refs_2_.refs_1_), custom_call_target="tpu_custom_call" | custom-call | flops 402653184 | bytes 4718592 | tf_op jit(solution)/shard_map/pair_grads/pallas_call | solution.py:94
  107.4 10.6 %collective-permute-done.2 = bf16[2,128,128]{2,1,0:T(8,128)(2,1)} collective-permute-done((bf16[2,128,128]{2,1,0:T(8,128)(2,1)}, bf16[2,128,128]{2,1,0:T(8,128)(2,1)}, u32[]{:S(2)}, u32[]{:S(2)}) %collective-permute-start.2) | collective-permute-done | bytes 65568 | tf_op jit(solution)/shard_map/ppermute | solution.py:24
  118.0 1.0 maximum_select_fusion
  119.0 1.6 collective-permute-start.7
  120.5 0.7 slice_bitcast_fusion
  121.2 5.0 %low_grads.1 = (bf16[2,2,32,4096]{3,2,1,0:T(8,128)(2,1)}, f32[2,2,32,4096]{3,2,1,0:T(8,128)}) custom-call(s32[1]{0:T(128)} %bitcast.10.bit_ref, bf16[256,128]{1,0:T(8,128)(2,1)} %get-tuple-element.50.b_ref, bf16[256,4096]{1,0:T(8,128)(2,1)} %f_ref.5, bf16[256,128]{1,0:T(8,128)(2,1)} %get-tuple-element.51.codes_ref.c_ref, bf16[256,4096]{1,0:T(8,128)(2,1)} %g_ref.9), custom_call_target="tpu_custom_call" | custom-call | flops 536870912 | bytes 7340032 | tf_op jit(solution)/shard_map/low_grads/pallas_call | solution.py:138
  126.5 2.4 add_convert_fusion.4
  128.9 4.9 %collective-permute-done.17.refs_3_.refs_1_ = bf16[256,1536]{1,0:T(8,128)(2,1)} collective-permute-done((bf16[256,1536]{1,0:T(8,128)(2,1)}, bf16[256,1536]{1,0:T(8,128)(2,1)}, u32[]{:S(2)}, u32[]{:S(2)}) %collective-permute-start.17) | collective-permute-done | bytes 786464 | tf_op jit(solution)/shard_map/ppermute | solution.py:24
  133.7 1.5 collective-permute-start.19
  135.2 3.2 %pair_grads.6 = (bf16[2,2,6,64,256]{4,3,2,1,0:T(8,128)(2,1)}, f32[2,2,6,64,256]{4,3,2,1,0:T(8,128)}) custom-call(s32[1]{0:T(128)} %bitcast.10.bit_ref, bf16[256,4096]{1,0:T(8,128)(2,1)} %g_ref.9, bf16[256,1536]{1,0:T(8,128)(2,1)} %collective-permute-done.15.refs_1_.refs_0_, bf16[256,1536]{1,0:T(8,128)(2,1)} %collective-permute-done.17.refs_3_.refs_1_), custom_call_target="tpu_custom_call" | custom-call | flops 402653184 | bytes 4718592 | tf_op jit(solution)/shard_map/pair_grads/pallas_call | solution.py:94
  138.6 2.3 collective-permute-done.19
  140.8 1.5 collective-permute-start.8
  142.4 0.6 collective-permute-start.9
  142.9 2.0 fusion.13
  145.0 2.9 %add_convert_fusion.3 = (bf16[1,2,6,64,256]{4,3,2,1,0:T(8,128)(2,1)}, f32[1,2,6,64,256]{4,3,2,1,0:T(8,128)}) fusion(f32[2,2,6,64,256]{4,3,2,1,0:T(8,128)} %get-tuple-element.24, s32[]{:T(128)S(6)} %select_n.65, bf16[2,2,6,64,256]{4,3,2,1,0:T(8,128)(2,1)} %collective-permute-done.22, s32[]{:T(128)S(6)} %select_n.64), kind=kLoop, calls=%fused_computation.6 | loop fusion | flops 983040 | bytes 3538952 | tf_op jit(solution)/shard_map/convert_element_type | solution.py:167
  147.9 4.1 %add_convert_fusion = (bf16[1,2,16,64,256]{4,3,2,1,0:T(8,128)(2,1)}, f32[1,2,16,64,256]{4,3,2,1,0:T(8,128)}) fusion(f32[2,2,16,64,256]{4,3,2,1,0:T(8,128)S(1)} %copy-done.3, s32[]{:T(128)S(6)} %select_n.65, bf16[2,2,16,64,256]{4,3,2,1,0:T(8,128)(2,1)} %collective-permute-done.30, s32[]{:T(128)S(6)} %select_n.64), kind=kLoop, calls=%fused_computation | loop fusion | flops 2621440 | bytes 9437192 | tf_op jit(solution)/shard_map/convert_element_type | solution.py:167
  152.0 3.8 %collective-permute-done.8.refs_6_.refs_4_ = bf16[2,2,256,256]{3,2,1,0:T(8,128)(2,1)S(1)} collective-permute-done((bf16[2,2,256,256]{3,2,1,0:T(8,128)(2,1)}, bf16[2,2,256,256]{3,2,1,0:T(8,128)(2,1)S(1)}, u32[]{:S(2)}, u32[]{:S(2)}) %collective-permute-start.8) | collective-permute-done | bytes 524320 | tf_op jit(solution)/shard_map/ppermute | solution.py:24
  155.9 0.5 collective-permute-start.12
  156.4 8.0 %collective-permute-done.9.refs_7_.refs_5_ = bf16[2,2,256,256]{3,2,1,0:T(8,128)(2,1)S(1)} collective-permute-done((bf16[2,2,256,256]{3,2,1,0:T(8,128)(2,1)}, bf16[2,2,256,256]{3,2,1,0:T(8,128)(2,1)S(1)}, u32[]{:S(2)}, u32[]{:S(2)}) %collective-permute-start.9) | collective-permute-done | bytes 524320 | tf_op jit(solution)/shard_map/ppermute | solution.py:24
  164.3 1.1 collective-permute-start.23
  165.4 1.0 collective-permute-start.31
  166.4 2.6 %add_convert_fusion.1 = (bf16[1,2,32,4096]{3,2,1,0:T(8,128)(2,1)}, f32[1,2,32,4096]{3,2,1,0:T(8,128)}) fusion(f32[2,2,32,4096]{3,2,1,0:T(8,128)S(1)} %copy-done.5, s32[]{:T(128)S(6)} %select_n.65, bf16[2,2,32,4096]{3,2,1,0:T(8,128)(2,1)} %collective-permute-done.32, s32[]{:T(128)S(6)} %select_n.64), kind=kLoop, calls=%fused_computation.2 | loop fusion | flops 1310720 | bytes 4718600 | tf_op jit(solution)/shard_map/convert_element_type | solution.py:167
  169.1 1.3 add_convert_fusion.2
  170.4 2.4 collective-permute-start.20
  172.8 1.5 collective-permute-start.33
  174.3 0.8 copy-done.11
  175.1 0.5 collective-permute-start.26
  175.7 8.4 %mixed.2.refs_10_ = bf16[256,4096]{1,0:T(8,128)(2,1)} custom-call(s32[64]{0:T(128)} %select_reduce_fusion.pos_ref, s32[1]{0:T(128)} %bitcast.item_ref, bf16[256,4096]{1,0:T(8,128)(2,1)} %f_ref.5, bf16[64,256,256]{2,1,0:T(8,128)(2,1)} %w_ref.5, bf16[256,128]{1,0:T(8,128)(2,1)} %get-tuple-element.51.codes_ref.c_ref, bf16[128,4096]{1,0:T(8,128)(2,1)} %low_ref.3, ...), custom_call_target="tpu_custom_call" | custom-call | flops 1811939328 | bytes 12582912 | tf_op jit(solution)/shard_map/mixed/pallas_call | solution.py:316
  184.1 5.4 %mixed.3 = bf16[256,4096]{1,0:T(8,128)(2,1)} custom-call(s32[64]{0:T(128)} %select_reduce_fusion.pos_ref, s32[1]{0:T(128)} %bitcast.item_ref, bf16[256,4096]{1,0:T(8,128)(2,1)} %f_ref.5, bf16[64,256,256]{2,1,0:T(8,128)(2,1)} %w_ref.5, bf16[256,128]{1,0:T(8,128)(2,1)} %get-tuple-element.51.codes_ref.c_ref, ...), custom_call_target="tpu_custom_call", output_to_operand_aliasing={{}: (16, {})} | custom-call | flops 603979776 | bytes 4194304 | tf_op jit(solution)/shard_map/mixed/pallas_call | solution.py:316
  189.5 1.1 collective-permute-start.21
  190.5 2.0 fusion.10
  192.6 25.7 %collective-permute-done.26 = bf16[1,2,6,64,256]{4,3,2,1,0:T(8,128)(2,1)} collective-permute-done((bf16[1,2,6,64,256]{4,3,2,1,0:T(8,128)(2,1)}, bf16[1,2,6,64,256]{4,3,2,1,0:T(8,128)(2,1)}, u32[]{:S(2)}, u32[]{:S(2)}) %collective-permute-start.26) | collective-permute-done | bytes 393248 | tf_op jit(solution)/shard_map/ppermute | solution.py:24
  218.3 2.4 collective-permute-start.24
  220.7 2.1 fusion.11
  222.8 3.2 %collective-permute-done.24.refs_0_ = bf16[6,64,256]{2,1,0:T(8,128)(2,1)S(1)} collective-permute-done((bf16[6,64,256]{2,1,0:T(8,128)(2,1)S(1)}, bf16[6,64,256]{2,1,0:T(8,128)(2,1)S(1)}, u32[]{:S(2)}, u32[]{:S(2)}) %collective-permute-start.24) | collective-permute-done | bytes 196640 | tf_op jit(solution)/shard_map/ppermute | solution.py:24
  226.0 0.7 copy-done.15
  226.7 3.2 %collective-permute-start.28 = (bf16[6,64,256]{2,1,0:T(8,128)(2,1)}, bf16[6,64,256]{2,1,0:T(8,128)(2,1)}, u32[]{:S(2)}, u32[]{:S(2)}) collective-permute-start(bf16[6,64,256]{2,1,0:T(8,128)(2,1)} %get-tuple-element.46), channel_id=1, source_target_pairs={{0,8},{4,12},{8,0},{12,4},{1,9},{5,13},{9,1},{13,5},{2,10},{6,14},... | collective-permute-start | bytes 589832 | tf_op jit(solution)/shard_map/ppermute | solution.py:24
  229.9 2.1 fusion
  232.0 4.3 %place.3.refs_4_ = f32[64,64,256]{2,1,0:T(8,128)} custom-call(s32[64]{0:T(128)} %select_reduce_fusion.pos_ref, f32[32,64,256]{2,1,0:T(8,128)} %bitcast.42, bf16[32,64,256]{2,1,0:T(8,128)(2,1)} %bitcast.18.refs_1_), custom_call_target="tpu_custom_call" | custom-call | bytes 4194304 | tf_op jit(solution)/shard_map/place/pallas_call | solution.py:378
  236.3 7.3 %collective-permute-done.28.refs_2_ = bf16[6,64,256]{2,1,0:T(8,128)(2,1)} collective-permute-done((bf16[6,64,256]{2,1,0:T(8,128)(2,1)}, bf16[6,64,256]{2,1,0:T(8,128)(2,1)}, u32[]{:S(2)}, u32[]{:S(2)}) %collective-permute-start.28) | collective-permute-done | bytes 196640 | tf_op jit(solution)/shard_map/ppermute | solution.py:24
  243.6 2.1 collective-permute-done.29.refs_3_
  245.7 3.0 %place.4.refs_2_ = f32[64,64,256]{2,1,0:T(8,128)} custom-call(s32[64]{0:T(128)} %select_reduce_fusion.pos_ref, bf16[6,64,256]{2,1,0:T(8,128)(2,1)} %copy-done.15, bf16[6,64,256]{2,1,0:T(8,128)(2,1)} %collective-permute-done.27.refs_1_, bf16[6,64,256]{2,1,0:T(8,128)(2,1)} %collective-permute-done.28.refs_2_, ...), custom_call_target="tpu_custom_call", output_to_operand_aliasing={{}: (5, {})} | custom-call | bytes 3145728 | tf_op jit(solution)/shard_map/place/pallas_call | solution.py:378
  248.8 2.5 place.5
  (73 shorter events, 1.0 us)
Async XLA Ops:
  0.6 2.7 %copy-start = (bf16[256,4096]{1,0:T(8,128)(2,1)S(1)}, bf16[256,4096]{1,0:T(8,128)(2,1)}, u32[]{:S(2)}) copy-start(bf16[256,4096]{1,0:T(8,128)(2,1)} %g_ref.9) | copy-start | bytes 6291460
  0.6 2.8 %copy-start.2 = (bf16[128,4096]{1,0:T(8,128)(2,1)S(1)}, bf16[128,4096]{1,0:T(8,128)(2,1)}, u32[]{:S(2)}) copy-start(bf16[128,4096]{1,0:T(8,128)(2,1)} %low_ref.3) | copy-start | bytes 3145732
  3.4 5.5 %copy-start.13 = (f32[256,128]{1,0:T(8,128)}, f32[256,128]{1,0:T(8,128)S(1)}, u32[]{:S(2)}) copy-start(f32[256,128]{1,0:T(8,128)S(1)} %fusion.24) | copy-start | bytes 393220
  3.4 4.5 %copy-start.1 = (bf16[256,4096]{1,0:T(8,128)(2,1)S(1)}, bf16[256,4096]{1,0:T(8,128)(2,1)}, u32[]{:S(2)}) copy-start(bf16[256,4096]{1,0:T(8,128)(2,1)} %f_ref.5) | copy-start | bytes 6291460
  4.1 6.5 %copy-start.14 = (f32[256,128]{1,0:T(8,128)}, f32[256,128]{1,0:T(8,128)S(1)}, u32[]{:S(2)}) copy-start(f32[256,128]{1,0:T(8,128)S(1)} %fusion.25) | copy-start | bytes 393220
  4.9 6.0 %copy-start.16 = (s32[64]{0:T(128)S(1)}, s32[64]{0:T(128)}, u32[]{:S(2)}) copy-start(s32[64]{0:T(128)} %param.11) | copy-start | bytes 772
  4.9 6.0 %copy-start.17 = (s32[64]{0:T(128)S(1)}, s32[64]{0:T(128)}, u32[]{:S(2)}) copy-start(s32[64]{0:T(128)} %param.10) | copy-start | bytes 772
  4.9 17.3 %collective-permute-start = (f32[2,128,128]{2,1,0:T(8,128)}, f32[2,128,128]{2,1,0:T(8,128)}, u32[]{:S(2)}, u32[]{:S(2)}) collective-permute-start(f32[2,128,128]{2,1,0:T(8,128)} %fusion.15), channel_id=1, source_target_pairs={{0,4},{4,0},{8,12},{12,8},{1,5},{5,1},{9,13},{13,9},{2,6},{6,2},{1... | collective-permute-start | bytes 393224 | tf_op jit(solution)/shard_map/ppermute | solution.py:24
  10.7 31.7 %collective-permute-start.3 = (bf16[256,1024]{1,0:T(8,128)(2,1)}, bf16[256,1024]{1,0:T(8,128)(2,1)}, u32[]{:S(2)}, u32[]{:S(2)}) collective-permute-start(bf16[256,1024]{1,0:T(8,128)(2,1)} %slice.82), channel_id=1, source_target_pairs={{0,4},{4,0},{8,12},{12,8},{1,5},{5,1},{9,13},{13,9},{2,6},{6,2},{1... | collective-permute-start | bytes 1572872 | tf_op jit(solution)/shard_map/ppermute | solution.py:24
  14.1 23.2 %collective-permute-start.6 = (bf16[2,256,256]{2,1,0:T(8,128)(2,1)}, bf16[2,256,256]{2,1,0:T(8,128)(2,1)}, u32[]{:S(2)}, u32[]{:S(2)}) collective-permute-start(bf16[2,256,256]{2,1,0:T(8,128)(2,1)} %get-tuple-element.21), channel_id=1, source_target_pairs={{0,8},{4,12},{8,0},{12,4},{1,9},{5,13},{9,1},{13,5},{2,10},{6,14},... | collective-permute-start | bytes 786440 | tf_op jit(solution)/shard_map/ppermute | solution.py:24
  22.1 120.3 %collective-permute-start.30 = (bf16[2,2,16,64,256]{4,3,2,1,0:T(8,128)(2,1)}, bf16[2,2,16,64,256]{4,3,2,1,0:T(8,128)(2,1)}, u32[]{:S(2)}, u32[]{:S(2)}) collective-permute-start(bf16[2,2,16,64,256]{4,3,2,1,0:T(8,128)(2,1)} %get-tuple-element.29), channel_id=1, source_target_pairs={{0,1},{1,0},{2,3},{3,2},{4,5},{5,4},{6,7},{7,6},{8,9},{9,8},{10,11... | collective-permute-start | bytes 6291464 | tf_op jit(solution)/shard_map/ppermute | solution.py:24
  23.1 14.2 %collective-permute-start.1 = (f32[2,128,128]{2,1,0:T(8,128)S(1)}, f32[2,128,128]{2,1,0:T(8,128)S(1)}, u32[]{:S(2)}, u32[]{:S(2)}) collective-permute-start(f32[2,128,128]{2,1,0:T(8,128)S(1)} %fusion.18), channel_id=1, source_target_pairs={{0,8},{4,12},{8,0},{12,4},{1,9},{5,13},{9,1},{13,5},{2,10},{6,14},... | collective-permute-start | bytes 393224 | tf_op jit(solution)/shard_map/ppermute | solution.py:24
  23.3 15.3 %collective-permute-start.5 = (bf16[2,256,256]{2,1,0:T(8,128)(2,1)}, bf16[2,256,256]{2,1,0:T(8,128)(2,1)}, u32[]{:S(2)}, u32[]{:S(2)}) collective-permute-start(bf16[2,256,256]{2,1,0:T(8,128)(2,1)} %get-tuple-element.20), channel_id=1, source_target_pairs={{0,4},{4,0},{8,12},{12,8},{1,5},{5,1},{9,13},{13,9},{2,6},{6,2},{1... | collective-permute-start | bytes 786440 | tf_op jit(solution)/shard_map/ppermute | solution.py:24
  37.4 62.8 %collective-permute-start.14 = (bf16[256,1536]{1,0:T(8,128)(2,1)}, bf16[256,1536]{1,0:T(8,128)(2,1)}, u32[]{:S(2)}, u32[]{:S(2)}) collective-permute-start(bf16[256,1536]{1,0:T(8,128)(2,1)} %slice.80), channel_id=1, source_target_pairs={{0,4},{4,0},{8,12},{12,8},{1,5},{5,1},{9,13},{13,9},{2,6},{6,2},{1... | collective-permute-start | bytes 2359304 | tf_op jit(solution)/shard_map/ppermute | solution.py:24
  37.4 64.9 %collective-permute-start.16 = (bf16[256,1536]{1,0:T(8,128)(2,1)}, bf16[256,1536]{1,0:T(8,128)(2,1)}, u32[]{:S(2)}, u32[]{:S(2)}) collective-permute-start(bf16[256,1536]{1,0:T(8,128)(2,1)} %slice.80), channel_id=1, source_target_pairs={{0,8},{4,12},{8,0},{12,4},{1,9},{5,13},{9,1},{13,5},{2,10},{6,14},... | collective-permute-start | bytes 2359304 | tf_op jit(solution)/shard_map/ppermute | solution.py:24
  38.6 58.7 %collective-permute-start.4 = (bf16[256,1024]{1,0:T(8,128)(2,1)}, bf16[256,1024]{1,0:T(8,128)(2,1)}, u32[]{:S(2)}, u32[]{:S(2)}) collective-permute-start(bf16[256,1024]{1,0:T(8,128)(2,1)} %slice.82), channel_id=1, source_target_pairs={{0,8},{4,12},{8,0},{12,4},{1,9},{5,13},{9,1},{13,5},{2,10},{6,14},... | collective-permute-start | bytes 1572872 | tf_op jit(solution)/shard_map/ppermute | solution.py:24
  42.3 76.6 %collective-permute-start.15 = (bf16[256,1536]{1,0:T(8,128)(2,1)}, bf16[256,1536]{1,0:T(8,128)(2,1)}, u32[]{:S(2)}, u32[]{:S(2)}) collective-permute-start(bf16[256,1536]{1,0:T(8,128)(2,1)} %slice.81), channel_id=1, source_target_pairs={{0,4},{4,0},{8,12},{12,8},{1,5},{5,1},{9,13},{13,9},{2,6},{6,2},{1... | collective-permute-start | bytes 2359304 | tf_op jit(solution)/shard_map/ppermute | solution.py:24
  97.3 36.5 %collective-permute-start.17 = (bf16[256,1536]{1,0:T(8,128)(2,1)}, bf16[256,1536]{1,0:T(8,128)(2,1)}, u32[]{:S(2)}, u32[]{:S(2)}) collective-permute-start(bf16[256,1536]{1,0:T(8,128)(2,1)} %slice.81), channel_id=1, source_target_pairs={{0,8},{4,12},{8,0},{12,4},{1,9},{5,13},{9,1},{13,5},{2,10},{6,14},... | collective-permute-start | bytes 2359304 | tf_op jit(solution)/shard_map/ppermute | solution.py:24
  100.1 17.9 %collective-permute-start.2 = (bf16[2,128,128]{2,1,0:T(8,128)(2,1)}, bf16[2,128,128]{2,1,0:T(8,128)(2,1)}, u32[]{:S(2)}, u32[]{:S(2)}) collective-permute-start(bf16[2,128,128]{2,1,0:T(8,128)(2,1)} %add_convert_fusion.5), channel_id=1, source_target_pairs={{0,4},{4,0},{8,12},{12,8},{1,5},{5,1},{9,13},{13,9},{2,6},{6,2},{1... | collective-permute-start | bytes 196616 | tf_op jit(solution)/shard_map/ppermute | solution.py:24
  102.2 24.0 %collective-permute-start.18 = (bf16[2,2,4,64,256]{4,3,2,1,0:T(8,128)(2,1)}, bf16[2,2,4,64,256]{4,3,2,1,0:T(8,128)(2,1)}, u32[]{:S(2)}, u32[]{:S(2)}) collective-permute-start(bf16[2,2,4,64,256]{4,3,2,1,0:T(8,128)(2,1)} %get-tuple-element.23), channel_id=1, source_target_pairs={{0,1},{1,0},{2,3},{3,2},{4,5},{5,4},{6,7},{7,6},{8,9},{9,8},{10,11... | collective-permute-start | bytes 1572872 | tf_op jit(solution)/shard_map/ppermute | solution.py:24
  118.0 24.4 %collective-permute-start.22 = (bf16[2,2,6,64,256]{4,3,2,1,0:T(8,128)(2,1)}, bf16[2,2,6,64,256]{4,3,2,1,0:T(8,128)(2,1)}, u32[]{:S(2)}, u32[]{:S(2)}) collective-permute-start(bf16[2,2,6,64,256]{4,3,2,1,0:T(8,128)(2,1)} %get-tuple-element.25), channel_id=1, source_target_pairs={{0,1},{1,0},{2,3},{3,2},{4,5},{5,4},{6,7},{7,6},{8,9},{9,8},{10,11... | collective-permute-start | bytes 2359304 | tf_op jit(solution)/shard_map/ppermute | solution.py:24
  119.0 19.5 %collective-permute-start.7 = (bf16[2,2,256,256]{3,2,1,0:T(8,128)(2,1)}, bf16[2,2,256,256]{3,2,1,0:T(8,128)(2,1)}, u32[]{:S(2)}, u32[]{:S(2)}) collective-permute-start(bf16[2,2,256,256]{3,2,1,0:T(8,128)(2,1)} %pad_maximum_fusion.refs_4_.refs_2_), channel_id=1, source_target_pairs={{0,2},{1,3},{2,0},{3,1},{4,6},{5,7},{6,4},{7,5},{8,10},{9,11},{10,... | collective-permute-start | bytes 1572872 | tf_op jit(solution)/shard_map/ppermute | solution.py:24
  126.2 38.1 %collective-permute-start.32 = (bf16[2,2,32,4096]{3,2,1,0:T(8,128)(2,1)}, bf16[2,2,32,4096]{3,2,1,0:T(8,128)(2,1)}, u32[]{:S(2)}, u32[]{:S(2)}) collective-permute-start(bf16[2,2,32,4096]{3,2,1,0:T(8,128)(2,1)} %get-tuple-element.31), channel_id=1, source_target_pairs={{0,1},{1,0},{2,3},{3,2},{4,5},{5,4},{6,7},{7,6},{8,9},{9,8},{10,11... | collective-permute-start | bytes 3145736 | tf_op jit(solution)/shard_map/ppermute | solution.py:24
  133.7 7.1 %collective-permute-start.19 = (bf16[1,2,4,64,256]{4,3,2,1,0:T(8,128)(2,1)}, bf16[1,2,4,64,256]{4,3,2,1,0:T(8,128)(2,1)}, u32[]{:S(2)}, u32[]{:S(2)}) collective-permute-start(bf16[1,2,4,64,256]{4,3,2,1,0:T(8,128)(2,1)} %get-tuple-element.42), channel_id=1, source_target_pairs={{0,2},{1,3},{2,0},{3,1},{4,6},{5,7},{6,4},{7,5},{8,10},{9,11},{10,... | collective-permute-start | bytes 786440 | tf_op jit(solution)/shard_map/ppermute | solution.py:24
  138.5 27.0 %collective-permute-start.25 = (bf16[2,2,6,64,256]{4,3,2,1,0:T(8,128)(2,1)}, bf16[2,2,6,64,256]{4,3,2,1,0:T(8,128)(2,1)S(1)}, u32[]{:S(2)}, u32[]{:S(2)}) collective-permute-start(bf16[2,2,6,64,256]{4,3,2,1,0:T(8,128)(2,1)} %get-tuple-element.27), channel_id=1, source_target_pairs={{0,1},{1,0},{2,3},{3,2},{4,5},{5,4},{6,7},{7,6},{8,9},{9,8},{10,11... | collective-permute-start | bytes 2359304 | tf_op jit(solution)/shard_map/ppermute | solution.py:24
  140.8 15.0 %collective-permute-start.8 = (bf16[2,2,256,256]{3,2,1,0:T(8,128)(2,1)}, bf16[2,2,256,256]{3,2,1,0:T(8,128)(2,1)S(1)}, u32[]{:S(2)}, u32[]{:S(2)}) collective-permute-start(bf16[2,2,256,256]{3,2,1,0:T(8,128)(2,1)} %pad_maximum_fusion.refs_4_.refs_2_), channel_id=1, source_target_pairs={{0,16},{16,0},{1,17},{17,1},{2,18},{18,2},{3,19},{19,3},{4,20},{20... | collective-permute-start | bytes 1572872 | tf_op jit(solution)/shard_map/ppermute | solution.py:24
  142.4 13.5 %collective-permute-start.10 = (bf16[2,2,256,256]{3,2,1,0:T(8,128)(2,1)}, bf16[2,2,256,256]{3,2,1,0:T(8,128)(2,1)S(1)}, u32[]{:S(2)}, u32[]{:S(2)}) collective-permute-start(bf16[2,2,256,256]{3,2,1,0:T(8,128)(2,1)} %pad_maximum_fusion.refs_4_.refs_2_), channel_id=1, source_target_pairs={{0,1},{1,0},{2,3},{3,2},{4,5},{5,4},{6,7},{7,6},{8,9},{9,8},{10,11... | collective-permute-start | bytes 1572872 | tf_op jit(solution)/shard_map/ppermute | solution.py:24
  142.4 21.9 %collective-permute-start.9 = (bf16[2,2,256,256]{3,2,1,0:T(8,128)(2,1)}, bf16[2,2,256,256]{3,2,1,0:T(8,128)(2,1)S(1)}, u32[]{:S(2)}, u32[]{:S(2)}) collective-permute-start(bf16[2,2,256,256]{3,2,1,0:T(8,128)(2,1)} %collective-permute-done.7.refs_5_.refs_3_), channel_id=1, source_target_pairs={{0,16},{16,0},{1,17},{17,1},{2,18},{18,2},{3,19},{19,3},{4,20},{20... | collective-permute-start | bytes 1572872 | tf_op jit(solution)/shard_map/ppermute | solution.py:24
  142.9 4.9 %copy-start.3 = (f32[2,2,16,64,256]{4,3,2,1,0:T(8,128)S(1)}, f32[2,2,16,64,256]{4,3,2,1,0:T(8,128)}, u32[]{:S(2)}) copy-start(f32[2,2,16,64,256]{4,3,2,1,0:T(8,128)} %get-tuple-element.28) | copy-start | bytes 12582916
  147.9 18.6 %copy-start.5 = (f32[2,2,32,4096]{3,2,1,0:T(8,128)S(1)}, f32[2,2,32,4096]{3,2,1,0:T(8,128)}, u32[]{:S(2)}) copy-start(f32[2,2,32,4096]{3,2,1,0:T(8,128)} %get-tuple-element.30) | copy-start | bytes 6291460
  155.8 13.2 %copy-start.6 = (bf16[2,2,256,256]{3,2,1,0:T(8,128)(2,1)}, bf16[2,2,256,256]{3,2,1,0:T(8,128)(2,1)S(1)}, u32[]{:S(2)}) copy-start(bf16[2,2,256,256]{3,2,1,0:T(8,128)(2,1)S(1)} %collective-permute-done.8.refs_6_.refs_4_) | copy-start | bytes 1572868
  155.8 14.6 %collective-permute-start.11 = (bf16[2,2,256,256]{3,2,1,0:T(8,128)(2,1)}, bf16[2,2,256,256]{3,2,1,0:T(8,128)(2,1)S(1)}, u32[]{:S(2)}, u32[]{:S(2)}) collective-permute-start(bf16[2,2,256,256]{3,2,1,0:T(8,128)(2,1)} %collective-permute-done.7.refs_5_.refs_3_), channel_id=1, source_target_pairs={{0,1},{1,0},{2,3},{3,2},{4,5},{5,4},{6,7},{7,6},{8,9},{9,8},{10,11... | collective-permute-start | bytes 1572872 | tf_op jit(solution)/shard_map/ppermute | solution.py:24
  155.9 13.2 %copy-start.7 = (bf16[2,2,256,256]{3,2,1,0:T(8,128)(2,1)}, bf16[2,2,256,256]{3,2,1,0:T(8,128)(2,1)S(1)}, u32[]{:S(2)}) copy-start(bf16[2,2,256,256]{3,2,1,0:T(8,128)(2,1)S(1)} %collective-permute-done.10.refs_8_.refs_6_) | copy-start | bytes 1572868
  155.9 16.9 %collective-permute-start.12 = (bf16[2,2,256,256]{3,2,1,0:T(8,128)(2,1)S(1)}, bf16[2,2,256,256]{3,2,1,0:T(8,128)(2,1)S(1)}, u32[]{:S(2)}, u32[]{:S(2)}) collective-permute-start(bf16[2,2,256,256]{3,2,1,0:T(8,128)(2,1)S(1)} %collective-permute-done.8.refs_6_.refs_4_), channel_id=1, source_target_pairs={{0,1},{1,0},{2,3},{3,2},{4,5},{5,4},{6,7},{7,6},{8,9},{9,8},{10,11... | collective-permute-start | bytes 1572872 | tf_op jit(solution)/shard_map/ppermute | solution.py:24
  164.3 4.8 %copy-start.8 = (bf16[2,2,256,256]{3,2,1,0:T(8,128)(2,1)}, bf16[2,2,256,256]{3,2,1,0:T(8,128)(2,1)S(1)}, u32[]{:S(2)}) copy-start(bf16[2,2,256,256]{3,2,1,0:T(8,128)(2,1)S(1)} %collective-permute-done.9.refs_7_.refs_5_) | copy-start | bytes 1572868
  164.3 10.0 %collective-permute-start.13 = (bf16[2,2,256,256]{3,2,1,0:T(8,128)(2,1)S(1)}, bf16[2,2,256,256]{3,2,1,0:T(8,128)(2,1)S(1)}, u32[]{:S(2)}, u32[]{:S(2)}) collective-permute-start(bf16[2,2,256,256]{3,2,1,0:T(8,128)(2,1)S(1)} %collective-permute-done.9.refs_7_.refs_5_), channel_id=1, source_target_pairs={{0,1},{1,0},{2,3},{3,2},{4,5},{5,4},{6,7},{7,6},{8,9},{9,8},{10,11... | collective-permute-start | bytes 1572872 | tf_op jit(solution)/shard_map/ppermute | solution.py:24
  164.3 25.1 %collective-permute-start.23 = (bf16[1,2,6,64,256]{4,3,2,1,0:T(8,128)(2,1)}, bf16[1,2,6,64,256]{4,3,2,1,0:T(8,128)(2,1)}, u32[]{:S(2)}, u32[]{:S(2)}) collective-permute-start(bf16[1,2,6,64,256]{4,3,2,1,0:T(8,128)(2,1)} %get-tuple-element.38), channel_id=1, source_target_pairs={{0,2},{1,3},{2,0},{3,1},{4,6},{5,7},{6,4},{7,5},{8,10},{9,11},{10,... | collective-permute-start | bytes 1179656 | tf_op jit(solution)/shard_map/ppermute | solution.py:24
  165.4 64.4 %collective-permute-start.31 = (bf16[1,2,16,64,256]{4,3,2,1,0:T(8,128)(2,1)}, bf16[1,2,16,64,256]{4,3,2,1,0:T(8,128)(2,1)}, u32[]{:S(2)}, u32[]{:S(2)}) collective-permute-start(bf16[1,2,16,64,256]{4,3,2,1,0:T(8,128)(2,1)} %get-tuple-element.32), channel_id=1, source_target_pairs={{0,2},{1,3},{2,0},{3,1},{4,6},{5,7},{6,4},{7,5},{8,10},{9,11},{10,... | collective-permute-start | bytes 3145736 | tf_op jit(solution)/shard_map/ppermute | solution.py:24
  166.4 2.7 %copy-start.12 = (f32[2,2,6,64,256]{4,3,2,1,0:T(8,128)S(1)}, f32[2,2,6,64,256]{4,3,2,1,0:T(8,128)}, u32[]{:S(2)}) copy-start(f32[2,2,6,64,256]{4,3,2,1,0:T(8,128)} %get-tuple-element.26) | copy-start | bytes 4718596
  170.4 3.9 %copy-start.9 = (bf16[2,2,256,256]{3,2,1,0:T(8,128)(2,1)}, bf16[2,2,256,256]{3,2,1,0:T(8,128)(2,1)S(1)}, u32[]{:S(2)}) copy-start(bf16[2,2,256,256]{3,2,1,0:T(8,128)(2,1)S(1)} %collective-permute-done.11.refs_9_.refs_7_) | copy-start | bytes 1572868
  170.4 78.3 %collective-permute-start.20 = (bf16[4,64,256]{2,1,0:T(8,128)(2,1)}, bf16[4,64,256]{2,1,0:T(8,128)(2,1)}, u32[]{:S(2)}, u32[]{:S(2)}) collective-permute-start(bf16[4,64,256]{2,1,0:T(8,128)(2,1)} %get-tuple-element.49), channel_id=1, source_target_pairs={{0,4},{4,0},{8,12},{12,8},{1,5},{5,1},{9,13},{13,9},{2,6},{6,2},{1... | collective-permute-start | bytes 393224 | tf_op jit(solution)/shard_map/ppermute | solution.py:24
  172.8 1.5 copy-start.10
  172.8 50.0 %collective-permute-start.33 = (bf16[1,2,32,4096]{3,2,1,0:T(8,128)(2,1)}, bf16[1,2,32,4096]{3,2,1,0:T(8,128)(2,1)}, u32[]{:S(2)}, u32[]{:S(2)}) collective-permute-start(bf16[1,2,32,4096]{3,2,1,0:T(8,128)(2,1)} %get-tuple-element.34), channel_id=1, source_target_pairs={{0,2},{1,3},{2,0},{3,1},{4,6},{5,7},{6,4},{7,5},{8,10},{9,11},{10,... | collective-permute-start | bytes 1572872 | tf_op jit(solution)/shard_map/ppermute | solution.py:24
  174.3 0.8 copy-start.11
  175.1 43.2 %collective-permute-start.26 = (bf16[1,2,6,64,256]{4,3,2,1,0:T(8,128)(2,1)}, bf16[1,2,6,64,256]{4,3,2,1,0:T(8,128)(2,1)}, u32[]{:S(2)}, u32[]{:S(2)}) collective-permute-start(bf16[1,2,6,64,256]{4,3,2,1,0:T(8,128)(2,1)} %get-tuple-element.36), channel_id=1, source_target_pairs={{0,2},{1,3},{2,0},{3,1},{4,6},{5,7},{6,4},{7,5},{8,10},{9,11},{10,... | collective-permute-start | bytes 1179656 | tf_op jit(solution)/shard_map/ppermute | solution.py:24
  189.5 40.4 %copy-start.4 = (f32[1,2,32,4096]{3,2,1,0:T(8,128)S(1)}, f32[1,2,32,4096]{3,2,1,0:T(8,128)}, u32[]{:S(2)}) copy-start(f32[1,2,32,4096]{3,2,1,0:T(8,128)} %get-tuple-element.35) | copy-start | bytes 3145732
  189.5 59.3 %collective-permute-start.21 = (bf16[4,64,256]{2,1,0:T(8,128)(2,1)}, bf16[4,64,256]{2,1,0:T(8,128)(2,1)}, u32[]{:S(2)}, u32[]{:S(2)}) collective-permute-start(bf16[4,64,256]{2,1,0:T(8,128)(2,1)} %get-tuple-element.48), channel_id=1, source_target_pairs={{0,8},{4,12},{8,0},{12,4},{1,9},{5,13},{9,1},{13,5},{2,10},{6,14},... | collective-permute-start | bytes 393224 | tf_op jit(solution)/shard_map/ppermute | solution.py:24
  218.3 7.7 %collective-permute-start.24 = (bf16[6,64,256]{2,1,0:T(8,128)(2,1)S(1)}, bf16[6,64,256]{2,1,0:T(8,128)(2,1)S(1)}, u32[]{:S(2)}, u32[]{:S(2)}) collective-permute-start(bf16[6,64,256]{2,1,0:T(8,128)(2,1)S(1)} %get-tuple-element.47), channel_id=1, source_target_pairs={{0,4},{4,0},{8,12},{12,8},{1,5},{5,1},{9,13},{13,9},{2,6},{6,2},{1... | collective-permute-start | bytes 589832 | tf_op jit(solution)/shard_map/ppermute | solution.py:24
  222.8 13.5 %collective-permute-start.27 = (bf16[6,64,256]{2,1,0:T(8,128)(2,1)}, bf16[6,64,256]{2,1,0:T(8,128)(2,1)}, u32[]{:S(2)}, u32[]{:S(2)}) collective-permute-start(bf16[6,64,256]{2,1,0:T(8,128)(2,1)} %get-tuple-element.45), channel_id=1, source_target_pairs={{0,4},{4,0},{8,12},{12,8},{1,5},{5,1},{9,13},{13,9},{2,6},{6,2},{1... | collective-permute-start | bytes 589832 | tf_op jit(solution)/shard_map/ppermute | solution.py:24
  226.0 0.7 copy-start.15
  226.7 16.9 %collective-permute-start.28 = (bf16[6,64,256]{2,1,0:T(8,128)(2,1)}, bf16[6,64,256]{2,1,0:T(8,128)(2,1)}, u32[]{:S(2)}, u32[]{:S(2)}) collective-permute-start(bf16[6,64,256]{2,1,0:T(8,128)(2,1)} %get-tuple-element.46), channel_id=1, source_target_pairs={{0,8},{4,12},{8,0},{12,4},{1,9},{5,13},{9,1},{13,5},{2,10},{6,14},... | collective-permute-start | bytes 589832 | tf_op jit(solution)/shard_map/ppermute | solution.py:24
  229.9 15.9 %collective-permute-start.29 = (bf16[6,64,256]{2,1,0:T(8,128)(2,1)}, bf16[6,64,256]{2,1,0:T(8,128)(2,1)}, u32[]{:S(2)}, u32[]{:S(2)}) collective-permute-start(bf16[6,64,256]{2,1,0:T(8,128)(2,1)} %get-tuple-element.44), channel_id=1, source_target_pairs={{0,8},{4,12},{8,0},{12,4},{1,9},{5,13},{9,1},{13,5},{2,10},{6,14},... | collective-permute-start | bytes 589832 | tf_op jit(solution)/shard_map/ppermute | solution.py:24

commit v5 on v4

--- a/solution.py
+++ b/solution.py
@@ -11,8 +11,7 @@
 WIDTH = 16384
 BLOCK = 256
 VMEM_LIMIT = 67_043_328
-CHUNK_SIZES = (6, 6, 4)
-EARLY_CHUNKS = 2
+CHUNK_SIZES = (4, 4, 5, 3)
 
 
 F32 = jnp.float32
@@ -238,8 +237,10 @@
     for step in range(steps):
         chunk = first + step
         cols = pl.ds(starts[chunk] * BLOCK, sizes[chunk] * BLOCK)
+        low_at, high_at = starts[chunk] // 2 * 2, (starts[chunk] + sizes[chunk] + 1) // 2 * 2
+        both = pl.ds(low_at * BLOCK, (high_at - low_at) * BLOCK)
         copies = [
-            pltpu.make_async_copy(f_ref.at[:, cols], f_buf.at[:, cols], in_sems.at[step, 0]),
+            pltpu.make_async_copy(f_ref.at[:, both], f_buf.at[:, both], in_sems.at[step, 0]),
             pltpu.make_async_copy(low_ref.at[:, cols], low_buf.at[:, cols], in_sems.at[step, 1]),
         ]
         for way in range(2):
@@ -507,8 +508,8 @@
     low = [keep[way] + came[way].astype(F32) for way in range(2)]
 
     mixed = None
-    early = min(EARLY_CHUNKS, chunks - 1)
-    for first, last in ((0, early), (early, chunks)):
+    cuts = [0, *range(max(1, chunks - 2), chunks + 1)]
+    for first, last in zip(cuts, cuts[1:]):
         mixed = mixed_kernel(
             features,
             block_weights,

time: 252 us -> 259 us (1.028)
  waiting for transfers between devices: 135 us -> 126 us
  starting transfers between devices: 34.5 us -> 42.8 us
  Pallas kernels: 45.5 us -> 51.8 us
  local copies, waits for them, and re-layouts: 4.99 us -> 9.32 us
  other arithmetic: 27.4 us -> 23.6 us
    ppermute x34 -> x40, starting transfers between devices: 34.5 us -> 42.8 us  [swapped(): lax.ppermute(block, axis, [(one, one ^ 1 << apart) for one in range(count)])]
    ppermute x34 -> x40, waiting for transfers between devices: 135 us -> 126 us  [swapped(): lax.ppermute(block, axis, [(one, one ^ 1 << apart) for one in range(count)])]
    pallas_call x2 -> x3, Pallas kernels: 13.8 us -> 17.6 us  [mixed_kernel(): pl.pallas_call(functools.partial(mixed_body, share, sizes, first, last, u...]
    convert_element_type x3 -> x4, other arithmetic: 6.16 us -> 3.14 us  [layer(): done = (keep[way] + came[way].astype(F32)).astype(BF16)]
    slice x3 -> x4, local copies, waits for them, and re-layouts: 2.75 us -> 5.46 us  [layer(): piece = source[:, first:first + sizes[one] * BLOCK]]
    pallas_call x4 -> x5, Pallas kernels: 14.4 us -> 16.8 us  [pair_grads(): pl.pallas_call(functools.partial(grad_body, pairs, part, first, step), in...]
    convert_element_type x5 -> x6, other arithmetic: 13.3 us -> 11.6 us  [items_sum(): came = swapped(leave.astype(BF16), 'items', level)]
  transfers between devices with their start and end apart: 34 -> 40, of which waited for: 11 -> 14; matrix products, arithmetic and copies ran while one was open for 12% -> 12% of each run, Pallas kernels for 17% -> 19%
where the time goes in v5:
time: 259 us; the launch traced here: 258 us
  waiting for transfers between devices  126 us (49%)
  Pallas kernels  51.8 us (20%)
  starting transfers between devices  42.8 us (17%)
  other arithmetic  23.6 us (9%)
  local copies, waits for them, and re-layouts  9.32 us (4%)
  matrix products  3.41 us (1%)
    ppermute x40, waiting for transfers between devices, swapped(): lax.ppermute(block, axis, [(one, one ^ 1 << apart) for one in range(count)])  126 us
    ppermute x40, starting transfers between devices, swapped(): lax.ppermute(block, axis, [(one, one ^ 1 << apart) for one in range(count)])  42.8 us
    pallas_call x3, Pallas kernels, mixed_kernel(): pl.pallas_call(functools.partial(mixed_body, share, sizes, first, last, u...  17.6 us
    pallas_call x5, Pallas kernels, pair_grads(): pl.pallas_call(functools.partial(grad_body, pairs, part, first, step), in...  16.8 us
    convert_element_type x6, other arithmetic, items_sum(): came = swapped(leave.astype(BF16), 'items', level)  11.6 us
    pallas_call x3, Pallas kernels, place_kernel(): pl.pallas_call(functools.partial(place_body, keys, pairs), in_specs=[pl.B...  9.76 us
    slice x4, local copies, waits for them, and re-layouts, layer(): piece = source[:, first:first + sizes[one] * BLOCK]  5.46 us
  transfers between devices with their start and end apart: 40, of which 14 were waited for; matrix products, arithmetic and copies ran while one was open for 12% of the time, Pallas kernels for 19%

profile of v5, /device:TPU:0, one launch (start us, length us, event | category | flops | bytes accessed | tf_op | source)
XLA Modules:
  0.0 258.3 jit_solution(5434106470960140229)
XLA Ops:
  0.7 2.7 %fusion.28 = f32[256,128]{1,0:T(8,128)S(1)} fusion(bf16[256,4096]{1,0:T(8,128)(2,1)} %f_ref.7, bf16[128,4096]{1,0:T(8,128)(2,1)} %param.12), kind=kOutput, calls=%fused_computation.67 | convolution fusion | flops 268435456 | bytes 3276800 | tf_op jit(solution)/shard_map/dot_general | solution.py:458
  4.8 3.1 %collective-permute-start = (f32[2,128,128]{2,1,0:T(8,128)}, f32[2,128,128]{2,1,0:T(8,128)}, u32[]{:S(2)}, u32[]{:S(2)}) collective-permute-start(f32[2,128,128]{2,1,0:T(8,128)} %fusion.17), channel_id=1, source_target_pairs={{0,4},{4,0},{8,12},{12,8},{1,5},{5,1},{9,13},{13,9},{2,6},{6,2},{1... | collective-permute-start | bytes 393224 | tf_op jit(solution)/shard_map/ppermute | solution.py:23
  8.6 2.6 weight_share.1
  11.2 2.7 %collective-permute-start.6 = (bf16[2,256,256]{2,1,0:T(8,128)(2,1)}, bf16[2,256,256]{2,1,0:T(8,128)(2,1)S(1)}, u32[]{:S(2)}, u32[]{:S(2)}) collective-permute-start(bf16[2,256,256]{2,1,0:T(8,128)(2,1)} %get-tuple-element.25), channel_id=1, source_target_pairs={{0,8},{4,12},{8,0},{12,4},{1,9},{5,13},{9,1},{13,5},{2,10},{6,14},... | collective-permute-start | bytes 786440 | tf_op jit(solution)/shard_map/ppermute | solution.py:23
  13.8 1.0 fusion.20
  15.5 1.6 collective-permute-start.5
  17.1 1.9 slice.99
  18.9 1.9 slice.100
  20.8 0.9 slice.101
  23.0 2.3 collective-permute-start.4
  25.3 6.1 %collective-permute-done.1 = f32[2,128,128]{2,1,0:T(8,128)S(1)} collective-permute-done((f32[2,128,128]{2,1,0:T(8,128)S(1)}, f32[2,128,128]{2,1,0:T(8,128)S(1)}, u32[]{:S(2)}, u32[]{:S(2)}) %collective-permute-start.1) | collective-permute-done | bytes 131104 | tf_op jit(solution)/shard_map/ppermute | solution.py:23
  31.4 0.8 collective-permute-start.16
  32.2 1.2 collective-permute-start.17
  34.8 0.8 collective-permute-start.2
  35.6 5.0 %pair_grads.9 = (bf16[2,2,16,64,256]{4,3,2,1,0:T(8,128)(2,1)}, f32[2,2,16,64,256]{4,3,2,1,0:T(8,128)}) custom-call(s32[1]{0:T(128)} %bitcast.10.bit_ref, bf16[256,4096]{1,0:T(8,128)(2,1)} %g_ref.11, bf16[256,4096]{1,0:T(8,128)(2,1)} %f_ref.7), custom_call_target="tpu_custom_call" | custom-call | flops 1073741824 | bytes 12582912 | tf_op jit(solution)/shard_map/pair_grads/pallas_call | solution.py:93
  40.7 31.3 %collective-permute-done.2 = bf16[2,128,128]{2,1,0:T(8,128)(2,1)} collective-permute-done((bf16[2,128,128]{2,1,0:T(8,128)(2,1)}, bf16[2,128,128]{2,1,0:T(8,128)(2,1)}, u32[]{:S(2)}, u32[]{:S(2)}) %collective-permute-start.2) | collective-permute-done | bytes 65568 | tf_op jit(solution)/shard_map/ppermute | solution.py:23
  72.0 2.9 %collective-permute-start.19 = (bf16[256,1024]{1,0:T(8,128)(2,1)}, bf16[256,1024]{1,0:T(8,128)(2,1)}, u32[]{:S(2)}, u32[]{:S(2)}) collective-permute-start(bf16[256,1024]{1,0:T(8,128)(2,1)} %slice.100), channel_id=1, source_target_pairs={{0,8},{4,12},{8,0},{12,4},{1,9},{5,13},{9,1},{13,5},{2,10},{6,14},... | collective-permute-start | bytes 1572872 | tf_op jit(solution)/shard_map/ppermute | solution.py:23
  74.9 2.5 collective-permute-start.15
  77.4 2.8 %pair_grads.5 = (bf16[2,2,3,64,256]{4,3,2,1,0:T(8,128)(2,1)}, f32[2,2,3,64,256]{4,3,2,1,0:T(8,128)}) custom-call(s32[1]{0:T(128)} %bitcast.10.bit_ref, bf16[256,4096]{1,0:T(8,128)(2,1)} %g_ref.11, bf16[256,768]{1,0:T(8,128)(2,1)} %collective-permute-done.3.refs_0_, bf16[256,768]{1,0:T(8,128)(2,1)} %collective-permute-done.4.refs_1_), custom_call_target="tpu_custom_call" | custom-call | flops 201326592 | bytes 2359296 | tf_op jit(solution)/shard_map/pair_grads/pallas_call | solution.py:93
  80.2 29.2 %collective-permute-done.18.refs_2_.refs_1_ = bf16[256,1024]{1,0:T(8,128)(2,1)} collective-permute-done((bf16[256,1024]{1,0:T(8,128)(2,1)}, bf16[256,1024]{1,0:T(8,128)(2,1)}, u32[]{:S(2)}, u32[]{:S(2)}) %collective-permute-start.18) | collective-permute-done | bytes 524320 | tf_op jit(solution)/shard_map/ppermute | solution.py:23
  109.3 1.9 pad_maximum_fusion.refs_4_.refs_2_
  111.2 2.8 %pair_grads.6 = (bf16[2,2,4,64,256]{4,3,2,1,0:T(8,128)(2,1)}, f32[2,2,4,64,256]{4,3,2,1,0:T(8,128)}) custom-call(s32[1]{0:T(128)} %bitcast.10.bit_ref, bf16[256,4096]{1,0:T(8,128)(2,1)} %g_ref.11, bf16[256,1024]{1,0:T(8,128)(2,1)} %collective-permute-done.16.refs_0_, bf16[256,1024]{1,0:T(8,128)(2,1)} %collective-permute-done.18.refs_2_.refs_1_), custom_call_target="tpu_custom_call" | custom-call | flops 268435456 | bytes 3145728 | tf_op jit(solution)/shard_map/pair_grads/pallas_call | solution.py:93
  114.0 20.5 %collective-permute-done.19.refs_3_.refs_1_ = bf16[256,1024]{1,0:T(8,128)(2,1)} collective-permute-done((bf16[256,1024]{1,0:T(8,128)(2,1)}, bf16[256,1024]{1,0:T(8,128)(2,1)}, u32[]{:S(2)}, u32[]{:S(2)}) %collective-permute-start.19) | collective-permute-done | bytes 524320 | tf_op jit(solution)/shard_map/ppermute | solution.py:23
  134.6 1.6 maximum_select_fusion
  136.2 2.8 %pair_grads.7 = (bf16[2,2,4,64,256]{4,3,2,1,0:T(8,128)(2,1)}, f32[2,2,4,64,256]{4,3,2,1,0:T(8,128)}) custom-call(s32[1]{0:T(128)} %bitcast.10.bit_ref, bf16[256,4096]{1,0:T(8,128)(2,1)} %g_ref.11, bf16[256,1024]{1,0:T(8,128)(2,1)} %collective-permute-done.17.refs_1_.refs_0_, bf16[256,1024]{1,0:T(8,128)(2,1)} %collective-permute-done.19.refs_3_.refs_1_), custom_call_target="tpu_custom_call" | custom-call | flops 268435456 | bytes 3145728 | tf_op jit(solution)/shard_map/pair_grads/pallas_call | solution.py:93
  139.6 9.0 %collective-permute-done.15.refs_1_ = bf16[256,1280]{1,0:T(8,128)(2,1)} collective-permute-done((bf16[256,1280]{1,0:T(8,128)(2,1)}, bf16[256,1280]{1,0:T(8,128)(2,1)}, u32[]{:S(2)}, u32[]{:S(2)}) %collective-permute-start.15) | collective-permute-done | bytes 655392 | tf_op jit(solution)/shard_map/ppermute | solution.py:23
  148.6 3.4 %pair_grads.8 = (bf16[2,2,5,64,256]{4,3,2,1,0:T(8,128)(2,1)}, f32[2,2,5,64,256]{4,3,2,1,0:T(8,128)}) custom-call(s32[1]{0:T(128)} %bitcast.10.bit_ref, bf16[256,4096]{1,0:T(8,128)(2,1)} %g_ref.11, bf16[256,1280]{1,0:T(8,128)(2,1)} %collective-permute-done.14.refs_0_, bf16[256,1280]{1,0:T(8,128)(2,1)} %collective-permute-done.15.refs_1_), custom_call_target="tpu_custom_call" | custom-call | flops 335544320 | bytes 3932160 | tf_op jit(solution)/shard_map/pair_grads/pallas_call | solution.py:93
  152.1 2.1 add_convert_fusion.5
  154.2 1.5 collective-permute-start.21
  155.7 1.6 slice_bitcast_fusion
  157.2 4.2 %collective-permute-done.21 = bf16[1,2,3,64,256]{4,3,2,1,0:T(8,128)(2,1)S(1)} collective-permute-done((bf16[1,2,3,64,256]{4,3,2,1,0:T(8,128)(2,1)S(1)}, bf16[1,2,3,64,256]{4,3,2,1,0:T(8,128)(2,1)S(1)}, u32[]{:S(2)}, u32[]{:S(2)}) %collective-permute-start.21) | collective-permute-done | bytes 196640 | tf_op jit(solution)/shard_map/ppermute | solution.py:23
  162.1 1.5 collective-permute-start.7
  163.6 5.0 %low_grads.1 = (bf16[2,2,32,4096]{3,2,1,0:T(8,128)(2,1)}, f32[2,2,32,4096]{3,2,1,0:T(8,128)}) custom-call(s32[1]{0:T(128)} %bitcast.10.bit_ref, bf16[256,128]{1,0:T(8,128)(2,1)} %get-tuple-element.60.b_ref, bf16[256,4096]{1,0:T(8,128)(2,1)} %f_ref.7, bf16[256,128]{1,0:T(8,128)(2,1)} %get-tuple-element.61.codes_ref.c_ref, bf16[256,4096]{1,0:T(8,128)(2,1)} %g_ref.11), custom_call_target="tpu_custom_call" | custom-call | flops 536870912 | bytes 7340032 | tf_op jit(solution)/shard_map/low_grads/pallas_call | solution.py:137
  168.7 1.6 add_convert_fusion.4
  171.7 1.3 add_convert_fusion.3
  173.0 4.2 %collective-permute-done.7.refs_5_.refs_3_ = bf16[2,2,256,256]{3,2,1,0:T(8,128)(2,1)} collective-permute-done((bf16[2,2,256,256]{3,2,1,0:T(8,128)(2,1)}, bf16[2,2,256,256]{3,2,1,0:T(8,128)(2,1)}, u32[]{:S(2)}, u32[]{:S(2)}) %collective-permute-start.7) | collective-permute-done | bytes 524320 | tf_op jit(solution)/shard_map/ppermute | solution.py:23
  177.2 1.5 collective-permute-start.8
  178.7 2.6 %collective-permute-done.25 = bf16[1,2,4,64,256]{4,3,2,1,0:T(8,128)(2,1)S(1)} collective-permute-done((bf16[1,2,4,64,256]{4,3,2,1,0:T(8,128)(2,1)S(1)}, bf16[1,2,4,64,256]{4,3,2,1,0:T(8,128)(2,1)S(1)}, u32[]{:S(2)}, u32[]{:S(2)}) %collective-permute-start.25) | collective-permute-done | bytes 262176 | tf_op jit(solution)/shard_map/ppermute | solution.py:23
  181.4 1.5 collective-permute-start.9
  183.7 1.5 collective-permute-start.28
  185.2 1.2 add_convert_fusion.2
  186.4 4.1 %add_convert_fusion = (bf16[1,2,16,64,256]{4,3,2,1,0:T(8,128)(2,1)}, f32[1,2,16,64,256]{4,3,2,1,0:T(8,128)}) fusion(f32[2,2,16,64,256]{4,3,2,1,0:T(8,128)S(1)} %copy-done.10, s32[]{:T(128)S(6)} %select_n.71, bf16[2,2,16,64,256]{4,3,2,1,0:T(8,128)(2,1)} %collective-permute-done.36, s32[]{:T(128)S(6)} %select_n.70), kind=kLoop, calls=%fused_computation | loop fusion | flops 2621440 | bytes 9437192 | tf_op jit(solution)/shard_map/convert_element_type | solution.py:166
  190.6 1.4 collective-permute-done.8.refs_6_.refs_4_
  192.5 7.1 %collective-permute-done.9.refs_7_.refs_5_ = bf16[2,2,256,256]{3,2,1,0:T(8,128)(2,1)S(1)} collective-permute-done((bf16[2,2,256,256]{3,2,1,0:T(8,128)(2,1)}, bf16[2,2,256,256]{3,2,1,0:T(8,128)(2,1)S(1)}, u32[]{:S(2)}, u32[]{:S(2)}) %collective-permute-start.9) | collective-permute-done | bytes 524320 | tf_op jit(solution)/shard_map/ppermute | solution.py:23
  199.6 1.5 collective-permute-start.31
  201.8 1.3 add_convert_fusion.1
  203.1 5.9 %collective-permute-done.31 = bf16[1,2,5,64,256]{4,3,2,1,0:T(8,128)(2,1)S(1)} collective-permute-done((bf16[1,2,5,64,256]{4,3,2,1,0:T(8,128)(2,1)S(1)}, bf16[1,2,5,64,256]{4,3,2,1,0:T(8,128)(2,1)S(1)}, u32[]{:S(2)}, u32[]{:S(2)}) %collective-permute-start.31) | collective-permute-done | bytes 327712 | tf_op jit(solution)/shard_map/ppermute | solution.py:23
  209.0 2.4 collective-permute-start.39
  212.2 0.8 fusion.11
  213.1 2.0 collective-permute-start.29
  215.1 0.8 copy-done.9
  216.4 6.7 %mixed.3.refs_10_ = bf16[256,4096]{1,0:T(8,128)(2,1)} custom-call(s32[64]{0:T(128)} %select_reduce_fusion.pos_ref, s32[1]{0:T(128)} %bitcast.item_ref, bf16[256,4096]{1,0:T(8,128)(2,1)} %f_ref.7, bf16[64,256,256]{2,1,0:T(8,128)(2,1)} %w_ref.7, bf16[256,128]{1,0:T(8,128)(2,1)} %get-tuple-element.61.codes_ref.c_ref, bf16[128,4096]{1,0:T(8,128)(2,1)} %low_ref.5, ...), custom_call_target="tpu_custom_call" | custom-call | flops 1207959552 | bytes 8388608 | tf_op jit(solution)/shard_map/mixed/pallas_call | solution.py:317
  223.1 5.9 %mixed.4.refs_10_ = bf16[256,4096]{1,0:T(8,128)(2,1)} custom-call(s32[64]{0:T(128)} %select_reduce_fusion.pos_ref, s32[1]{0:T(128)} %bitcast.item_ref, bf16[256,4096]{1,0:T(8,128)(2,1)} %f_ref.7, bf16[64,256,256]{2,1,0:T(8,128)(2,1)} %w_ref.7, bf16[256,128]{1,0:T(8,128)(2,1)} %get-tuple-element.61.codes_ref.c_ref, ...), custom_call_target="tpu_custom_call", output_to_operand_aliasing={{}: (16, {})} | custom-call | flops 754974720 | bytes 5242880 | tf_op jit(solution)/shard_map/mixed/pallas_call | solution.py:317
  229.1 4.9 %mixed.5 = bf16[256,4096]{1,0:T(8,128)(2,1)} custom-call(s32[64]{0:T(128)} %select_reduce_fusion.pos_ref, s32[1]{0:T(128)} %bitcast.item_ref, bf16[256,4096]{1,0:T(8,128)(2,1)} %f_ref.7, bf16[64,256,256]{2,1,0:T(8,128)(2,1)} %w_ref.7, bf16[256,128]{1,0:T(8,128)(2,1)} %get-tuple-element.61.codes_ref.c_ref, ...), custom_call_target="tpu_custom_call", output_to_operand_aliasing={{}: (16, {})} | custom-call | flops 452984832 | bytes 3145728 | tf_op jit(solution)/shard_map/mixed/pallas_call | solution.py:317
  234.0 1.9 collective-permute-start.22
  236.6 2.2 collective-permute-start.34
  238.9 1.7 collective-permute-done.39
  240.5 2.4 collective-permute-start.35
  243.0 2.4 fusion
  245.4 4.3 %place.3.refs_6_ = f32[64,64,256]{2,1,0:T(8,128)} custom-call(s32[64]{0:T(128)} %select_reduce_fusion.pos_ref, f32[32,64,256]{2,1,0:T(8,128)} %bitcast.46, bf16[32,64,256]{2,1,0:T(8,128)(2,1)} %bitcast.20.refs_1_), custom_call_target="tpu_custom_call" | custom-call | bytes 4194304 | tf_op jit(solution)/shard_map/place/pallas_call | solution.py:379
  249.7 1.2 collective-permute-done.34.refs_4_
  250.9 1.8 collective-permute-done.35.refs_5_
  252.7 3.1 %place.4.refs_2_ = f32[64,64,256]{2,1,0:T(8,128)} custom-call(s32[64]{0:T(128)} %select_reduce_fusion.pos_ref, bf16[4,64,256]{2,1,0:T(8,128)(2,1)} %collective-permute-done.26.refs_0_, bf16[4,64,256]{2,1,0:T(8,128)(2,1)} %collective-permute-done.29.refs_1_, bf16[5,64,256]{2,1,0:T(8,128)(2,1)} %collective-permute-done.32.refs_2_, ...), custom_call_target="tpu_custom_call", output_to_operand_aliasing={{}: (7, {})} | custom-call | bytes 3407872 | tf_op jit(solution)/shard_map/place/pallas_call | solution.py:379
  255.8 2.4 place.5
  (100 shorter events, 12.3 us)
Async XLA Ops:
  0.6 2.7 %copy-start = (bf16[256,4096]{1,0:T(8,128)(2,1)S(1)}, bf16[256,4096]{1,0:T(8,128)(2,1)}, u32[]{:S(2)}) copy-start(bf16[256,4096]{1,0:T(8,128)(2,1)} %g_ref.11) | copy-start | bytes 6291460
  0.6 2.8 %copy-start.2 = (bf16[128,4096]{1,0:T(8,128)(2,1)S(1)}, bf16[128,4096]{1,0:T(8,128)(2,1)}, u32[]{:S(2)}) copy-start(bf16[128,4096]{1,0:T(8,128)(2,1)} %low_ref.5) | copy-start | bytes 3145732
  3.4 0.7 copy-start.14
  3.4 4.5 %copy-start.21 = (s32[64]{0:T(128)S(1)}, s32[64]{0:T(128)}, u32[]{:S(2)}) copy-start(s32[64]{0:T(128)} %param.11) | copy-start | bytes 772
  3.4 4.5 %copy-start.22 = (s32[64]{0:T(128)S(1)}, s32[64]{0:T(128)}, u32[]{:S(2)}) copy-start(s32[64]{0:T(128)} %param.10) | copy-start | bytes 772
  4.1 0.7 copy-start.15
  4.8 9.0 %collective-permute-start = (f32[2,128,128]{2,1,0:T(8,128)}, f32[2,128,128]{2,1,0:T(8,128)}, u32[]{:S(2)}, u32[]{:S(2)}) collective-permute-start(f32[2,128,128]{2,1,0:T(8,128)} %fusion.17), channel_id=1, source_target_pairs={{0,4},{4,0},{8,12},{12,8},{1,5},{5,1},{9,13},{13,9},{2,6},{6,2},{1... | collective-permute-start | bytes 393224 | tf_op jit(solution)/shard_map/ppermute | solution.py:23
  11.2 9.6 %copy-start.1 = (bf16[256,4096]{1,0:T(8,128)(2,1)S(1)}, bf16[256,4096]{1,0:T(8,128)(2,1)}, u32[]{:S(2)}) copy-start(bf16[256,4096]{1,0:T(8,128)(2,1)} %f_ref.7) | copy-start | bytes 6291460
  11.2 21.0 %collective-permute-start.6 = (bf16[2,256,256]{2,1,0:T(8,128)(2,1)}, bf16[2,256,256]{2,1,0:T(8,128)(2,1)S(1)}, u32[]{:S(2)}, u32[]{:S(2)}) collective-permute-start(bf16[2,256,256]{2,1,0:T(8,128)(2,1)} %get-tuple-element.25), channel_id=1, source_target_pairs={{0,8},{4,12},{8,0},{12,4},{1,9},{5,13},{9,1},{13,5},{2,10},{6,14},... | collective-permute-start | bytes 786440 | tf_op jit(solution)/shard_map/ppermute | solution.py:23
  14.8 16.6 %collective-permute-start.1 = (f32[2,128,128]{2,1,0:T(8,128)S(1)}, f32[2,128,128]{2,1,0:T(8,128)S(1)}, u32[]{:S(2)}, u32[]{:S(2)}) collective-permute-start(f32[2,128,128]{2,1,0:T(8,128)S(1)} %fusion.20), channel_id=1, source_target_pairs={{0,8},{4,12},{8,0},{12,4},{1,9},{5,13},{9,1},{13,5},{2,10},{6,14},... | collective-permute-start | bytes 393224 | tf_op jit(solution)/shard_map/ppermute | solution.py:23
  15.5 18.6 %collective-permute-start.5 = (bf16[2,256,256]{2,1,0:T(8,128)(2,1)}, bf16[2,256,256]{2,1,0:T(8,128)(2,1)S(1)}, u32[]{:S(2)}, u32[]{:S(2)}) collective-permute-start(bf16[2,256,256]{2,1,0:T(8,128)(2,1)} %get-tuple-element.24), channel_id=1, source_target_pairs={{0,4},{4,0},{8,12},{12,8},{1,5},{5,1},{9,13},{13,9},{2,6},{6,2},{1... | collective-permute-start | bytes 786440 | tf_op jit(solution)/shard_map/ppermute | solution.py:23
  22.5 49.4 %collective-permute-start.3 = (bf16[256,768]{1,0:T(8,128)(2,1)}, bf16[256,768]{1,0:T(8,128)(2,1)}, u32[]{:S(2)}, u32[]{:S(2)}) collective-permute-start(bf16[256,768]{1,0:T(8,128)(2,1)} %slice.102), channel_id=1, source_target_pairs={{0,4},{4,0},{8,12},{12,8},{1,5},{5,1},{9,13},{13,9},{2,6},{6,2},{1... | collective-permute-start | bytes 1179656 | tf_op jit(solution)/shard_map/ppermute | solution.py:23
  23.0 49.0 %collective-permute-start.4 = (bf16[256,768]{1,0:T(8,128)(2,1)}, bf16[256,768]{1,0:T(8,128)(2,1)}, u32[]{:S(2)}, u32[]{:S(2)}) collective-permute-start(bf16[256,768]{1,0:T(8,128)(2,1)} %slice.102), channel_id=1, source_target_pairs={{0,8},{4,12},{8,0},{12,4},{1,9},{5,13},{9,1},{13,5},{2,10},{6,14},... | collective-permute-start | bytes 1179656 | tf_op jit(solution)/shard_map/ppermute | solution.py:23
  31.4 43.5 %collective-permute-start.16 = (bf16[256,1024]{1,0:T(8,128)(2,1)}, bf16[256,1024]{1,0:T(8,128)(2,1)}, u32[]{:S(2)}, u32[]{:S(2)}) collective-permute-start(bf16[256,1024]{1,0:T(8,128)(2,1)} %slice.99), channel_id=1, source_target_pairs={{0,4},{4,0},{8,12},{12,8},{1,5},{5,1},{9,13},{13,9},{2,6},{6,2},{1... | collective-permute-start | bytes 1572872 | tf_op jit(solution)/shard_map/ppermute | solution.py:23
  32.2 1.9 copy-start.17
  32.2 42.7 %collective-permute-start.17 = (bf16[256,1024]{1,0:T(8,128)(2,1)}, bf16[256,1024]{1,0:T(8,128)(2,1)}, u32[]{:S(2)}, u32[]{:S(2)}) collective-permute-start(bf16[256,1024]{1,0:T(8,128)(2,1)} %slice.100), channel_id=1, source_target_pairs={{0,4},{4,0},{8,12},{12,8},{1,5},{5,1},{9,13},{13,9},{2,6},{6,2},{1... | collective-permute-start | bytes 1572872 | tf_op jit(solution)/shard_map/ppermute | solution.py:23
  34.1 0.7 copy-start.18
  34.8 37.1 %collective-permute-start.2 = (bf16[2,128,128]{2,1,0:T(8,128)(2,1)}, bf16[2,128,128]{2,1,0:T(8,128)(2,1)}, u32[]{:S(2)}, u32[]{:S(2)}) collective-permute-start(bf16[2,128,128]{2,1,0:T(8,128)(2,1)} %add_convert_fusion.6), channel_id=1, source_target_pairs={{0,4},{4,0},{8,12},{12,8},{1,5},{5,1},{9,13},{13,9},{2,6},{6,2},{1... | collective-permute-start | bytes 196616 | tf_op jit(solution)/shard_map/ppermute | solution.py:23
  71.9 111.7 %collective-permute-start.36 = (bf16[2,2,16,64,256]{4,3,2,1,0:T(8,128)(2,1)}, bf16[2,2,16,64,256]{4,3,2,1,0:T(8,128)(2,1)}, u32[]{:S(2)}, u32[]{:S(2)}) collective-permute-start(bf16[2,2,16,64,256]{4,3,2,1,0:T(8,128)(2,1)} %get-tuple-element.35), channel_id=1, source_target_pairs={{0,1},{1,0},{2,3},{3,2},{4,5},{5,4},{6,7},{7,6},{8,9},{9,8},{10,11... | collective-permute-start | bytes 6291464 | tf_op jit(solution)/shard_map/ppermute | solution.py:23
  71.9 37.4 %collective-permute-start.18 = (bf16[256,1024]{1,0:T(8,128)(2,1)}, bf16[256,1024]{1,0:T(8,128)(2,1)}, u32[]{:S(2)}, u32[]{:S(2)}) collective-permute-start(bf16[256,1024]{1,0:T(8,128)(2,1)} %slice.99), channel_id=1, source_target_pairs={{0,8},{4,12},{8,0},{12,4},{1,9},{5,13},{9,1},{13,5},{2,10},{6,14},... | collective-permute-start | bytes 1572872 | tf_op jit(solution)/shard_map/ppermute | solution.py:23
  72.0 62.6 %collective-permute-start.19 = (bf16[256,1024]{1,0:T(8,128)(2,1)}, bf16[256,1024]{1,0:T(8,128)(2,1)}, u32[]{:S(2)}, u32[]{:S(2)}) collective-permute-start(bf16[256,1024]{1,0:T(8,128)(2,1)} %slice.100), channel_id=1, source_target_pairs={{0,8},{4,12},{8,0},{12,4},{1,9},{5,13},{9,1},{13,5},{2,10},{6,14},... | collective-permute-start | bytes 1572872 | tf_op jit(solution)/shard_map/ppermute | solution.py:23
  74.9 64.2 %collective-permute-start.14 = (bf16[256,1280]{1,0:T(8,128)(2,1)}, bf16[256,1280]{1,0:T(8,128)(2,1)}, u32[]{:S(2)}, u32[]{:S(2)}) collective-permute-start(bf16[256,1280]{1,0:T(8,128)(2,1)} %slice.101), channel_id=1, source_target_pairs={{0,4},{4,0},{8,12},{12,8},{1,5},{5,1},{9,13},{13,9},{2,6},{6,2},{1... | collective-permute-start | bytes 1966088 | tf_op jit(solution)/shard_map/ppermute | solution.py:23
  74.9 73.7 %collective-permute-start.15 = (bf16[256,1280]{1,0:T(8,128)(2,1)}, bf16[256,1280]{1,0:T(8,128)(2,1)}, u32[]{:S(2)}, u32[]{:S(2)}) collective-permute-start(bf16[256,1280]{1,0:T(8,128)(2,1)} %slice.101), channel_id=1, source_target_pairs={{0,8},{4,12},{8,0},{12,4},{1,9},{5,13},{9,1},{13,5},{2,10},{6,14},... | collective-permute-start | bytes 1966088 | tf_op jit(solution)/shard_map/ppermute | solution.py:23
  109.3 42.8 %collective-permute-start.20 = (bf16[2,2,3,64,256]{4,3,2,1,0:T(8,128)(2,1)}, bf16[2,2,3,64,256]{4,3,2,1,0:T(8,128)(2,1)}, u32[]{:S(2)}, u32[]{:S(2)}) collective-permute-start(bf16[2,2,3,64,256]{4,3,2,1,0:T(8,128)(2,1)} %get-tuple-element.27), channel_id=1, source_target_pairs={{0,1},{1,0},{2,3},{3,2},{4,5},{5,4},{6,7},{7,6},{8,9},{9,8},{10,11... | collective-permute-start | bytes 1179656 | tf_op jit(solution)/shard_map/ppermute | solution.py:23
  134.6 34.1 %collective-permute-start.24 = (bf16[2,2,4,64,256]{4,3,2,1,0:T(8,128)(2,1)}, bf16[2,2,4,64,256]{4,3,2,1,0:T(8,128)(2,1)}, u32[]{:S(2)}, u32[]{:S(2)}) collective-permute-start(bf16[2,2,4,64,256]{4,3,2,1,0:T(8,128)(2,1)} %get-tuple-element.29), channel_id=1, source_target_pairs={{0,1},{1,0},{2,3},{3,2},{4,5},{5,4},{6,7},{7,6},{8,9},{9,8},{10,11... | collective-permute-start | bytes 1572872 | tf_op jit(solution)/shard_map/ppermute | solution.py:23
  139.1 31.3 %collective-permute-start.27 = (bf16[2,2,4,64,256]{4,3,2,1,0:T(8,128)(2,1)}, bf16[2,2,4,64,256]{4,3,2,1,0:T(8,128)(2,1)}, u32[]{:S(2)}, u32[]{:S(2)}) collective-permute-start(bf16[2,2,4,64,256]{4,3,2,1,0:T(8,128)(2,1)} %get-tuple-element.31), channel_id=1, source_target_pairs={{0,1},{1,0},{2,3},{3,2},{4,5},{5,4},{6,7},{7,6},{8,9},{9,8},{10,11... | collective-permute-start | bytes 1572872 | tf_op jit(solution)/shard_map/ppermute | solution.py:23
  152.0 29.4 %collective-permute-start.30 = (bf16[2,2,5,64,256]{4,3,2,1,0:T(8,128)(2,1)}, bf16[2,2,5,64,256]{4,3,2,1,0:T(8,128)(2,1)}, u32[]{:S(2)}, u32[]{:S(2)}) collective-permute-start(bf16[2,2,5,64,256]{4,3,2,1,0:T(8,128)(2,1)} %get-tuple-element.33), channel_id=1, source_target_pairs={{0,1},{1,0},{2,3},{3,2},{4,5},{5,4},{6,7},{7,6},{8,9},{9,8},{10,11... | collective-permute-start | bytes 1966088 | tf_op jit(solution)/shard_map/ppermute | solution.py:23
  154.2 7.3 %collective-permute-start.21 = (bf16[1,2,3,64,256]{4,3,2,1,0:T(8,128)(2,1)S(1)}, bf16[1,2,3,64,256]{4,3,2,1,0:T(8,128)(2,1)S(1)}, u32[]{:S(2)}, u32[]{:S(2)}) collective-permute-start(bf16[1,2,3,64,256]{4,3,2,1,0:T(8,128)(2,1)S(1)} %get-tuple-element.50), channel_id=1, source_target_pairs={{0,2},{1,3},{2,0},{3,1},{4,6},{5,7},{6,4},{7,5},{8,10},{9,11},{10,... | collective-permute-start | bytes 589832 | tf_op jit(solution)/shard_map/ppermute | solution.py:23
  161.4 0.7 copy-start.19
  162.1 15.1 %collective-permute-start.7 = (bf16[2,2,256,256]{3,2,1,0:T(8,128)(2,1)}, bf16[2,2,256,256]{3,2,1,0:T(8,128)(2,1)}, u32[]{:S(2)}, u32[]{:S(2)}) collective-permute-start(bf16[2,2,256,256]{3,2,1,0:T(8,128)(2,1)} %pad_maximum_fusion.refs_4_.refs_2_), channel_id=1, source_target_pairs={{0,2},{1,3},{2,0},{3,1},{4,6},{5,7},{6,4},{7,5},{8,10},{9,11},{10,... | collective-permute-start | bytes 1572872 | tf_op jit(solution)/shard_map/ppermute | solution.py:23
  168.6 2.3 copy-start.12
  168.6 2.3 copy-start.20
  168.6 3.1 %copy-start.16 = (f32[2,2,4,64,256]{4,3,2,1,0:T(8,128)S(1)}, f32[2,2,4,64,256]{4,3,2,1,0:T(8,128)}, u32[]{:S(2)}) copy-start(f32[2,2,4,64,256]{4,3,2,1,0:T(8,128)} %get-tuple-element.30) | copy-start | bytes 3145732
  168.6 32.5 %collective-permute-start.38 = (bf16[2,2,32,4096]{3,2,1,0:T(8,128)(2,1)}, bf16[2,2,32,4096]{3,2,1,0:T(8,128)(2,1)S(1)}, u32[]{:S(2)}, u32[]{:S(2)}) collective-permute-start(bf16[2,2,32,4096]{3,2,1,0:T(8,128)(2,1)} %get-tuple-element.37), channel_id=1, source_target_pairs={{0,1},{1,0},{2,3},{3,2},{4,5},{5,4},{6,7},{7,6},{8,9},{9,8},{10,11... | collective-permute-start | bytes 3145736 | tf_op jit(solution)/shard_map/ppermute | solution.py:23
  170.3 6.9 %copy-start.3 = (bf16[2,2,256,256]{3,2,1,0:T(8,128)(2,1)S(1)}, bf16[2,2,256,256]{3,2,1,0:T(8,128)(2,1)}, u32[]{:S(2)}) copy-start(bf16[2,2,256,256]{3,2,1,0:T(8,128)(2,1)} %pad_maximum_fusion.refs_4_.refs_2_) | copy-start | bytes 1572868
  170.3 11.0 %collective-permute-start.25 = (bf16[1,2,4,64,256]{4,3,2,1,0:T(8,128)(2,1)S(1)}, bf16[1,2,4,64,256]{4,3,2,1,0:T(8,128)(2,1)S(1)}, u32[]{:S(2)}, u32[]{:S(2)}) collective-permute-start(bf16[1,2,4,64,256]{4,3,2,1,0:T(8,128)(2,1)S(1)} %get-tuple-element.48), channel_id=1, source_target_pairs={{0,2},{1,3},{2,0},{3,1},{4,6},{5,7},{6,4},{7,5},{8,10},{9,11},{10,... | collective-permute-start | bytes 786440 | tf_op jit(solution)/shard_map/ppermute | solution.py:23
  170.9 14.2 %copy-start.13 = (f32[2,2,5,64,256]{4,3,2,1,0:T(8,128)S(1)}, f32[2,2,5,64,256]{4,3,2,1,0:T(8,128)}, u32[]{:S(2)}) copy-start(f32[2,2,5,64,256]{4,3,2,1,0:T(8,128)} %get-tuple-element.32) | copy-start | bytes 3932164
  171.7 14.7 %copy-start.10 = (f32[2,2,16,64,256]{4,3,2,1,0:T(8,128)S(1)}, f32[2,2,16,64,256]{4,3,2,1,0:T(8,128)}, u32[]{:S(2)}) copy-start(f32[2,2,16,64,256]{4,3,2,1,0:T(8,128)} %get-tuple-element.34) | copy-start | bytes 12582916
  177.2 14.8 %collective-permute-start.8 = (bf16[2,2,256,256]{3,2,1,0:T(8,128)(2,1)S(1)}, bf16[2,2,256,256]{3,2,1,0:T(8,128)(2,1)S(1)}, u32[]{:S(2)}, u32[]{:S(2)}) collective-permute-start(bf16[2,2,256,256]{3,2,1,0:T(8,128)(2,1)S(1)} %copy-done.3), channel_id=1, source_target_pairs={{0,16},{16,0},{1,17},{17,1},{2,18},{18,2},{3,19},{19,3},{4,20},{20... | collective-permute-start | bytes 1572872 | tf_op jit(solution)/shard_map/ppermute | solution.py:23
  181.4 10.7 %collective-permute-start.10 = (bf16[2,2,256,256]{3,2,1,0:T(8,128)(2,1)S(1)}, bf16[2,2,256,256]{3,2,1,0:T(8,128)(2,1)S(1)}, u32[]{:S(2)}, u32[]{:S(2)}) collective-permute-start(bf16[2,2,256,256]{3,2,1,0:T(8,128)(2,1)S(1)} %copy-done.3), channel_id=1, source_target_pairs={{0,1},{1,0},{2,3},{3,2},{4,5},{5,4},{6,7},{7,6},{8,9},{9,8},{10,11... | collective-permute-start | bytes 1572872 | tf_op jit(solution)/shard_map/ppermute | solution.py:23
  181.4 18.3 %collective-permute-start.9 = (bf16[2,2,256,256]{3,2,1,0:T(8,128)(2,1)}, bf16[2,2,256,256]{3,2,1,0:T(8,128)(2,1)S(1)}, u32[]{:S(2)}, u32[]{:S(2)}) collective-permute-start(bf16[2,2,256,256]{3,2,1,0:T(8,128)(2,1)} %collective-permute-done.7.refs_5_.refs_3_), channel_id=1, source_target_pairs={{0,16},{16,0},{1,17},{17,1},{2,18},{18,2},{3,19},{19,3},{4,20},{20... | collective-permute-start | bytes 1572872 | tf_op jit(solution)/shard_map/ppermute | solution.py:23
  183.7 17.5 %collective-permute-start.28 = (bf16[1,2,4,64,256]{4,3,2,1,0:T(8,128)(2,1)S(1)}, bf16[1,2,4,64,256]{4,3,2,1,0:T(8,128)(2,1)S(1)}, u32[]{:S(2)}, u32[]{:S(2)}) collective-permute-start(bf16[1,2,4,64,256]{4,3,2,1,0:T(8,128)(2,1)S(1)} %get-tuple-element.46), channel_id=1, source_target_pairs={{0,2},{1,3},{2,0},{3,1},{4,6},{5,7},{6,4},{7,5},{8,10},{9,11},{10,... | collective-permute-start | bytes 786440 | tf_op jit(solution)/shard_map/ppermute | solution.py:23
  186.4 15.3 %copy-start.11 = (f32[2,2,32,4096]{3,2,1,0:T(8,128)S(1)}, f32[2,2,32,4096]{3,2,1,0:T(8,128)}, u32[]{:S(2)}) copy-start(f32[2,2,32,4096]{3,2,1,0:T(8,128)} %get-tuple-element.36) | copy-start | bytes 6291460
  192.0 11.0 %copy-start.4 = (bf16[2,2,256,256]{3,2,1,0:T(8,128)(2,1)}, bf16[2,2,256,256]{3,2,1,0:T(8,128)(2,1)S(1)}, u32[]{:S(2)}) copy-start(bf16[2,2,256,256]{3,2,1,0:T(8,128)(2,1)S(1)} %collective-permute-done.8.refs_6_.refs_4_) | copy-start | bytes 1572868
  192.0 21.0 %collective-permute-start.11 = (bf16[2,2,256,256]{3,2,1,0:T(8,128)(2,1)}, bf16[2,2,256,256]{3,2,1,0:T(8,128)(2,1)S(1)}, u32[]{:S(2)}, u32[]{:S(2)}) collective-permute-start(bf16[2,2,256,256]{3,2,1,0:T(8,128)(2,1)} %collective-permute-done.7.refs_5_.refs_3_), channel_id=1, source_target_pairs={{0,1},{1,0},{2,3},{3,2},{4,5},{5,4},{6,7},{7,6},{8,9},{9,8},{10,11... | collective-permute-start | bytes 1572872 | tf_op jit(solution)/shard_map/ppermute | solution.py:23
  192.0 11.0 %copy-start.5 = (bf16[2,2,256,256]{3,2,1,0:T(8,128)(2,1)}, bf16[2,2,256,256]{3,2,1,0:T(8,128)(2,1)S(1)}, u32[]{:S(2)}) copy-start(bf16[2,2,256,256]{3,2,1,0:T(8,128)(2,1)S(1)} %collective-permute-done.10.refs_8_.refs_6_) | copy-start | bytes 1572868
  192.0 21.0 %collective-permute-start.12 = (bf16[2,2,256,256]{3,2,1,0:T(8,128)(2,1)S(1)}, bf16[2,2,256,256]{3,2,1,0:T(8,128)(2,1)S(1)}, u32[]{:S(2)}, u32[]{:S(2)}) collective-permute-start(bf16[2,2,256,256]{3,2,1,0:T(8,128)(2,1)S(1)} %collective-permute-done.8.refs_6_.refs_4_), channel_id=1, source_target_pairs={{0,1},{1,0},{2,3},{3,2},{4,5},{5,4},{6,7},{7,6},{8,9},{9,8},{10,11... | collective-permute-start | bytes 1572872 | tf_op jit(solution)/shard_map/ppermute | solution.py:23
  199.6 3.4 %copy-start.6 = (bf16[2,2,256,256]{3,2,1,0:T(8,128)(2,1)}, bf16[2,2,256,256]{3,2,1,0:T(8,128)(2,1)S(1)}, u32[]{:S(2)}) copy-start(bf16[2,2,256,256]{3,2,1,0:T(8,128)(2,1)S(1)} %collective-permute-done.9.refs_7_.refs_5_) | copy-start | bytes 1572868
  199.6 9.3 %collective-permute-start.31 = (bf16[1,2,5,64,256]{4,3,2,1,0:T(8,128)(2,1)S(1)}, bf16[1,2,5,64,256]{4,3,2,1,0:T(8,128)(2,1)S(1)}, u32[]{:S(2)}, u32[]{:S(2)}) collective-permute-start(bf16[1,2,5,64,256]{4,3,2,1,0:T(8,128)(2,1)S(1)} %get-tuple-element.42), channel_id=1, source_target_pairs={{0,2},{1,3},{2,0},{3,1},{4,6},{5,7},{6,4},{7,5},{8,10},{9,11},{10,... | collective-permute-start | bytes 983048 | tf_op jit(solution)/shard_map/ppermute | solution.py:23
  201.1 13.9 %collective-permute-start.13 = (bf16[2,2,256,256]{3,2,1,0:T(8,128)(2,1)S(1)}, bf16[2,2,256,256]{3,2,1,0:T(8,128)(2,1)S(1)}, u32[]{:S(2)}, u32[]{:S(2)}) collective-permute-start(bf16[2,2,256,256]{3,2,1,0:T(8,128)(2,1)S(1)} %collective-permute-done.9.refs_7_.refs_5_), channel_id=1, source_target_pairs={{0,1},{1,0},{2,3},{3,2},{4,5},{5,4},{6,7},{7,6},{8,9},{9,8},{10,11... | collective-permute-start | bytes 1572872 | tf_op jit(solution)/shard_map/ppermute | solution.py:23
  201.1 39.4 %collective-permute-start.37 = (bf16[1,2,16,64,256]{4,3,2,1,0:T(8,128)(2,1)}, bf16[1,2,16,64,256]{4,3,2,1,0:T(8,128)(2,1)}, u32[]{:S(2)}, u32[]{:S(2)}) collective-permute-start(bf16[1,2,16,64,256]{4,3,2,1,0:T(8,128)(2,1)} %get-tuple-element.38), channel_id=1, source_target_pairs={{0,2},{1,3},{2,0},{3,1},{4,6},{5,7},{6,4},{7,5},{8,10},{9,11},{10,... | collective-permute-start | bytes 3145736 | tf_op jit(solution)/shard_map/ppermute | solution.py:23
  209.0 31.5 %collective-permute-start.39 = (bf16[1,2,32,4096]{3,2,1,0:T(8,128)(2,1)}, bf16[1,2,32,4096]{3,2,1,0:T(8,128)(2,1)}, u32[]{:S(2)}, u32[]{:S(2)}) collective-permute-start(bf16[1,2,32,4096]{3,2,1,0:T(8,128)(2,1)} %get-tuple-element.40), channel_id=1, source_target_pairs={{0,2},{1,3},{2,0},{3,1},{4,6},{5,7},{6,4},{7,5},{8,10},{9,11},{10,... | collective-permute-start | bytes 1572872 | tf_op jit(solution)/shard_map/ppermute | solution.py:23
  213.0 2.0 copy-start.7
  213.0 21.0 %collective-permute-start.26 = (bf16[4,64,256]{2,1,0:T(8,128)(2,1)}, bf16[4,64,256]{2,1,0:T(8,128)(2,1)}, u32[]{:S(2)}, u32[]{:S(2)}) collective-permute-start(bf16[4,64,256]{2,1,0:T(8,128)(2,1)} %get-tuple-element.57), channel_id=1, source_target_pairs={{0,4},{4,0},{8,12},{12,8},{1,5},{5,1},{9,13},{13,9},{2,6},{6,2},{1... | collective-permute-start | bytes 393224 | tf_op jit(solution)/shard_map/ppermute | solution.py:23
  213.0 2.0 copy-start.8
  213.1 22.9 %collective-permute-start.29 = (bf16[4,64,256]{2,1,0:T(8,128)(2,1)}, bf16[4,64,256]{2,1,0:T(8,128)(2,1)}, u32[]{:S(2)}, u32[]{:S(2)}) collective-permute-start(bf16[4,64,256]{2,1,0:T(8,128)(2,1)} %get-tuple-element.55), channel_id=1, source_target_pairs={{0,4},{4,0},{8,12},{12,8},{1,5},{5,1},{9,13},{13,9},{2,6},{6,2},{1... | collective-permute-start | bytes 393224 | tf_op jit(solution)/shard_map/ppermute | solution.py:23
  215.1 0.8 copy-start.9
  215.9 20.8 %collective-permute-start.33 = (bf16[4,64,256]{2,1,0:T(8,128)(2,1)}, bf16[4,64,256]{2,1,0:T(8,128)(2,1)}, u32[]{:S(2)}, u32[]{:S(2)}) collective-permute-start(bf16[4,64,256]{2,1,0:T(8,128)(2,1)} %get-tuple-element.56), channel_id=1, source_target_pairs={{0,8},{4,12},{8,0},{12,4},{1,9},{5,13},{9,1},{13,5},{2,10},{6,14},... | collective-permute-start | bytes 393224 | tf_op jit(solution)/shard_map/ppermute | solution.py:23
  234.0 21.7 %collective-permute-start.22 = (bf16[3,64,256]{2,1,0:T(8,128)(2,1)}, bf16[3,64,256]{2,1,0:T(8,128)(2,1)}, u32[]{:S(2)}, u32[]{:S(2)}) collective-permute-start(bf16[3,64,256]{2,1,0:T(8,128)(2,1)} %get-tuple-element.59), channel_id=1, source_target_pairs={{0,4},{4,0},{8,12},{12,8},{1,5},{5,1},{9,13},{13,9},{2,6},{6,2},{1... | collective-permute-start | bytes 294920 | tf_op jit(solution)/shard_map/ppermute | solution.py:23
  235.9 19.8 %collective-permute-start.23 = (bf16[3,64,256]{2,1,0:T(8,128)(2,1)}, bf16[3,64,256]{2,1,0:T(8,128)(2,1)}, u32[]{:S(2)}, u32[]{:S(2)}) collective-permute-start(bf16[3,64,256]{2,1,0:T(8,128)(2,1)} %get-tuple-element.58), channel_id=1, source_target_pairs={{0,8},{4,12},{8,0},{12,4},{1,9},{5,13},{9,1},{13,5},{2,10},{6,14},... | collective-permute-start | bytes 294920 | tf_op jit(solution)/shard_map/ppermute | solution.py:23
  236.6 14.3 %collective-permute-start.34 = (bf16[4,64,256]{2,1,0:T(8,128)(2,1)}, bf16[4,64,256]{2,1,0:T(8,128)(2,1)}, u32[]{:S(2)}, u32[]{:S(2)}) collective-permute-start(bf16[4,64,256]{2,1,0:T(8,128)(2,1)} %get-tuple-element.54), channel_id=1, source_target_pairs={{0,8},{4,12},{8,0},{12,4},{1,9},{5,13},{9,1},{13,5},{2,10},{6,14},... | collective-permute-start | bytes 393224 | tf_op jit(solution)/shard_map/ppermute | solution.py:23
  240.5 10.4 %collective-permute-start.32 = (bf16[5,64,256]{2,1,0:T(8,128)(2,1)}, bf16[5,64,256]{2,1,0:T(8,128)(2,1)}, u32[]{:S(2)}, u32[]{:S(2)}) collective-permute-start(bf16[5,64,256]{2,1,0:T(8,128)(2,1)} %get-tuple-element.53), channel_id=1, source_target_pairs={{0,4},{4,0},{8,12},{12,8},{1,5},{5,1},{9,13},{13,9},{2,6},{6,2},{1... | collective-permute-start | bytes 491528 | tf_op jit(solution)/shard_map/ppermute | solution.py:23
  240.5 12.1 %collective-permute-start.35 = (bf16[5,64,256]{2,1,0:T(8,128)(2,1)}, bf16[5,64,256]{2,1,0:T(8,128)(2,1)}, u32[]{:S(2)}, u32[]{:S(2)}) collective-permute-start(bf16[5,64,256]{2,1,0:T(8,128)(2,1)} %get-tuple-element.52), channel_id=1, source_target_pairs={{0,8},{4,12},{8,0},{12,4},{1,9},{5,13},{9,1},{13,5},{2,10},{6,14},... | collective-permute-start | bytes 491528 | tf_op jit(solution)/shard_map/ppermute | solution.py:23

commit v6 on v5

--- a/solution.py
+++ b/solution.py
@@ -112,17 +112,43 @@
     )(bit, cotangent, *features)
 
 
-def low_body(part, bit_ref, b_ref, f_ref, c_ref, g_ref, send_ref, keep_ref, acc_ref):
+def low_body(part, step, bit_ref, b_ref, f_ref, c_ref, g_ref, send_ref, keep_ref, *refs):
+    f_buf, g_buf, send_buf, keep_buf, in_sems, out_sems = refs
     bit = bit_ref[0]
-    for slot, (small, wide) in enumerate(((b_ref, f_ref), (c_ref, g_ref))):
-        acc_ref[...] = lax.dot_general(
-            small[...], wide[...], (((0,), (0,)), ((), ())), preferred_element_type=F32
+    groups = f_buf.shape[1] // step
+    loads, stores = [], []
+    for group in range(groups):
+        cols = pl.ds(group * step, step)
+        loads.append(
+            [
+                pltpu.make_async_copy(ref.at[:, cols], buf.at[:, cols], in_sems.at[group, one])
+                for one, (ref, buf) in enumerate(((f_ref, f_buf), (g_ref, g_buf)))
+            ]
         )
-        for half in range(send_ref.shape[0]):
-            first = pl.multiple_of((2 * half + bit) * part, part)
-            other = pl.multiple_of((2 * half + 1 - bit) * part, part)
-            keep_ref[half, slot] = acc_ref[pl.ds(first, part), :]
-            send_ref[half, slot] = acc_ref[pl.ds(other, part), :].astype(BF16)
+    for copies in loads:
+        for copy in copies:
+            copy.start()
+    for group in range(groups):
+        cols = slice(group * step, (group + 1) * step)
+        for slot, (small, wide) in enumerate(((b_ref, f_buf), (c_ref, g_buf))):
+            loads[group][slot].wait()
+            total = lax.dot_general(
+                small[...], wide[:, cols], (((0,), (0,)), ((), ())), preferred_element_type=F32
+            )
+            for half in range(send_ref.shape[0]):
+                low = total[2 * half * part : (2 * half + 1) * part]
+                high = total[(2 * half + 1) * part : (2 * half + 2) * part]
+                keep_buf[half, slot, :, cols] = jnp.where(bit == 0, low, high)
+                send_buf[half, slot, :, cols] = jnp.where(bit == 0, high, low).astype(BF16)
+        span = pl.ds(group * step, step)
+        for which, (buf, ref) in enumerate(((send_buf, send_ref), (keep_buf, keep_ref))):
+            copy = pltpu.make_async_copy(
+                buf.at[:, :, :, span], ref.at[:, :, :, span], out_sems.at[group, which]
+            )
+            copy.start()
+            stores.append(copy)
+    for copy in stores:
+        copy.wait()
 
 
 def low_kernel(bit, backs, features, codes, cotangent, parts):
@@ -130,19 +156,20 @@
     rank = codes.shape[1]
     part = rank // parts
     step = min(1024, width)
-    out_spec = pl.BlockSpec((parts // 2, 2, part, step), lambda at, bit_ref: (0, 0, 0, at))
     shape = (parts // 2, 2, part, width)
-    wide = pl.BlockSpec((rows_here, step), lambda at, bit_ref: (0, at))
-    small = pl.BlockSpec((rows_here, rank), lambda at, bit_ref: (0, 0))
+    hbm, vmem = pl.BlockSpec(memory_space=pltpu.HBM), pl.BlockSpec(memory_space=pltpu.VMEM)
     return pl.pallas_call(
-        functools.partial(low_body, part),
-        grid_spec=pltpu.PrefetchScalarGridSpec(
-            num_scalar_prefetch=1,
-            grid=(width // step,),
-            in_specs=[small, wide, small, wide],
-            out_specs=(out_spec, out_spec),
-            scratch_shapes=[pltpu.VMEM((rank, step), F32)],
-        ),
+        functools.partial(low_body, part, step),
+        in_specs=[pl.BlockSpec(memory_space=pltpu.SMEM), vmem, hbm, vmem, hbm],
+        out_specs=(hbm, hbm),
+        scratch_shapes=[
+            pltpu.VMEM((rows_here, width), BF16),
+            pltpu.VMEM((rows_here, width), BF16),
+            pltpu.VMEM(shape, BF16),
+            pltpu.VMEM(shape, F32),
+            pltpu.SemaphoreType.DMA((width // step, 2)),
+            pltpu.SemaphoreType.DMA((width // step, 2)),
+        ],
         out_shape=(jax.ShapeDtypeStruct(shape, BF16), jax.ShapeDtypeStruct(shape, F32)),
         compiler_params=pltpu.CompilerParams(vmem_limit_bytes=VMEM_LIMIT),
         cost_estimate=pl.CostEstimate(
@@ -223,16 +250,18 @@
     gathered = []
     for way in range(2):
         for slot, apart in enumerate(order):
-            for one in range(units):
-                number = (item ^ apart) * units + one
-                block, piece = lax.div(number, pieces), lax.rem(number, pieces)
-                rows = pl.ds(pl.multiple_of(piece * unit, unit), unit)
-                copy = pltpu.make_async_copy(
-                    far_w[slot].at[way, one],
-                    w_buf.at[2 + way, block, rows, :],
-                    far_w_sems.at[way, number],
-                )
-                gathered.append(((block >= first_col) & (block < last_col), copy))
+            owner = item ^ apart
+            source = far_w[slot].at[way]
+            if pieces == 1:
+                block, after_block = owner * units, owner * units + units
+                into = w_buf.at[2 + way, pl.ds(block, units)]
+            else:
+                block = lax.div(owner, pieces)
+                after_block = block + 1
+                rows = pl.ds(pl.multiple_of(lax.rem(owner, pieces) * unit, unit), unit)
+                into = w_buf.at[2 + way, pl.ds(block, 1), rows, :]
+            copy = pltpu.make_async_copy(source, into, far_w_sems.at[way, owner])
+            gathered.append(((after_block > first_col) & (block < last_col), copy))
     loads = []
     for step in range(steps):
         chunk = first + step
@@ -267,16 +296,13 @@
         for copy in copies:
             copy.start()
     for way in range(2):
-        for at in range(first_col, last_col):
-            for piece in range(pieces):
-                rows = pl.ds(piece * unit, unit)
-                loads[[starts[one] <= at < starts[one] + sizes[one] for one in range(first, last)].index(True)].append(
-                    pltpu.make_async_copy(
-                        far_w[0].at[way, 0],
-                        w_buf.at[2 + way, at, rows, :],
-                        far_w_sems.at[way, at * pieces + piece],
-                    )
-                )
+        for owner in range(first_col * pieces // units, -(-last_col * pieces // units)):
+            block = max(owner * units // pieces, first_col)
+            rows = pl.ds(owner % pieces * unit, unit)
+            into = w_buf.at[2 + way, pl.ds(owner * units // pieces, units), rows, :]
+            copy = pltpu.make_async_copy(far_w[0].at[way], into, far_w_sems.at[way, owner])
+            step = [starts[one] <= block < starts[one] + sizes[one] for one in range(first, last)]
+            loads[step.index(True)].append(copy)
     stores = []
     for step in range(steps):
         chunk = first + step
@@ -329,7 +355,7 @@
             pltpu.VMEM((rows_here, width), BF16),
             pltpu.SemaphoreType.DMA((last - first, 4)),
             pltpu.SemaphoreType.DMA((2, share)),
-            pltpu.SemaphoreType.DMA((2, len(order) * units)),
+            pltpu.SemaphoreType.DMA((2, len(order))),
             pltpu.SemaphoreType.DMA((last - first,)),
         ],
         compiler_params=pltpu.CompilerParams(vmem_limit_bytes=VMEM_LIMIT),
@@ -508,7 +534,7 @@
     low = [keep[way] + came[way].astype(F32) for way in range(2)]
 
     mixed = None
-    cuts = [0, *range(max(1, chunks - 2), chunks + 1)]
+    cuts = [0, max(1, chunks - 1), chunks]
     for first, last in zip(cuts, cuts[1:]):
         mixed = mixed_kernel(
             features,

time: 259 us -> 256 us (0.988)
  Pallas kernels: 51.8 us -> 47.7 us
    pallas_call x3 -> x2, Pallas kernels: 17.6 us -> 13.5 us  [mixed_kernel(): pl.pallas_call(functools.partial(mixed_body, share, sizes, first, last, u...]
  transfers between devices with their start and end apart: 40 -> 40, of which waited for: 14 -> 12; matrix products, arithmetic and copies ran while one was open for 12% -> 12% of each run, Pallas kernels for 19% -> 18%
where the time goes in v6:
time: 256 us; the launch traced here: 255 us
  waiting for transfers between devices  127 us (50%)
  Pallas kernels  47.7 us (19%)
  starting transfers between devices  42.7 us (17%)
  other arithmetic  23.6 us (9%)
  local copies, waits for them, and re-layouts  9.32 us (4%)
  matrix products  3.41 us (1%)
    ppermute x40, waiting for transfers between devices, swapped(): lax.ppermute(block, axis, [(one, one ^ 1 << apart) for one in range(count)])  127 us
    ppermute x40, starting transfers between devices, swapped(): lax.ppermute(block, axis, [(one, one ^ 1 << apart) for one in range(count)])  42.7 us
    pallas_call x5, Pallas kernels, pair_grads(): pl.pallas_call(functools.partial(grad_body, pairs, part, first, step), in...  16.8 us
    pallas_call x2, Pallas kernels, mixed_kernel(): pl.pallas_call(functools.partial(mixed_body, share, sizes, first, last, u...  13.5 us
    convert_element_type x6, other arithmetic, items_sum(): came = swapped(leave.astype(BF16), 'items', level)  11.6 us
    pallas_call x3, Pallas kernels, place_kernel(): pl.pallas_call(functools.partial(place_body, keys, pairs), in_specs=[pl.B...  9.76 us
    slice x4, local copies, waits for them, and re-layouts, layer(): piece = source[:, first:first + sizes[one] * BLOCK]  5.46 us
  transfers between devices with their start and end apart: 40, of which 12 were waited for; matrix products, arithmetic and copies ran while one was open for 12% of the time, Pallas kernels for 18%

profile of v6, /device:TPU:0, one launch (start us, length us, event | category | flops | bytes accessed | tf_op | source)
XLA Modules:
  0.0 255.4 jit_solution(18067229577064972522)
XLA Ops:
  0.7 2.7 %fusion.28 = f32[256,128]{1,0:T(8,128)S(1)} fusion(bf16[256,4096]{1,0:T(8,128)(2,1)} %f_ref.5, bf16[128,4096]{1,0:T(8,128)(2,1)} %param.12), kind=kOutput, calls=%fused_computation.67 | convolution fusion | flops 268435456 | bytes 3276800 | tf_op jit(solution)/shard_map/dot_general | solution.py:484
  4.8 3.1 %collective-permute-start = (f32[2,128,128]{2,1,0:T(8,128)}, f32[2,128,128]{2,1,0:T(8,128)}, u32[]{:S(2)}, u32[]{:S(2)}) collective-permute-start(f32[2,128,128]{2,1,0:T(8,128)} %fusion.17), channel_id=1, source_target_pairs={{0,4},{4,0},{8,12},{12,8},{1,5},{5,1},{9,13},{13,9},{2,6},{6,2},{1... | collective-permute-start | bytes 393224 | tf_op jit(solution)/shard_map/ppermute | solution.py:23
  8.6 2.6 %weight_share.1 = (bf16[2,256,256]{2,1,0:T(8,128)(2,1)}, bf16[2,256,256]{2,1,0:T(8,128)(2,1)}) custom-call(s32[64]{0:T(128)} %select_reduce_fusion.pos_ref, s32[1]{0:T(128)} %bitcast.item_ref, bf16[64,256,256]{2,1,0:T(8,128)(2,1)} %w_ref.5), custom_call_target="tpu_custom_call" | custom-call | bytes 1048576 | tf_op jit(solution)/shard_map/weight_share/pallas_call | solution.py:220
  11.2 2.7 %collective-permute-start.6 = (bf16[2,256,256]{2,1,0:T(8,128)(2,1)}, bf16[2,256,256]{2,1,0:T(8,128)(2,1)S(1)}, u32[]{:S(2)}, u32[]{:S(2)}) collective-permute-start(bf16[2,256,256]{2,1,0:T(8,128)(2,1)} %get-tuple-element.25), channel_id=1, source_target_pairs={{0,8},{4,12},{8,0},{12,4},{1,9},{5,13},{9,1},{13,5},{2,10},{6,14},... | collective-permute-start | bytes 786440 | tf_op jit(solution)/shard_map/ppermute | solution.py:23
  13.8 1.0 fusion.20
  15.5 1.6 collective-permute-start.5
  17.1 1.9 slice.99
  18.9 1.9 slice.100
  20.8 0.9 slice.101
  21.8 0.8 slice.102
  23.0 2.3 collective-permute-start.4
  25.3 6.1 %collective-permute-done.1 = f32[2,128,128]{2,1,0:T(8,128)S(1)} collective-permute-done((f32[2,128,128]{2,1,0:T(8,128)S(1)}, f32[2,128,128]{2,1,0:T(8,128)S(1)}, u32[]{:S(2)}, u32[]{:S(2)}) %collective-permute-start.1) | collective-permute-done | bytes 131104 | tf_op jit(solution)/shard_map/ppermute | solution.py:23
  31.4 0.8 collective-permute-start.14
  32.2 1.2 collective-permute-start.15
  34.8 0.8 collective-permute-start.2
  35.6 5.0 %pair_grads.9 = (bf16[2,2,16,64,256]{4,3,2,1,0:T(8,128)(2,1)}, f32[2,2,16,64,256]{4,3,2,1,0:T(8,128)}) custom-call(s32[1]{0:T(128)} %bitcast.10.bit_ref, bf16[256,4096]{1,0:T(8,128)(2,1)} %g_ref.11, bf16[256,4096]{1,0:T(8,128)(2,1)} %f_ref.5), custom_call_target="tpu_custom_call" | custom-call | flops 1073741824 | bytes 12582912 | tf_op jit(solution)/shard_map/pair_grads/pallas_call | solution.py:93
  40.7 31.3 %collective-permute-done.2 = bf16[2,128,128]{2,1,0:T(8,128)(2,1)} collective-permute-done((bf16[2,128,128]{2,1,0:T(8,128)(2,1)}, bf16[2,128,128]{2,1,0:T(8,128)(2,1)}, u32[]{:S(2)}, u32[]{:S(2)}) %collective-permute-start.2) | collective-permute-done | bytes 65568 | tf_op jit(solution)/shard_map/ppermute | solution.py:23
  72.0 2.9 %collective-permute-start.18 = (bf16[256,1024]{1,0:T(8,128)(2,1)}, bf16[256,1024]{1,0:T(8,128)(2,1)}, u32[]{:S(2)}, u32[]{:S(2)}) collective-permute-start(bf16[256,1024]{1,0:T(8,128)(2,1)} %slice.100), channel_id=1, source_target_pairs={{0,8},{4,12},{8,0},{12,4},{1,9},{5,13},{9,1},{13,5},{2,10},{6,14},... | collective-permute-start | bytes 1572872 | tf_op jit(solution)/shard_map/ppermute | solution.py:23
  74.9 2.5 collective-permute-start.19
  77.4 2.8 %pair_grads.5 = (bf16[2,2,3,64,256]{4,3,2,1,0:T(8,128)(2,1)}, f32[2,2,3,64,256]{4,3,2,1,0:T(8,128)}) custom-call(s32[1]{0:T(128)} %bitcast.10.bit_ref, bf16[256,4096]{1,0:T(8,128)(2,1)} %g_ref.11, bf16[256,768]{1,0:T(8,128)(2,1)} %collective-permute-done.3.refs_0_, bf16[256,768]{1,0:T(8,128)(2,1)} %collective-permute-done.4.refs_1_), custom_call_target="tpu_custom_call" | custom-call | flops 201326592 | bytes 2359296 | tf_op jit(solution)/shard_map/pair_grads/pallas_call | solution.py:93
  80.2 29.2 %collective-permute-done.17.refs_3_.refs_1_ = bf16[256,1024]{1,0:T(8,128)(2,1)} collective-permute-done((bf16[256,1024]{1,0:T(8,128)(2,1)}, bf16[256,1024]{1,0:T(8,128)(2,1)}, u32[]{:S(2)}, u32[]{:S(2)}) %collective-permute-start.17) | collective-permute-done | bytes 524320 | tf_op jit(solution)/shard_map/ppermute | solution.py:23
  109.3 1.9 pad_maximum_fusion.refs_6_.refs_2_
  111.2 2.8 %pair_grads.6 = (bf16[2,2,4,64,256]{4,3,2,1,0:T(8,128)(2,1)}, f32[2,2,4,64,256]{4,3,2,1,0:T(8,128)}) custom-call(s32[1]{0:T(128)} %bitcast.10.bit_ref, bf16[256,4096]{1,0:T(8,128)(2,1)} %g_ref.11, bf16[256,1024]{1,0:T(8,128)(2,1)} %collective-permute-done.14.refs_0_, bf16[256,1024]{1,0:T(8,128)(2,1)} %collective-permute-done.17.refs_3_.refs_1_), custom_call_target="tpu_custom_call" | custom-call | flops 268435456 | bytes 3145728 | tf_op jit(solution)/shard_map/pair_grads/pallas_call | solution.py:93
  114.0 20.5 %collective-permute-done.18.refs_4_.refs_1_ = bf16[256,1024]{1,0:T(8,128)(2,1)} collective-permute-done((bf16[256,1024]{1,0:T(8,128)(2,1)}, bf16[256,1024]{1,0:T(8,128)(2,1)}, u32[]{:S(2)}, u32[]{:S(2)}) %collective-permute-start.18) | collective-permute-done | bytes 524320 | tf_op jit(solution)/shard_map/ppermute | solution.py:23
  134.6 1.6 maximum_select_fusion
  136.2 2.8 %pair_grads.7 = (bf16[2,2,4,64,256]{4,3,2,1,0:T(8,128)(2,1)}, f32[2,2,4,64,256]{4,3,2,1,0:T(8,128)}) custom-call(s32[1]{0:T(128)} %bitcast.10.bit_ref, bf16[256,4096]{1,0:T(8,128)(2,1)} %g_ref.11, bf16[256,1024]{1,0:T(8,128)(2,1)} %collective-permute-done.15.refs_1_.refs_0_, bf16[256,1024]{1,0:T(8,128)(2,1)} %collective-permute-done.18.refs_4_.refs_1_), custom_call_target="tpu_custom_call" | custom-call | flops 268435456 | bytes 3145728 | tf_op jit(solution)/shard_map/pair_grads/pallas_call | solution.py:93
  139.6 9.0 %collective-permute-done.19.refs_5_.refs_1_ = bf16[256,1280]{1,0:T(8,128)(2,1)} collective-permute-done((bf16[256,1280]{1,0:T(8,128)(2,1)}, bf16[256,1280]{1,0:T(8,128)(2,1)}, u32[]{:S(2)}, u32[]{:S(2)}) %collective-permute-start.19) | collective-permute-done | bytes 655392 | tf_op jit(solution)/shard_map/ppermute | solution.py:23
  148.6 3.4 %pair_grads.8 = (bf16[2,2,5,64,256]{4,3,2,1,0:T(8,128)(2,1)}, f32[2,2,5,64,256]{4,3,2,1,0:T(8,128)}) custom-call(s32[1]{0:T(128)} %bitcast.10.bit_ref, bf16[256,4096]{1,0:T(8,128)(2,1)} %g_ref.11, bf16[256,1280]{1,0:T(8,128)(2,1)} %collective-permute-done.16.refs_2_.refs_0_, bf16[256,1280]{1,0:T(8,128)(2,1)} %collective-permute-done.19.refs_5_.refs_1_), custom_call_target="tpu_custom_call" | custom-call | flops 335544320 | bytes 3932160 | tf_op jit(solution)/shard_map/pair_grads/pallas_call | solution.py:93
  152.1 2.1 add_convert_fusion.5
  154.2 1.5 collective-permute-start.21
  155.7 1.6 slice_bitcast_fusion
  157.2 4.2 %collective-permute-done.21 = bf16[1,2,3,64,256]{4,3,2,1,0:T(8,128)(2,1)S(1)} collective-permute-done((bf16[1,2,3,64,256]{4,3,2,1,0:T(8,128)(2,1)S(1)}, bf16[1,2,3,64,256]{4,3,2,1,0:T(8,128)(2,1)S(1)}, u32[]{:S(2)}, u32[]{:S(2)}) %collective-permute-start.21) | collective-permute-done | bytes 196640 | tf_op jit(solution)/shard_map/ppermute | solution.py:23
  162.1 1.5 collective-permute-start.7
  163.6 5.0 %low_grads.1 = (bf16[2,2,32,4096]{3,2,1,0:T(8,128)(2,1)}, f32[2,2,32,4096]{3,2,1,0:T(8,128)}) custom-call(s32[1]{0:T(128)} %bitcast.10.bit_ref, bf16[256,128]{1,0:T(8,128)(2,1)} %get-tuple-element.60.b_ref, bf16[256,4096]{1,0:T(8,128)(2,1)} %f_ref.5, bf16[256,128]{1,0:T(8,128)(2,1)} %get-tuple-element.61.codes_ref.c_ref, bf16[256,4096]{1,0:T(8,128)(2,1)} %g_ref.11), custom_call_target="tpu_custom_call" | custom-call | flops 536870912 | bytes 7340032 | tf_op jit(solution)/shard_map/low_grads/pallas_call | solution.py:161
  168.8 1.6 add_convert_fusion.4
  171.7 1.3 add_convert_fusion.3
  173.0 4.2 %collective-permute-done.7.refs_7_.refs_3_ = bf16[2,2,256,256]{3,2,1,0:T(8,128)(2,1)} collective-permute-done((bf16[2,2,256,256]{3,2,1,0:T(8,128)(2,1)}, bf16[2,2,256,256]{3,2,1,0:T(8,128)(2,1)}, u32[]{:S(2)}, u32[]{:S(2)}) %collective-permute-start.7) | collective-permute-done | bytes 524320 | tf_op jit(solution)/shard_map/ppermute | solution.py:23
  177.2 1.5 collective-permute-start.8
  178.7 2.6 %collective-permute-done.25 = bf16[1,2,4,64,256]{4,3,2,1,0:T(8,128)(2,1)S(1)} collective-permute-done((bf16[1,2,4,64,256]{4,3,2,1,0:T(8,128)(2,1)S(1)}, bf16[1,2,4,64,256]{4,3,2,1,0:T(8,128)(2,1)S(1)}, u32[]{:S(2)}, u32[]{:S(2)}) %collective-permute-start.25) | collective-permute-done | bytes 262176 | tf_op jit(solution)/shard_map/ppermute | solution.py:23
  181.4 1.5 collective-permute-start.9
  182.9 0.8 fusion.14
  183.7 1.5 collective-permute-start.28
  185.2 1.2 add_convert_fusion.2
  186.4 4.1 %add_convert_fusion = (bf16[1,2,16,64,256]{4,3,2,1,0:T(8,128)(2,1)}, f32[1,2,16,64,256]{4,3,2,1,0:T(8,128)}) fusion(f32[2,2,16,64,256]{4,3,2,1,0:T(8,128)S(1)} %copy-done.4, s32[]{:T(128)S(6)} %select_n.71, bf16[2,2,16,64,256]{4,3,2,1,0:T(8,128)(2,1)} %collective-permute-done.36, s32[]{:T(128)S(6)} %select_n.70), kind=kLoop, calls=%fused_computation | loop fusion | flops 2621440 | bytes 9437192 | tf_op jit(solution)/shard_map/convert_element_type | solution.py:193
  190.6 1.4 collective-permute-done.8.refs_8_.refs_4_
  192.5 7.1 %collective-permute-done.9.refs_9_.refs_5_ = bf16[2,2,256,256]{3,2,1,0:T(8,128)(2,1)S(1)} collective-permute-done((bf16[2,2,256,256]{3,2,1,0:T(8,128)(2,1)}, bf16[2,2,256,256]{3,2,1,0:T(8,128)(2,1)S(1)}, u32[]{:S(2)}, u32[]{:S(2)}) %collective-permute-start.9) | collective-permute-done | bytes 524320 | tf_op jit(solution)/shard_map/ppermute | solution.py:23
  199.6 1.5 collective-permute-start.31
  201.8 1.3 add_convert_fusion.1
  203.1 5.9 %collective-permute-done.31 = bf16[1,2,5,64,256]{4,3,2,1,0:T(8,128)(2,1)S(1)} collective-permute-done((bf16[1,2,5,64,256]{4,3,2,1,0:T(8,128)(2,1)S(1)}, bf16[1,2,5,64,256]{4,3,2,1,0:T(8,128)(2,1)S(1)}, u32[]{:S(2)}, u32[]{:S(2)}) %collective-permute-start.31) | collective-permute-done | bytes 327712 | tf_op jit(solution)/shard_map/ppermute | solution.py:23
  209.0 2.4 collective-permute-start.39
  211.4 0.8 fusion.15
  212.2 0.8 fusion.11
  213.1 2.0 collective-permute-start.29
  215.1 0.8 copy-done.11
  216.4 8.7 %mixed.2.refs_10_ = bf16[256,4096]{1,0:T(8,128)(2,1)} custom-call(s32[64]{0:T(128)} %select_reduce_fusion.pos_ref, s32[1]{0:T(128)} %bitcast.item_ref, bf16[256,4096]{1,0:T(8,128)(2,1)} %f_ref.5, bf16[64,256,256]{2,1,0:T(8,128)(2,1)} %w_ref.5, bf16[256,128]{1,0:T(8,128)(2,1)} %get-tuple-element.61.codes_ref.c_ref, bf16[128,4096]{1,0:T(8,128)(2,1)} %low_ref.3, ...), custom_call_target="tpu_custom_call" | custom-call | flops 1962934272 | bytes 13631488 | tf_op jit(solution)/shard_map/mixed/pallas_call | solution.py:343
  225.1 4.8 %mixed.3 = bf16[256,4096]{1,0:T(8,128)(2,1)} custom-call(s32[64]{0:T(128)} %select_reduce_fusion.pos_ref, s32[1]{0:T(128)} %bitcast.item_ref, bf16[256,4096]{1,0:T(8,128)(2,1)} %f_ref.5, bf16[64,256,256]{2,1,0:T(8,128)(2,1)} %w_ref.5, bf16[256,128]{1,0:T(8,128)(2,1)} %get-tuple-element.61.codes_ref.c_ref, ...), custom_call_target="tpu_custom_call", output_to_operand_aliasing={{}: (16, {})} | custom-call | flops 452984832 | bytes 3145728 | tf_op jit(solution)/shard_map/mixed/pallas_call | solution.py:343
  229.9 1.9 collective-permute-start.22
  232.6 2.2 collective-permute-start.34
  234.8 5.7 %collective-permute-done.39 = bf16[1,2,32,4096]{3,2,1,0:T(8,128)(2,1)} collective-permute-done((bf16[1,2,32,4096]{3,2,1,0:T(8,128)(2,1)}, bf16[1,2,32,4096]{3,2,1,0:T(8,128)(2,1)}, u32[]{:S(2)}, u32[]{:S(2)}) %collective-permute-start.39) | collective-permute-done | bytes 524320 | tf_op jit(solution)/shard_map/ppermute | solution.py:23
  240.5 2.4 collective-permute-start.35
  243.0 2.4 fusion
  245.4 4.3 %place.3.refs_6_ = f32[64,64,256]{2,1,0:T(8,128)} custom-call(s32[64]{0:T(128)} %select_reduce_fusion.pos_ref, f32[32,64,256]{2,1,0:T(8,128)} %bitcast.46, bf16[32,64,256]{2,1,0:T(8,128)(2,1)} %bitcast.20.refs_1_), custom_call_target="tpu_custom_call" | custom-call | bytes 4194304 | tf_op jit(solution)/shard_map/place/pallas_call | solution.py:405
  249.7 3.1 %place.4.refs_2_ = f32[64,64,256]{2,1,0:T(8,128)} custom-call(s32[64]{0:T(128)} %select_reduce_fusion.pos_ref, bf16[4,64,256]{2,1,0:T(8,128)(2,1)} %collective-permute-done.26.refs_0_, bf16[4,64,256]{2,1,0:T(8,128)(2,1)} %collective-permute-done.29.refs_1_, bf16[5,64,256]{2,1,0:T(8,128)(2,1)} %collective-permute-done.32.refs_2_, ...), custom_call_target="tpu_custom_call", output_to_operand_aliasing={{}: (7, {})} | custom-call | bytes 3407872 | tf_op jit(solution)/shard_map/place/pallas_call | solution.py:405
  252.8 2.4 place.5
  (99 shorter events, 10.0 us)
Async XLA Ops:
  0.6 2.7 %copy-start = (bf16[256,4096]{1,0:T(8,128)(2,1)S(1)}, bf16[256,4096]{1,0:T(8,128)(2,1)}, u32[]{:S(2)}) copy-start(bf16[256,4096]{1,0:T(8,128)(2,1)} %g_ref.11) | copy-start | bytes 6291460
  0.6 2.8 %copy-start.2 = (bf16[128,4096]{1,0:T(8,128)(2,1)S(1)}, bf16[128,4096]{1,0:T(8,128)(2,1)}, u32[]{:S(2)}) copy-start(bf16[128,4096]{1,0:T(8,128)(2,1)} %low_ref.3) | copy-start | bytes 3145732
  3.4 0.7 copy-start.14
  3.4 4.5 %copy-start.21 = (s32[64]{0:T(128)S(1)}, s32[64]{0:T(128)}, u32[]{:S(2)}) copy-start(s32[64]{0:T(128)} %param.11) | copy-start | bytes 772
  3.4 4.5 %copy-start.22 = (s32[64]{0:T(128)S(1)}, s32[64]{0:T(128)}, u32[]{:S(2)}) copy-start(s32[64]{0:T(128)} %param.10) | copy-start | bytes 772
  4.1 0.7 copy-start.15
  4.8 9.0 %collective-permute-start = (f32[2,128,128]{2,1,0:T(8,128)}, f32[2,128,128]{2,1,0:T(8,128)}, u32[]{:S(2)}, u32[]{:S(2)}) collective-permute-start(f32[2,128,128]{2,1,0:T(8,128)} %fusion.17), channel_id=1, source_target_pairs={{0,4},{4,0},{8,12},{12,8},{1,5},{5,1},{9,13},{13,9},{2,6},{6,2},{1... | collective-permute-start | bytes 393224 | tf_op jit(solution)/shard_map/ppermute | solution.py:23
  11.2 9.6 %copy-start.1 = (bf16[256,4096]{1,0:T(8,128)(2,1)S(1)}, bf16[256,4096]{1,0:T(8,128)(2,1)}, u32[]{:S(2)}) copy-start(bf16[256,4096]{1,0:T(8,128)(2,1)} %f_ref.5) | copy-start | bytes 6291460
  11.2 21.0 %collective-permute-start.6 = (bf16[2,256,256]{2,1,0:T(8,128)(2,1)}, bf16[2,256,256]{2,1,0:T(8,128)(2,1)S(1)}, u32[]{:S(2)}, u32[]{:S(2)}) collective-permute-start(bf16[2,256,256]{2,1,0:T(8,128)(2,1)} %get-tuple-element.25), channel_id=1, source_target_pairs={{0,8},{4,12},{8,0},{12,4},{1,9},{5,13},{9,1},{13,5},{2,10},{6,14},... | collective-permute-start | bytes 786440 | tf_op jit(solution)/shard_map/ppermute | solution.py:23
  14.8 16.6 %collective-permute-start.1 = (f32[2,128,128]{2,1,0:T(8,128)S(1)}, f32[2,128,128]{2,1,0:T(8,128)S(1)}, u32[]{:S(2)}, u32[]{:S(2)}) collective-permute-start(f32[2,128,128]{2,1,0:T(8,128)S(1)} %fusion.20), channel_id=1, source_target_pairs={{0,8},{4,12},{8,0},{12,4},{1,9},{5,13},{9,1},{13,5},{2,10},{6,14},... | collective-permute-start | bytes 393224 | tf_op jit(solution)/shard_map/ppermute | solution.py:23
  15.5 18.6 %collective-permute-start.5 = (bf16[2,256,256]{2,1,0:T(8,128)(2,1)}, bf16[2,256,256]{2,1,0:T(8,128)(2,1)S(1)}, u32[]{:S(2)}, u32[]{:S(2)}) collective-permute-start(bf16[2,256,256]{2,1,0:T(8,128)(2,1)} %get-tuple-element.24), channel_id=1, source_target_pairs={{0,4},{4,0},{8,12},{12,8},{1,5},{5,1},{9,13},{13,9},{2,6},{6,2},{1... | collective-permute-start | bytes 786440 | tf_op jit(solution)/shard_map/ppermute | solution.py:23
  22.5 49.4 %collective-permute-start.3 = (bf16[256,768]{1,0:T(8,128)(2,1)}, bf16[256,768]{1,0:T(8,128)(2,1)}, u32[]{:S(2)}, u32[]{:S(2)}) collective-permute-start(bf16[256,768]{1,0:T(8,128)(2,1)} %slice.102), channel_id=1, source_target_pairs={{0,4},{4,0},{8,12},{12,8},{1,5},{5,1},{9,13},{13,9},{2,6},{6,2},{1... | collective-permute-start | bytes 1179656 | tf_op jit(solution)/shard_map/ppermute | solution.py:23
  23.0 49.0 %collective-permute-start.4 = (bf16[256,768]{1,0:T(8,128)(2,1)}, bf16[256,768]{1,0:T(8,128)(2,1)}, u32[]{:S(2)}, u32[]{:S(2)}) collective-permute-start(bf16[256,768]{1,0:T(8,128)(2,1)} %slice.102), channel_id=1, source_target_pairs={{0,8},{4,12},{8,0},{12,4},{1,9},{5,13},{9,1},{13,5},{2,10},{6,14},... | collective-permute-start | bytes 1179656 | tf_op jit(solution)/shard_map/ppermute | solution.py:23
  31.4 43.5 %collective-permute-start.14 = (bf16[256,1024]{1,0:T(8,128)(2,1)}, bf16[256,1024]{1,0:T(8,128)(2,1)}, u32[]{:S(2)}, u32[]{:S(2)}) collective-permute-start(bf16[256,1024]{1,0:T(8,128)(2,1)} %slice.99), channel_id=1, source_target_pairs={{0,4},{4,0},{8,12},{12,8},{1,5},{5,1},{9,13},{13,9},{2,6},{6,2},{1... | collective-permute-start | bytes 1572872 | tf_op jit(solution)/shard_map/ppermute | solution.py:23
  32.2 1.9 copy-start.17
  32.2 42.7 %collective-permute-start.15 = (bf16[256,1024]{1,0:T(8,128)(2,1)}, bf16[256,1024]{1,0:T(8,128)(2,1)}, u32[]{:S(2)}, u32[]{:S(2)}) collective-permute-start(bf16[256,1024]{1,0:T(8,128)(2,1)} %slice.100), channel_id=1, source_target_pairs={{0,4},{4,0},{8,12},{12,8},{1,5},{5,1},{9,13},{13,9},{2,6},{6,2},{1... | collective-permute-start | bytes 1572872 | tf_op jit(solution)/shard_map/ppermute | solution.py:23
  34.1 0.7 copy-start.18
  34.8 37.1 %collective-permute-start.2 = (bf16[2,128,128]{2,1,0:T(8,128)(2,1)}, bf16[2,128,128]{2,1,0:T(8,128)(2,1)}, u32[]{:S(2)}, u32[]{:S(2)}) collective-permute-start(bf16[2,128,128]{2,1,0:T(8,128)(2,1)} %add_convert_fusion.6), channel_id=1, source_target_pairs={{0,4},{4,0},{8,12},{12,8},{1,5},{5,1},{9,13},{13,9},{2,6},{6,2},{1... | collective-permute-start | bytes 196616 | tf_op jit(solution)/shard_map/ppermute | solution.py:23
  71.9 111.7 %collective-permute-start.36 = (bf16[2,2,16,64,256]{4,3,2,1,0:T(8,128)(2,1)}, bf16[2,2,16,64,256]{4,3,2,1,0:T(8,128)(2,1)}, u32[]{:S(2)}, u32[]{:S(2)}) collective-permute-start(bf16[2,2,16,64,256]{4,3,2,1,0:T(8,128)(2,1)} %get-tuple-element.35), channel_id=1, source_target_pairs={{0,1},{1,0},{2,3},{3,2},{4,5},{5,4},{6,7},{7,6},{8,9},{9,8},{10,11... | collective-permute-start | bytes 6291464 | tf_op jit(solution)/shard_map/ppermute | solution.py:23
  71.9 37.4 %collective-permute-start.17 = (bf16[256,1024]{1,0:T(8,128)(2,1)}, bf16[256,1024]{1,0:T(8,128)(2,1)}, u32[]{:S(2)}, u32[]{:S(2)}) collective-permute-start(bf16[256,1024]{1,0:T(8,128)(2,1)} %slice.99), channel_id=1, source_target_pairs={{0,8},{4,12},{8,0},{12,4},{1,9},{5,13},{9,1},{13,5},{2,10},{6,14},... | collective-permute-start | bytes 1572872 | tf_op jit(solution)/shard_map/ppermute | solution.py:23
  72.0 62.6 %collective-permute-start.18 = (bf16[256,1024]{1,0:T(8,128)(2,1)}, bf16[256,1024]{1,0:T(8,128)(2,1)}, u32[]{:S(2)}, u32[]{:S(2)}) collective-permute-start(bf16[256,1024]{1,0:T(8,128)(2,1)} %slice.100), channel_id=1, source_target_pairs={{0,8},{4,12},{8,0},{12,4},{1,9},{5,13},{9,1},{13,5},{2,10},{6,14},... | collective-permute-start | bytes 1572872 | tf_op jit(solution)/shard_map/ppermute | solution.py:23
  74.9 64.2 %collective-permute-start.16 = (bf16[256,1280]{1,0:T(8,128)(2,1)}, bf16[256,1280]{1,0:T(8,128)(2,1)}, u32[]{:S(2)}, u32[]{:S(2)}) collective-permute-start(bf16[256,1280]{1,0:T(8,128)(2,1)} %slice.101), channel_id=1, source_target_pairs={{0,4},{4,0},{8,12},{12,8},{1,5},{5,1},{9,13},{13,9},{2,6},{6,2},{1... | collective-permute-start | bytes 1966088 | tf_op jit(solution)/shard_map/ppermute | solution.py:23
  74.9 73.7 %collective-permute-start.19 = (bf16[256,1280]{1,0:T(8,128)(2,1)}, bf16[256,1280]{1,0:T(8,128)(2,1)}, u32[]{:S(2)}, u32[]{:S(2)}) collective-permute-start(bf16[256,1280]{1,0:T(8,128)(2,1)} %slice.101), channel_id=1, source_target_pairs={{0,8},{4,12},{8,0},{12,4},{1,9},{5,13},{9,1},{13,5},{2,10},{6,14},... | collective-permute-start | bytes 1966088 | tf_op jit(solution)/shard_map/ppermute | solution.py:23
  109.3 42.8 %collective-permute-start.20 = (bf16[2,2,3,64,256]{4,3,2,1,0:T(8,128)(2,1)}, bf16[2,2,3,64,256]{4,3,2,1,0:T(8,128)(2,1)}, u32[]{:S(2)}, u32[]{:S(2)}) collective-permute-start(bf16[2,2,3,64,256]{4,3,2,1,0:T(8,128)(2,1)} %get-tuple-element.27), channel_id=1, source_target_pairs={{0,1},{1,0},{2,3},{3,2},{4,5},{5,4},{6,7},{7,6},{8,9},{9,8},{10,11... | collective-permute-start | bytes 1179656 | tf_op jit(solution)/shard_map/ppermute | solution.py:23
  134.6 34.1 %collective-permute-start.24 = (bf16[2,2,4,64,256]{4,3,2,1,0:T(8,128)(2,1)}, bf16[2,2,4,64,256]{4,3,2,1,0:T(8,128)(2,1)}, u32[]{:S(2)}, u32[]{:S(2)}) collective-permute-start(bf16[2,2,4,64,256]{4,3,2,1,0:T(8,128)(2,1)} %get-tuple-element.29), channel_id=1, source_target_pairs={{0,1},{1,0},{2,3},{3,2},{4,5},{5,4},{6,7},{7,6},{8,9},{9,8},{10,11... | collective-permute-start | bytes 1572872 | tf_op jit(solution)/shard_map/ppermute | solution.py:23
  139.1 31.3 %collective-permute-start.27 = (bf16[2,2,4,64,256]{4,3,2,1,0:T(8,128)(2,1)}, bf16[2,2,4,64,256]{4,3,2,1,0:T(8,128)(2,1)}, u32[]{:S(2)}, u32[]{:S(2)}) collective-permute-start(bf16[2,2,4,64,256]{4,3,2,1,0:T(8,128)(2,1)} %get-tuple-element.31), channel_id=1, source_target_pairs={{0,1},{1,0},{2,3},{3,2},{4,5},{5,4},{6,7},{7,6},{8,9},{9,8},{10,11... | collective-permute-start | bytes 1572872 | tf_op jit(solution)/shard_map/ppermute | solution.py:23
  152.0 29.4 %collective-permute-start.30 = (bf16[2,2,5,64,256]{4,3,2,1,0:T(8,128)(2,1)}, bf16[2,2,5,64,256]{4,3,2,1,0:T(8,128)(2,1)}, u32[]{:S(2)}, u32[]{:S(2)}) collective-permute-start(bf16[2,2,5,64,256]{4,3,2,1,0:T(8,128)(2,1)} %get-tuple-element.33), channel_id=1, source_target_pairs={{0,1},{1,0},{2,3},{3,2},{4,5},{5,4},{6,7},{7,6},{8,9},{9,8},{10,11... | collective-permute-start | bytes 1966088 | tf_op jit(solution)/shard_map/ppermute | solution.py:23
  154.2 7.3 %collective-permute-start.21 = (bf16[1,2,3,64,256]{4,3,2,1,0:T(8,128)(2,1)S(1)}, bf16[1,2,3,64,256]{4,3,2,1,0:T(8,128)(2,1)S(1)}, u32[]{:S(2)}, u32[]{:S(2)}) collective-permute-start(bf16[1,2,3,64,256]{4,3,2,1,0:T(8,128)(2,1)S(1)} %get-tuple-element.50), channel_id=1, source_target_pairs={{0,2},{1,3},{2,0},{3,1},{4,6},{5,7},{6,4},{7,5},{8,10},{9,11},{10,... | collective-permute-start | bytes 589832 | tf_op jit(solution)/shard_map/ppermute | solution.py:23
  161.4 0.7 copy-start.19
  162.1 15.1 %collective-permute-start.7 = (bf16[2,2,256,256]{3,2,1,0:T(8,128)(2,1)}, bf16[2,2,256,256]{3,2,1,0:T(8,128)(2,1)}, u32[]{:S(2)}, u32[]{:S(2)}) collective-permute-start(bf16[2,2,256,256]{3,2,1,0:T(8,128)(2,1)} %pad_maximum_fusion.refs_6_.refs_2_), channel_id=1, source_target_pairs={{0,2},{1,3},{2,0},{3,1},{4,6},{5,7},{6,4},{7,5},{8,10},{9,11},{10,... | collective-permute-start | bytes 1572872 | tf_op jit(solution)/shard_map/ppermute | solution.py:23
  168.6 2.3 copy-start.12
  168.6 2.3 copy-start.20
  168.7 3.1 %copy-start.16 = (f32[2,2,4,64,256]{4,3,2,1,0:T(8,128)S(1)}, f32[2,2,4,64,256]{4,3,2,1,0:T(8,128)}, u32[]{:S(2)}) copy-start(f32[2,2,4,64,256]{4,3,2,1,0:T(8,128)} %get-tuple-element.30) | copy-start | bytes 3145732
  168.7 32.5 %collective-permute-start.38 = (bf16[2,2,32,4096]{3,2,1,0:T(8,128)(2,1)}, bf16[2,2,32,4096]{3,2,1,0:T(8,128)(2,1)S(1)}, u32[]{:S(2)}, u32[]{:S(2)}) collective-permute-start(bf16[2,2,32,4096]{3,2,1,0:T(8,128)(2,1)} %get-tuple-element.37), channel_id=1, source_target_pairs={{0,1},{1,0},{2,3},{3,2},{4,5},{5,4},{6,7},{7,6},{8,9},{9,8},{10,11... | collective-permute-start | bytes 3145736 | tf_op jit(solution)/shard_map/ppermute | solution.py:23
  170.3 6.9 %copy-start.3 = (bf16[2,2,256,256]{3,2,1,0:T(8,128)(2,1)S(1)}, bf16[2,2,256,256]{3,2,1,0:T(8,128)(2,1)}, u32[]{:S(2)}) copy-start(bf16[2,2,256,256]{3,2,1,0:T(8,128)(2,1)} %pad_maximum_fusion.refs_6_.refs_2_) | copy-start | bytes 1572868
  170.4 11.0 %collective-permute-start.25 = (bf16[1,2,4,64,256]{4,3,2,1,0:T(8,128)(2,1)S(1)}, bf16[1,2,4,64,256]{4,3,2,1,0:T(8,128)(2,1)S(1)}, u32[]{:S(2)}, u32[]{:S(2)}) collective-permute-start(bf16[1,2,4,64,256]{4,3,2,1,0:T(8,128)(2,1)S(1)} %get-tuple-element.48), channel_id=1, source_target_pairs={{0,2},{1,3},{2,0},{3,1},{4,6},{5,7},{6,4},{7,5},{8,10},{9,11},{10,... | collective-permute-start | bytes 786440 | tf_op jit(solution)/shard_map/ppermute | solution.py:23
  171.0 14.2 %copy-start.13 = (f32[2,2,5,64,256]{4,3,2,1,0:T(8,128)S(1)}, f32[2,2,5,64,256]{4,3,2,1,0:T(8,128)}, u32[]{:S(2)}) copy-start(f32[2,2,5,64,256]{4,3,2,1,0:T(8,128)} %get-tuple-element.32) | copy-start | bytes 3932164
  171.7 14.7 %copy-start.4 = (f32[2,2,16,64,256]{4,3,2,1,0:T(8,128)S(1)}, f32[2,2,16,64,256]{4,3,2,1,0:T(8,128)}, u32[]{:S(2)}) copy-start(f32[2,2,16,64,256]{4,3,2,1,0:T(8,128)} %get-tuple-element.34) | copy-start | bytes 12582916
  177.2 14.8 %collective-permute-start.8 = (bf16[2,2,256,256]{3,2,1,0:T(8,128)(2,1)S(1)}, bf16[2,2,256,256]{3,2,1,0:T(8,128)(2,1)S(1)}, u32[]{:S(2)}, u32[]{:S(2)}) collective-permute-start(bf16[2,2,256,256]{3,2,1,0:T(8,128)(2,1)S(1)} %copy-done.3), channel_id=1, source_target_pairs={{0,16},{16,0},{1,17},{17,1},{2,18},{18,2},{3,19},{19,3},{4,20},{20... | collective-permute-start | bytes 1572872 | tf_op jit(solution)/shard_map/ppermute | solution.py:23
  181.4 10.7 %collective-permute-start.10 = (bf16[2,2,256,256]{3,2,1,0:T(8,128)(2,1)S(1)}, bf16[2,2,256,256]{3,2,1,0:T(8,128)(2,1)S(1)}, u32[]{:S(2)}, u32[]{:S(2)}) collective-permute-start(bf16[2,2,256,256]{3,2,1,0:T(8,128)(2,1)S(1)} %copy-done.3), channel_id=1, source_target_pairs={{0,1},{1,0},{2,3},{3,2},{4,5},{5,4},{6,7},{7,6},{8,9},{9,8},{10,11... | collective-permute-start | bytes 1572872 | tf_op jit(solution)/shard_map/ppermute | solution.py:23
  181.4 18.3 %collective-permute-start.9 = (bf16[2,2,256,256]{3,2,1,0:T(8,128)(2,1)}, bf16[2,2,256,256]{3,2,1,0:T(8,128)(2,1)S(1)}, u32[]{:S(2)}, u32[]{:S(2)}) collective-permute-start(bf16[2,2,256,256]{3,2,1,0:T(8,128)(2,1)} %collective-permute-done.7.refs_7_.refs_3_), channel_id=1, source_target_pairs={{0,16},{16,0},{1,17},{17,1},{2,18},{18,2},{3,19},{19,3},{4,20},{20... | collective-permute-start | bytes 1572872 | tf_op jit(solution)/shard_map/ppermute | solution.py:23
  183.7 17.5 %collective-permute-start.28 = (bf16[1,2,4,64,256]{4,3,2,1,0:T(8,128)(2,1)S(1)}, bf16[1,2,4,64,256]{4,3,2,1,0:T(8,128)(2,1)S(1)}, u32[]{:S(2)}, u32[]{:S(2)}) collective-permute-start(bf16[1,2,4,64,256]{4,3,2,1,0:T(8,128)(2,1)S(1)} %get-tuple-element.46), channel_id=1, source_target_pairs={{0,2},{1,3},{2,0},{3,1},{4,6},{5,7},{6,4},{7,5},{8,10},{9,11},{10,... | collective-permute-start | bytes 786440 | tf_op jit(solution)/shard_map/ppermute | solution.py:23
  186.4 15.3 %copy-start.5 = (f32[2,2,32,4096]{3,2,1,0:T(8,128)S(1)}, f32[2,2,32,4096]{3,2,1,0:T(8,128)}, u32[]{:S(2)}) copy-start(f32[2,2,32,4096]{3,2,1,0:T(8,128)} %get-tuple-element.36) | copy-start | bytes 6291460
  192.0 11.0 %copy-start.6 = (bf16[2,2,256,256]{3,2,1,0:T(8,128)(2,1)}, bf16[2,2,256,256]{3,2,1,0:T(8,128)(2,1)S(1)}, u32[]{:S(2)}) copy-start(bf16[2,2,256,256]{3,2,1,0:T(8,128)(2,1)S(1)} %collective-permute-done.8.refs_8_.refs_4_) | copy-start | bytes 1572868
  192.0 21.0 %collective-permute-start.11 = (bf16[2,2,256,256]{3,2,1,0:T(8,128)(2,1)}, bf16[2,2,256,256]{3,2,1,0:T(8,128)(2,1)S(1)}, u32[]{:S(2)}, u32[]{:S(2)}) collective-permute-start(bf16[2,2,256,256]{3,2,1,0:T(8,128)(2,1)} %collective-permute-done.7.refs_7_.refs_3_), channel_id=1, source_target_pairs={{0,1},{1,0},{2,3},{3,2},{4,5},{5,4},{6,7},{7,6},{8,9},{9,8},{10,11... | collective-permute-start | bytes 1572872 | tf_op jit(solution)/shard_map/ppermute | solution.py:23
  192.0 11.0 %copy-start.7 = (bf16[2,2,256,256]{3,2,1,0:T(8,128)(2,1)}, bf16[2,2,256,256]{3,2,1,0:T(8,128)(2,1)S(1)}, u32[]{:S(2)}) copy-start(bf16[2,2,256,256]{3,2,1,0:T(8,128)(2,1)S(1)} %collective-permute-done.10.refs_10_.refs_6_) | copy-start | bytes 1572868
  192.0 21.0 %collective-permute-start.12 = (bf16[2,2,256,256]{3,2,1,0:T(8,128)(2,1)S(1)}, bf16[2,2,256,256]{3,2,1,0:T(8,128)(2,1)S(1)}, u32[]{:S(2)}, u32[]{:S(2)}) collective-permute-start(bf16[2,2,256,256]{3,2,1,0:T(8,128)(2,1)S(1)} %collective-permute-done.8.refs_8_.refs_4_), channel_id=1, source_target_pairs={{0,1},{1,0},{2,3},{3,2},{4,5},{5,4},{6,7},{7,6},{8,9},{9,8},{10,11... | collective-permute-start | bytes 1572872 | tf_op jit(solution)/shard_map/ppermute | solution.py:23
  199.6 3.4 %copy-start.8 = (bf16[2,2,256,256]{3,2,1,0:T(8,128)(2,1)}, bf16[2,2,256,256]{3,2,1,0:T(8,128)(2,1)S(1)}, u32[]{:S(2)}) copy-start(bf16[2,2,256,256]{3,2,1,0:T(8,128)(2,1)S(1)} %collective-permute-done.9.refs_9_.refs_5_) | copy-start | bytes 1572868
  199.6 9.3 %collective-permute-start.31 = (bf16[1,2,5,64,256]{4,3,2,1,0:T(8,128)(2,1)S(1)}, bf16[1,2,5,64,256]{4,3,2,1,0:T(8,128)(2,1)S(1)}, u32[]{:S(2)}, u32[]{:S(2)}) collective-permute-start(bf16[1,2,5,64,256]{4,3,2,1,0:T(8,128)(2,1)S(1)} %get-tuple-element.42), channel_id=1, source_target_pairs={{0,2},{1,3},{2,0},{3,1},{4,6},{5,7},{6,4},{7,5},{8,10},{9,11},{10,... | collective-permute-start | bytes 983048 | tf_op jit(solution)/shard_map/ppermute | solution.py:23
  201.1 13.9 %collective-permute-start.13 = (bf16[2,2,256,256]{3,2,1,0:T(8,128)(2,1)S(1)}, bf16[2,2,256,256]{3,2,1,0:T(8,128)(2,1)S(1)}, u32[]{:S(2)}, u32[]{:S(2)}) collective-permute-start(bf16[2,2,256,256]{3,2,1,0:T(8,128)(2,1)S(1)} %collective-permute-done.9.refs_9_.refs_5_), channel_id=1, source_target_pairs={{0,1},{1,0},{2,3},{3,2},{4,5},{5,4},{6,7},{7,6},{8,9},{9,8},{10,11... | collective-permute-start | bytes 1572872 | tf_op jit(solution)/shard_map/ppermute | solution.py:23
  201.1 39.4 %collective-permute-start.37 = (bf16[1,2,16,64,256]{4,3,2,1,0:T(8,128)(2,1)}, bf16[1,2,16,64,256]{4,3,2,1,0:T(8,128)(2,1)}, u32[]{:S(2)}, u32[]{:S(2)}) collective-permute-start(bf16[1,2,16,64,256]{4,3,2,1,0:T(8,128)(2,1)} %get-tuple-element.38), channel_id=1, source_target_pairs={{0,2},{1,3},{2,0},{3,1},{4,6},{5,7},{6,4},{7,5},{8,10},{9,11},{10,... | collective-permute-start | bytes 3145736 | tf_op jit(solution)/shard_map/ppermute | solution.py:23
  209.0 31.5 %collective-permute-start.39 = (bf16[1,2,32,4096]{3,2,1,0:T(8,128)(2,1)}, bf16[1,2,32,4096]{3,2,1,0:T(8,128)(2,1)}, u32[]{:S(2)}, u32[]{:S(2)}) collective-permute-start(bf16[1,2,32,4096]{3,2,1,0:T(8,128)(2,1)} %get-tuple-element.40), channel_id=1, source_target_pairs={{0,2},{1,3},{2,0},{3,1},{4,6},{5,7},{6,4},{7,5},{8,10},{9,11},{10,... | collective-permute-start | bytes 1572872 | tf_op jit(solution)/shard_map/ppermute | solution.py:23
  213.0 2.0 copy-start.9
  213.0 16.9 %collective-permute-start.26 = (bf16[4,64,256]{2,1,0:T(8,128)(2,1)}, bf16[4,64,256]{2,1,0:T(8,128)(2,1)}, u32[]{:S(2)}, u32[]{:S(2)}) collective-permute-start(bf16[4,64,256]{2,1,0:T(8,128)(2,1)} %get-tuple-element.57), channel_id=1, source_target_pairs={{0,4},{4,0},{8,12},{12,8},{1,5},{5,1},{9,13},{13,9},{2,6},{6,2},{1... | collective-permute-start | bytes 393224 | tf_op jit(solution)/shard_map/ppermute | solution.py:23
  213.0 2.0 copy-start.10
  213.1 18.8 %collective-permute-start.29 = (bf16[4,64,256]{2,1,0:T(8,128)(2,1)}, bf16[4,64,256]{2,1,0:T(8,128)(2,1)}, u32[]{:S(2)}, u32[]{:S(2)}) collective-permute-start(bf16[4,64,256]{2,1,0:T(8,128)(2,1)} %get-tuple-element.55), channel_id=1, source_target_pairs={{0,4},{4,0},{8,12},{12,8},{1,5},{5,1},{9,13},{13,9},{2,6},{6,2},{1... | collective-permute-start | bytes 393224 | tf_op jit(solution)/shard_map/ppermute | solution.py:23
  215.1 0.8 copy-start.11
  215.9 16.7 %collective-permute-start.33 = (bf16[4,64,256]{2,1,0:T(8,128)(2,1)}, bf16[4,64,256]{2,1,0:T(8,128)(2,1)}, u32[]{:S(2)}, u32[]{:S(2)}) collective-permute-start(bf16[4,64,256]{2,1,0:T(8,128)(2,1)} %get-tuple-element.56), channel_id=1, source_target_pairs={{0,8},{4,12},{8,0},{12,4},{1,9},{5,13},{9,1},{13,5},{2,10},{6,14},... | collective-permute-start | bytes 393224 | tf_op jit(solution)/shard_map/ppermute | solution.py:23
  229.9 22.8 %collective-permute-start.22 = (bf16[3,64,256]{2,1,0:T(8,128)(2,1)}, bf16[3,64,256]{2,1,0:T(8,128)(2,1)}, u32[]{:S(2)}, u32[]{:S(2)}) collective-permute-start(bf16[3,64,256]{2,1,0:T(8,128)(2,1)} %get-tuple-element.59), channel_id=1, source_target_pairs={{0,4},{4,0},{8,12},{12,8},{1,5},{5,1},{9,13},{13,9},{2,6},{6,2},{1... | collective-permute-start | bytes 294920 | tf_op jit(solution)/shard_map/ppermute | solution.py:23
  231.9 20.9 %collective-permute-start.23 = (bf16[3,64,256]{2,1,0:T(8,128)(2,1)}, bf16[3,64,256]{2,1,0:T(8,128)(2,1)}, u32[]{:S(2)}, u32[]{:S(2)}) collective-permute-start(bf16[3,64,256]{2,1,0:T(8,128)(2,1)} %get-tuple-element.58), channel_id=1, source_target_pairs={{0,8},{4,12},{8,0},{12,4},{1,9},{5,13},{9,1},{13,5},{2,10},{6,14},... | collective-permute-start | bytes 294920 | tf_op jit(solution)/shard_map/ppermute | solution.py:23
  232.6 17.1 %collective-permute-start.34 = (bf16[4,64,256]{2,1,0:T(8,128)(2,1)}, bf16[4,64,256]{2,1,0:T(8,128)(2,1)}, u32[]{:S(2)}, u32[]{:S(2)}) collective-permute-start(bf16[4,64,256]{2,1,0:T(8,128)(2,1)} %get-tuple-element.54), channel_id=1, source_target_pairs={{0,8},{4,12},{8,0},{12,4},{1,9},{5,13},{9,1},{13,5},{2,10},{6,14},... | collective-permute-start | bytes 393224 | tf_op jit(solution)/shard_map/ppermute | solution.py:23
  240.5 9.1 %collective-permute-start.32 = (bf16[5,64,256]{2,1,0:T(8,128)(2,1)}, bf16[5,64,256]{2,1,0:T(8,128)(2,1)}, u32[]{:S(2)}, u32[]{:S(2)}) collective-permute-start(bf16[5,64,256]{2,1,0:T(8,128)(2,1)} %get-tuple-element.53), channel_id=1, source_target_pairs={{0,4},{4,0},{8,12},{12,8},{1,5},{5,1},{9,13},{13,9},{2,6},{6,2},{1... | collective-permute-start | bytes 491528 | tf_op jit(solution)/shard_map/ppermute | solution.py:23
  240.5 9.2 %collective-permute-start.35 = (bf16[5,64,256]{2,1,0:T(8,128)(2,1)}, bf16[5,64,256]{2,1,0:T(8,128)(2,1)}, u32[]{:S(2)}, u32[]{:S(2)}) collective-permute-start(bf16[5,64,256]{2,1,0:T(8,128)(2,1)} %get-tuple-element.52), channel_id=1, source_target_pairs={{0,8},{4,12},{8,0},{12,4},{1,9},{5,13},{9,1},{13,5},{2,10},{6,14},... | collective-permute-start | bytes 491528 | tf_op jit(solution)/shard_map/ppermute | solution.py:23
